TPU v7x, 32 devices: a whole 2x2x4 slice. The times are simulated.
32 devices in a mesh: dp: 8 (over z, y), tensor: 4 (over x, core).
Axes of the slice: x: 2, y: 2, z: 4, core: 2. Of those that a mesh axis runs over, the one named last changes fastest.
Arguments:
- tokens: bfloat16 [16, 1024, 768], P('dp', 'tensor'), may hold values from -6 to 6
- lengths: int32 [16], P('dp'), may hold values from 256 to 1024, as said below
- mem_mask: int32 [16, 2, 2], P('dp'), may hold values 0 or 1
- cotangent: bfloat16 [16, 1024, 768], P('dp', 'tensor'), may hold values from -6 to 6
- w_qkv: bfloat16 [3, 768, 768], P(None, 'dp', 'tensor'), may hold values from -0.21875 to 0.21875
- w_gauss: bfloat16 [2, 12, 64], P(None, 'tensor', 'dp'), may hold values from -0.75 to 0.75
- w_out: bfloat16 [768, 768], P('tensor', 'dp'), may hold values from -0.625 to 0.625
- ln_gain: float32 [768], P(('dp', 'tensor')), may hold values from 0.5 to 1.5
- ln_bias: float32 [768], P(('dp', 'tensor')), may hold values from -1.5 to 1.5
- w_up: bfloat16 [768, 3072], P('dp', 'tensor'), may hold values from -0.21875 to 0.21875
- w_down: bfloat16 [3072, 768], P('tensor', 'dp'), may hold values from -0.109375 to 0.109375
Outputs:
- output: float32 [16, 1024, 768], P('dp', 'tensor')
- grad_tokens: float32 [16, 1024, 768], P('dp', 'tensor')
- grad_qkv: float32 [3, 768, 768], P(None, 'dp', 'tensor')
- grad_gauss: float32 [2, 12, 64], P(None, 'tensor', 'dp')
- grad_out: float32 [768, 768], P('tensor', 'dp')
- grad_gain: float32 [768], P(('dp', 'tensor'))
- grad_bias: float32 [768], P(('dp', 'tensor'))
- grad_up: float32 [768, 3072], P('dp', 'tensor')
- grad_down: float32 [3072, 768], P('tensor', 'dp')
Inputs may be any that keep to these rules, and one draw needn't show every extreme that they name: `lengths`: sequence 0 uses all 1024 slots.
All inputs are finite; a program needn't handle non-finite values. No bound on the sum of `mem_mask` on one device may be relied on, other than what follows from the above.
Results may differ from a plain program's by a relative error of at most 0.014.
The roundings to bfloat16 on the way count: a program that leaves them out, or rounds other values in their place, can miss the bound.
Values may be sent and summed in bfloat16 or wider, within the bound.
No kernel may reach another device: no remote copies, remote signals or barrier semaphores. Data moves between devices by JAX's collectives and lax.ppermute only.
A program may use at most 192 MiB of HBM per device.

v0:
```python
import jax
import jax.numpy as jnp
from jax import lax
from jax.sharding import PartitionSpec as P

DH = 64
NB = 256
SEGL = 512


highest = lax.Precision.HIGHEST


def ridge_matrix(basis_count, sample_count):
    centres = (jnp.arange(basis_count, dtype=jnp.float32) + 0.5) / basis_count
    samples = (jnp.arange(sample_count, dtype=jnp.float32) + 0.5) / sample_count
    spacing = 1.0 / basis_count
    basis_rows = jnp.exp(-0.5 * ((samples[None, :] - centres[:, None]) / spacing) ** 2)
    gram_matrix = jnp.dot(basis_rows, basis_rows.T, precision=highest) + 0.5 * jnp.eye(
        basis_count, dtype=jnp.float32
    )
    factor = jnp.linalg.cholesky(gram_matrix)
    forward_solve = lax.linalg.triangular_solve(factor, basis_rows, left_side=True, lower=True)
    return lax.linalg.triangular_solve(
        factor, forward_solve, left_side=True, lower=True, transpose_a=True
    )


def memory_pairs(visible):
    segment_ids = jnp.arange(visible.shape[0])
    return jnp.where(segment_ids[None, :] < segment_ids[:, None], visible.astype(jnp.float32), 0.0)


def project(left, right):
    return jnp.dot(left, right, preferred_element_type=jnp.float32)


def allowed_mask(validity, blocks):
    positions = jnp.arange(SEGL)
    causal = positions[None, :] <= positions[:, None]
    diagonal = positions[None, :] == positions[:, None]
    live_keys = validity.reshape(blocks, SEGL)
    return causal[None, None] & ((live_keys[:, None, None, :] > 0.5) | diagonal[None, None])


def density_of(mean_logit, var_logit, basis_count):
    basis_var = (1.0 / basis_count) ** 2
    centre_pos = jax.nn.sigmoid(mean_logit)
    spread_sq = 0.05 * jax.nn.softplus(var_logit) + basis_var
    centres = (jnp.arange(basis_count, dtype=jnp.float32) + 0.5) / basis_count
    return jnp.sqrt(basis_var / spread_sq)[..., None] * jnp.exp(
        -0.5 * (centre_pos[..., None] - centres) ** 2 / spread_sq[..., None]
    )


def attention_scores(query_heads, key_heads, validity, blocks):
    scores = jnp.einsum(
        "bqhd,bkhd->bhqk", query_heads, key_heads, preferred_element_type=jnp.float32
    ) * DH ** (-0.5)
    return jnp.where(allowed_mask(validity, blocks), scores, -1e30)


def mix_forward(whole, weight_qkv, gaussian, weight_out, validity, pairing, ridge_fit):
    point_count = whole.shape[0]
    blocks = point_count // SEGL
    columns = weight_qkv.shape[2]
    head_count = columns // DH
    basis_count = ridge_fit.shape[0]
    qkv = jnp.einsum("pd,tdc->tpc", whole, weight_qkv, preferred_element_type=jnp.float32).astype(
        jnp.bfloat16
    )
    query_heads = qkv[0].reshape(blocks, SEGL, head_count, DH)
    key_heads = qkv[1].reshape(blocks, SEGL, head_count, DH)
    value_heads = qkv[2].reshape(blocks, SEGL, head_count, DH)
    scores = attention_scores(query_heads, key_heads, validity, blocks)
    row_max = jnp.max(scores, axis=-1, keepdims=True)
    exponent = jnp.exp(scores - row_max)
    total = jnp.sum(exponent, axis=-1, keepdims=True)
    log_total = row_max + jnp.log(total)
    attn = (exponent / total).astype(jnp.bfloat16)
    attended = jnp.einsum("bhqk,bkhd->bqhd", attn, value_heads, preferred_element_type=jnp.float32)
    mean_logit = jnp.einsum(
        "bqhd,hd->bqh", query_heads, gaussian[0], preferred_element_type=jnp.float32
    )
    var_logit = jnp.einsum(
        "bqhd,hd->bqh", query_heads, gaussian[1], preferred_element_type=jnp.float32
    )
    density = density_of(mean_logit, var_logit, basis_count).astype(jnp.bfloat16)
    masked = (qkv[2].astype(jnp.float32) * validity[:, None]).reshape(blocks, SEGL, columns)
    counts = jnp.maximum(jnp.sum(pairing, axis=1), 1.0)
    pooled = (
        jnp.einsum("sj,jpc->spc", pairing, masked, precision=highest) / counts[:, None, None]
    ).astype(jnp.bfloat16)
    coef = jnp.einsum("np,spc->snc", ridge_fit, pooled, preferred_element_type=jnp.float32).astype(
        jnp.bfloat16
    )
    recalled = jnp.einsum(
        "bqhn,bnhd->bqhd",
        density,
        coef.reshape(blocks, basis_count, head_count, DH),
        preferred_element_type=jnp.float32,
    )
    heads_out = (attended + recalled).reshape(point_count, columns).astype(jnp.bfloat16)
    mixed_part = project(heads_out, weight_out)
    return (mixed_part, (qkv, log_total, mean_logit, var_logit, density, coef, heads_out))


def mix_backward(
    whole, weight_qkv, gaussian, weight_out, validity, pairing, ridge_fit, saved, mix_grad
):
    qkv, log_total, mean_logit, var_logit, density, coef, heads_out = saved
    point_count = whole.shape[0]
    blocks = point_count // SEGL
    columns = weight_qkv.shape[2]
    head_count = columns // DH
    basis_count = ridge_fit.shape[0]
    grad_out = jnp.einsum("pc,pd->cd", heads_out, mix_grad, preferred_element_type=jnp.float32)
    head_grad = jnp.einsum(
        "pd,cd->pc", mix_grad, weight_out, preferred_element_type=jnp.float32
    ).astype(jnp.bfloat16)
    head_grad = head_grad.reshape(blocks, SEGL, head_count, DH)
    coef_heads = coef.reshape(blocks, basis_count, head_count, DH)
    density_grad = jnp.einsum(
        "bqhd,bnhd->bqhn", head_grad, coef_heads, preferred_element_type=jnp.float32
    )
    coef_grad = jnp.einsum(
        "bqhn,bqhd->bnhd", density, head_grad, preferred_element_type=jnp.float32
    ).astype(jnp.bfloat16)
    coef_grad = coef_grad.reshape(blocks, basis_count, columns)
    pooled_grad = jnp.einsum(
        "np,snc->spc", ridge_fit, coef_grad, preferred_element_type=jnp.float32
    )
    counts = jnp.maximum(jnp.sum(pairing, axis=1), 1.0)
    masked_grad = jnp.einsum(
        "sj,spc->jpc", pairing, pooled_grad / counts[:, None, None], precision=highest
    )
    masked_grad = masked_grad.reshape(point_count, columns) * validity[:, None]
    _, density_back = jax.vjp(
        lambda mean_in, var_in: density_of(mean_in, var_in, basis_count), mean_logit, var_logit
    )
    mean_grad, var_grad = density_back(density_grad)
    query_heads = qkv[0].reshape(blocks, SEGL, head_count, DH)
    key_heads = qkv[1].reshape(blocks, SEGL, head_count, DH)
    value_heads = qkv[2].reshape(blocks, SEGL, head_count, DH)
    probs = jnp.exp(attention_scores(query_heads, key_heads, validity, blocks) - log_total)
    attn = probs.astype(jnp.bfloat16)
    value_grad = jnp.einsum("bhqk,bqhd->bkhd", attn, head_grad, preferred_element_type=jnp.float32)
    prob_grad = jnp.einsum(
        "bqhd,bkhd->bhqk", head_grad, value_heads, preferred_element_type=jnp.float32
    )
    score_grad = (probs * (prob_grad - jnp.sum(prob_grad * probs, axis=-1, keepdims=True))).astype(
        jnp.bfloat16
    )
    scale = DH ** (-0.5)
    gauss_float = gaussian.astype(jnp.float32)
    query_grad = (
        jnp.einsum("bhqk,bkhd->bqhd", score_grad, key_heads, preferred_element_type=jnp.float32)
        * scale
    )
    query_grad = (
        query_grad + mean_grad[..., None] * gauss_float[0] + var_grad[..., None] * gauss_float[1]
    )
    key_grad = (
        jnp.einsum("bhqk,bqhd->bkhd", score_grad, query_heads, preferred_element_type=jnp.float32)
        * scale
    )
    value_total = value_grad.reshape(point_count, columns) + masked_grad
    qkv_grad = jnp.stack(
        [
            query_grad.reshape(point_count, columns),
            key_grad.reshape(point_count, columns),
            value_total,
        ]
    ).astype(jnp.bfloat16)
    query_float = query_heads.astype(jnp.float32)
    gauss_grad = jnp.stack(
        [
            jnp.einsum("bqhd,bqh->hd", query_float, mean_grad, precision=highest),
            jnp.einsum("bqhd,bqh->hd", query_float, var_grad, precision=highest),
        ]
    )
    grad_qkv = jnp.einsum("pd,tpc->tdc", whole, qkv_grad, preferred_element_type=jnp.float32)
    whole_grad = jnp.einsum("tpc,tdc->pd", qkv_grad, weight_qkv, preferred_element_type=jnp.float32)
    return (whole_grad, grad_qkv, gauss_grad, grad_out)


def layer_norm(residual, norm_gain, norm_bias):
    centred = residual - jnp.mean(residual, axis=-1, keepdims=True)
    return (
        centred * lax.rsqrt(jnp.mean(centred * centred, axis=-1, keepdims=True) + 1e-05) * norm_gain
        + norm_bias
    )


def gelu_tanh(value):
    return jax.nn.gelu(value, approximate=True)


def feed_forward(normed, weight_up, weight_down):
    pre = project(normed, weight_up)
    hidden = gelu_tanh(pre).astype(jnp.bfloat16)
    return (project(hidden, weight_down), (pre, hidden))


def feed_backward(normed, weight_up, weight_down, saved, seed):
    pre, hidden = saved
    grad_down = jnp.einsum("pf,pd->fd", hidden, seed, preferred_element_type=jnp.float32)
    hidden_grad = (
        jnp.einsum("pd,fd->pf", seed, weight_down, preferred_element_type=jnp.float32)
        .astype(jnp.bfloat16)
        .astype(jnp.float32)
    )
    _, gelu_back = jax.vjp(gelu_tanh, pre)
    pre_grad = gelu_back(hidden_grad)[0].astype(jnp.bfloat16)
    grad_up = jnp.einsum("pd,pf->df", normed, pre_grad, preferred_element_type=jnp.float32)
    normed_part = jnp.einsum("pf,df->pd", pre_grad, weight_up, preferred_element_type=jnp.float32)
    return (normed_part, grad_up, grad_down)


def local(
    tokens, lengths, mem_mask, cotangent, w_qkv, w_gauss, w_out, ln_gain, ln_bias, w_up, w_down
):
    micro_count = tokens.shape[0]
    row_count = tokens.shape[1]
    rank_count = lax.axis_size("tensor")
    point_count = row_count * rank_count
    row_start = lax.axis_index("tensor") * row_count
    ridge_fit = ridge_matrix(NB, SEGL).astype(jnp.bfloat16)
    norm_gain, norm_bias = (
        lax.all_gather(ln_gain, ("dp", "tensor"), axis=0, tiled=True),
        lax.all_gather(ln_bias, ("dp", "tensor"), axis=0, tiled=True),
    )

    def prepare(micro_step):
        validity = (jnp.arange(point_count) < lengths[micro_step]).astype(jnp.float32)
        return (validity, memory_pairs(mem_mask[micro_step]))

    kept_state = []
    outputs = []
    for micro_step in range(micro_count):
        weights = (
            lax.all_gather(w_qkv, "dp", axis=1, tiled=True),
            lax.all_gather(w_gauss, "dp", axis=2, tiled=True),
            lax.all_gather(w_out, "dp", axis=1, tiled=True),
            lax.all_gather(w_up, "dp", axis=0, tiled=True),
            lax.all_gather(w_down, "dp", axis=1, tiled=True),
        )
        validity, pairing = prepare(micro_step)
        whole = lax.all_gather(tokens[micro_step], "tensor", axis=0, tiled=True)
        mixed_part, mix_saved = mix_forward(
            whole, weights[0], weights[1], weights[2], validity, pairing, ridge_fit
        )
        mixed = lax.psum_scatter(mixed_part, "tensor", scatter_dimension=0, tiled=True)
        residual = tokens[micro_step].astype(jnp.float32) + mixed
        normed_own = layer_norm(residual, norm_gain, norm_bias).astype(jnp.bfloat16)
        normed = lax.all_gather(normed_own, "tensor", axis=0, tiled=True)
        fed_part, feed_saved = feed_forward(normed, weights[3], weights[4])
        fed = lax.psum_scatter(fed_part, "tensor", scatter_dimension=0, tiled=True)
        outputs.append(residual + fed)
        kept_state.append((whole, residual, normed, None, None, None))
    weight_totals = None
    gain_total = jnp.zeros_like(norm_gain)
    bias_total = jnp.zeros_like(norm_bias)
    input_grads = []
    for micro_step in range(micro_count):
        whole, residual, normed, weights, mix_saved, feed_saved = kept_state[micro_step]
        validity, pairing = prepare(micro_step)
        weights = (
            lax.all_gather(w_qkv, "dp", axis=1, tiled=True),
            lax.all_gather(w_gauss, "dp", axis=2, tiled=True),
            lax.all_gather(w_out, "dp", axis=1, tiled=True),
            lax.all_gather(w_up, "dp", axis=0, tiled=True),
            lax.all_gather(w_down, "dp", axis=1, tiled=True),
        )
        _, mix_saved = mix_forward(
            whole, weights[0], weights[1], weights[2], validity, pairing, ridge_fit
        )
        _, feed_saved = feed_forward(normed, weights[3], weights[4])
        own_valid = lax.dynamic_slice_in_dim(validity, row_start, row_count)
        seed_rows = (cotangent[micro_step].astype(jnp.float32) * own_valid[:, None]).astype(
            jnp.bfloat16
        )
        seed_whole = lax.all_gather(seed_rows, "tensor", axis=0, tiled=True)
        normed_part, grad_up_part, grad_down_part = feed_backward(
            normed, weights[3], weights[4], feed_saved, seed_whole
        )
        normed_grad = lax.psum_scatter(normed_part, "tensor", scatter_dimension=0, tiled=True)
        normed_grad = normed_grad.astype(jnp.bfloat16).astype(jnp.float32)
        _, norm_back = jax.vjp(layer_norm, residual, norm_gain, norm_bias)
        resid_from_norm, gain_part, bias_part = norm_back(normed_grad)
        resid_grad = seed_rows.astype(jnp.float32) + resid_from_norm
        resid_whole = lax.all_gather(resid_grad.astype(jnp.bfloat16), "tensor", axis=0, tiled=True)
        whole_grad, grad_qkv_part, grad_gauss_part, grad_out_part = mix_backward(
            whole,
            weights[0],
            weights[1],
            weights[2],
            validity,
            pairing,
            ridge_fit,
            mix_saved,
            resid_whole,
        )
        input_part = lax.psum_scatter(whole_grad, "tensor", scatter_dimension=0, tiled=True)
        input_grads.append(input_part + resid_grad)
        step_grads = (grad_qkv_part, grad_gauss_part, grad_out_part, grad_up_part, grad_down_part)
        if weight_totals is None:
            weight_totals = step_grads
        else:
            weight_totals = tuple((total + part for total, part in zip(weight_totals, step_grads)))
        gain_total = gain_total + gain_part
        bias_total = bias_total + bias_part
    summed = (
        lax.psum_scatter(weight_totals[0], "dp", scatter_dimension=1, tiled=True),
        lax.psum_scatter(weight_totals[1], "dp", scatter_dimension=2, tiled=True),
        lax.psum_scatter(weight_totals[2], "dp", scatter_dimension=1, tiled=True),
        lax.psum_scatter(weight_totals[3], "dp", scatter_dimension=0, tiled=True),
        lax.psum_scatter(weight_totals[4], "dp", scatter_dimension=1, tiled=True),
    )
    norm_sums = (
        lax.psum_scatter(gain_total, ("dp", "tensor"), scatter_dimension=0, tiled=True),
        lax.psum_scatter(bias_total, ("dp", "tensor"), scatter_dimension=0, tiled=True),
    )
    output = jnp.stack(outputs)
    grad_tokens = jnp.stack(input_grads)
    return (
        output,
        grad_tokens,
        summed[0],
        summed[1],
        summed[2],
        norm_sums[0],
        norm_sums[1],
        summed[3],
        summed[4],
    )


def solution(mesh):
    return jax.shard_map(
        local,
        mesh=mesh,
        in_specs=(
            P("dp", "tensor", None),
            P("dp"),
            P("dp", None, None),
            P("dp", "tensor", None),
            P(None, "dp", "tensor"),
            P(None, "tensor", "dp"),
            P("tensor", "dp"),
            P(("dp", "tensor")),
            P(("dp", "tensor")),
            P("dp", "tensor"),
            P("tensor", "dp"),
        ),
        out_specs=(
            P("dp", "tensor", None),
            P("dp", "tensor", None),
            P(None, "dp", "tensor"),
            P(None, "tensor", "dp"),
            P("tensor", "dp"),
            P(("dp", "tensor")),
            P(("dp", "tensor")),
            P("dp", "tensor"),
            P("tensor", "dp"),
        ),
        check_vma=False,
    )
```

profile of v0, /device:TPU:0, one launch (start us, length us, event | category | flops | bytes accessed | tf_op | source)
XLA Modules:
  0.0 1016.8 jit_solution(15015933361610988029)
XLA Ops:
  12.5 11.7 %cholesky.49 = f32[128,128]{1,0:T(8,128)S(1)} custom-call(f32[128,128]{1,0:T(8,128)S(1)} %cholesky.115), custom_call_target="Cholesky" | custom-call | tf_op jit(solution)/shard_map/jit(cholesky)/cholesky | solution.py:22
  34.5 11.7 %cholesky.103 = f32[128,128]{1,0:T(8,128)S(1)} custom-call(f32[128,128]{1,0:T(8,128)S(1)} %convolution_subtract_fusion.2), custom_call_target="Cholesky" | custom-call | tf_op jit(solution)/shard_map/jit(cholesky)/cholesky | solution.py:22
  52.7 19.7 %custom-call.17 = f32[2,128,128]{1,2,0:T(8,128)S(1)} custom-call(f32[2,128,128]{2,1,0:T(8,128)S(1)} %get-tuple-element.24), custom_call_target="InvertDiagBlocksLowerTriangular" | custom-call | tf_op jit(solution)/shard_map/triangular_solve | solution.py:24
  74.8 32.4 %all_gather.62 = bf16[2,3,64]{1,0,2:T(2,128)(2,1)S(1)} all-gather(bf16[2,3,8]{1,0,2:T(2,128)(2,1)S(1)} %copy.175), channel_id=1, replica_groups=mesh['dp'=8,'tensor'=4] {'dp'}, dimensions={2}, use_global_device_ids=true | all-gather | bytes 864 | tf_op jit(solution)/shard_map/all_gather | solution.py:243
  108.0 31.2 %all_gather.63 = bf16[192,768]{0,1:T(8,128)(2,1)S(1)} all-gather(bf16[192,96]{0,1:T(8,128)(2,1)S(1)} %copy.180), channel_id=1, replica_groups=mesh['dp'=8,'tensor'=4] {'dp'}, dimensions={1}, use_global_device_ids=true | all-gather | bytes 331776 | tf_op jit(solution)/shard_map/all_gather | solution.py:244
  145.6 38.4 %all_gather.60 = bf16[3,768,192]{2,0,1:T(4,128)(2,1)S(1)} all-gather(bf16[3,96,192]{2,0,1:T(4,128)(2,1)S(1)} %copy.167), channel_id=1, replica_groups=mesh['dp'=8,'tensor'=4] {'dp'}, dimensions={1}, use_global_device_ids=true | all-gather | bytes 995328 | tf_op jit(solution)/shard_map/all_gather | solution.py:242
  239.9 41.4 %all-reduce.7 = (f32[768]{0:T(1024)S(1)}, f32[768]{0:T(1024)S(1)}) all-reduce(f32[768]{0:T(1024)S(1)} %dynamic-update-slice.12, f32[768]{0:T(1024)S(1)} %dynamic-update-slice.11), channel_id=1, replica_groups=mesh['dp'=8,'tensor'=4] {'dp','tensor'}, use_global_device_ids=true, to_apply=%add.2 | all-reduce | flops 1536 | bytes 12288
  281.4 17.3 %reduce-scatter.18.cloned.1.call-done = f32[256,768]{1,0:T(8,128)} async-done(((f32[1024,768]{1,0:T(8,128)}), f32[256,768]{1,0:T(8,128)}) %reduce-scatter.18.cloned.1.call-update) | async-done | bytes 786448 | tf_op jit(solution)/shard_map/reduce_scatter | solution.py:253
  306.8 14.7 %all-gather.19.cloned.1.call-done = bf16[1024,768]{1,0:T(8,128)(2,1)} async-done(((bf16[256,768]{1,0:T(8,128)(2,1)}), bf16[1024,768]{1,0:T(8,128)(2,1)}) %all-gather.19.cloned.1.call-update) | async-done | bytes 1572880 | tf_op jit(solution)/shard_map/all_gather | solution.py:256
  326.4 38.6 %all-gather.17.cloned.1.call-done = bf16[768,768]{0,1:T(8,128)(2,1)} async-done(((bf16[768,96]{0,1:T(8,128)(2,1)}), bf16[768,768]{0,1:T(8,128)(2,1)}) %all-gather.17.cloned.1.call-update) | async-done | bytes 1179664 | tf_op jit(solution)/shard_map/all_gather | solution.py:246
  365.0 19.5 %all-gather.25.cloned.1.call-done = bf16[1024,768]{1,0:T(8,128)(2,1)} async-done(((bf16[256,768]{1,0:T(8,128)(2,1)}), bf16[1024,768]{1,0:T(8,128)(2,1)}) %all-gather.25.cloned.1.call-update) | async-done | bytes 1572880 | tf_op jit(solution)/shard_map/all_gather | solution.py:283
  394.8 11.3 %all-gather.13.cloned.1.call-done = bf16[1024,768]{1,0:T(8,128)(2,1)} async-done(((bf16[256,768]{1,0:T(8,128)(2,1)}), bf16[1024,768]{1,0:T(8,128)(2,1)}) %all-gather.13.cloned.1.call-update) | async-done | bytes 1572880 | tf_op jit(solution)/shard_map/all_gather | solution.py:256
  410.9 16.4 %all-gather.21.cloned.1.call-done = bf16[1024,768]{1,0:T(8,128)(2,1)} async-done(((bf16[256,768]{1,0:T(8,128)(2,1)}), bf16[1024,768]{1,0:T(8,128)(2,1)}) %all-gather.21.cloned.1.call-update) | async-done | bytes 1572880 | tf_op jit(solution)/shard_map/all_gather | solution.py:283
  449.5 17.9 %reduce-scatter.30.cloned.1.call-done = f32[256,768]{1,0:T(8,128)} async-done(((f32[1024,768]{1,0:T(8,128)}), f32[256,768]{1,0:T(8,128)}) %reduce-scatter.30.cloned.1.call-update) | async-done | bytes 786448 | tf_op jit(solution)/shard_map/reduce_scatter | solution.py:287
  467.4 40.2 %reduce-scatter.26.cloned.1.call-done = f32[256,768]{1,0:T(8,128)} async-done(((f32[1024,768]{1,0:T(8,128)}), f32[256,768]{1,0:T(8,128)}) %reduce-scatter.26.cloned.1.call-update) | async-done | bytes 786448 | tf_op jit(solution)/shard_map/reduce_scatter | solution.py:287
  512.2 35.5 %reduce-scatter.20.cloned.1.call-done = f32[256,768]{1,0:T(8,128)} async-done(((f32[1024,768]{1,0:T(8,128)}), f32[256,768]{1,0:T(8,128)}) %reduce-scatter.20.cloned.1.call-update) | async-done | bytes 786448 | tf_op jit(solution)/shard_map/reduce_scatter | solution.py:258
  547.7 40.3 %reduce-scatter.24.cloned.1.call-done = f32[256,768]{1,0:T(8,128)} async-done(((f32[1024,768]{1,0:T(8,128)}), f32[256,768]{1,0:T(8,128)}) %reduce-scatter.24.cloned.1.call-update) | async-done | bytes 786448 | tf_op jit(solution)/shard_map/reduce_scatter | solution.py:258
  598.0 15.7 %all-gather.27.cloned.1.call-done = bf16[1024,768]{1,0:T(8,128)(2,1)} async-done(((bf16[256,768]{1,0:T(8,128)(2,1)}), bf16[1024,768]{1,0:T(8,128)(2,1)}) %all-gather.27.cloned.1.call-update) | async-done | bytes 1572880 | tf_op jit(solution)/shard_map/all_gather | solution.py:292
  728.2 39.6 %all-reduce.6 = (f32[768]{0:T(1024)S(1)}, f32[768]{0:T(1024)S(1)}) all-reduce(f32[768]{0:T(1024)S(1)} %add.371, f32[768]{0:T(1024)S(1)} %add.372), channel_id=15, replica_groups=mesh['dp'=8,'tensor'=4] {'dp','tensor'}, use_global_device_ids=true, to_apply=%region_39.41.clone | all-reduce | flops 1536 | bytes 12288
  774.8 21.0 %all-reduce.3 = f32[2,3,64]{2,1,0:T(4,128)S(1)} all-reduce(f32[2,3,64]{2,1,0:T(4,128)S(1)} %maximum_add_fusion), channel_id=13, replica_groups=mesh['dp'=8,'tensor'=4] {'dp'}, use_global_device_ids=true, to_apply=%region_35.37.clone | all-reduce | flops 384 | bytes 3072
  800.0 21.7 %reduce-scatter.28.cloned.1.call-done = f32[256,768]{1,0:T(8,128)} async-done(((f32[1024,768]{1,0:T(8,128)}), f32[256,768]{1,0:T(8,128)}) %reduce-scatter.28.cloned.1.call-update) | async-done | bytes 786448 | tf_op jit(solution)/shard_map/reduce_scatter | solution.py:304
  823.0 39.0 %reduce-scatter.32.cloned.1.call-done = f32[256,768]{1,0:T(8,128)} async-done(((f32[1024,768]{1,0:T(8,128)}), f32[256,768]{1,0:T(8,128)}) %reduce-scatter.32.cloned.1.call-update) | async-done | bytes 786448 | tf_op jit(solution)/shard_map/reduce_scatter | solution.py:304
  864.5 71.4 %reduce-scatter.34.cloned.1.call-done = f32[96,768]{1,0:T(8,128)} async-done(((f32[768,768]{1,0:T(8,128)}), f32[96,768]{1,0:T(8,128)}) %reduce-scatter.34.cloned.1.call-update) | async-done | bytes 294928 | tf_op jit(solution)/shard_map/reduce_scatter | solution.py:317
  935.9 73.1 %reduce-scatter.36.cloned.1.call-done = f32[768,96]{0,1:T(8,128)} async-done(((f32[768,768]{0,1:T(8,128)}), f32[768,96]{0,1:T(8,128)}) %reduce-scatter.36.cloned.1.call-update) | async-done | bytes 294928 | tf_op jit(solution)/shard_map/reduce_scatter | solution.py:318
  (557 shorter events, 280.7 us)
Async XLA Ops:
  8.0 176.1 %all-gather.31.cloned.1.call-start = ((), (), s32[]{:S(2)}) async-start(), calls=%async_computation.31 | async-start | bytes 1966080 | tf_op jit(solution)/shard_map/all_gather | solution.py:249
  10.1 180.3 %all-gather.29.cloned.1.call-start = ((), (), s32[]{:S(2)}) async-start(), calls=%async_computation.30 | async-start | bytes 1966080 | tf_op jit(solution)/shard_map/all_gather | solution.py:249
  10.9 270.5 %reduce-scatter.22.cloned.1.call-start = ((), (), s32[]{:S(2)}) async-start(), calls=%async_computation.17 | async-start | bytes 3932160 | tf_op jit(solution)/shard_map/reduce_scatter | solution.py:253
  12.1 95.8 %copy-start.86 = (bf16[192,96]{1,0:T(8,128)(2,1)S(1)}, bf16[192,96]{1,0:T(8,128)(2,1)}, u32[]{:S(2)}) copy-start(bf16[192,96]{1,0:T(8,128)(2,1)} %param.18) | copy-start | bytes 110596
  218.3 80.4 %reduce-scatter.18.cloned.1.call-start = ((), (), s32[]{:S(2)}) async-start(), calls=%async_computation.12 | async-start | bytes 3932160 | tf_op jit(solution)/shard_map/reduce_scatter | solution.py:253
  238.8 68.0 %all-gather.15.cloned.1.call-start = ((), (), s32[]{:S(2)}) async-start(), calls=%async_computation.14 | async-start | bytes 1327104 | tf_op jit(solution)/shard_map/all_gather | solution.py:245
  239.4 82.1 %all-gather.19.cloned.1.call-start = ((), (), s32[]{:S(2)}) async-start(), calls=%async_computation.18 | async-start | bytes 1966080 | tf_op jit(solution)/shard_map/all_gather | solution.py:256
  300.7 206.9 %copy-start.108 = (f32[256]{0:T(256)}, f32[256]{0:T(256)S(1)}, u32[]{:S(2)}) copy-start(f32[256]{0:T(256)S(1)} %fusion.232) | copy-start | bytes 3076
  302.0 63.0 %all-gather.17.cloned.1.call-start = ((), (), s32[]{:S(2)}) async-start(), calls=%async_computation.15 | async-start | bytes 1327104 | tf_op jit(solution)/shard_map/all_gather | solution.py:246
  302.6 81.9 %all-gather.25.cloned.1.call-start = ((), (), s32[]{:S(2)}) async-start(), calls=%async_computation.24 | async-start | bytes 1966080 | tf_op jit(solution)/shard_map/all_gather | solution.py:283
  305.2 100.9 %all-gather.13.cloned.1.call-start = ((), (), s32[]{:S(2)}) async-start(), calls=%async_computation.13 | async-start | bytes 1966080 | tf_op jit(solution)/shard_map/all_gather | solution.py:256
  306.0 121.3 %all-gather.21.cloned.1.call-start = ((), (), s32[]{:S(2)}) async-start(), calls=%async_computation.20 | async-start | bytes 1966080 | tf_op jit(solution)/shard_map/all_gather | solution.py:283
  306.7 160.7 %reduce-scatter.30.cloned.1.call-start = ((), (), s32[]{:S(2)}) async-start(), calls=%async_computation.25 | async-start | bytes 3932160 | tf_op jit(solution)/shard_map/reduce_scatter | solution.py:287
  394.4 113.2 %reduce-scatter.26.cloned.1.call-start = ((), (), s32[]{:S(2)}) async-start(), calls=%async_computation.21 | async-start | bytes 3932160 | tf_op jit(solution)/shard_map/reduce_scatter | solution.py:287
  437.2 110.6 %reduce-scatter.20.cloned.1.call-start = ((), (), s32[]{:S(2)}) async-start(), calls=%async_computation.16 | async-start | bytes 3932160 | tf_op jit(solution)/shard_map/reduce_scatter | solution.py:258
  443.6 144.5 %reduce-scatter.24.cloned.1.call-start = ((), (), s32[]{:S(2)}) async-start(), calls=%async_computation.19 | async-start | bytes 3932160 | tf_op jit(solution)/shard_map/reduce_scatter | solution.py:258
  449.5 164.2 %all-gather.27.cloned.1.call-start = ((), (), s32[]{:S(2)}) async-start(), calls=%async_computation.26 | async-start | bytes 1966080 | tf_op jit(solution)/shard_map/all_gather | solution.py:292
  593.9 40.9 %all-gather.23.cloned.1.call-start = ((), (), s32[]{:S(2)}) async-start(), calls=%async_computation.22 | async-start | bytes 1966080 | tf_op jit(solution)/shard_map/all_gather | solution.py:292
  597.7 198.8 %reduce-scatter.40.cloned.1.call-start = ((), (), s32[]{:S(2)}) async-start(), calls=%async_computation.33 | async-start | bytes 884736
  649.2 148.9 %reduce-scatter.38.cloned.1.call-start = ((), (), s32[]{:S(2)}) async-start(), calls=%async_computation.32 | async-start | bytes 2211840
  702.4 119.3 %reduce-scatter.28.cloned.1.call-start = ((), (), s32[]{:S(2)}) async-start(), calls=%async_computation.23 | async-start | bytes 3932160 | tf_op jit(solution)/shard_map/reduce_scatter | solution.py:304
  707.4 154.5 %reduce-scatter.32.cloned.1.call-start = ((), (), s32[]{:S(2)}) async-start(), calls=%async_computation.27 | async-start | bytes 3932160 | tf_op jit(solution)/shard_map/reduce_scatter | solution.py:304
  712.1 223.7 %reduce-scatter.34.cloned.1.call-start = ((), (), s32[]{:S(2)}) async-start(), calls=%async_computation.28 | async-start | bytes 2654208 | tf_op jit(solution)/shard_map/reduce_scatter | solution.py:317
  719.6 289.5 %reduce-scatter.36.cloned.1.call-start = ((), (), s32[]{:S(2)}) async-start(), calls=%async_computation.29 | async-start | bytes 2654208 | tf_op jit(solution)/shard_map/reduce_scatter | solution.py:318
  (147 other events, 1435.4 us)
Sparse Core Ops, SparseCore 0:
  10.9 22.4 all-gather.30
  35.0 19.7 all-gather.28
  218.4 39.6 reduce-scatter.21
  260.5 38.0 reduce-scatter.17
  594.0 19.6 all-gather.26
  615.1 19.6 all-gather.22
Sparse Core Ops, SparseCore 1:
  241.5 42.6 all-gather.14
  302.1 19.4 all-gather.18
  323.6 41.4 all-gather.16
  366.6 17.8 all-gather.24
  386.6 19.5 all-gather.12
  407.7 19.5 all-gather.20
  429.7 37.7 reduce-scatter.29
  469.8 37.7 reduce-scatter.25
  510.0 37.7 reduce-scatter.19
  550.3 37.7 reduce-scatter.23
  649.3 63.3 reduce-scatter.39
  716.2 66.5 reduce-scatter.37
  785.1 36.5 reduce-scatter.27
  824.2 37.7 reduce-scatter.31
  866.1 69.8 reduce-scatter.33
  940.0 69.0 reduce-scatter.35
where the time goes:
time: 1030 us; the launch traced here: 1020 us
  waiting for transfers between devices  482 us (47%)
  blocking collectives  204 us (20%)
  matrix products  151 us (15%)
  other arithmetic  97.1 us (9%)
  local copies, waits for them, and re-layouts  60.8 us (6%)
  between operations  20.4 us (2%)
    unnamed x3, blocking collectives  102 us
    reduce_scatter x2, waiting for transfers between devices, local(): fed = lax.psum_scatter(fed_part, 'tensor', scatter_dimension=0, tiled=True)  75.8 us
    reduce_scatter x1, waiting for transfers between devices, local(): lax.psum_scatter(weight_totals[4], 'dp', scatter_dimension=1, tiled=True)  73.1 us
    reduce_scatter x1, waiting for transfers between devices, local(): lax.psum_scatter(weight_totals[3], 'dp', scatter_dimension=0, tiled=True)  71.4 us
    reduce_scatter x2, waiting for transfers between devices, local(): lax.psum_scatter(whole_grad, 'tensor', scatter_dimension=0, tiled=True)  60.6 us
    reduce_scatter x2, waiting for transfers between devices, local(): lax.psum_scatter(normed_part, 'tensor', scatter_dimension=0, tiled=True)  58.1 us
    all_gather x1, waiting for transfers between devices, local(): lax.all_gather(w_down, 'dp', axis=1, tiled=True)  38.6 us
    all_gather x1, blocking collectives, local(): lax.all_gather(w_qkv, 'dp', axis=1, tiled=True)  38.4 us
  transfers between devices with their start and end apart: 22, of which 16 were waited for; matrix products, arithmetic and copies ran while one was open for 24% of the time, Pallas kernels for 0%

commit v1 on v0

v1 whole, which is shorter than its diff:
```python
import jax
import jax.numpy as jnp
import numpy as np
from jax import lax
from jax.sharding import PartitionSpec as P

D = 768
H = 12
DH = 64
NB = 256
SEGL = 512
AXES = ("dp", "tensor")
F32 = jnp.float32
BF16 = jnp.bfloat16


def ridge_matrix():
    centres = (np.arange(NB) + 0.5) / NB
    samples = (np.arange(SEGL) + 0.5) / SEGL
    rows = np.exp(-0.5 * ((samples[None, :] - centres[:, None]) * NB) ** 2)
    gram = rows @ rows.T + 0.5 * np.eye(NB)
    return np.linalg.solve(gram, rows).astype(np.float32).astype(jnp.bfloat16)


def xor_permute(value, dp_mask, tensor_mask):
    dp_count, rank_count = lax.axis_size("dp"), lax.axis_size("tensor")
    pairs = [
        (d * rank_count + t, (d ^ dp_mask) * rank_count + (t ^ tensor_mask))
        for d in range(dp_count)
        for t in range(rank_count)
    ]
    return lax.ppermute(value, AXES, pairs)


MASKS = {"c": (0, 1), "x": (0, 2), "y": (1, 0)}


def gather_pieces(piece, order):
    arrays = {(): piece[None]}
    value = piece
    stacked = value
    keys = [dict(c=0, x=0, y=0, z=0)]
    for letter in order:
        if letter == "z":
            parts = [stacked] + [xor_permute(stacked, 2 * k, 0) for k in (1, 2, 3)]
        else:
            parts = [stacked, xor_permute(stacked, *MASKS[letter])]
        keys = [dict(key, **{letter: k}) for k in range(len(parts)) for key in keys]
        stacked = jnp.stack(parts).reshape((-1,) + piece.shape)
    return stacked, [(k["z"] * 2 + k["y"]) * 4 + k["x"] * 2 + k["c"] for k in keys]


def gather_all(piece, order):
    if lax.axis_size("dp") != 8:
        return lax.all_gather(piece, AXES, axis=0)
    stacked, flat = gather_pieces(piece, order)
    me = lax.axis_index("dp") * 4 + lax.axis_index("tensor")
    position = np.argsort(np.array(flat))
    return jnp.take(stacked, jnp.asarray(position)[jnp.arange(32) ^ me], axis=0)


def scatter_all(parts, order):
    if lax.axis_size("dp") != 8:
        return lax.psum_scatter(parts, AXES, scatter_dimension=0)
    me = lax.axis_index("dp") * 4 + lax.axis_index("tensor")
    value = jnp.take(parts.astype(BF16), jnp.arange(32) ^ me, axis=0)
    value = value.reshape((4, 2, 2, 2) + parts.shape[1:])
    axes = "zyxc"
    for letter in order:
        at = axes.index(letter)
        own = lax.index_in_dim(value, 0, at, keepdims=False).astype(F32)
        if letter == "z":
            for k in (1, 2, 3):
                own = own + xor_permute(
                    lax.index_in_dim(value, k, at, keepdims=False), 2 * k, 0
                ).astype(F32)
        else:
            own = own + xor_permute(
                lax.index_in_dim(value, 1, at, keepdims=False), *MASKS[letter]
            ).astype(F32)
        axes = axes.replace(letter, "")
        value = own.astype(BF16) if axes else own
    return value


def swap(value):
    rank_count = lax.axis_size("tensor")
    return lax.ppermute(value, "tensor", [(t, t ^ 1) for t in range(rank_count)])


def to_segment(local):
    core = lax.axis_index("tensor") % 2
    own = lax.dynamic_index_in_dim(local, core, 0, keepdims=False)
    other = swap(lax.dynamic_index_in_dim(local, 1 - core, 0, keepdims=False))
    return jnp.where(core == 0, jnp.concatenate([own, other]), jnp.concatenate([other, own]))


def from_segment(segment):
    core = lax.axis_index("tensor") % 2
    halves = segment.reshape((2, -1) + segment.shape[1:])
    own = lax.dynamic_index_in_dim(halves, core, 0, keepdims=False)
    other = swap(lax.dynamic_index_in_dim(halves, 1 - core, 0, keepdims=False))
    return jnp.where(core == 0, jnp.stack([own, other]), jnp.stack([other, own]))


def dot(left, right, left_dim, right_dim):
    return lax.dot_general(
        left, right, (((left_dim,), (right_dim,)), ((), ())), preferred_element_type=F32
    )


def density_of(mean_logit, var_logit):
    basis_var = (1.0 / NB) ** 2
    centre_pos = jax.nn.sigmoid(mean_logit)
    spread_sq = 0.05 * jax.nn.softplus(var_logit) + basis_var
    centres = (jnp.arange(NB, dtype=F32) + 0.5) / NB
    return jnp.sqrt(basis_var / spread_sq)[..., None] * jnp.exp(
        -0.5 * (centre_pos[..., None] - centres) ** 2 / spread_sq[..., None]
    )


def layer_norm(residual, norm_gain, norm_bias):
    centred = residual - jnp.mean(residual, axis=-1, keepdims=True)
    return (
        centred * lax.rsqrt(jnp.mean(centred * centred, axis=-1, keepdims=True) + 1e-05) * norm_gain
        + norm_bias
    )


def gelu_tanh(value):
    return jax.nn.gelu(value, approximate=True)


def local(
    tokens, lengths, mem_mask, cotangent, w_qkv, w_gauss, w_out, ln_gain, ln_bias, w_up, w_down
):
    dp_count = lax.axis_size("dp")
    rank = lax.axis_index("tensor")
    core, segment = rank % 2, rank // 2
    ridge = jnp.asarray(ridge_matrix())
    rows = D // dp_count

    qkv_parts = gather_all(w_qkv, "zyxc")
    small = jnp.concatenate([w_gauss.astype(F32).reshape(-1), ln_gain, ln_bias])
    small_parts = gather_all(small, "zyxc")
    out_parts = gather_all(w_out.T, "zyxc")
    up_parts = gather_all(w_up, "zyxc")
    down_parts = gather_all(w_down.T, "xzyc")
    parts_of = lambda parts: parts.reshape((dp_count, 4) + parts.shape[1:])
    weight_qkv = parts_of(qkv_parts).transpose(2, 0, 3, 1, 4).reshape(3, D, D)
    weight_out_t = parts_of(out_parts).transpose(0, 2, 1, 3).reshape(D, D)
    weight_up = parts_of(up_parts).transpose(0, 2, 1, 3).reshape(D, 4 * D)
    weight_down_t = parts_of(down_parts).transpose(0, 2, 1, 3).reshape(D, 4 * D)
    gauss_size = w_gauss.size
    gauss = parts_of(small_parts[:, :gauss_size]).reshape(dp_count, 4, 2, 3, -1)
    gauss = gauss.transpose(2, 1, 3, 0, 4).reshape(2, H, DH)
    norm_gain = small_parts[:, gauss_size : gauss_size + ln_gain.size].reshape(D)
    norm_bias = small_parts[:, gauss_size + ln_gain.size :].reshape(D)

    x = to_segment(tokens)
    valid = (
        segment * SEGL + jnp.arange(SEGL) < lax.dynamic_index_in_dim(lengths, core, 0, False)
    ).astype(F32)
    pair = lax.dynamic_index_in_dim(mem_mask, core, 0, False)[1, 0].astype(F32)
    pair_scale = pair / jnp.maximum(pair, 1.0)
    seed = (to_segment(cotangent).astype(F32) * valid[:, None]).astype(BF16)

    q, k, v = (dot(x, weight_qkv[i], 1, 0).astype(BF16) for i in range(3))
    pooled = (v.astype(F32) * (valid * pair_scale)[:, None]).astype(BF16)
    coef_next = dot(ridge, pooled, 1, 0).astype(BF16)
    coef = lax.ppermute(coef_next, "tensor", [(0, 2), (1, 3)])
    heads = lambda value: value.reshape(value.shape[0], H, DH)
    positions = jnp.arange(SEGL)
    allowed = (positions[None, :] < positions[:, None]) & (valid[None, :] > 0.5)
    allowed = allowed | (positions[None, :] == positions[:, None])
    qh, kh, vh = heads(q), heads(k), heads(v)
    scores = jnp.einsum("qhd,khd->hqk", qh, kh, preferred_element_type=F32) * DH**-0.5
    scores = jnp.where(allowed[None], scores, -1e30)
    exponent = jnp.exp(scores - jnp.max(scores, axis=-1, keepdims=True))
    attn = (exponent / jnp.sum(exponent, axis=-1, keepdims=True)).astype(BF16)
    attended = jnp.einsum("hqk,khd->qhd", attn, vh, preferred_element_type=F32)
    logits = [jnp.einsum("qhd,hd->qh", qh.astype(F32), gauss[i]) for i in range(2)]
    density = density_of(*logits).astype(BF16)
    coef_heads = heads(coef)
    recalled = jnp.einsum("qhn,nhd->qhd", density, coef_heads, preferred_element_type=F32)
    heads_out = (attended + recalled).reshape(SEGL, D).astype(BF16)
    residual = x.astype(F32) + dot(heads_out, weight_out_t, 1, 1)
    normed = layer_norm(residual, norm_gain, norm_bias).astype(BF16)

    pre = dot(normed, weight_up, 1, 0)
    hidden = gelu_tanh(pre).astype(BF16)
    output = residual + dot(hidden, weight_down_t, 1, 1)

    grad_down_t = dot(seed, hidden, 0, 0)
    hidden_grad = dot(seed, weight_down_t, 1, 0).astype(BF16).astype(F32)
    _, gelu_back = jax.vjp(gelu_tanh, pre)
    pre_grad = gelu_back(hidden_grad)[0].astype(BF16)
    grad_up = dot(normed, pre_grad, 0, 0)
    normed_grad = dot(pre_grad, weight_up, 1, 1).astype(BF16).astype(F32)
    _, norm_back = jax.vjp(layer_norm, residual, norm_gain, norm_bias)
    resid_from_norm, gain_part, bias_part = norm_back(normed_grad)
    resid_grad = seed.astype(F32) + resid_from_norm
    mix_grad = resid_grad.astype(BF16)

    grad_out_t = dot(mix_grad, heads_out, 0, 0)
    head_grad = heads(dot(mix_grad, weight_out_t, 1, 0).astype(BF16))
    coef_grad = jnp.einsum("qhn,qhd->nhd", density, head_grad, preferred_element_type=F32)
    coef_grad = lax.ppermute(coef_grad.reshape(NB, D).astype(BF16), "tensor", [(2, 0), (3, 1)])
    masked_grad = dot(ridge, coef_grad, 0, 0) * (valid * pair_scale)[:, None]
    density_grad = jnp.einsum("qhd,nhd->qhn", head_grad, coef_heads, preferred_element_type=F32)
    _, density_back = jax.vjp(density_of, *logits)
    logit_grads = density_back(density_grad)
    value_grad = jnp.einsum("hqk,qhd->khd", attn, head_grad, preferred_element_type=F32)
    prob_grad = jnp.einsum("qhd,khd->hqk", head_grad, vh, preferred_element_type=F32)
    probs = attn.astype(F32)
    score_grad = (
        probs * (prob_grad - jnp.sum(prob_grad * probs, axis=-1, keepdims=True))
    ).astype(BF16)
    query_grad = jnp.einsum("hqk,khd->qhd", score_grad, kh, preferred_element_type=F32) * DH**-0.5
    for i in range(2):
        query_grad = query_grad + logit_grads[i][..., None] * gauss[i]
    key_grad = jnp.einsum("hqk,qhd->khd", score_grad, qh, preferred_element_type=F32) * DH**-0.5
    value_grad = value_grad.reshape(SEGL, D) + masked_grad
    qkv_grad = [
        query_grad.reshape(SEGL, D).astype(BF16),
        key_grad.reshape(SEGL, D).astype(BF16),
        value_grad.astype(BF16),
    ]
    gauss_grad = jnp.stack([jnp.einsum("qhd,qh->hd", qh.astype(F32), g) for g in logit_grads])
    grad_qkv = jnp.stack([dot(x, g, 0, 0) for g in qkv_grad])
    whole_grad = sum(dot(g, weight_qkv[i], 1, 1) for i, g in enumerate(qkv_grad))
    grad_tokens = whole_grad + resid_grad

    split = lambda grad: grad.reshape(dp_count, rows, 4, -1).transpose(0, 2, 1, 3).reshape(
        dp_count * 4, rows, -1
    )
    own_down = scatter_all(split(grad_down_t), "cyzx").T
    own_up = scatter_all(split(grad_up), "cxyz")
    own_out = scatter_all(split(grad_out_t), "cxyz").T
    own_qkv = scatter_all(jnp.stack([split(g) for g in grad_qkv], axis=1), "cxyz")
    gauss_parts = gauss_grad.reshape(2, 4, 3, dp_count, -1).transpose(3, 1, 0, 2, 4)
    small_grads = jnp.concatenate(
        [
            gauss_parts.reshape(dp_count * 4, -1),
            gain_part.reshape(dp_count * 4, -1),
            bias_part.reshape(dp_count * 4, -1),
        ],
        axis=1,
    )
    own_small = scatter_all(small_grads, "cxyz")
    own_gauss = own_small[:gauss_size].reshape(w_gauss.shape)
    own_gain = own_small[gauss_size : gauss_size + ln_gain.size]
    own_bias = own_small[gauss_size + ln_gain.size :]
    return (
        from_segment(output),
        from_segment(grad_tokens),
        own_qkv,
        own_gauss,
        own_out,
        own_gain,
        own_bias,
        own_up,
        own_down,
    )


def solution(mesh):
    return jax.shard_map(
        local,
        mesh=mesh,
        in_specs=(
            P("dp", "tensor", None),
            P("dp"),
            P("dp", None, None),
            P("dp", "tensor", None),
            P(None, "dp", "tensor"),
            P(None, "tensor", "dp"),
            P("tensor", "dp"),
            P(("dp", "tensor")),
            P(("dp", "tensor")),
            P("dp", "tensor"),
            P("tensor", "dp"),
        ),
        out_specs=(
            P("dp", "tensor", None),
            P("dp", "tensor", None),
            P(None, "dp", "tensor"),
            P(None, "tensor", "dp"),
            P("tensor", "dp"),
            P(("dp", "tensor")),
            P(("dp", "tensor")),
            P("dp", "tensor"),
            P("tensor", "dp"),
        ),
        check_vma=False,
    )
```

time: 1030 us -> 596 us (0.58)
  waiting for transfers between devices: 482 us -> 133 us
  blocking collectives: 204 us -> 0 us
  local copies, waits for them, and re-layouts: 60.8 us -> 163 us
  starting transfers between devices: 1.51 us -> 78.1 us
  matrix products: 151 us -> 101 us
  between operations: 20.4 us -> 3.07 us
  other arithmetic: 97.1 us -> 109 us
    reduce_scatter x10 -> x0, waiting for transfers between devices: 356 us -> none  [the longest x2 75.8 us: local(): fed = lax.psum_scatter(fed_part, 'tensor', scatter_dimension=0, tiled=True)]
    ppermute x0 -> x66, waiting for transfers between devices: none -> 133 us  [the longest x60 133 us: xor_permute(): return lax.ppermute(value, AXES, pairs)]
    all_gather x10 -> x0, waiting for transfers between devices: 122 us -> none  [the longest x1 38.6 us: local(): lax.all_gather(w_down, 'dp', axis=1, tiled=True)]
    all_gather x3 -> x0, blocking collectives: 102 us -> none  [the longest x1 38.4 us: local(): lax.all_gather(w_qkv, 'dp', axis=1, tiled=True)]
    unnamed x3 -> x0, blocking collectives: 102 us -> none
    ppermute x0 -> x66, starting transfers between devices: none -> 78.1 us  [the longest x60 73.4 us: xor_permute(): return lax.ppermute(value, AXES, pairs)]
    dot_general x59 -> x32, matrix products: 147 us -> 92.3 us  [the longest x20 61.4 us: dot(): lax.dot_general(left, right, (((left_dim,), (right_dim,)), ((), ())), pre...]
    gather x0 -> x12, local copies, waits for them, and re-layouts: none -> 42.1 us  [the longest x7 23.1 us: gather_all(): return jnp.take(stacked, jnp.asarray(position)[jnp.arange(32) ^ me], axis=0)]
  transfers between devices with their start and end apart: 22 -> 66, of which waited for: 16 -> 20; matrix products, arithmetic and copies ran while one was open for 24% -> 45% of each run, Pallas kernels for 0% -> 0%
where the time goes in v1:
time: 596 us; the launch traced here: 588 us
  local copies, waits for them, and re-layouts  163 us (27%)
  waiting for transfers between devices  133 us (22%)
  other arithmetic  109 us (18%)
  matrix products  101 us (17%)
  starting transfers between devices  78.1 us (13%)
    ppermute x60, waiting for transfers between devices, xor_permute(): return lax.ppermute(value, AXES, pairs)  133 us
    ppermute x60, starting transfers between devices, xor_permute(): return lax.ppermute(value, AXES, pairs)  73.4 us
    dot_general x20, matrix products, dot(): lax.dot_general(left, right, (((left_dim,), (right_dim,)), ((), ())), pre...  61.4 us
    another operation x20, other arithmetic, gather_pieces(): stacked = jnp.stack(parts).reshape((-1,) + piece.shape)  34.8 us
    convert_element_type x4, local copies, waits for them, and re-layouts, scatter_all(): value = jnp.take(parts.astype(BF16), jnp.arange(32) ^ me, axis=0)  30.8 us
    gather x7, local copies, waits for them, and re-layouts, gather_all(): return jnp.take(stacked, jnp.asarray(position)[jnp.arange(32) ^ me], axis=0)  23.1 us
    gather x5, local copies, waits for them, and re-layouts, scatter_all(): value = jnp.take(parts.astype(BF16), jnp.arange(32) ^ me, axis=0)  19 us
    unnamed x182, local copies, waits for them, and re-layouts  12.2 us
  transfers between devices with their start and end apart: 66, of which 20 were waited for; matrix products, arithmetic and copies ran while one was open for 45% of the time, Pallas kernels for 0%

profile of v1, /device:TPU:0, one launch (start us, length us, event | category | flops | bytes accessed | tf_op | source)
XLA Modules:
  0.0 587.5 jit_solution(961684230038385016)
XLA Ops:
  35.5 5.6 collective-permute-done.2
  47.7 6.4 %collective-permute-done.4 = bf16[4,3,96,192]{3,2,1,0:T(8,128)(2,1)S(1)} collective-permute-done((bf16[4,3,96,192]{3,2,1,0:T(8,128)(2,1)S(1)}, bf16[4,3,96,192]{3,2,1,0:T(8,128)(2,1)S(1)}, u32[]{:S(2)}, u32[]{:S(2)}) %collective-permute-start.4) | collective-permute-done | bytes 442400 | tf_op jit(solution)/shard_map/ppermute | solution.py:32
  62.0 20.1 %collective-permute-done.26 = bf16[96,768]{1,0:T(8,128)(2,1)S(1)} collective-permute-done((bf16[96,768]{1,0:T(8,128)(2,1)}, bf16[96,768]{1,0:T(8,128)(2,1)S(1)}, u32[]{:S(2)}, u32[]{:S(2)}) %collective-permute-start.26) | collective-permute-done | bytes 147488 | tf_op jit(solution)/shard_map/ppermute | solution.py:32
  96.5 9.5 %collective-permute-done.28 = bf16[2,96,768]{2,1,0:T(8,128)(2,1)} collective-permute-done((bf16[2,96,768]{2,1,0:T(8,128)(2,1)}, bf16[2,96,768]{2,1,0:T(8,128)(2,1)}, u32[]{:S(2)}, u32[]{:S(2)}) %collective-permute-start.28) | collective-permute-done | bytes 294944 | tf_op jit(solution)/shard_map/ppermute | solution.py:32
  159.5 5.5 gather_fusion.4
  204.5 8.4 %fusion.118 = (f32[12,512]{1,0:T(8,128)S(1)}, f32[12,512,512]{1,2,0:T(8,128)}) fusion(pred[512,512]{0,1:T(8,128)(4,1)} %fusion.49, bf16[512,12,64]{0,2,1:T(8,128)(2,1)S(1)} %bitcast.558, bf16[512,12,64]{0,2,1:T(8,128)(2,1)S(1)} %bitcast.590), kind=kOutput, calls=%fused_computation.325 | convolution fusion | flops 415236608 | bytes 14442496 | tf_op jit(solution)/shard_map/sub | solution.py:179
  212.9 9.1 %divide_convert_fusion = bf16[12,512,512]{1,2,0:T(8,128)(2,1)} fusion(f32[12,512,512]{1,2,0:T(8,128)} %get-tuple-element.107, f32[12,512]{1,0:T(8,128)S(1)} %get-tuple-element.106), kind=kLoop, calls=%fused_computation.17 | loop fusion | flops 6291456 | bytes 18898944 | tf_op jit(solution)/shard_map/convert_element_type | solution.py:180
  237.3 5.5 gather_fusion.7
  278.6 7.7 %fusion.6 = bf16[512,3072]{1,0:T(8,128)(2,1)S(1)} fusion(f32[512,3072]{1,0:T(8,128)S(1)} %fusion.110, bf16[768,3072]{1,0:T(8,128)(2,1)S(1)} %bitcast.580, bf16[256,768]{1,0:T(8,128)(2,1)} %collective-permute-done.33, bf16[256,768]{1,0:T(8,128)(2,1)S(1)} %copy-done.13, f32[512]{0:T(512)S(1)} %fusion.95, pred[]{:T(512)S(6)} %eq.33), kind=kOutput, calls=%fused_computation.29 | convolution fusion | flops 2455240704 | bytes 14944257 | tf_op jit(solution)/shard_map/dot_general | solution.py:107
  310.4 6.5 %fusion.1 = (f32[12,512]{1,0:T(8,128)S(1)}, f32[12,512,512]{1,2,0:T(8,128)}) fusion(bf16[12,512,512]{1,2,0:T(8,128)(2,1)S(1)} %bitcast.535, bf16[512,12,64]{0,2,1:T(8,128)(2,1)S(1)} %bitcast.568, bf16[512,12,64]{0,2,1:T(8,128)(2,1)S(1)} %bitcast.563), kind=kOutput, calls=%fused_computation.15 | convolution fusion | flops 412084224 | bytes 20471808 | tf_op jit(solution)/shard_map/qhd,khd->hqk/dot_general | solution.py:214
  316.9 6.1 %convolution_convert_fusion = bf16[768,3072]{1,0:T(8,128)(2,1)} fusion(f32[512,3072]{1,0:T(8,128)S(1)} %bitcast.645, bf16[256,768]{1,0:T(8,128)(2,1)} %collective-permute-done.33, bf16[256,768]{1,0:T(8,128)(2,1)S(1)} %copy-done.13, f32[512]{0:T(512)S(1)} %fusion.95, pred[]{:T(512)S(6)} %eq.33), kind=kOutput, calls=%fused_computation.53 | convolution fusion | flops 2437152768 | bytes 11798529 | tf_op jit(solution)/shard_map/dot_general | solution.py:107
  323.0 9.8 %convert_element_type.540 = bf16[8,96,4,768]{3,2,1,0:T(4,128)(2,1)} reshape(bf16[768,3072]{1,0:T(8,128)(2,1)} %convolution_convert_fusion) | data formatting | bytes 9437184 | tf_op jit(solution)/shard_map/convert_element_type | solution.py:66
  339.7 10.1 %convert_element_type.519 = bf16[8,96,4,768]{3,2,1,0:T(4,128)(2,1)} reshape(bf16[768,3072]{1,0:T(8,128)(2,1)} %convolution_convert_fusion.1) | data formatting | bytes 9437184 | tf_op jit(solution)/shard_map/convert_element_type | solution.py:66
  349.8 5.5 copy.153
  366.2 5.9 %fusion.15 = (f32[512,12]{0,1:T(8,128)S(1)}, f32[512,12]{0,1:T(8,128)S(1)}, f32[512,12]{0,1:T(8,128)S(1)}) fusion(f32[512,12]{0,1:T(8,128)S(1)} %copy-done.58, f32[256]{0:T(256)S(1)} %copy-done.76, f32[512,12]{0,1:T(8,128)S(1)} %copy-done.53, f32[512,12]{0,1:T(8,128)S(1)} %copy-done.56, f32[512,12]{0,1:T(8,128)S(1)} %copy-done.54, ...), kind=kOutput, calls=%fused_computation.38 | convolution fusion | flops 226473984 | bytes 1352704 | tf_op jit(solution)/shard_map/qhd,nhd->qhn/dot_general | solution.py:210
  383.4 8.4 %broadcast_select_fusion = (bf16[32,96,768]{2,1,0:T(8,128)(2,1)}, bf16[32,96,768]{2,1,0:T(8,128)(2,1)}) fusion(bf16[32,96,768]{2,1,0:T(8,128)(2,1)} %gather_fusion.11, pred[32]{0:T(512)(128)(4,1)S(1)} %copy-done.69, bf16[32,96,768]{2,1,0:T(8,128)(2,1)} %gather_fusion.10), kind=kLoop, calls=%fused_computation.65 | loop fusion | flops 4718592 | bytes 18874400 | tf_op jit(solution)/shard_map/jit(_take)/select_n | solution.py:66
  398.3 6.1 %fusion.2 = bf16[12,512,512]{1,2,0:T(8,128)(2,1)S(1)} fusion(f32[12,512,512]{1,2,0:T(8,128)} %get-tuple-element.111, f32[12,512]{1,0:T(8,128)S(1)} %get-tuple-element.110, f32[12,512,512]{1,2,0:T(8,128)S(1)} %bitcast.537, f32[12,512]{1,0:T(8,128)S(1)} %copy-done.50), kind=kLoop, calls=%fused_computation.16 | loop fusion | flops 18874368 | bytes 31506432 | tf_op jit(solution)/shard_map/convert_element_type | solution.py:218
  462.5 6.5 %collective-permute-done.49 = bf16[4,2,96,192]{3,2,1,0:T(8,128)(2,1)S(1)} collective-permute-done((bf16[4,2,96,192]{3,2,1,0:T(8,128)(2,1)S(1)}, bf16[4,2,96,192]{3,2,1,0:T(8,128)(2,1)S(1)}, u32[]{:S(2)}, u32[]{:S(2)}) %collective-permute-start.49) | collective-permute-done | bytes 294944 | tf_op jit(solution)/shard_map/ppermute | solution.py:32
  488.8 21.2 %collective-permute-done.37 = bf16[4,2,3,96,192]{4,3,2,1,0:T(8,128)(2,1)} collective-permute-done((bf16[4,2,3,96,192]{4,3,2,1,0:T(8,128)(2,1)}, bf16[4,2,3,96,192]{4,3,2,1,0:T(8,128)(2,1)}, u32[]{:S(2)}, u32[]{:S(2)}) %collective-permute-start.37) | collective-permute-done | bytes 884768 | tf_op jit(solution)/shard_map/ppermute | solution.py:32
  519.8 7.8 %collective-permute-done.38 = bf16[4,3,96,192]{3,2,1,0:T(8,128)(2,1)S(1)} collective-permute-done((bf16[4,3,96,192]{3,2,1,0:T(8,128)(2,1)S(1)}, bf16[4,3,96,192]{3,2,1,0:T(8,128)(2,1)S(1)}, u32[]{:S(2)}, u32[]{:S(2)}) %collective-permute-start.38) | collective-permute-done | bytes 442400 | tf_op jit(solution)/shard_map/ppermute | solution.py:32
  533.7 8.8 %collective-permute-done.55 = bf16[4,2,96,768]{3,2,1,0:T(8,128)(2,1)S(1)} collective-permute-done((bf16[4,2,96,768]{3,2,1,0:T(8,128)(2,1)S(1)}, bf16[4,2,96,768]{3,2,1,0:T(8,128)(2,1)S(1)}, u32[]{:S(2)}, u32[]{:S(2)}) %collective-permute-start.55) | collective-permute-done | bytes 1179680 | tf_op jit(solution)/shard_map/ppermute | solution.py:32
  547.2 7.0 %collective-permute-done.64 = bf16[2,96,768]{2,1,0:T(8,128)(2,1)S(1)} collective-permute-done((bf16[2,96,768]{2,1,0:T(8,128)(2,1)S(1)}, bf16[2,96,768]{2,1,0:T(8,128)(2,1)S(1)}, u32[]{:S(2)}, u32[]{:S(2)}) %collective-permute-start.64) | collective-permute-done | bytes 294944 | tf_op jit(solution)/shard_map/ppermute | solution.py:32
  554.3 15.3 %collective-permute-done.63 = bf16[2,96,768]{2,1,0:T(8,128)(2,1)S(1)} collective-permute-done((bf16[2,96,768]{2,1,0:T(8,128)(2,1)S(1)}, bf16[2,96,768]{2,1,0:T(8,128)(2,1)S(1)}, u32[]{:S(2)}, u32[]{:S(2)}) %collective-permute-start.63) | collective-permute-done | bytes 294944 | tf_op jit(solution)/shard_map/ppermute | solution.py:32
  580.1 6.4 %collective-permute-done.58 = bf16[96,768]{1,0:T(8,128)(2,1)S(1)} collective-permute-done((bf16[96,768]{1,0:T(8,128)(2,1)S(1)}, bf16[96,768]{1,0:T(8,128)(2,1)S(1)}, u32[]{:S(2)}, u32[]{:S(2)}) %collective-permute-start.58) | collective-permute-done | bytes 147488 | tf_op jit(solution)/shard_map/ppermute | solution.py:32
  (502 shorter events, 375.2 us)
Async XLA Ops:
  8.0 49.6 %collective-permute-start.15 = (bf16[96,192]{0,1:T(8,128)(2,1)}, bf16[96,192]{0,1:T(8,128)(2,1)S(1)}, u32[]{:S(2)}, u32[]{:S(2)}) collective-permute-start(bf16[96,192]{0,1:T(8,128)(2,1)} %bitcast.623), channel_id=1, source_target_pairs={{0,16},{1,17},{2,18},{3,19},{4,20},{5,21},{6,22},{7,23},{8,24},{9,... | collective-permute-start | bytes 110600 | tf_op jit(solution)/shard_map/ppermute | solution.py:32
  10.3 47.4 %collective-permute-start.14 = (bf16[96,192]{0,1:T(8,128)(2,1)}, bf16[96,192]{0,1:T(8,128)(2,1)}, u32[]{:S(2)}, u32[]{:S(2)}) collective-permute-start(bf16[96,192]{0,1:T(8,128)(2,1)} %bitcast.624), channel_id=1, source_target_pairs={{0,8},{1,9},{2,10},{3,11},{4,12},{5,13},{6,14},{7,15},{8,0},{9,1},... | collective-permute-start | bytes 110600 | tf_op jit(solution)/shard_map/ppermute | solution.py:32
  32.0 27.1 %collective-permute-start.16 = (bf16[96,192]{0,1:T(8,128)(2,1)S(1)}, bf16[96,192]{0,1:T(8,128)(2,1)}, u32[]{:S(2)}, u32[]{:S(2)}) collective-permute-start(bf16[96,192]{0,1:T(8,128)(2,1)S(1)} %bitcast.625), channel_id=1, source_target_pairs={{0,24},{1,25},{2,26},{3,27},{4,28},{5,29},{6,30},{7,31},{8,16},{9,... | collective-permute-start | bytes 110600 | tf_op jit(solution)/shard_map/ppermute | solution.py:32
  54.3 38.8 %collective-permute-start.5 = (bf16[8,3,96,192]{3,2,1,0:T(8,128)(2,1)S(1)}, bf16[8,3,96,192]{3,2,1,0:T(8,128)(2,1)S(1)}, u32[]{:S(2)}, u32[]{:S(2)}) collective-permute-start(bf16[8,3,96,192]{3,2,1,0:T(8,128)(2,1)S(1)} %bitcast.583), channel_id=1, source_target_pairs={{0,2},{1,3},{2,0},{3,1},{4,6},{5,7},{6,4},{7,5},{8,10},{9,11},{10,... | collective-permute-start | bytes 2654216 | tf_op jit(solution)/shard_map/ppermute | solution.py:32
  56.5 25.7 %collective-permute-start.26 = (bf16[96,768]{1,0:T(8,128)(2,1)}, bf16[96,768]{1,0:T(8,128)(2,1)S(1)}, u32[]{:S(2)}, u32[]{:S(2)}) collective-permute-start(bf16[96,768]{1,0:T(8,128)(2,1)} %bitcast.81), channel_id=1, source_target_pairs={{0,2},{1,3},{2,0},{3,1},{4,6},{5,7},{6,4},{7,5},{8,10},{9,11},{10,... | collective-permute-start | bytes 442376 | tf_op jit(solution)/shard_map/ppermute | solution.py:32
  57.6 28.6 %collective-permute-start.20 = (bf16[96,768]{1,0:T(8,128)(2,1)S(1)}, bf16[96,768]{1,0:T(8,128)(2,1)S(1)}, u32[]{:S(2)}, u32[]{:S(2)}) collective-permute-start(bf16[96,768]{1,0:T(8,128)(2,1)S(1)} %copy-done.47), channel_id=1, source_target_pairs={{0,8},{1,9},{2,10},{3,11},{4,12},{5,13},{6,14},{7,15},{8,0},{9,1},... | collective-permute-start | bytes 442376 | tf_op jit(solution)/shard_map/ppermute | solution.py:32
  57.7 28.7 %collective-permute-start.22 = (bf16[96,768]{1,0:T(8,128)(2,1)S(1)}, bf16[96,768]{1,0:T(8,128)(2,1)S(1)}, u32[]{:S(2)}, u32[]{:S(2)}) collective-permute-start(bf16[96,768]{1,0:T(8,128)(2,1)S(1)} %copy-done.47), channel_id=1, source_target_pairs={{0,24},{1,25},{2,26},{3,27},{4,28},{5,29},{6,30},{7,31},{8,16},{9,... | collective-permute-start | bytes 442376 | tf_op jit(solution)/shard_map/ppermute | solution.py:32
  59.1 29.1 %collective-permute-start.21 = (bf16[96,768]{1,0:T(8,128)(2,1)S(1)}, bf16[96,768]{1,0:T(8,128)(2,1)S(1)}, u32[]{:S(2)}, u32[]{:S(2)}) collective-permute-start(bf16[96,768]{1,0:T(8,128)(2,1)S(1)} %copy-done.47), channel_id=1, source_target_pairs={{0,16},{1,17},{2,18},{3,19},{4,20},{5,21},{6,22},{7,23},{8,24},{9,... | collective-permute-start | bytes 442376 | tf_op jit(solution)/shard_map/ppermute | solution.py:32
  106.0 48.7 %collective-permute-start.6 = (bf16[16,3,96,192]{3,2,1,0:T(8,128)(2,1)S(1)}, bf16[16,3,96,192]{3,2,1,0:T(8,128)(2,1)}, u32[]{:S(2)}, u32[]{:S(2)}) collective-permute-start(bf16[16,3,96,192]{3,2,1,0:T(8,128)(2,1)S(1)} %bitcast.564), channel_id=1, source_target_pairs={{0,1},{1,0},{2,3},{3,2},{4,5},{5,4},{6,7},{7,6},{8,9},{9,8},{10,11... | collective-permute-start | bytes 5308424 | tf_op jit(solution)/shard_map/ppermute | solution.py:32
  107.8 40.2 %collective-permute-start.30 = (bf16[8,96,768]{2,1,0:T(8,128)(2,1)S(1)}, bf16[8,96,768]{2,1,0:T(8,128)(2,1)}, u32[]{:S(2)}, u32[]{:S(2)}) collective-permute-start(bf16[8,96,768]{2,1,0:T(8,128)(2,1)S(1)} %bitcast.585), channel_id=1, source_target_pairs={{0,4},{1,5},{2,6},{3,7},{4,0},{5,1},{6,2},{7,3},{8,12},{9,13},{10,... | collective-permute-start | bytes 3538952 | tf_op jit(solution)/shard_map/ppermute | solution.py:32
  114.2 37.0 %collective-permute-start.24 = (bf16[8,96,768]{2,1,0:T(8,128)(2,1)}, bf16[8,96,768]{2,1,0:T(8,128)(2,1)}, u32[]{:S(2)}, u32[]{:S(2)}) collective-permute-start(bf16[8,96,768]{2,1,0:T(8,128)(2,1)} %bitcast.73), channel_id=1, source_target_pairs={{0,2},{1,3},{2,0},{3,1},{4,6},{5,7},{6,4},{7,5},{8,10},{9,11},{10,... | collective-permute-start | bytes 3538952 | tf_op jit(solution)/shard_map/ppermute | solution.py:32
  127.5 151.1 %collective-permute-start.33 = (bf16[256,768]{1,0:T(8,128)(2,1)}, bf16[256,768]{1,0:T(8,128)(2,1)}, u32[]{:S(2)}, u32[]{:S(2)}) collective-permute-start(bf16[256,768]{1,0:T(8,128)(2,1)} %get-tuple-element.68), channel_id=1, source_target_pairs={{0,1},{1,0},{2,3},{3,2},{4,5},{5,4},{6,7},{7,6},{8,9},{9,8},{10,11... | collective-permute-start | bytes 1179656 | tf_op jit(solution)/shard_map/ppermute | solution.py:88
  151.0 81.3 %collective-permute-start.31 = (bf16[16,96,768]{2,1,0:T(8,128)(2,1)}, bf16[16,96,768]{2,1,0:T(8,128)(2,1)}, u32[]{:S(2)}, u32[]{:S(2)}) collective-permute-start(bf16[16,96,768]{2,1,0:T(8,128)(2,1)} %bitcast.92), channel_id=1, source_target_pairs={{0,1},{1,0},{2,3},{3,2},{4,5},{5,4},{6,7},{7,6},{8,9},{9,8},{10,11... | collective-permute-start | bytes 7077896 | tf_op jit(solution)/shard_map/ppermute | solution.py:32
  154.5 98.1 %collective-permute-start.25 = (bf16[16,96,768]{2,1,0:T(8,128)(2,1)}, bf16[16,96,768]{2,1,0:T(8,128)(2,1)}, u32[]{:S(2)}, u32[]{:S(2)}) collective-permute-start(bf16[16,96,768]{2,1,0:T(8,128)(2,1)} %bitcast.76), channel_id=1, source_target_pairs={{0,1},{1,0},{2,3},{3,2},{4,5},{5,4},{6,7},{7,6},{8,9},{9,8},{10,11... | collective-permute-start | bytes 7077896 | tf_op jit(solution)/shard_map/ppermute | solution.py:32
  379.8 31.9 %collective-permute-start.42 = (bf16[4,2,2,96]{3,0,1,2:T(4,128)(2,1)S(1)}, bf16[4,2,2,96]{3,0,1,2:T(4,128)(2,1)S(1)}, u32[]{:S(2)}, u32[]{:S(2)}) collective-permute-start(bf16[4,2,2,96]{3,0,1,2:T(4,128)(2,1)S(1)} %slice_bitcast_fusion.40), channel_id=1, source_target_pairs={{0,1},{1,0},{2,3},{3,2},{4,5},{5,4},{6,7},{7,6},{8,9},{9,8},{10,11... | collective-permute-start | bytes 9224 | tf_op jit(solution)/shard_map/ppermute | solution.py:32
  379.9 53.1 %collective-permute-start.34 = (bf16[256,768]{0,1:T(8,128)(2,1)}, bf16[256,768]{0,1:T(8,128)(2,1)}, u32[]{:S(2)}, u32[]{:S(2)}) collective-permute-start(bf16[256,768]{0,1:T(8,128)(2,1)} %bitcast.641), channel_id=1, source_target_pairs={{2,0},{3,1},{6,4},{7,5},{10,8},{11,9},{14,12},{15,13},{18,16},{19,... | collective-permute-start | bytes 1179656 | tf_op jit(solution)/shard_map/ppermute | solution.py:208
  382.9 71.9 %collective-permute-start.48 = (bf16[4,2,2,96,192]{4,3,2,1,0:T(8,128)(2,1)}, bf16[4,2,2,96,192]{4,3,2,1,0:T(8,128)(2,1)}, u32[]{:S(2)}, u32[]{:S(2)}) collective-permute-start(bf16[4,2,2,96,192]{4,3,2,1,0:T(8,128)(2,1)} %slice_bitcast_fusion.12), channel_id=1, source_target_pairs={{0,1},{1,0},{2,3},{3,2},{4,5},{5,4},{6,7},{7,6},{8,9},{9,8},{10,11... | collective-permute-start | bytes 1769480 | tf_op jit(solution)/shard_map/ppermute | solution.py:32
  427.2 43.3 %collective-permute-start.32 = (f32[256,768]{1,0:T(8,128)}, f32[256,768]{1,0:T(8,128)}, u32[]{:S(2)}, u32[]{:S(2)}) collective-permute-start(f32[256,768]{1,0:T(8,128)} %get-tuple-element.63), channel_id=1, source_target_pairs={{0,1},{1,0},{2,3},{3,2},{4,5},{5,4},{6,7},{7,6},{8,9},{9,8},{10,11... | collective-permute-start | bytes 2359304 | tf_op jit(solution)/shard_map/ppermute | solution.py:88
  430.1 53.9 %collective-permute-start.60 = (bf16[4,2,2,96,768]{4,3,2,1,0:T(8,128)(2,1)}, bf16[4,2,2,96,768]{4,3,2,1,0:T(8,128)(2,1)}, u32[]{:S(2)}, u32[]{:S(2)}) collective-permute-start(bf16[4,2,2,96,768]{4,3,2,1,0:T(8,128)(2,1)} %slice_bitcast_fusion), channel_id=1, source_target_pairs={{0,1},{1,0},{2,3},{3,2},{4,5},{5,4},{6,7},{7,6},{8,9},{9,8},{10,11... | collective-permute-start | bytes 7077896 | tf_op jit(solution)/shard_map/ppermute | solution.py:32
  431.7 81.5 %collective-permute-start.54 = (bf16[4,2,2,96,768]{4,3,2,1,0:T(8,128)(2,1)}, bf16[4,2,2,96,768]{4,3,2,1,0:T(8,128)(2,1)}, u32[]{:S(2)}, u32[]{:S(2)}) collective-permute-start(bf16[4,2,2,96,768]{4,3,2,1,0:T(8,128)(2,1)} %slice_bitcast_fusion.2), channel_id=1, source_target_pairs={{0,1},{1,0},{2,3},{3,2},{4,5},{5,4},{6,7},{7,6},{8,9},{9,8},{10,11... | collective-permute-start | bytes 7077896 | tf_op jit(solution)/shard_map/ppermute | solution.py:32
  481.3 35.8 %collective-permute-start.35 = (f32[256,768]{1,0:T(8,128)}, f32[256,768]{1,0:T(8,128)}, u32[]{:S(2)}, u32[]{:S(2)}) collective-permute-start(f32[256,768]{1,0:T(8,128)} %get-tuple-element.61), channel_id=1, source_target_pairs={{0,1},{1,0},{2,3},{3,2},{4,5},{5,4},{6,7},{7,6},{8,9},{9,8},{10,11... | collective-permute-start | bytes 2359304 | tf_op jit(solution)/shard_map/ppermute | solution.py:88
  481.8 28.2 %collective-permute-start.37 = (bf16[4,2,3,96,192]{4,3,2,1,0:T(8,128)(2,1)}, bf16[4,2,3,96,192]{4,3,2,1,0:T(8,128)(2,1)}, u32[]{:S(2)}, u32[]{:S(2)}) collective-permute-start(bf16[4,2,3,96,192]{4,3,2,1,0:T(8,128)(2,1)} %slice_bitcast_fusion.10), channel_id=1, source_target_pairs={{0,2},{1,3},{2,0},{3,1},{4,6},{5,7},{6,4},{7,5},{8,10},{9,11},{10,... | collective-permute-start | bytes 2654216 | tf_op jit(solution)/shard_map/ppermute | solution.py:32
  487.3 44.0 %collective-permute-start.61 = (bf16[4,2,96,768]{3,2,1,0:T(8,128)(2,1)S(1)}, bf16[4,2,96,768]{3,2,1,0:T(8,128)(2,1)S(1)}, u32[]{:S(2)}, u32[]{:S(2)}) collective-permute-start(bf16[4,2,96,768]{3,2,1,0:T(8,128)(2,1)S(1)} %slice_bitcast_fusion.6), channel_id=1, source_target_pairs={{0,4},{1,5},{2,6},{3,7},{4,0},{5,1},{6,2},{7,3},{8,12},{9,13},{10,... | collective-permute-start | bytes 3538952 | tf_op jit(solution)/shard_map/ppermute | solution.py:32
  515.7 26.8 %collective-permute-start.55 = (bf16[4,2,96,768]{3,2,1,0:T(8,128)(2,1)S(1)}, bf16[4,2,96,768]{3,2,1,0:T(8,128)(2,1)S(1)}, u32[]{:S(2)}, u32[]{:S(2)}) collective-permute-start(bf16[4,2,96,768]{3,2,1,0:T(8,128)(2,1)S(1)} %slice_bitcast_fusion.8), channel_id=1, source_target_pairs={{0,2},{1,3},{2,0},{3,1},{4,6},{5,7},{6,4},{7,5},{8,10},{9,11},{10,... | collective-permute-start | bytes 3538952 | tf_op jit(solution)/shard_map/ppermute | solution.py:32
  (131 other events, 1371.8 us)

commit v2 on v1

v2 whole, which is shorter than its diff:
```python
import functools

import jax
import jax.numpy as jnp
import numpy as np
from jax import lax
from jax.experimental import pallas as pl
from jax.experimental.pallas import tpu as pltpu
from jax.sharding import PartitionSpec as P

D = 768
H = 12
DH = 64
NB = 256
SEGL = 512
FF = 3072
PAIRS = H // 2
AXES = ("dp", "tensor")
F32 = jnp.float32
BF16 = jnp.bfloat16
BASIS_VAR = (1.0 / NB) ** 2
VMEM = pltpu.VMEM
SMEM = pltpu.SMEM


def ridge_matrix():
    centres = (np.arange(NB) + 0.5) / NB
    samples = (np.arange(SEGL) + 0.5) / SEGL
    rows = np.exp(-0.5 * ((samples[None, :] - centres[:, None]) * NB) ** 2)
    gram = rows @ rows.T + 0.5 * np.eye(NB)
    return np.linalg.solve(gram, rows).astype(np.float32).astype(jnp.bfloat16)


SIZES = {"z": 4, "y": 2, "x": 2, "c": 2}


def xor_permute(value, letter, k):
    dp_mask, tensor_mask = {"z": (2 * k, 0), "y": (k, 0), "x": (0, 2 * k), "c": (0, k)}[letter]
    dp_count, rank_count = lax.axis_size("dp"), lax.axis_size("tensor")
    pairs = [
        (d * rank_count + t, (d ^ dp_mask) * rank_count + (t ^ tensor_mask))
        for d in range(dp_count)
        for t in range(rank_count)
    ]
    return lax.ppermute(value, AXES, pairs)


def swap(value):
    return xor_permute(value, "c", 1)


def piece_table(order):
    first, second, third = order
    table = []
    for at, (k3, kc) in enumerate([(0, 0), (1, 0), (0, 1), (1, 1)]):
        for i2 in range(SIZES[second]):
            for i1 in range(SIZES[first]):
                k = {first: i1, second: i2, third: k3}
                table.append((at, (i2, i1), k["z"] * 2 + k["y"], k["x"], kc))
    return table


def gather(piece, order):
    first, second, third = order
    for letter in (first, second):
        piece = jnp.stack(
            [piece] + [xor_permute(piece, letter, k) for k in range(1, SIZES[letter])]
        )
    other = xor_permute(piece, third, 1)
    return [piece, other, swap(piece), swap(other)]


def as_gathered(whole, order):
    first, second, third = order
    whole = whole.reshape((4, 2) + whole.shape[1:])
    at = {"z": 0, "y": 1, "x": 2, "c": 3}
    rest = list(range(4, whole.ndim))
    whole = whole.transpose([at["c"], at[third], at[second], at[first]] + rest)
    return [whole[0, 0], whole[0, 1], whole[1, 0], whole[1, 1]]


def scatter(keep, send, order):
    received = swap(send)
    total = lambda k: keep[k].astype(F32) + received[k].astype(F32)
    for letter in order:
        own = total(0)
        arrived = [
            xor_permute(total(k).astype(BF16), letter, k) for k in range(1, SIZES[letter])
        ]
        total = lambda k, own=own, arrived=arrived: sum(
            (a[k].astype(F32) for a in arrived), own[k]
        )
        last = (own, arrived)
    own, arrived = last
    return sum((a.astype(F32) for a in arrived), own)


def whole_from(keep, send, order):
    first, second, third = order
    whole = jnp.stack([keep, send])
    at = {"c": 0, first: 1, second: 2, third: 3}
    rest = list(range(4, whole.ndim))
    whole = whole.transpose([at["z"], at["y"], at["x"], at["c"]] + rest)
    return whole.reshape((8,) + whole.shape[2:])


def to_segment_parts(local):
    core = lax.axis_index("tensor") % 2
    own = lax.dynamic_index_in_dim(local, core, 0, keepdims=False)
    return own, swap(lax.dynamic_index_in_dim(local, 1 - core, 0, keepdims=False))


def from_segment(segment):
    core = lax.axis_index("tensor") % 2
    half = segment.shape[0] // 2
    own = lax.dynamic_slice_in_dim(segment, core * half, half)
    other = swap(lax.dynamic_slice_in_dim(segment, (1 - core) * half, half))
    return jnp.where(core == 0, jnp.stack([own, other]), jnp.stack([other, own]))


def exact_triple(value):
    high = lax.reduce_precision(value, 8, 7)
    middle = lax.reduce_precision(value - high, 8, 7)
    return [part.astype(BF16) for part in (high, middle, value - high - middle)]


def dot(left, right, left_dim=1, right_dim=0):
    return lax.dot_general(
        left, right, (((left_dim,), (right_dim,)), ((), ())), preferred_element_type=F32
    )


def flip(value):
    return jnp.transpose(value.astype(F32))


def aligned(value, step):
    return pl.multiple_of(value * step, step)


def wide_copies(info, table, arrays, target, sems):
    for at, index, r, kx, kc in table:
        rows = pl.ds(aligned(info[0] ^ r, 96), 96)
        j = kx * 2 + kc
        yield pltpu.make_async_copy(
            arrays[at].at[index], target.at[rows, pl.ds(j * D, D)], sems.at[j]
        )


def wait_wide(target, sems, j):
    block = target.at[:, pl.ds(j * D, D)]
    pltpu.make_async_copy(block, block, sems.at[j]).wait()


def narrow_copies(info, table, arrays, spots, sem):
    for at, index, r, kx, kc in table:
        rows = pl.ds(pl.multiple_of((info[0] ^ r) * 96 + (info[2] ^ kc) * 48, 48), 48)
        columns = pl.ds(aligned(info[1] ^ kx, 384), 384)
        for first, target in spots:
            yield pltpu.make_async_copy(
                arrays[at].at[index + (pl.ds(first, 48),)], target.at[rows, columns], sem
            )


def wait_whole(target, sem):
    pltpu.make_async_copy(target, target, sem).wait()


def out_narrow(info, order, keep, send, spots, sem):
    for at, index, r, kx, kc in scatter_table(order):
        rows = pl.ds(pl.multiple_of((info[0] ^ r) * 96 + (info[2] ^ kc) * 48, 48), 48)
        columns = pl.ds(aligned(info[1] ^ kx, 384), 384)
        for first, source in spots:
            yield pltpu.make_async_copy(
                source.at[rows, columns], (keep, send)[kc].at[index + (pl.ds(first, 48),)], sem
            )


def scatter_table(order):
    a, b, c = order
    table = []
    for kc in range(2):
        for i in range(SIZES[a]):
            for j in range(SIZES[b]):
                for l in range(SIZES[c]):
                    k = {a: i, b: j, c: l}
                    table.append((kc, (i, j, l), k["z"] * 2 + k["y"], k["x"], kc))
    return table


def column_validity(info):
    return (lax.broadcasted_iota(jnp.int32, (SEGL, 1), 0) < info[3]).astype(F32)


def qkv_kernel(table_qk, table_v, info, own, other, ridge, *refs):
    qk, v_parts = refs[0:4], refs[4:8]
    x_out, q_out, k_out, v_out, coef_out = refs[8:13]
    wq, wk, wv, sems = refs[13:]
    copies = list(narrow_copies(info, table_qk, qk, [(0, wq), (48, wk)], sems.at[0]))
    copies += list(narrow_copies(info, table_v, v_parts, [(0, wv)], sems.at[1]))
    for copy in copies:
        copy.start()
    core = info[5]
    x_out[pl.ds(aligned(core, 256), 256), :] = own[...]
    x_out[pl.ds(aligned(1 - core, 256), 256), :] = other[...]
    scale = column_validity(info) * info[4].astype(F32)
    pair_wait = pltpu.make_async_copy(wq, wq, sems.at[0])
    pair_wait.wait()
    pair_wait.wait()

    def project(w, out):
        @pl.loop(0, 3)
        def _(step):
            at = pl.ds(aligned(step, 256), 256)
            out[:, at] = dot(x_out[...], w[:, at]).astype(BF16)

    project(wq, q_out)
    project(wk, k_out)
    wait_whole(wv, sems.at[1])

    @pl.loop(0, 3)
    def _(step):
        at = pl.ds(aligned(step, 256), 256)
        values = dot(x_out[...], wv[:, at]).astype(BF16)
        v_out[:, at] = values
        pooled = (values.astype(F32) * scale).astype(BF16)
        coef_out[:, at] = dot(ridge[...], pooled).astype(BF16)


def density_rows(logits, h):
    mean_logit, var_logit = logits[h : h + 1], logits[2 + h : 3 + h]
    mu = jax.nn.sigmoid(mean_logit)
    softplus = jnp.maximum(var_logit, 0.0) + jnp.log1p(jnp.exp(-jnp.abs(var_logit)))
    return mu, 0.05 * softplus + BASIS_VAR, var_logit


def centre_column():
    return (lax.broadcasted_iota(jnp.int32, (NB, 1), 0).astype(F32) + 0.5) / NB


def half_lanes(h):
    lane = lax.broadcasted_iota(jnp.int32, (1, 128), 1)
    return (lane < DH) if h == 0 else (lane >= DH)


def attend_kernel(info, q, k, v, gauss, attn_t, local_t, dens_t, bias):
    @pl.when(pl.program_id(0) == 0)
    def _():
        key = lax.broadcasted_iota(jnp.int32, (SEGL, SEGL), 0)
        query = lax.broadcasted_iota(jnp.int32, (SEGL, SEGL), 1)
        allowed = ((key < query) & (key < info[3])) | (key == query)
        bias[...] = jnp.where(allowed, 0.0, -1e30)

    values_t = flip(v[...]).astype(BF16)
    logits = dot(gauss[0], q[...], 1, 1)
    centres = centre_column()
    for h in range(2):
        rows = slice(h * DH, (h + 1) * DH)
        keys = jnp.where(half_lanes(h), k[...].astype(F32) * DH**-0.5, 0.0).astype(BF16)
        for block in range(2):
            n = 256 * (block + 1)
            at = slice(256 * block, n)
            scores = dot(keys[:n], q[at], 1, 1) + bias[:n, at]
            exponent = jnp.exp(scores - jnp.max(scores, axis=0, keepdims=True))
            total = jnp.sum(exponent, axis=0, keepdims=True)
            probs = (exponent * (1.0 / total)).astype(BF16)
            attn_t[h, :n, at] = probs
            local_t[rows, at] = dot(values_t[rows, :n], probs)
        mu, spread, _ = density_rows(logits, h)
        offset = mu - centres
        dens_t[h] = (
            jnp.sqrt(BASIS_VAR / spread) * jnp.exp(offset * offset * (-0.5 / spread))
        ).astype(BF16)


def layer_stats(residual):
    mean = jnp.mean(residual, axis=-1, keepdims=True)
    centred = residual - mean
    return centred, lax.rsqrt(jnp.mean(centred * centred, axis=-1, keepdims=True) + 1e-05)


def recall_kernel(table, info, dens_t, coef, local_t, x, gain, bias, *refs):
    parts = refs[0:4]
    heads_out, residual, normed, normed_t = refs[4:8]
    w_out, sem = refs[8:]
    step = pl.program_id(0)

    @pl.when(step == 0)
    def _():
        for copy in narrow_copies(info, table, parts, [(48, w_out)], sem):
            copy.start()

    coef_t = flip(coef[...]).astype(BF16)
    recalled = [dot(coef_t[h * DH : (h + 1) * DH], dens_t[h]) for h in range(2)]
    both = local_t[...] + jnp.concatenate(recalled, axis=0)
    heads_out[:, pl.ds(aligned(step, 128), 128)] = flip(both).astype(BF16)

    @pl.when(step == PAIRS - 1)
    def _():
        wait_whole(w_out, sem)

        @pl.loop(0, 3)
        def _(chunk):
            at = pl.ds(aligned(chunk, 256), 256)
            residual[:, at] = x[:, at].astype(F32) + dot(heads_out[...], w_out[at, :], 1, 1)

        centred, scale = layer_stats(residual[...])
        value = (centred * scale * gain[...] + bias[...]).astype(BF16)
        normed[...] = value
        normed_t[...] = flip(value).astype(BF16)


def gelu_parts(pre):
    c0, c1 = 0.7978845608028654, 0.044715
    square = pre * pre
    inner = jnp.tanh(c0 * pre * (1.0 + c1 * square))
    half = 0.5 * (1.0 + inner)
    slope = half + 0.5 * pre * (1.0 - inner * inner) * (c0 * (1.0 + 3.0 * c1 * square))
    return pre * half, slope


def wide_out(info, order, keep, send, source, sems):
    for at, index, r, kx, kc in scatter_table(order):
        rows = pl.ds(aligned(info[0] ^ r, 96), 96)
        j = kx * 2 + kc
        yield j, pltpu.make_async_copy(
            source.at[rows, pl.ds(j * D, D)], (keep, send)[kc].at[index], sems.at[j]
        )


def wait_out(source, sems):
    for j in range(4):
        wait_wide(source, sems, j)


def up_kernel(table, order, info, normed, seed_t, *refs):
    parts = refs[0:4]
    hidden, slope, keep, send = refs[4:8]
    w_up, grad, sems, out_sems = refs[8:]
    for copy in wide_copies(info, table, parts, w_up, sems):
        copy.start()
    outs = list(wide_out(info, order, keep, send, grad, out_sems))
    for j in (0, 2, 1, 3):
        wait_wide(w_up, sems, j)

        @pl.loop(0, 3)
        def _(chunk):
            at = pl.ds(pl.multiple_of(j * D + chunk * 256, 256), 256)
            value, derivative = gelu_parts(dot(normed[...], w_up[:, at]))
            value = value.astype(BF16)
            hidden[:, at] = value
            slope[:, at] = derivative.astype(BF16)
            grad[:, at] = dot(seed_t[...], value).astype(BF16)

        for owner, copy in outs:
            if owner == j:
                copy.start()
    wait_out(grad, out_sems)


def down_kernel(tables, order, info, seed, normed_t, slope, residual, gain, *refs):
    down_parts, up_parts = refs[0:4], refs[4:8]
    keep, send, resid_grad, gain_grad, bias_grad = refs[8:13]
    w_down, w_up, grad, total, down_sems, up_sems, out_sems = refs[13:]
    for copy in wide_copies(info, tables[0], down_parts, w_down, down_sems):
        copy.start()
    for copy in wide_copies(info, tables[1], up_parts, w_up, up_sems):
        copy.start()
    outs = list(wide_out(info, order, keep, send, grad, out_sems))
    total[...] = jnp.zeros_like(total)
    for j in (0, 2, 1, 3):
        wait_wide(w_down, down_sems, j)
        wait_wide(w_up, up_sems, j)

        @pl.loop(0, 3)
        def _(chunk):
            at = pl.ds(pl.multiple_of(j * D + chunk * 256, 256), 256)
            back = dot(seed[...], w_down[:, at]).astype(BF16).astype(F32)
            back = (back * slope[:, at].astype(F32)).astype(BF16)
            grad[:, at] = dot(normed_t[...], back).astype(BF16)
            total[...] += dot(back, w_up[:, at], 1, 1)

        for owner, copy in outs:
            if owner == j:
                copy.start()
    normed_grad = total[...].astype(BF16).astype(F32)
    centred, scale = layer_stats(residual[...])
    unit = centred * scale
    gain_grad[...] = jnp.sum(normed_grad * unit, axis=0, keepdims=True)
    bias_grad[...] = jnp.sum(normed_grad, axis=0, keepdims=True)
    back = normed_grad * gain[...]
    back = back - jnp.mean(back, axis=-1, keepdims=True) - unit * jnp.mean(
        back * unit, axis=-1, keepdims=True
    )
    resid_grad[...] = seed[...].astype(F32) + scale * back
    wait_out(grad, out_sems)


def mix_back_kernel(table, order, info, resid_grad, heads_out, dens_t, *refs):
    parts = refs[0:4]
    head_grad, coef_grad, keep, send = refs[4:8]
    w_out, grad, mix_t, sem, out_sem = refs[8:]
    step = pl.program_id(0)

    @pl.when(step == 0)
    def _():
        for copy in narrow_copies(info, table, parts, [(48, w_out)], sem):
            copy.start()
        mix = resid_grad[...].astype(BF16)
        mix_t[...] = flip(mix).astype(BF16)
        wait_whole(w_out, sem)

        @pl.loop(0, 3)
        def _(chunk):
            at = pl.ds(aligned(chunk, 256), 256)
            head_grad[:, at] = dot(resid_grad[...].astype(BF16), w_out[:, at]).astype(BF16)
            grad[:, at] = dot(mix_t[...], heads_out[:, at]).astype(BF16)

        for copy in out_narrow(info, order, keep, send, [(0, grad)], out_sem):
            copy.start()

    pair_grad = head_grad[:, pl.ds(aligned(step, 128), 128)].astype(F32)
    sums = [
        dot(dens_t[h], jnp.where(half_lanes(h), pair_grad, 0.0).astype(BF16)) for h in range(2)
    ]
    coef_grad[...] = (sums[0] + sums[1]).astype(BF16)

    @pl.when(step == PAIRS - 1)
    def _():
        wait_whole(grad, out_sem)


def attend_back_kernel(
    attn_t, q, k, v, grad, local_t, dens_t, coef, gauss, gauss_column, *refs
):
    dq_out, dk_out, dv_out, gauss_grad, dq_t, dk_sum, dv_sum, rows_of = refs
    keys_t = flip(k[...]).astype(BF16)
    grad_t = flip(grad[...])
    logits = dot(gauss[0], q[...], 1, 1)
    centres = centre_column()
    dk_sum[...] = jnp.zeros_like(dk_sum)
    dv_sum[...] = jnp.zeros_like(dv_sum)
    rows_of[...] = jnp.zeros_like(rows_of)
    only = lambda h, value: jnp.where(half_lanes(h), value.astype(F32), 0.0).astype(BF16)
    for h in range(2):
        rows = slice(h * DH, (h + 1) * DH)
        values, queries, grads = only(h, v[...]), only(h, q[...]), only(h, grad[...])
        delta = jnp.sum(grad_t[rows] * local_t[rows], axis=0, keepdims=True)
        for block in range(2):
            n = 256 * (block + 1)
            at = slice(256 * block, n)
            probs = attn_t[h, :n, at]
            prob_grad = dot(values[:n], grad[at], 1, 1)
            score_grad = (probs.astype(F32) * (prob_grad - delta[:, at])).astype(BF16)
            dv_sum[:n] += dot(probs, grads[at])
            dk_sum[:n] += dot(score_grad, queries[at])
            dq_t[rows, at] = dot(keys_t[rows, :n], score_grad) * DH**-0.5
        mu, spread, var_logit = density_rows(logits, h)
        inverse = 1.0 / spread
        offset = mu - centres
        weighted = dot(only(h, coef[...]), grad[...], 1, 1) * dens_t[h].astype(F32)
        first = weighted * offset
        sum0 = jnp.sum(weighted, axis=0, keepdims=True)
        sum1 = jnp.sum(first, axis=0, keepdims=True)
        sum2 = jnp.sum(first * offset, axis=0, keepdims=True)
        mean_grad = -sum1 * inverse * mu * (1.0 - mu)
        spread_grad = 0.5 * inverse * (sum2 * inverse - sum0)
        var_grad = spread_grad * 0.05 * jax.nn.sigmoid(var_logit)
        rows_of[h : h + 1] = mean_grad
        rows_of[2 + h : 3 + h] = var_grad
        column = gauss_column[0, rows]
        dq_t[rows] += column[:, 0:1] * mean_grad + column[:, 1:2] * var_grad
    dq_out[...] = jnp.transpose(dq_t[...]).astype(BF16)
    dk_out[...] = (dk_sum[...] * DH**-0.5).astype(BF16)
    dv_out[...] = dv_sum[...]
    high = rows_of[...].astype(BF16)
    gauss_grad[0] = dot(high, q[...]) + dot((rows_of[...] - high.astype(F32)).astype(BF16), q[...])


def qkv_grad_kernel(orders, info, x, dq, dk, dv, coef_grad, ridge_t, *refs):
    keep_qk, send_qk, keep_v, send_v, dv_out, x_t, gq, gk, gv, sems = refs
    x_t[...] = flip(x[...]).astype(BF16)
    scale = column_validity(info) * info[4].astype(F32)

    def weight(source, out):
        @pl.loop(0, 3)
        def _(chunk):
            at = pl.ds(aligned(chunk, 256), 256)
            out[:, at] = dot(x_t[...], source[:, at]).astype(BF16)

    weight(dq, gq)
    weight(dk, gk)
    for copy in out_narrow(info, orders[0], keep_qk, send_qk, [(0, gq), (48, gk)], sems.at[0]):
        copy.start()

    @pl.loop(0, 3)
    def _(chunk):
        at = pl.ds(aligned(chunk, 256), 256)
        pooled_grad = dot(ridge_t[...], coef_grad[:, at])
        dv_out[:, at] = (dv[:, at] + pooled_grad * scale).astype(BF16)
        gv[:, at] = dot(x_t[...], dv_out[:, at]).astype(BF16)

    for copy in out_narrow(info, orders[1], keep_v, send_v, [(0, gv)], sems.at[1]):
        copy.start()
    both = pltpu.make_async_copy(gq, gq, sems.at[0])
    both.wait()
    both.wait()
    wait_whole(gv, sems.at[1])


def input_grad_kernel(table_qk, table_v, info, dq, dk, dv, resid_grad, *refs):
    qk, v_parts = refs[0:4], refs[4:8]
    out, wq, wk, wv, sems = refs[8:]
    for copy in narrow_copies(info, table_qk, qk, [(0, wq), (48, wk)], sems.at[0]):
        copy.start()
    for copy in narrow_copies(info, table_v, v_parts, [(0, wv)], sems.at[1]):
        copy.start()
    pair_wait = pltpu.make_async_copy(wq, wq, sems.at[0])
    pair_wait.wait()
    pair_wait.wait()
    wait_whole(wv, sems.at[1])

    @pl.loop(0, 3)
    def _(chunk):
        at = pl.ds(aligned(chunk, 256), 256)
        part = dot(dq[...], wq[at, :], 1, 1) + dot(dk[...], wk[at, :], 1, 1)
        out[:, at] = resid_grad[:, at] + part + dot(dv[...], wv[at, :], 1, 1)


def output_kernel(table, info, hidden, residual, *refs):
    parts = refs[0:4]
    out, w_down, sems = refs[4:]
    for copy in wide_copies(info, table, parts, w_down, sems):
        copy.start()
    wait_out(w_down, sems)

    @pl.loop(0, 3)
    def _(chunk):
        at = pl.ds(aligned(chunk, 256), 256)
        out[:, at] = residual[:, at] + dot(hidden[...], w_down[at, :], 1, 1)


FULL = pl.BlockSpec(memory_space=VMEM)
ANY = pl.BlockSpec(memory_space=pl.ANY)
SCALARS = pl.BlockSpec(memory_space=SMEM)
MATRIX = (D, D)
WIDE = (D, FF)
DMA = pltpu.SemaphoreType.DMA


def shape(dims, dtype=BF16):
    return jax.ShapeDtypeStruct(dims, dtype)


def run(body, name, args, in_specs, outs, out_specs, scratch=(), grid=None, cost=5.0):
    kwargs = {} if grid is None else {"grid": grid}
    return pl.pallas_call(
        body,
        name=name,
        out_shape=tuple(outs),
        in_specs=list(in_specs),
        out_specs=tuple(out_specs),
        scratch_shapes=list(scratch),
        cost_estimate=pl.CostEstimate(
            flops=int(cost * 9e8), bytes_accessed=int(1e6), transcendentals=0
        ),
        compiler_params=pltpu.CompilerParams(vmem_limit_bytes=48 * 1024 * 1024),
        **kwargs,
    )(*args)


PAIR_COLUMNS = pl.BlockSpec((SEGL, 128), lambda p: (0, p))
PAIR_ROWS = pl.BlockSpec((128, SEGL), lambda p: (p, 0))
PAIR_COEF = pl.BlockSpec((NB, 128), lambda p: (0, p))
PAIR_ATTN = pl.BlockSpec((2, SEGL, SEGL), lambda p: (p, 0, 0))
PAIR_DENS = pl.BlockSpec((2, NB, SEGL), lambda p: (p, 0, 0))


def pair_block(*dims):
    return pl.BlockSpec((1,) + dims, lambda p: (p, 0, 0))


ORDER_QK, ORDER_V, ORDER_UP, ORDER_DOWN = "zyx", "zxy", "zyx", "xzy"
BACK_QK, BACK_V, BACK_UP, BACK_DOWN = "xyz", "yxz", "xyz", "yzx"


def local(
    tokens, lengths, mem_mask, cotangent, w_qkv, w_gauss, w_out, ln_gain, ln_bias, w_up, w_down
):
    dp_count = lax.axis_size("dp")
    dp, rank = lax.axis_index("dp"), lax.axis_index("tensor")
    core, segment = rank % 2, rank // 2
    near = dp_count == 8
    gauss_size, gain_size = w_gauss.size, ln_gain.size
    ridge = ridge_matrix()

    used = lax.dynamic_index_in_dim(lengths, core, 0, False)
    valid_count = jnp.clip(used - segment * SEGL, 0, SEGL)
    pair = lax.dynamic_index_in_dim(mem_mask, core, 0, False)[1, 0]
    where = (dp, segment, core) if near else (0, 0, 0)
    info = jnp.stack(
        [jnp.asarray(value, jnp.int32) for value in where + (valid_count, pair, core)]
    )

    projections = jnp.concatenate([w_qkv, w_out.T[None]])
    if near:
        mine = lax.dynamic_slice_in_dim(projections, core * 48, 48, axis=1)
        partner = swap(lax.dynamic_slice_in_dim(projections, (1 - core) * 48, 48, axis=1))
        projections = jnp.where(
            core == 0,
            jnp.concatenate([mine, partner], axis=2),
            jnp.concatenate([partner, mine], axis=2),
        )
        small = jnp.concatenate(
            [w_gauss.reshape(-1)] + exact_triple(jnp.concatenate([ln_gain, ln_bias]))
        )
        small_rows = jnp.pad(small[None], ((0, 15), (0, 384 - small.size)))
        qk_parts = gather(projections[:2].reshape(96, 384), ORDER_QK)
        v_parts = gather(
            jnp.concatenate([projections[2], projections[3], small_rows]), ORDER_V
        )
        up_parts = gather(w_up, ORDER_UP)
        down_parts = gather(w_down.T, ORDER_DOWN)
        rows = jnp.concatenate(
            [part[:, :, 96, : small.size].reshape(-1, small.size) for part in v_parts]
        )
        flat = [r * 4 + kx * 2 + kc for _, _, r, kx, kc in piece_table(ORDER_V)]
        position = jnp.asarray(np.argsort(np.array(flat)))
        rows = rows[position[jnp.arange(32) ^ (dp * 4 + rank)]]
        triple = rows[:, gauss_size:].astype(F32).reshape(32, 3, 2, gain_size)
        scales = triple[:, 0] + triple[:, 1] + triple[:, 2]
        gauss_parts = rows[:, :gauss_size]
    else:
        every = lambda value: lax.all_gather(value, AXES, axis=0)
        cut = lambda value: value.reshape((8, dp_count // 8) + value.shape[1:])
        both = cut(every(projections).reshape(dp_count, 4, 4, -1, 192))
        both = both.transpose(0, 3, 1, 4, 2, 5).reshape(8, 4, 2, 48, 2, 384)
        both = both.transpose(0, 4, 2, 1, 3, 5)
        qk_parts = as_gathered(both[:, :, :, :2].reshape(8, 2, 2, 96, 384), ORDER_QK)
        v_parts = as_gathered(
            jnp.pad(both[:, :, :, 2:].reshape(8, 2, 2, 96, 384), ((0, 0),) * 3 + ((0, 16), (0, 0))),
            ORDER_V,
        )
        wide = lambda value: cut(every(value).reshape(dp_count, 4, -1, D)).transpose(
            0, 2, 1, 3, 4
        ).reshape(8, 2, 2, 96, D)
        up_parts = as_gathered(wide(w_up), ORDER_UP)
        down_parts = as_gathered(wide(w_down.T), ORDER_DOWN)
        scales = every(jnp.stack([ln_gain, ln_bias]))
        gauss_parts = every(w_gauss.reshape(-1))
    norm_gain, norm_bias = scales[:, 0].reshape(1, D), scales[:, 1].reshape(1, D)
    gauss = gauss_parts.reshape(dp_count, 4, 2, 3, -1).transpose(2, 1, 3, 0, 4)
    gauss = gauss.reshape(2, PAIRS, 2, DH)
    spread_rows = jnp.eye(2, dtype=BF16)[None, None, :, :, None] * gauss[:, :, :, None, :]
    gauss_rows = spread_rows.transpose(1, 0, 2, 3, 4).reshape(PAIRS, 4, 128)
    gauss_rows = jnp.pad(gauss_rows, ((0, 0), (0, 12), (0, 0)))
    gauss_column = gauss.astype(F32).reshape(2, PAIRS, 128).transpose(1, 2, 0)
    gauss_column = jnp.pad(gauss_column, ((0, 0), (0, 0), (0, 126)))
    table_qk, table_v = piece_table(ORDER_QK), piece_table(ORDER_V)
    table_up, table_down = piece_table(ORDER_UP), piece_table(ORDER_DOWN)

    own, other = to_segment_parts(tokens)
    seed_own, seed_other = to_segment_parts(cotangent)
    seed = jnp.where(
        core == 0,
        jnp.concatenate([seed_own, seed_other]),
        jnp.concatenate([seed_other, seed_own]),
    )
    seed = jnp.where(jnp.arange(SEGL)[:, None] < valid_count, seed, 0.0).astype(BF16)
    seed_t = seed.T

    tall = shape((SEGL, D))
    x, q, k, v, coef = run(
        functools.partial(qkv_kernel, table_qk, table_v),
        "qkv",
        [info, own, other, jnp.asarray(ridge)] + qk_parts + v_parts,
        [SCALARS, FULL, FULL, FULL] + [ANY] * 8,
        [tall] * 4 + [shape((NB, D))],
        [FULL] * 5,
        [VMEM(MATRIX, BF16)] * 3 + [DMA((2,))],
        cost=6.0,
    )
    coef = lax.ppermute(coef, "tensor", [(0, 2), (1, 3)])
    attn_t, local_t, dens_t = run(
        attend_kernel,
        "attend",
        [info, q, k, v, gauss_rows],
        [SCALARS] + [PAIR_COLUMNS] * 3 + [pair_block(16, 128)],
        [shape((H, SEGL, SEGL)), shape((D, SEGL), F32), shape((H, NB, SEGL))],
        [PAIR_ATTN, PAIR_ROWS, PAIR_DENS],
        [VMEM((SEGL, SEGL), F32)],
        grid=(PAIRS,),
        cost=12.0,
    )
    whole = lambda *dims: pl.BlockSpec(dims, lambda p: (0,) * len(dims))
    heads_out, residual, normed, normed_t = run(
        functools.partial(recall_kernel, table_v),
        "recall",
        [info, dens_t, coef, local_t, x, norm_gain, norm_bias] + v_parts,
        [SCALARS, PAIR_DENS, PAIR_COEF, PAIR_ROWS, whole(SEGL, D), whole(1, D), whole(1, D)]
        + [ANY] * 4,
        [tall, shape((SEGL, D), F32), tall, shape((D, SEGL))],
        [whole(SEGL, D)] * 3 + [whole(D, SEGL)],
        [VMEM(MATRIX, BF16), DMA(())],
        grid=(PAIRS,),
        cost=7.0,
    )
    piece_dims = lambda order: tuple(SIZES[letter] for letter in order)
    wide_grad = [shape(piece_dims(BACK_DOWN) + (96, D))] * 2
    hidden, slope, keep_down, send_down = run(
        functools.partial(up_kernel, table_up, BACK_DOWN),
        "up",
        [info, normed, seed_t] + up_parts,
        [SCALARS, FULL, FULL] + [ANY] * 4,
        [shape((SEGL, FF))] * 2 + wide_grad,
        [FULL] * 2 + [ANY] * 2,
        [VMEM(WIDE, BF16)] * 2 + [DMA((4,))] * 2,
        cost=12.0,
    )
    own_down = collect(keep_down, send_down, BACK_DOWN, dp_count, D).T
    wide_grad = [shape(piece_dims(BACK_UP) + (96, D))] * 2
    row = shape((1, D), F32)
    keep_up, send_up, resid_grad, gain_part, bias_part = run(
        functools.partial(down_kernel, (table_down, table_up), BACK_UP),
        "down",
        [info, seed, normed_t, slope, residual, norm_gain] + down_parts + up_parts,
        [SCALARS] + [FULL] * 5 + [ANY] * 8,
        wide_grad + [shape((SEGL, D), F32), row, row],
        [ANY] * 2 + [FULL] * 3,
        [VMEM(WIDE, BF16)] * 3 + [VMEM((SEGL, D), F32)] + [DMA((4,))] * 3,
        cost=15.0,
    )
    own_up = collect(keep_up, send_up, BACK_UP, dp_count, D)
    narrow_grad = [shape(piece_dims(BACK_V) + (48, 384))] * 2
    head_grad, coef_grad, keep_out, send_out = run(
        functools.partial(mix_back_kernel, table_v, BACK_V),
        "mix_back",
        [info, resid_grad, heads_out, dens_t] + v_parts,
        [SCALARS, whole(SEGL, D), whole(SEGL, D), PAIR_DENS] + [ANY] * 4,
        [tall, shape((NB, D))] + narrow_grad,
        [whole(SEGL, D), PAIR_COEF] + [ANY] * 2,
        [VMEM(MATRIX, BF16)] * 2 + [VMEM((D, SEGL), BF16)] + [DMA(())] * 2,
        grid=(PAIRS,),
        cost=6.0,
    )
    coef_grad = lax.ppermute(coef_grad, "tensor", [(2, 0), (3, 1)])
    dq, dk, dv, gauss_grad = run(
        attend_back_kernel,
        "attend_back",
        [attn_t, q, k, v, head_grad, local_t, dens_t, coef, gauss_rows, gauss_column],
        [PAIR_ATTN]
        + [PAIR_COLUMNS] * 4
        + [PAIR_ROWS, PAIR_DENS, PAIR_COEF, pair_block(16, 128), pair_block(128, 128)],
        [tall, tall, shape((SEGL, D), F32), shape((PAIRS, 16, 128), F32)],
        [PAIR_COLUMNS] * 3 + [pair_block(16, 128)],
        [
            VMEM((128, SEGL), F32),
            VMEM((SEGL, 128), F32),
            VMEM((SEGL, 128), F32),
            VMEM((16, SEGL), F32),
        ],
        grid=(PAIRS,),
        cost=16.0,
    )
    keep_qk, send_qk, keep_v, send_v, dv = run(
        functools.partial(qkv_grad_kernel, (BACK_QK, BACK_V)),
        "qkv_grad",
        [info, x, dq, dk, dv, coef_grad, jnp.asarray(ridge.T)],
        [SCALARS] + [FULL] * 6,
        [shape(piece_dims(BACK_QK) + (96, 384))] * 2 + narrow_grad + [tall],
        [ANY] * 4 + [FULL],
        [VMEM((D, SEGL), BF16)] + [VMEM(MATRIX, BF16)] * 3 + [DMA((2,))],
        cost=6.0,
    )

    gauss_grad = gauss_grad[:, :4].reshape(PAIRS, 2, 2, 2, DH)
    gauss_grad = jnp.stack([gauss_grad[:, :, h, h] for h in range(2)], axis=2)
    gauss_grad = gauss_grad.transpose(1, 0, 2, 3).reshape(2, 4, 3, dp_count, -1)
    small_grads = jnp.concatenate(
        [
            gauss_grad.transpose(3, 1, 0, 2, 4).reshape(dp_count * 4, -1),
            gain_part.reshape(dp_count * 4, -1),
            bias_part.reshape(dp_count * 4, -1),
        ],
        axis=1,
    )
    count = small_grads.shape[1]
    if near:
        small_grads = small_grads[jnp.arange(32) ^ (dp * 4 + rank)]
        at = {"z": 0, "y": 1, "x": 2, "c": 3}
        small_grads = small_grads.reshape(4, 2, 2, 2, count).transpose(
            [at["c"]] + [at[letter] for letter in BACK_V] + [4]
        )
        small_grads = jnp.pad(small_grads[..., None, :], ((0, 0),) * 4 + ((0, 15), (0, 384 - count)))
        small_grads = small_grads.astype(BF16)
        joined = [
            jnp.concatenate(parts, axis=3)
            for parts in ((keep_v, keep_out, small_grads[0]), (send_v, send_out, small_grads[1]))
        ]
        own_v = scatter(*joined, BACK_V)
        own_small = own_v[96, :count]
        own_qk = scatter(keep_qk, send_qk, BACK_QK)
        narrow = jnp.concatenate([own_qk, own_v[:96]]).reshape(4, 48, 384)
        mine = lax.dynamic_slice_in_dim(narrow, core * 192, 192, axis=2)
        partner = swap(lax.dynamic_slice_in_dim(narrow, (1 - core) * 192, 192, axis=2))
        narrow = jnp.where(
            core == 0,
            jnp.concatenate([mine, partner], axis=1),
            jnp.concatenate([partner, mine], axis=1),
        )
    else:
        own_small = lax.psum_scatter(small_grads, AXES, scatter_dimension=0)
        pieces = [
            whole_from(keep_qk, send_qk, BACK_QK).reshape(8, 2, 2, 2, 48, 384),
            whole_from(keep_v, send_v, BACK_V)[:, :, :, None],
            whole_from(keep_out, send_out, BACK_V)[:, :, :, None],
        ]
        pieces = jnp.concatenate(pieces, axis=3).transpose(0, 2, 4, 3, 1, 5)
        pieces = pieces.reshape(dp_count, D // dp_count, 4, 4, 192).transpose(0, 3, 2, 1, 4)
        narrow = lax.psum_scatter(
            pieces.reshape((-1,) + pieces.shape[2:]).astype(F32), AXES, scatter_dimension=0
        )
    own_qkv, own_out = narrow[:3], narrow[3].T
    own_gauss = own_small[:gauss_size].reshape(w_gauss.shape)
    own_gain = own_small[gauss_size : gauss_size + gain_size]
    own_bias = own_small[gauss_size + gain_size :]

    (grad_tokens,) = run(
        functools.partial(input_grad_kernel, table_qk, table_v),
        "input_grad",
        [info, dq, dk, dv, resid_grad] + qk_parts + v_parts,
        [SCALARS] + [FULL] * 4 + [ANY] * 8,
        [shape((SEGL, D), F32)],
        [FULL],
        [VMEM(MATRIX, BF16)] * 3 + [DMA((2,))],
        cost=5.0,
    )
    (output,) = run(
        functools.partial(output_kernel, table_down),
        "output",
        [info, hidden, residual] + down_parts,
        [SCALARS] + [FULL] * 2 + [ANY] * 4,
        [shape((SEGL, D), F32)],
        [FULL],
        [VMEM(WIDE, BF16), DMA((4,))],
        cost=6.0,
    )
    return (
        from_segment(output),
        from_segment(grad_tokens),
        own_qkv,
        own_gauss,
        own_out,
        own_gain,
        own_bias,
        own_up,
        own_down,
    )


def collect(keep, send, order, dp_count, columns):
    if dp_count == 8:
        return scatter(keep, send, order)
    whole = whole_from(keep, send, order).transpose(0, 3, 1, 2, 4)
    whole = whole.reshape(dp_count, D // dp_count, 4, columns).transpose(0, 2, 1, 3)
    return lax.psum_scatter(
        whole.reshape((-1,) + whole.shape[2:]).astype(F32), AXES, scatter_dimension=0
    )


def solution(mesh):
    return jax.shard_map(
        local,
        mesh=mesh,
        in_specs=(
            P("dp", "tensor", None),
            P("dp"),
            P("dp", None, None),
            P("dp", "tensor", None),
            P(None, "dp", "tensor"),
            P(None, "tensor", "dp"),
            P("tensor", "dp"),
            P(("dp", "tensor")),
            P(("dp", "tensor")),
            P("dp", "tensor"),
            P("tensor", "dp"),
        ),
        out_specs=(
            P("dp", "tensor", None),
            P("dp", "tensor", None),
            P(None, "dp", "tensor"),
            P(None, "tensor", "dp"),
            P("tensor", "dp"),
            P(("dp", "tensor")),
            P(("dp", "tensor")),
            P("dp", "tensor"),
            P("tensor", "dp"),
        ),
        check_vma=False,
    )
```

time: 596 us -> 340 us (0.57); the launches traced: 588 us -> 338 us
  local copies, waits for them, and re-layouts: 163 us -> 42.7 us
  Pallas kernels: 0 us -> 115 us
  matrix products: 101 us -> 0 us
  other arithmetic: 109 us -> 32 us
  waiting for transfers between devices: 133 us -> 72.1 us
    pallas_call x0 -> x10, Pallas kernels: none -> 115 us  [run(): pl.pallas_call(body, name=name, out_shape=tuple(outs), in_specs=list(in_s...]
    dot_general x32 -> x0, matrix products: 92.3 us -> none  [the longest x20 61.4 us: dot(): lax.dot_general(left, right, (((left_dim,), (right_dim,)), ((), ())), pre...]
    ppermute x60 -> x58, waiting for transfers between devices: 133 us -> 69.4 us  [xor_permute(): return lax.ppermute(value, AXES, pairs)]
    gather x12 -> x3, local copies, waits for them, and re-layouts: 42.1 us -> 4.13 us  [the longest x2 3.4 us: local(): rows = rows[position[jnp.arange(32) ^ dp * 4 + rank]]]
    convert_element_type x8 -> x0, local copies, waits for them, and re-layouts: 37.1 us -> none  [the longest x4 30.8 us: scatter_all(): value = jnp.take(parts.astype(BF16), jnp.arange(32) ^ me, axis=0)]
    another operation x21 -> x9, other arithmetic: 37.7 us -> 4.64 us  [gather(): jnp.stack([piece] + [xor_permute(piece, letter, k) for k in range(1, SIZE...]
    squeeze x30 -> x5, local copies, waits for them, and re-layouts: 27.5 us -> 2.06 us  [the longest x1 1.96 us: to_segment_parts(): lax.dynamic_index_in_dim(local, 1 - core, 0, keepdims=False)]
    select_n x14 -> x5, other arithmetic: 22.9 us -> 1.79 us  [the longest x1 1.39 us: local(): jnp.where(core == 0, jnp.concatenate([mine, partner], axis=1), jnp.concat...]
  transfers between devices with their start and end apart: 66 -> 60, of which waited for: 20 -> 20; matrix products, arithmetic and copies ran while one was open for 45% -> 17% of each run, Pallas kernels for 0% -> 34%
where the time goes in v2:
time: 340 us; the launch traced here: 338 us
  Pallas kernels  115 us (34%)
  starting transfers between devices  74.5 us (22%)
  waiting for transfers between devices  72.1 us (21%)
  local copies, waits for them, and re-layouts  42.7 us (13%)
  other arithmetic  32 us (9%)
    pallas_call x10, Pallas kernels, run(): pl.pallas_call(body, name=name, out_shape=tuple(outs), in_specs=list(in_s...  115 us
    ppermute x58, waiting for transfers between devices, xor_permute(): return lax.ppermute(value, AXES, pairs)  69.4 us
    ppermute x58, starting transfers between devices, xor_permute(): return lax.ppermute(value, AXES, pairs)  69.4 us
    unnamed x75, local copies, waits for them, and re-layouts  16.8 us
    convert_element_type x11, other arithmetic, scatter(): total(k).astype(BF16)  14.1 us
  transfers between devices with their start and end apart: 60, of which 20 were waited for; matrix products, arithmetic and copies ran while one was open for 17% of the time, Pallas kernels for 34%

profile of v2, /device:TPU:0, one launch (start us, length us, event | category | flops | bytes accessed | tf_op | source)
XLA Modules:
  0.0 338.3 jit_solution(9859487039681078652)
XLA Ops:
  14.3 3.5 %collective-permute-start.3 = (bf16[96,384]{1,0:T(8,128)(2,1)S(1)}, bf16[96,384]{1,0:T(8,128)(2,1)S(1)}, u32[]{:S(2)}, u32[]{:S(2)}) collective-permute-start(bf16[96,384]{1,0:T(8,128)(2,1)S(1)} %bitcast.390), channel_id=1, source_target_pairs={{0,16},{1,17},{2,18},{3,19},{4,20},{5,21},{6,22},{7,23},{8,24},{9,... | collective-permute-start | bytes 221192 | tf_op jit(solution)/shard_map/ppermute | solution.py:45
  17.7 3.1 collective-permute-done.10
  20.8 4.6 %collective-permute-start.4 = (bf16[96,384]{1,0:T(8,128)(2,1)S(1)}, bf16[96,384]{1,0:T(8,128)(2,1)S(1)}, u32[]{:S(2)}, u32[]{:S(2)}) collective-permute-start(bf16[96,384]{1,0:T(8,128)(2,1)S(1)} %bitcast.391), channel_id=1, source_target_pairs={{0,24},{1,25},{2,26},{3,27},{4,28},{5,29},{6,30},{7,31},{8,16},{9,... | collective-permute-start | bytes 221192 | tf_op jit(solution)/shard_map/ppermute | solution.py:45
  28.6 3.7 %collective-permute-start.20 = (bf16[96,768]{1,0:T(8,128)(2,1)S(1)}, bf16[96,768]{1,0:T(8,128)(2,1)S(1)}, u32[]{:S(2)}, u32[]{:S(2)}) collective-permute-start(bf16[96,768]{1,0:T(8,128)(2,1)S(1)} %copy-done.27), channel_id=1, source_target_pairs={{0,24},{1,25},{2,26},{3,27},{4,28},{5,29},{6,30},{7,31},{8,16},{9,... | collective-permute-start | bytes 442376 | tf_op jit(solution)/shard_map/ppermute | solution.py:45
  45.3 14.7 %collective-permute-done.27 = bf16[2,96,768]{2,1,0:T(8,128)(2,1)S(1)} collective-permute-done((bf16[2,96,768]{2,1,0:T(8,128)(2,1)S(1)}, bf16[2,96,768]{2,1,0:T(8,128)(2,1)S(1)}, u32[]{:S(2)}, u32[]{:S(2)}) %collective-permute-start.27) | collective-permute-done | bytes 294944 | tf_op jit(solution)/shard_map/ppermute | solution.py:45
  71.3 3.7 %collective-permute-done.6.refs_1_ = bf16[2,4,96,384]{3,2,1,0:T(8,128)(2,1)} collective-permute-done((bf16[2,4,96,384]{3,2,1,0:T(8,128)(2,1)}, bf16[2,4,96,384]{3,2,1,0:T(8,128)(2,1)}, u32[]{:S(2)}, u32[]{:S(2)}) %collective-permute-start.6) | collective-permute-done | bytes 589856 | tf_op jit(solution)/shard_map/ppermute | solution.py:45
  93.0 7.9 %qkv.1 = (bf16[512,768]{1,0:T(8,128)(2,1)}, bf16[512,768]{1,0:T(8,128)(2,1)}, bf16[512,768]{1,0:T(8,128)(2,1)}, bf16[512,768]{1,0:T(8,128)(2,1)}, bf16[256,768]{1,0:T(8,128)(2,1)}) custom-call(s32[6]{0:T(128)S(1)} %stack.144.info, bf16[256,768]{1,0:T(8,128)(2,1)S(1)} %get-tuple-element.142.own, bf16[256,768]{1,0:T(8,128)(2,1)} %collective-permute-done.other, ...), custom_call_target="tpu_custom_call" | custom-call | flops 5400000000 | bytes 1000000 | tf_op jit(solution)/shard_map/qkv/pallas_call | solution.py:557
  101.0 3.9 %collective-permute-start.16 = (bf16[256,768]{1,0:T(8,128)(2,1)}, bf16[256,768]{1,0:T(8,128)(2,1)}, u32[]{:S(2)}, u32[]{:S(2)}) collective-permute-start(bf16[256,768]{1,0:T(8,128)(2,1)} %get-tuple-element.47), channel_id=1, source_target_pairs={{0,2},{1,3},{4,6},{5,7},{8,10},{9,11},{12,14},{13,15},{16,18},{17,... | collective-permute-start | bytes 1179656 | tf_op jit(solution)/shard_map/ppermute | solution.py:683
  108.2 12.7 %attend.1 = (bf16[12,512,512]{2,1,0:T(8,128)(2,1)}, f32[768,512]{1,0:T(8,128)S(1)}, bf16[12,256,512]{2,1,0:T(8,128)(2,1)}) custom-call(s32[6]{0:T(128)S(1)} %stack.144.info, bf16[512,768]{1,0:T(8,128)(2,1)S(1)} %copy-done.14, bf16[512,768]{1,0:T(8,128)(2,1)S(1)} %copy-done.16, bf16[512,768]{1,0:T(8,128)(2,1)S(1)} %copy-done.18, ...), custom_call_target="tpu_custom_call" | custom-call | flops 10800000000 | bytes 1000000 | tf_op jit(solution)/shard_map/attend/pallas_call | solution.py:557
  125.3 8.5 %recall.1 = (bf16[512,768]{1,0:T(8,128)(2,1)S(1)}, f32[512,768]{1,0:T(8,128)}, bf16[512,768]{1,0:T(8,128)(2,1)S(1)}, bf16[768,512]{1,0:T(8,128)(2,1)S(1)}) custom-call(s32[6]{0:T(128)S(1)} %stack.144.info, bf16[12,256,512]{2,1,0:T(8,128)(2,1)} %get-tuple-element.46.dens_t, bf16[256,768]{1,0:T(8,128)(2,1)} %collective-permute-done.16.coef, ...), custom_call_target="tpu_custom_call" | custom-call | flops 6300000256 | bytes 1000000 | tf_op jit(solution)/shard_map/recall/pallas_call | solution.py:557
  133.9 18.5 %up.1 = (bf16[512,3072]{1,0:T(8,128)(2,1)}, bf16[512,3072]{1,0:T(8,128)(2,1)}, bf16[2,4,2,96,768]{4,3,2,1,0:T(8,128)(2,1)}, bf16[2,4,2,96,768]{4,3,2,1,0:T(8,128)(2,1)}) custom-call(s32[6]{0:T(128)S(1)} %stack.144.info, bf16[512,768]{1,0:T(8,128)(2,1)S(1)} %get-tuple-element.50.normed, bf16[768,512]{1,0:T(8,128)(2,1)S(1)} %copy-done.3, ...), custom_call_target="tpu_custom_call" | custom-call | flops 10800000000 | bytes 1000000 | tf_op jit(solution)/shard_map/up/pallas_call | solution.py:557
  152.5 20.8 %down.1 = (bf16[2,2,4,96,768]{4,3,2,1,0:T(8,128)(2,1)}, bf16[2,2,4,96,768]{4,3,2,1,0:T(8,128)(2,1)}, f32[512,768]{1,0:T(8,128)}, f32[1,768]{1,0:T(1,128)S(1)}, f32[1,768]{1,0:T(1,128)S(1)}) custom-call(s32[6]{0:T(128)S(1)} %stack.144.info, bf16[512,768]{1,0:T(8,128)(2,1)S(1)} %fusion.5.seed, bf16[768,512]{1,0:T(8,128)(2,1)S(1)} %get-tuple-element.54.normed_t, ...), custom_call_target="tpu_custom_call" | custom-call | flops 13500000256 | bytes 1000000 | tf_op jit(solution)/shard_map/down/pallas_call | solution.py:557
  173.9 9.8 %mix_back.1 = (bf16[512,768]{1,0:T(8,128)(2,1)S(1)}, bf16[256,768]{1,0:T(8,128)(2,1)}, bf16[2,2,4,48,384]{4,3,2,1,0:T(8,128)(2,1)S(1)}, bf16[2,2,4,48,384]{4,3,2,1,0:T(8,128)(2,1)S(1)}) custom-call(s32[6]{0:T(128)S(1)} %stack.144.info, f32[512,768]{1,0:T(8,128)} %get-tuple-element.56.resid_grad, bf16[512,768]{1,0:T(8,128)(2,1)S(1)} %get-tuple-element.57.heads_out, ...), custom_call_target="tpu_custom_call" | custom-call | flops 5400000000 | bytes 1000000 | tf_op jit(solution)/shard_map/mix_back/pallas_call | solution.py:557
  185.0 13.3 %attend_back.1 = (bf16[512,768]{1,0:T(8,128)(2,1)S(1)}, bf16[512,768]{1,0:T(8,128)(2,1)S(1)}, f32[512,768]{1,0:T(8,128)}, f32[6,16,128]{2,1,0:T(8,128)S(1)}) custom-call(bf16[12,512,512]{2,1,0:T(8,128)(2,1)} %get-tuple-element.53.attn_t, bf16[512,768]{1,0:T(8,128)(2,1)S(1)} %copy-done.15, bf16[512,768]{1,0:T(8,128)(2,1)S(1)} %copy-done.17, ...), custom_call_target="tpu_custom_call" | custom-call | flops 14400000000 | bytes 1000000 | tf_op jit(solution)/shard_map/attend_back/pallas_call | solution.py:557
  205.0 6.8 %qkv_grad.1 = (bf16[2,2,4,96,384]{4,3,2,1,0:T(8,128)(2,1)S(1)}, bf16[2,2,4,96,384]{4,3,2,1,0:T(8,128)(2,1)}, bf16[2,2,4,48,384]{4,3,2,1,0:T(8,128)(2,1)S(1)}, bf...) custom-call(s32[6]{0:T(128)S(1)} %stack.144.info, bf16[512,768]{1,0:T(8,128)(2,1)S(1)} %copy-done.13, ...), custom_call_target="tpu_custom_call" | custom-call | flops 5400000000 | bytes 1000000 | tf_op jit(solution)/shard_map/qkv_grad/pallas_call | solution.py:557
  212.8 8.8 %output.1 = f32[512,768]{1,0:T(8,128)} custom-call(s32[6]{0:T(128)S(1)} %stack.144.info, bf16[512,3072]{1,0:T(8,128)(2,1)} %get-tuple-element.51.hidden, f32[512,768]{1,0:T(8,128)} %get-tuple-element.52.residual, bf16[4,2,96,768]{3,2,1,0:T(8,128)(2,1)S(1)} %pad_maximum_fusion.3.refs_0_, bf16[4,2,96,768]{3,2,1,0:T(8,128)(2,1)} %collective-permute-done.29.refs_1_, ...), custom_call_target="tpu_custom_call" | custom-call | flops 5400000000 | bytes 1000000 | tf_op jit(solution)/shard_map/output/pallas_call | solution.py:557
  223.7 7.7 %input_grad.1 = f32[512,768]{1,0:T(8,128)} custom-call(s32[6]{0:T(128)S(1)} %stack.144.info, bf16[512,768]{1,0:T(8,128)(2,1)S(1)} %copy-done.8, bf16[512,768]{1,0:T(8,128)(2,1)} %copy-done.9, bf16[512,768]{1,0:T(8,128)(2,1)} %copy-done.11, f32[512,768]{1,0:T(8,128)} %get-tuple-element.56.resid_grad, bf16[2,4,96,384]{3,2,1,0:T(8,128)(2,1)} %pad_maximum_fusion.5.refs_0_, ...), custom_call_target="tpu_custom_call" | custom-call | flops 4499999744 | bytes 1000000 | tf_op jit(solution)/shard_map/input_grad/pallas_call | solution.py:557
  240.6 9.4 %collective-permute-done.36 = bf16[2,4,96,384]{3,2,1,0:T(8,128)(2,1)S(1)} collective-permute-done((bf16[2,4,96,384]{3,2,1,0:T(8,128)(2,1)S(1)}, bf16[2,4,96,384]{3,2,1,0:T(8,128)(2,1)S(1)}, u32[]{:S(2)}, u32[]{:S(2)}) %collective-permute-start.36) | collective-permute-done | bytes 589856 | tf_op jit(solution)/shard_map/ppermute | solution.py:45
  251.7 3.2 fusion.1
  257.8 4.0 %fusion = (bf16[2,4,96,768]{3,2,1,0:T(8,128)(2,1)}, f32[1,2,4,96,768]{4,3,2,1,0:T(8,128)}) fusion(bf16[2,2,4,96,768]{4,3,2,1,0:T(8,128)(2,1)} %collective-permute-done.48, bf16[2,2,4,96,768]{4,3,2,1,0:T(8,128)(2,1)S(1)} %copy-done.21), kind=kLoop, calls=%fused_computation.13 | loop fusion | flops 4128768 | bytes 8257536 | tf_op jit(solution)/shard_map/convert_element_type | solution.py:88
  283.5 3.6 %collective-permute-done.55 = bf16[4,2,96,768]{3,2,1,0:T(8,128)(2,1)} collective-permute-done((bf16[4,2,96,768]{3,2,1,0:T(8,128)(2,1)}, bf16[4,2,96,768]{3,2,1,0:T(8,128)(2,1)}, u32[]{:S(2)}, u32[]{:S(2)}) %collective-permute-start.55) | collective-permute-done | bytes 1179680 | tf_op jit(solution)/shard_map/ppermute | solution.py:45
  304.4 11.7 %collective-permute-done.57 = bf16[2,96,768]{2,1,0:T(8,128)(2,1)} collective-permute-done((bf16[2,96,768]{2,1,0:T(8,128)(2,1)}, bf16[2,96,768]{2,1,0:T(8,128)(2,1)}, u32[]{:S(2)}, u32[]{:S(2)}) %collective-permute-start.57) | collective-permute-done | bytes 294944 | tf_op jit(solution)/shard_map/ppermute | solution.py:45
  318.7 5.4 %collective-permute-start.51 = (bf16[96,768]{1,0:T(8,128)(2,1)S(1)}, bf16[96,768]{1,0:T(8,128)(2,1)S(1)}, u32[]{:S(2)}, u32[]{:S(2)}) collective-permute-start(bf16[96,768]{1,0:T(8,128)(2,1)S(1)} %get-tuple-element.124), channel_id=1, source_target_pairs={{0,8},{1,9},{2,10},{3,11},{4,12},{5,13},{6,14},{7,15},{8,0},{9,1},... | collective-permute-start | bytes 442376 | tf_op jit(solution)/shard_map/ppermute | solution.py:45
  328.7 7.8 %collective-permute-done.52 = bf16[96,768]{1,0:T(8,128)(2,1)S(1)} collective-permute-done((bf16[96,768]{1,0:T(8,128)(2,1)S(1)}, bf16[96,768]{1,0:T(8,128)(2,1)S(1)}, u32[]{:S(2)}, u32[]{:S(2)}) %collective-permute-start.52) | collective-permute-done | bytes 147488 | tf_op jit(solution)/shard_map/ppermute | solution.py:45
  (290 shorter events, 139.1 us)
Async XLA Ops:
  3.2 29.2 %collective-permute-start.25 = (bf16[96,768]{1,0:T(8,128)(2,1)}, bf16[96,768]{1,0:T(8,128)(2,1)S(1)}, u32[]{:S(2)}, u32[]{:S(2)}) collective-permute-start(bf16[96,768]{1,0:T(8,128)(2,1)} %bitcast.400), channel_id=1, source_target_pairs={{0,2},{1,3},{2,0},{3,1},{4,6},{5,7},{6,4},{7,5},{8,10},{9,11},{10,... | collective-permute-start | bytes 442376 | tf_op jit(solution)/shard_map/ppermute | solution.py:45
  38.1 22.0 %collective-permute-start.27 = (bf16[2,96,768]{2,1,0:T(8,128)(2,1)S(1)}, bf16[2,96,768]{2,1,0:T(8,128)(2,1)S(1)}, u32[]{:S(2)}, u32[]{:S(2)}) collective-permute-start(bf16[2,96,768]{2,1,0:T(8,128)(2,1)S(1)} %get-tuple-element.150), channel_id=1, source_target_pairs={{0,16},{1,17},{2,18},{3,19},{4,20},{5,21},{6,22},{7,23},{8,24},{9,... | collective-permute-start | bytes 884744 | tf_op jit(solution)/shard_map/ppermute | solution.py:45
  38.1 23.4 %collective-permute-start.28 = (bf16[2,96,768]{2,1,0:T(8,128)(2,1)S(1)}, bf16[2,96,768]{2,1,0:T(8,128)(2,1)S(1)}, u32[]{:S(2)}, u32[]{:S(2)}) collective-permute-start(bf16[2,96,768]{2,1,0:T(8,128)(2,1)S(1)} %get-tuple-element.150), channel_id=1, source_target_pairs={{0,24},{1,25},{2,26},{3,27},{4,28},{5,29},{6,30},{7,31},{8,16},{9,... | collective-permute-start | bytes 884744 | tf_op jit(solution)/shard_map/ppermute | solution.py:45
  40.2 29.0 %collective-permute-start.13 = (bf16[2,4,112,384]{3,2,1,0:T(8,128)(2,1)}, bf16[2,4,112,384]{3,2,1,0:T(8,128)(2,1)}, u32[]{:S(2)}, u32[]{:S(2)}) collective-permute-start(bf16[2,4,112,384]{3,2,1,0:T(8,128)(2,1)} %pad_maximum_fusion.4.refs_4_.refs_0_), channel_id=1, source_target_pairs={{0,4},{1,5},{2,6},{3,7},{4,0},{5,1},{6,2},{7,3},{8,12},{9,13},{10,... | collective-permute-start | bytes 2064392 | tf_op jit(solution)/shard_map/ppermute | solution.py:45
  41.8 21.5 %collective-permute-start.17 = (bf16[256,768]{1,0:T(8,128)(2,1)S(1)}, bf16[256,768]{1,0:T(8,128)(2,1)S(1)}, u32[]{:S(2)}, u32[]{:S(2)}) collective-permute-start(bf16[256,768]{1,0:T(8,128)(2,1)S(1)} %get-tuple-element.140), channel_id=1, source_target_pairs={{0,1},{1,0},{2,3},{3,2},{4,5},{5,4},{6,7},{7,6},{8,9},{9,8},{10,11... | collective-permute-start | bytes 1179656 | tf_op jit(solution)/shard_map/ppermute | solution.py:45
  44.5 26.8 %collective-permute-start.21 = (bf16[4,96,768]{2,1,0:T(8,128)(2,1)}, bf16[4,96,768]{2,1,0:T(8,128)(2,1)}, u32[]{:S(2)}, u32[]{:S(2)}) collective-permute-start(bf16[4,96,768]{2,1,0:T(8,128)(2,1)} %get-tuple-element.144), channel_id=1, source_target_pairs={{0,4},{1,5},{2,6},{3,7},{4,0},{5,1},{6,2},{7,3},{8,12},{9,13},{10,... | collective-permute-start | bytes 1769480 | tf_op jit(solution)/shard_map/ppermute | solution.py:45
  61.6 30.4 %collective-permute-start.29 = (bf16[4,2,96,768]{3,2,1,0:T(8,128)(2,1)S(1)}, bf16[4,2,96,768]{3,2,1,0:T(8,128)(2,1)}, u32[]{:S(2)}, u32[]{:S(2)}) collective-permute-start(bf16[4,2,96,768]{3,2,1,0:T(8,128)(2,1)S(1)} %pad_maximum_fusion.3.refs_0_), channel_id=1, source_target_pairs={{0,4},{1,5},{2,6},{3,7},{4,0},{5,1},{6,2},{7,3},{8,12},{9,13},{10,... | collective-permute-start | bytes 3538952 | tf_op jit(solution)/shard_map/ppermute | solution.py:45
  71.2 19.7 %collective-permute-start.7 = (bf16[2,4,96,384]{3,2,1,0:T(8,128)(2,1)}, bf16[2,4,96,384]{3,2,1,0:T(8,128)(2,1)}, u32[]{:S(2)}, u32[]{:S(2)}) collective-permute-start(bf16[2,4,96,384]{3,2,1,0:T(8,128)(2,1)} %pad_maximum_fusion.5.refs_0_), channel_id=1, source_target_pairs={{0,1},{1,0},{2,3},{3,2},{4,5},{5,4},{6,7},{7,6},{8,9},{9,8},{10,11... | collective-permute-start | bytes 1769480 | tf_op jit(solution)/shard_map/ppermute | solution.py:45
  79.2 73.3 %collective-permute-start.30 = (bf16[4,2,96,768]{3,2,1,0:T(8,128)(2,1)S(1)}, bf16[4,2,96,768]{3,2,1,0:T(8,128)(2,1)}, u32[]{:S(2)}, u32[]{:S(2)}) collective-permute-start(bf16[4,2,96,768]{3,2,1,0:T(8,128)(2,1)S(1)} %pad_maximum_fusion.3.refs_0_), channel_id=1, source_target_pairs={{0,1},{1,0},{2,3},{3,2},{4,5},{5,4},{6,7},{7,6},{8,9},{9,8},{10,11... | collective-permute-start | bytes 3538952 | tf_op jit(solution)/shard_map/ppermute | solution.py:45
  90.7 31.4 %collective-permute-start.22 = (bf16[2,4,96,768]{3,2,1,0:T(8,128)(2,1)S(1)}, bf16[2,4,96,768]{3,2,1,0:T(8,128)(2,1)}, u32[]{:S(2)}, u32[]{:S(2)}) collective-permute-start(bf16[2,4,96,768]{3,2,1,0:T(8,128)(2,1)S(1)} %pad_maximum_fusion.2.refs_0_.refs_4_), channel_id=1, source_target_pairs={{0,2},{1,3},{2,0},{3,1},{4,6},{5,7},{6,4},{7,5},{8,10},{9,11},{10,... | collective-permute-start | bytes 3538952 | tf_op jit(solution)/shard_map/ppermute | solution.py:45
  91.0 42.9 %collective-permute-start.23 = (bf16[2,4,96,768]{3,2,1,0:T(8,128)(2,1)S(1)}, bf16[2,4,96,768]{3,2,1,0:T(8,128)(2,1)}, u32[]{:S(2)}, u32[]{:S(2)}) collective-permute-start(bf16[2,4,96,768]{3,2,1,0:T(8,128)(2,1)S(1)} %pad_maximum_fusion.2.refs_0_.refs_4_), channel_id=1, source_target_pairs={{0,1},{1,0},{2,3},{3,2},{4,5},{5,4},{6,7},{7,6},{8,9},{9,8},{10,11... | collective-permute-start | bytes 3538952 | tf_op jit(solution)/shard_map/ppermute | solution.py:45
  92.0 60.4 %collective-permute-start.31 = (bf16[4,2,96,768]{3,2,1,0:T(8,128)(2,1)}, bf16[4,2,96,768]{3,2,1,0:T(8,128)(2,1)}, u32[]{:S(2)}, u32[]{:S(2)}) collective-permute-start(bf16[4,2,96,768]{3,2,1,0:T(8,128)(2,1)} %collective-permute-done.29.refs_1_), channel_id=1, source_target_pairs={{0,1},{1,0},{2,3},{3,2},{4,5},{5,4},{6,7},{7,6},{8,9},{9,8},{10,11... | collective-permute-start | bytes 3538952 | tf_op jit(solution)/shard_map/ppermute | solution.py:45
  101.0 24.4 %collective-permute-start.16 = (bf16[256,768]{1,0:T(8,128)(2,1)}, bf16[256,768]{1,0:T(8,128)(2,1)}, u32[]{:S(2)}, u32[]{:S(2)}) collective-permute-start(bf16[256,768]{1,0:T(8,128)(2,1)} %get-tuple-element.47), channel_id=1, source_target_pairs={{0,2},{1,3},{4,6},{5,7},{8,10},{9,11},{12,14},{13,15},{16,18},{17,... | collective-permute-start | bytes 1179656 | tf_op jit(solution)/shard_map/ppermute | solution.py:683
  152.4 99.4 %collective-permute-start.54 = (bf16[2,4,2,96,768]{4,3,2,1,0:T(8,128)(2,1)}, bf16[2,4,2,96,768]{4,3,2,1,0:T(8,128)(2,1)}, u32[]{:S(2)}, u32[]{:S(2)}) collective-permute-start(bf16[2,4,2,96,768]{4,3,2,1,0:T(8,128)(2,1)} %get-tuple-element.76), channel_id=1, source_target_pairs={{0,1},{1,0},{2,3},{3,2},{4,5},{5,4},{6,7},{7,6},{8,9},{9,8},{10,11... | collective-permute-start | bytes 7077896 | tf_op jit(solution)/shard_map/ppermute | solution.py:45
  173.3 84.0 %collective-permute-start.48 = (bf16[2,2,4,96,768]{4,3,2,1,0:T(8,128)(2,1)}, bf16[2,2,4,96,768]{4,3,2,1,0:T(8,128)(2,1)}, u32[]{:S(2)}, u32[]{:S(2)}) collective-permute-start(bf16[2,2,4,96,768]{4,3,2,1,0:T(8,128)(2,1)} %get-tuple-element.74), channel_id=1, source_target_pairs={{0,1},{1,0},{2,3},{3,2},{4,5},{5,4},{6,7},{7,6},{8,9},{9,8},{10,11... | collective-permute-start | bytes 7077896 | tf_op jit(solution)/shard_map/ppermute | solution.py:45
  183.6 18.0 %collective-permute-start.33 = (bf16[256,768]{1,0:T(8,128)(2,1)}, bf16[256,768]{1,0:T(8,128)(2,1)S(1)}, u32[]{:S(2)}, u32[]{:S(2)}) collective-permute-start(bf16[256,768]{1,0:T(8,128)(2,1)} %get-tuple-element.62), channel_id=1, source_target_pairs={{2,0},{3,1},{6,4},{7,5},{10,8},{11,9},{14,12},{15,13},{18,16},{19,... | collective-permute-start | bytes 1179656 | tf_op jit(solution)/shard_map/ppermute | solution.py:746
  211.8 21.1 %collective-permute-start.35 = (bf16[2,2,4,96,384]{4,3,2,1,0:T(8,128)(2,1)}, bf16[2,2,4,96,384]{4,3,2,1,0:T(8,128)(2,1)S(1)}, u32[]{:S(2)}, u32[]{:S(2)}) collective-permute-start(bf16[2,2,4,96,384]{4,3,2,1,0:T(8,128)(2,1)} %get-tuple-element.65), channel_id=1, source_target_pairs={{0,1},{1,0},{2,3},{3,2},{4,5},{5,4},{6,7},{7,6},{8,9},{9,8},{10,11... | collective-permute-start | bytes 3538952 | tf_op jit(solution)/shard_map/ppermute | solution.py:45
  212.7 24.7 %collective-permute-start.41 = (bf16[2,2,4,112,384]{4,3,2,1,0:T(8,128)(2,1)S(1)}, bf16[2,2,4,112,384]{4,3,2,1,0:T(8,128)(2,1)S(1)}, u32[]{:S(2)}, u32[]{:S(2)}) collective-permute-start(bf16[2,2,4,112,384]{4,3,2,1,0:T(8,128)(2,1)S(1)} %pad_maximum_fusion.1), channel_id=1, source_target_pairs={{0,1},{1,0},{2,3},{3,2},{4,5},{5,4},{6,7},{7,6},{8,9},{9,8},{10,11... | collective-permute-start | bytes 4128776 | tf_op jit(solution)/shard_map/ppermute | solution.py:45
  237.7 18.4 %collective-permute-start.42 = (bf16[2,4,112,384]{3,2,1,0:T(8,128)(2,1)S(1)}, bf16[2,4,112,384]{3,2,1,0:T(8,128)(2,1)S(1)}, u32[]{:S(2)}, u32[]{:S(2)}) collective-permute-start(bf16[2,4,112,384]{3,2,1,0:T(8,128)(2,1)S(1)} %get-tuple-element.118), channel_id=1, source_target_pairs={{0,4},{1,5},{2,6},{3,7},{4,0},{5,1},{6,2},{7,3},{8,12},{9,13},{10,... | collective-permute-start | bytes 2064392 | tf_op jit(solution)/shard_map/ppermute | solution.py:45
  254.9 32.1 %collective-permute-start.55 = (bf16[4,2,96,768]{3,2,1,0:T(8,128)(2,1)}, bf16[4,2,96,768]{3,2,1,0:T(8,128)(2,1)}, u32[]{:S(2)}, u32[]{:S(2)}) collective-permute-start(bf16[4,2,96,768]{3,2,1,0:T(8,128)(2,1)} %get-tuple-element.108), channel_id=1, source_target_pairs={{0,4},{1,5},{2,6},{3,7},{4,0},{5,1},{6,2},{7,3},{8,12},{9,13},{10,... | collective-permute-start | bytes 3538952 | tf_op jit(solution)/shard_map/ppermute | solution.py:45
  261.8 33.0 %collective-permute-start.49 = (bf16[2,4,96,768]{3,2,1,0:T(8,128)(2,1)}, bf16[2,4,96,768]{3,2,1,0:T(8,128)(2,1)}, u32[]{:S(2)}, u32[]{:S(2)}) collective-permute-start(bf16[2,4,96,768]{3,2,1,0:T(8,128)(2,1)} %get-tuple-element.110), channel_id=1, source_target_pairs={{0,2},{1,3},{2,0},{3,1},{4,6},{5,7},{6,4},{7,5},{8,10},{9,11},{10,... | collective-permute-start | bytes 3538952 | tf_op jit(solution)/shard_map/ppermute | solution.py:45
  292.3 23.7 %collective-permute-start.57 = (bf16[2,96,768]{2,1,0:T(8,128)(2,1)}, bf16[2,96,768]{2,1,0:T(8,128)(2,1)}, u32[]{:S(2)}, u32[]{:S(2)}) collective-permute-start(bf16[2,96,768]{2,1,0:T(8,128)(2,1)} %get-tuple-element.114), channel_id=1, source_target_pairs={{0,16},{1,17},{2,18},{3,19},{4,20},{5,21},{6,22},{7,23},{8,24},{9,... | collective-permute-start | bytes 884744 | tf_op jit(solution)/shard_map/ppermute | solution.py:45
  293.3 22.8 %collective-permute-start.58 = (bf16[2,96,768]{2,1,0:T(8,128)(2,1)}, bf16[2,96,768]{2,1,0:T(8,128)(2,1)}, u32[]{:S(2)}, u32[]{:S(2)}) collective-permute-start(bf16[2,96,768]{2,1,0:T(8,128)(2,1)} %get-tuple-element.113), channel_id=1, source_target_pairs={{0,24},{1,25},{2,26},{3,27},{4,28},{5,29},{6,30},{7,31},{8,16},{9,... | collective-permute-start | bytes 884744 | tf_op jit(solution)/shard_map/ppermute | solution.py:45
  297.2 20.3 %collective-permute-start.50 = (bf16[4,96,768]{2,1,0:T(8,128)(2,1)}, bf16[4,96,768]{2,1,0:T(8,128)(2,1)}, u32[]{:S(2)}, u32[]{:S(2)}) collective-permute-start(bf16[4,96,768]{2,1,0:T(8,128)(2,1)} %get-tuple-element.116), channel_id=1, source_target_pairs={{0,4},{1,5},{2,6},{3,7},{4,0},{5,1},{6,2},{7,3},{8,12},{9,13},{10,... | collective-permute-start | bytes 1769480 | tf_op jit(solution)/shard_map/ppermute | solution.py:45
  (70 other events, 724.2 us)

commit v3 on v2

--- a/solution.py
+++ b/solution.py
@@ -49,10 +49,14 @@
     return xor_permute(value, "c", 1)
 
 
-def piece_table(order):
+def after(value, *others):
+    return lax.optimization_barrier((value,) + others)[0]
+
+
+def piece_table(order, cores=2):
     first, second, third = order
     table = []
-    for at, (k3, kc) in enumerate([(0, 0), (1, 0), (0, 1), (1, 1)]):
+    for at, (kc, k3) in enumerate([(0, 0), (0, 1), (1, 0), (1, 1)][: 2 * cores]):
         for i2 in range(SIZES[second]):
             for i1 in range(SIZES[first]):
                 k = {first: i1, second: i2, third: k3}
@@ -60,14 +64,8 @@
     return table
 
 
-def gather(piece, order):
-    first, second, third = order
-    for letter in (first, second):
-        piece = jnp.stack(
-            [piece] + [xor_permute(piece, letter, k) for k in range(1, SIZES[letter])]
-        )
-    other = xor_permute(piece, third, 1)
-    return [piece, other, swap(piece), swap(other)]
+def spread(piece, letter):
+    return [piece] + [xor_permute(piece, letter, k) for k in range(1, SIZES[letter])]
 
 
 def as_gathered(whole, order):
@@ -79,25 +77,23 @@
     return [whole[0, 0], whole[0, 1], whole[1, 0], whole[1, 1]]
 
 
-def scatter(keep, send, order):
-    received = swap(send)
-    total = lambda k: keep[k].astype(F32) + received[k].astype(F32)
-    for letter in order:
-        own = total(0)
-        arrived = [
-            xor_permute(total(k).astype(BF16), letter, k) for k in range(1, SIZES[letter])
-        ]
-        total = lambda k, own=own, arrived=arrived: sum(
-            (a[k].astype(F32) for a in arrived), own[k]
-        )
-        last = (own, arrived)
-    own, arrived = last
+def stage(total, letter):
+    own = total(0)
+    arrived = [xor_permute(total(k).astype(BF16), letter, k) for k in range(1, SIZES[letter])]
+    return own, arrived
+
+
+def combined(own, arrived):
+    return lambda k: sum((a[k].astype(F32) for a in arrived), own[k])
+
+
+def final_sum(own, arrived):
     return sum((a.astype(F32) for a in arrived), own)
 
 
-def whole_from(keep, send, order):
+def whole_from(parts, order):
     first, second, third = order
-    whole = jnp.stack([keep, send])
+    whole = jnp.stack(parts)
     at = {"c": 0, first: 1, second: 2, third: 3}
     rest = list(range(4, whole.ndim))
     whole = whole.transpose([at["z"], at["y"], at["x"], at["c"]] + rest)
@@ -139,11 +135,10 @@
 
 
 def wide_copies(info, table, arrays, target, sems):
-    for at, index, r, kx, kc in table:
+    for at, index, r, kx, _ in table:
         rows = pl.ds(aligned(info[0] ^ r, 96), 96)
-        j = kx * 2 + kc
         yield pltpu.make_async_copy(
-            arrays[at].at[index], target.at[rows, pl.ds(j * D, D)], sems.at[j]
+            arrays[at].at[index], target.at[rows, pl.ds(kx * D, D)], sems.at[kx]
         )
 
 
@@ -167,7 +162,7 @@
 
 
 def out_narrow(info, order, keep, send, spots, sem):
-    for at, index, r, kx, kc in scatter_table(order):
+    for index, r, kx, kc in scatter_table(order):
         rows = pl.ds(pl.multiple_of((info[0] ^ r) * 96 + (info[2] ^ kc) * 48, 48), 48)
         columns = pl.ds(aligned(info[1] ^ kx, 384), 384)
         for first, source in spots:
@@ -176,15 +171,15 @@
             )
 
 
-def scatter_table(order):
+def scatter_table(order, cores=2):
     a, b, c = order
     table = []
-    for kc in range(2):
+    for kc in range(cores):
         for i in range(SIZES[a]):
             for j in range(SIZES[b]):
                 for l in range(SIZES[c]):
                     k = {a: i, b: j, c: l}
-                    table.append((kc, (i, j, l), k["z"] * 2 + k["y"], k["x"], kc))
+                    table.append(((i, j, l), k["z"] * 2 + k["y"], k["x"], kc))
     return table
 
 
@@ -281,8 +276,8 @@
 
 def recall_kernel(table, info, dens_t, coef, local_t, x, gain, bias, *refs):
     parts = refs[0:4]
-    heads_out, residual, normed, normed_t = refs[4:8]
-    w_out, sem = refs[8:]
+    heads_out, residual, normed = refs[4:7]
+    w_out, sem = refs[7:]
     step = pl.program_id(0)
 
     @pl.when(step == 0)
@@ -305,9 +300,7 @@
             residual[:, at] = x[:, at].astype(F32) + dot(heads_out[...], w_out[at, :], 1, 1)
 
         centred, scale = layer_stats(residual[...])
-        value = (centred * scale * gain[...] + bias[...]).astype(BF16)
-        normed[...] = value
-        normed_t[...] = flip(value).astype(BF16)
+        normed[...] = (centred * scale * gain[...] + bias[...]).astype(BF16)
 
 
 def gelu_parts(pre):
@@ -319,38 +312,40 @@
     return pre * half, slope
 
 
-def wide_out(info, order, keep, send, source, sems):
-    for at, index, r, kx, kc in scatter_table(order):
+def wide_out(info, order, keep, source, sems):
+    for index, r, kx, _ in scatter_table(order, 1):
         rows = pl.ds(aligned(info[0] ^ r, 96), 96)
-        j = kx * 2 + kc
-        yield j, pltpu.make_async_copy(
-            source.at[rows, pl.ds(j * D, D)], (keep, send)[kc].at[index], sems.at[j]
+        yield kx, pltpu.make_async_copy(
+            source.at[rows, pl.ds(kx * D, D)], keep.at[index], sems.at[kx]
         )
 
 
 def wait_out(source, sems):
-    for j in range(4):
+    for j in range(2):
         wait_wide(source, sems, j)
 
 
-def up_kernel(table, order, info, normed, seed_t, *refs):
-    parts = refs[0:4]
-    hidden, slope, keep, send = refs[4:8]
-    w_up, grad, sems, out_sems = refs[8:]
+def up_kernel(table, order, info, own, other, seed_t, *refs):
+    parts = refs[0:2]
+    hidden, slope, keep = refs[2:5]
+    w_up, grad, sems, out_sems = refs[5:]
     for copy in wide_copies(info, table, parts, w_up, sems):
         copy.start()
-    outs = list(wide_out(info, order, keep, send, grad, out_sems))
-    for j in (0, 2, 1, 3):
+    outs = list(wide_out(info, order, keep, grad, out_sems))
+    for j in range(2):
         wait_wide(w_up, sems, j)
 
         @pl.loop(0, 3)
         def _(chunk):
             at = pl.ds(pl.multiple_of(j * D + chunk * 256, 256), 256)
-            value, derivative = gelu_parts(dot(normed[...], w_up[:, at]))
-            value = value.astype(BF16)
-            hidden[:, at] = value
-            slope[:, at] = derivative.astype(BF16)
-            grad[:, at] = dot(seed_t[...], value).astype(BF16)
+            sums = []
+            for half, source in enumerate((own, other)):
+                value, derivative = gelu_parts(dot(source[...], w_up[:, at]))
+                value = value.astype(BF16)
+                hidden[half, :, at] = value
+                slope[half, :, at] = derivative.astype(BF16)
+                sums.append(dot(seed_t[:, half * SEGL : (half + 1) * SEGL], value))
+            grad[:, at] = (sums[0] + sums[1]).astype(BF16)
 
         for owner, copy in outs:
             if owner == j:
@@ -358,62 +353,70 @@
     wait_out(grad, out_sems)
 
 
-def down_kernel(tables, order, info, seed, normed_t, slope, residual, gain, *refs):
-    down_parts, up_parts = refs[0:4], refs[4:8]
-    keep, send, resid_grad, gain_grad, bias_grad = refs[8:13]
-    w_down, w_up, grad, total, down_sems, up_sems, out_sems = refs[13:]
+def down_kernel(tables, order, info, seed, own, other, slope, *refs):
+    down_parts, up_parts = refs[0:2], refs[2:4]
+    keep, own_grad, other_grad = refs[4:7]
+    w_down, w_up, grad, total, normed_t, down_sems, up_sems, out_sems = refs[7:]
     for copy in wide_copies(info, tables[0], down_parts, w_down, down_sems):
         copy.start()
     for copy in wide_copies(info, tables[1], up_parts, w_up, up_sems):
         copy.start()
-    outs = list(wide_out(info, order, keep, send, grad, out_sems))
+    outs = list(wide_out(info, order, keep, grad, out_sems))
     total[...] = jnp.zeros_like(total)
-    for j in (0, 2, 1, 3):
+    normed_t[:, :SEGL] = flip(own[...]).astype(BF16)
+    normed_t[:, SEGL:] = flip(other[...]).astype(BF16)
+    for j in range(2):
         wait_wide(w_down, down_sems, j)
         wait_wide(w_up, up_sems, j)
 
         @pl.loop(0, 3)
         def _(chunk):
             at = pl.ds(pl.multiple_of(j * D + chunk * 256, 256), 256)
-            back = dot(seed[...], w_down[:, at]).astype(BF16).astype(F32)
-            back = (back * slope[:, at].astype(F32)).astype(BF16)
-            grad[:, at] = dot(normed_t[...], back).astype(BF16)
-            total[...] += dot(back, w_up[:, at], 1, 1)
+            sums = []
+            for half in range(2):
+                back = dot(seed[half], w_down[:, at]).astype(BF16).astype(F32)
+                back = (back * slope[half, :, at].astype(F32)).astype(BF16)
+                sums.append(dot(normed_t[:, half * SEGL : (half + 1) * SEGL], back))
+                total[half] += dot(back, w_up[:, at], 1, 1)
+            grad[:, at] = (sums[0] + sums[1]).astype(BF16)
 
         for owner, copy in outs:
             if owner == j:
                 copy.start()
-    normed_grad = total[...].astype(BF16).astype(F32)
-    centred, scale = layer_stats(residual[...])
-    unit = centred * scale
-    gain_grad[...] = jnp.sum(normed_grad * unit, axis=0, keepdims=True)
-    bias_grad[...] = jnp.sum(normed_grad, axis=0, keepdims=True)
-    back = normed_grad * gain[...]
-    back = back - jnp.mean(back, axis=-1, keepdims=True) - unit * jnp.mean(
-        back * unit, axis=-1, keepdims=True
-    )
-    resid_grad[...] = seed[...].astype(F32) + scale * back
+    own_grad[...] = total[0]
+    other_grad[...] = total[1].astype(BF16)
     wait_out(grad, out_sems)
 
 
-def mix_back_kernel(table, order, info, resid_grad, heads_out, dens_t, *refs):
+def mix_back_kernel(table, order, info, own, other, seed, residual, gain, heads_out, dens_t, *refs):
     parts = refs[0:4]
-    head_grad, coef_grad, keep, send = refs[4:8]
-    w_out, grad, mix_t, sem, out_sem = refs[8:]
+    resid_grad, head_grad, coef_grad, gain_grad, bias_grad, keep, send = refs[4:11]
+    w_out, grad, mix, mix_t, sem, out_sem = refs[11:]
     step = pl.program_id(0)
 
     @pl.when(step == 0)
     def _():
         for copy in narrow_copies(info, table, parts, [(48, w_out)], sem):
             copy.start()
-        mix = resid_grad[...].astype(BF16)
-        mix_t[...] = flip(mix).astype(BF16)
+        normed_grad = (own[...] + other[...].astype(F32)).astype(BF16).astype(F32)
+        centred, scale = layer_stats(residual[...])
+        unit = centred * scale
+        gain_grad[...] = jnp.sum(normed_grad * unit, axis=0, keepdims=True)
+        bias_grad[...] = jnp.sum(normed_grad, axis=0, keepdims=True)
+        back = normed_grad * gain[...]
+        back = back - jnp.mean(back, axis=-1, keepdims=True) - unit * jnp.mean(
+            back * unit, axis=-1, keepdims=True
+        )
+        back = seed[...].astype(F32) + scale * back
+        resid_grad[...] = back
+        mix[...] = back.astype(BF16)
+        mix_t[...] = flip(mix[...]).astype(BF16)
         wait_whole(w_out, sem)
 
         @pl.loop(0, 3)
         def _(chunk):
             at = pl.ds(aligned(chunk, 256), 256)
-            head_grad[:, at] = dot(resid_grad[...].astype(BF16), w_out[:, at]).astype(BF16)
+            head_grad[:, at] = dot(mix[...], w_out[:, at]).astype(BF16)
             grad[:, at] = dot(mix_t[...], heads_out[:, at]).astype(BF16)
 
         for copy in out_narrow(info, order, keep, send, [(0, grad)], out_sem):
@@ -528,8 +531,8 @@
 
 
 def output_kernel(table, info, hidden, residual, *refs):
-    parts = refs[0:4]
-    out, w_down, sems = refs[4:]
+    parts = refs[0:2]
+    out, other, w_down, sems = refs[2:]
     for copy in wide_copies(info, table, parts, w_down, sems):
         copy.start()
     wait_out(w_down, sems)
@@ -537,14 +540,16 @@
     @pl.loop(0, 3)
     def _(chunk):
         at = pl.ds(aligned(chunk, 256), 256)
-        out[:, at] = residual[:, at] + dot(hidden[...], w_down[at, :], 1, 1)
-
-
-FULL = pl.BlockSpec(memory_space=VMEM)
+        out[:, at] = residual[:, at] + dot(hidden[0], w_down[at, :], 1, 1)
+        other[:, at] = dot(hidden[1], w_down[at, :], 1, 1)
+
+
+FULL = pl.BlockSpec()
 ANY = pl.BlockSpec(memory_space=pl.ANY)
 SCALARS = pl.BlockSpec(memory_space=SMEM)
 MATRIX = (D, D)
-WIDE = (D, FF)
+HALF = FF // 2
+WIDE = (D, HALF)
 DMA = pltpu.SemaphoreType.DMA
 
 
@@ -552,19 +557,25 @@
     return jax.ShapeDtypeStruct(dims, dtype)
 
 
-def run(body, name, args, in_specs, outs, out_specs, scratch=(), grid=None, cost=5.0):
+def run(body, name, args, in_specs, outs, out_specs, scratch=(), grid=None, cost=5.0, vmem=48):
     kwargs = {} if grid is None else {"grid": grid}
+    args = [
+        value
+        if spec is SCALARS
+        else pltpu.with_memory_space_constraint(value, pltpu.HBM)
+        for value, spec in zip(args, in_specs)
+    ]
     return pl.pallas_call(
         body,
         name=name,
-        out_shape=tuple(outs),
+        out_shape=tuple(pltpu.HBM(out.shape, out.dtype) for out in outs),
         in_specs=list(in_specs),
         out_specs=tuple(out_specs),
         scratch_shapes=list(scratch),
         cost_estimate=pl.CostEstimate(
-            flops=int(cost * 9e8), bytes_accessed=int(1e6), transcendentals=0
+            flops=int(cost * 2e8), bytes_accessed=int(1e6), transcendentals=0
         ),
-        compiler_params=pltpu.CompilerParams(vmem_limit_bytes=48 * 1024 * 1024),
+        compiler_params=pltpu.CompilerParams(vmem_limit_bytes=vmem * 1024 * 1024),
         **kwargs,
     )(*args)
 
@@ -594,13 +605,13 @@
     gauss_size, gain_size = w_gauss.size, ln_gain.size
     ridge = ridge_matrix()
 
-    used = lax.dynamic_index_in_dim(lengths, core, 0, False)
-    valid_count = jnp.clip(used - segment * SEGL, 0, SEGL)
+    used = [
+        jnp.clip(lax.dynamic_index_in_dim(lengths, at, 0, False) - segment * SEGL, 0, SEGL)
+        for at in (core, 1 - core)
+    ]
     pair = lax.dynamic_index_in_dim(mem_mask, core, 0, False)[1, 0]
     where = (dp, segment, core) if near else (0, 0, 0)
-    info = jnp.stack(
-        [jnp.asarray(value, jnp.int32) for value in where + (valid_count, pair, core)]
-    )
+    info = jnp.stack([jnp.asarray(value, jnp.int32) for value in where + (used[0], pair, core)])
 
     projections = jnp.concatenate([w_qkv, w_out.T[None]])
     if near:
@@ -615,21 +626,19 @@
             [w_gauss.reshape(-1)] + exact_triple(jnp.concatenate([ln_gain, ln_bias]))
         )
         small_rows = jnp.pad(small[None], ((0, 15), (0, 384 - small.size)))
-        qk_parts = gather(projections[:2].reshape(96, 384), ORDER_QK)
-        v_parts = gather(
-            jnp.concatenate([projections[2], projections[3], small_rows]), ORDER_V
-        )
-        up_parts = gather(w_up, ORDER_UP)
-        down_parts = gather(w_down.T, ORDER_DOWN)
-        rows = jnp.concatenate(
-            [part[:, :, 96, : small.size].reshape(-1, small.size) for part in v_parts]
-        )
-        flat = [r * 4 + kx * 2 + kc for _, _, r, kx, kc in piece_table(ORDER_V)]
-        position = jnp.asarray(np.argsort(np.array(flat)))
-        rows = rows[position[jnp.arange(32) ^ (dp * 4 + rank)]]
-        triple = rows[:, gauss_size:].astype(F32).reshape(32, 3, 2, gain_size)
-        scales = triple[:, 0] + triple[:, 1] + triple[:, 2]
-        gauss_parts = rows[:, :gauss_size]
+        along_z = spread(jnp.concatenate([projections.reshape(192, 384), small_rows]), "z")
+        qk_parts = spread(jnp.stack([part[:96] for part in along_z]), "y")
+        v_parts = spread(jnp.stack([part[96:] for part in along_z]), "x")
+        qk_parts = spread(jnp.stack(qk_parts), "x")
+        v_parts = spread(jnp.stack(v_parts), "y")
+        qk_parts = qk_parts + [swap(part) for part in qk_parts]
+        v_parts = v_parts + [swap(part) for part in v_parts]
+        up_parts = spread(after(w_up, *along_z[1:]), "z")
+        up_parts = spread(jnp.stack(up_parts), "y")
+        up_parts = spread(jnp.stack(up_parts), "x")
+        down_parts = spread(after(w_down.T, *along_z[1:]), "x")
+        down_parts = spread(jnp.stack(down_parts), "z")
+        down_parts = spread(jnp.stack(down_parts), "y")
     else:
         every = lambda value: lax.all_gather(value, AXES, axis=0)
         cut = lambda value: value.reshape((8, dp_count // 8) + value.shape[1:])
@@ -641,11 +650,44 @@
             jnp.pad(both[:, :, :, 2:].reshape(8, 2, 2, 96, 384), ((0, 0),) * 3 + ((0, 16), (0, 0))),
             ORDER_V,
         )
-        wide = lambda value: cut(every(value).reshape(dp_count, 4, -1, D)).transpose(
-            0, 2, 1, 3, 4
-        ).reshape(8, 2, 2, 96, D)
-        up_parts = as_gathered(wide(w_up), ORDER_UP)
-        down_parts = as_gathered(wide(w_down.T), ORDER_DOWN)
+
+        def wide(value):
+            value = cut(every(value).reshape(dp_count, 4, -1, D)).transpose(0, 2, 1, 3, 4)
+            value = value.reshape(8, 2, 2, 96, D)
+            return lax.dynamic_slice_in_dim(value, core, 1, axis=2)
+
+        double = lambda value: jnp.concatenate([value, value], axis=2)
+        up_parts = as_gathered(double(wide(w_up)), ORDER_UP)[:2]
+        down_parts = as_gathered(double(wide(w_down.T)), ORDER_DOWN)[:2]
+    table_qk, table_v = piece_table(ORDER_QK), piece_table(ORDER_V)
+    table_up, table_down = piece_table(ORDER_UP, 1), piece_table(ORDER_DOWN, 1)
+
+    own, other = to_segment_parts(tokens)
+    tall = shape((SEGL, D))
+    x, q, k, v, coef = run(
+        functools.partial(qkv_kernel, table_qk, table_v),
+        "qkv",
+        [info, own, other, jnp.asarray(ridge)] + qk_parts + v_parts,
+        [SCALARS, FULL, FULL, FULL] + [ANY] * 8,
+        [tall] * 4 + [shape((NB, D))],
+        [FULL] * 5,
+        [VMEM(MATRIX, BF16)] * 3 + [DMA((2,))],
+        cost=6.0,
+        vmem=14,
+    )
+    coef = lax.ppermute(coef, "tensor", [(0, 2), (1, 3)])
+
+    if near:
+        rows = jnp.concatenate(
+            [part[:, :, 96, : small.size].reshape(-1, small.size) for part in v_parts]
+        )
+        flat = [r * 4 + kx * 2 + kc for _, _, r, kx, kc in table_v]
+        position = jnp.asarray(np.argsort(np.array(flat)))
+        rows = rows[position[jnp.arange(32) ^ (dp * 4 + rank)]]
+        triple = rows[:, gauss_size:].astype(F32).reshape(32, 3, 2, gain_size)
+        scales = triple[:, 0] + triple[:, 1] + triple[:, 2]
+        gauss_parts = rows[:, :gauss_size]
+    else:
         scales = every(jnp.stack([ln_gain, ln_bias]))
         gauss_parts = every(w_gauss.reshape(-1))
     norm_gain, norm_bias = scales[:, 0].reshape(1, D), scales[:, 1].reshape(1, D)
@@ -656,31 +698,25 @@
     gauss_rows = jnp.pad(gauss_rows, ((0, 0), (0, 12), (0, 0)))
     gauss_column = gauss.astype(F32).reshape(2, PAIRS, 128).transpose(1, 2, 0)
     gauss_column = jnp.pad(gauss_column, ((0, 0), (0, 0), (0, 126)))
-    table_qk, table_v = piece_table(ORDER_QK), piece_table(ORDER_V)
-    table_up, table_down = piece_table(ORDER_UP), piece_table(ORDER_DOWN)
-
-    own, other = to_segment_parts(tokens)
-    seed_own, seed_other = to_segment_parts(cotangent)
-    seed = jnp.where(
+
+    cotangent = after(cotangent, q)
+    theirs = swap(cotangent)
+    everything = jnp.where(
         core == 0,
-        jnp.concatenate([seed_own, seed_other]),
-        jnp.concatenate([seed_other, seed_own]),
-    )
-    seed = jnp.where(jnp.arange(SEGL)[:, None] < valid_count, seed, 0.0).astype(BF16)
-    seed_t = seed.T
-
-    tall = shape((SEGL, D))
-    x, q, k, v, coef = run(
-        functools.partial(qkv_kernel, table_qk, table_v),
-        "qkv",
-        [info, own, other, jnp.asarray(ridge)] + qk_parts + v_parts,
-        [SCALARS, FULL, FULL, FULL] + [ANY] * 8,
-        [tall] * 4 + [shape((NB, D))],
-        [FULL] * 5,
-        [VMEM(MATRIX, BF16)] * 3 + [DMA((2,))],
-        cost=6.0,
-    )
-    coef = lax.ppermute(coef, "tensor", [(0, 2), (1, 3)])
+        jnp.concatenate([cotangent, theirs], axis=1),
+        jnp.concatenate([theirs, cotangent], axis=1),
+    )
+    seed = jnp.stack(
+        [lax.dynamic_index_in_dim(everything, at, 0, False) for at in (core, 1 - core)]
+    )
+    seed = jnp.stack(
+        [
+            jnp.where(jnp.arange(SEGL)[:, None] < count, part, 0.0).astype(BF16)
+            for count, part in zip(used, seed)
+        ]
+    )
+    seed_t = seed.reshape(2 * SEGL, D).T
+
     attn_t, local_t, dens_t = run(
         attend_kernel,
         "attend",
@@ -691,59 +727,76 @@
         [VMEM((SEGL, SEGL), F32)],
         grid=(PAIRS,),
         cost=12.0,
+        vmem=14,
     )
     whole = lambda *dims: pl.BlockSpec(dims, lambda p: (0,) * len(dims))
-    heads_out, residual, normed, normed_t = run(
+    heads_out, residual, normed = run(
         functools.partial(recall_kernel, table_v),
         "recall",
         [info, dens_t, coef, local_t, x, norm_gain, norm_bias] + v_parts,
         [SCALARS, PAIR_DENS, PAIR_COEF, PAIR_ROWS, whole(SEGL, D), whole(1, D), whole(1, D)]
         + [ANY] * 4,
-        [tall, shape((SEGL, D), F32), tall, shape((D, SEGL))],
-        [whole(SEGL, D)] * 3 + [whole(D, SEGL)],
+        [tall, shape((SEGL, D), F32), tall],
+        [whole(SEGL, D)] * 3,
         [VMEM(MATRIX, BF16), DMA(())],
         grid=(PAIRS,),
         cost=7.0,
-    )
+        vmem=18,
+    )
+    normed_other = swap(normed)
     piece_dims = lambda order: tuple(SIZES[letter] for letter in order)
-    wide_grad = [shape(piece_dims(BACK_DOWN) + (96, D))] * 2
-    hidden, slope, keep_down, send_down = run(
+    hidden, slope, keep_down = run(
         functools.partial(up_kernel, table_up, BACK_DOWN),
         "up",
-        [info, normed, seed_t] + up_parts,
-        [SCALARS, FULL, FULL] + [ANY] * 4,
-        [shape((SEGL, FF))] * 2 + wide_grad,
-        [FULL] * 2 + [ANY] * 2,
-        [VMEM(WIDE, BF16)] * 2 + [DMA((4,))] * 2,
+        [info, normed, normed_other, seed_t] + up_parts,
+        [SCALARS, FULL, FULL, FULL] + [ANY] * 2,
+        [shape((2, SEGL, HALF))] * 2 + [shape(piece_dims(BACK_DOWN) + (96, D))],
+        [FULL] * 2 + [ANY],
+        [VMEM(WIDE, BF16)] * 2 + [DMA((2,))] * 2,
         cost=12.0,
-    )
-    own_down = collect(keep_down, send_down, BACK_DOWN, dp_count, D).T
-    wide_grad = [shape(piece_dims(BACK_UP) + (96, D))] * 2
-    row = shape((1, D), F32)
-    keep_up, send_up, resid_grad, gain_part, bias_part = run(
+        vmem=22,
+    )
+    if near:
+        down_1 = stage(lambda k: keep_down[k].astype(F32), BACK_DOWN[0])
+    keep_up, own_grad, other_grad = run(
         functools.partial(down_kernel, (table_down, table_up), BACK_UP),
         "down",
-        [info, seed, normed_t, slope, residual, norm_gain] + down_parts + up_parts,
-        [SCALARS] + [FULL] * 5 + [ANY] * 8,
-        wide_grad + [shape((SEGL, D), F32), row, row],
-        [ANY] * 2 + [FULL] * 3,
-        [VMEM(WIDE, BF16)] * 3 + [VMEM((SEGL, D), F32)] + [DMA((4,))] * 3,
+        [info, seed, normed, normed_other, slope] + down_parts + up_parts,
+        [SCALARS] + [FULL] * 4 + [ANY] * 4,
+        [shape(piece_dims(BACK_UP) + (96, D)), shape((SEGL, D), F32), tall],
+        [ANY] + [FULL] * 2,
+        [VMEM(WIDE, BF16)] * 3
+        + [VMEM((2, SEGL, D), F32), VMEM((D, 2 * SEGL), BF16)]
+        + [DMA((2,))] * 3,
         cost=15.0,
-    )
-    own_up = collect(keep_up, send_up, BACK_UP, dp_count, D)
+        vmem=30,
+    )
+    if near:
+        up_1 = stage(lambda k: keep_up[k].astype(F32), BACK_UP[0])
+    other_grad = swap(other_grad)
     narrow_grad = [shape(piece_dims(BACK_V) + (48, 384))] * 2
-    head_grad, coef_grad, keep_out, send_out = run(
+    row = shape((1, D), F32)
+    resid_grad, head_grad, coef_grad, gain_part, bias_part, keep_out, send_out = run(
         functools.partial(mix_back_kernel, table_v, BACK_V),
         "mix_back",
-        [info, resid_grad, heads_out, dens_t] + v_parts,
-        [SCALARS, whole(SEGL, D), whole(SEGL, D), PAIR_DENS] + [ANY] * 4,
-        [tall, shape((NB, D))] + narrow_grad,
-        [whole(SEGL, D), PAIR_COEF] + [ANY] * 2,
-        [VMEM(MATRIX, BF16)] * 2 + [VMEM((D, SEGL), BF16)] + [DMA(())] * 2,
+        [info, own_grad, other_grad, seed[0], residual, norm_gain, heads_out, dens_t] + v_parts,
+        [SCALARS]
+        + [whole(SEGL, D)] * 4
+        + [whole(1, D), whole(SEGL, D), PAIR_DENS]
+        + [ANY] * 4,
+        [shape((SEGL, D), F32), tall, shape((NB, D)), row, row] + narrow_grad,
+        [whole(SEGL, D), whole(SEGL, D), PAIR_COEF, whole(1, D), whole(1, D)] + [ANY] * 2,
+        [VMEM(MATRIX, BF16)] * 2
+        + [VMEM((SEGL, D), BF16), VMEM((D, SEGL), BF16)]
+        + [DMA(())] * 2,
         grid=(PAIRS,),
         cost=6.0,
+        vmem=26,
     )
     coef_grad = lax.ppermute(coef_grad, "tensor", [(2, 0), (3, 1)])
+    if near:
+        head_grad = after(head_grad, *down_1[1])
+        down_2 = stage(combined(*down_1), BACK_DOWN[1])
     dq, dk, dv, gauss_grad = run(
         attend_back_kernel,
         "attend_back",
@@ -761,7 +814,11 @@
         ],
         grid=(PAIRS,),
         cost=16.0,
-    )
+        vmem=16,
+    )
+    if near:
+        dq = after(dq, *up_1[1])
+        up_2 = stage(combined(*up_1), BACK_UP[1])
     keep_qk, send_qk, keep_v, send_v, dv = run(
         functools.partial(qkv_grad_kernel, (BACK_QK, BACK_V)),
         "qkv_grad",
@@ -771,6 +828,7 @@
         [ANY] * 4 + [FULL],
         [VMEM((D, SEGL), BF16)] + [VMEM(MATRIX, BF16)] * 3 + [DMA((2,))],
         cost=6.0,
+        vmem=18,
     )
 
     gauss_grad = gauss_grad[:, :4].reshape(PAIRS, 2, 2, 2, DH)
@@ -793,14 +851,61 @@
         )
         small_grads = jnp.pad(small_grads[..., None, :], ((0, 0),) * 4 + ((0, 15), (0, 384 - count)))
         small_grads = small_grads.astype(BF16)
-        joined = [
+        keep_v, send_v = (
             jnp.concatenate(parts, axis=3)
             for parts in ((keep_v, keep_out, small_grads[0]), (send_v, send_out, small_grads[1]))
-        ]
-        own_v = scatter(*joined, BACK_V)
-        own_small = own_v[96, :count]
-        own_qk = scatter(keep_qk, send_qk, BACK_QK)
-        narrow = jnp.concatenate([own_qk, own_v[:96]]).reshape(4, 48, 384)
+        )
+        got_qk, got_v = swap(send_qk), swap(send_v)
+        first_qk = [(keep_qk[k].astype(F32) + got_qk[k].astype(F32)) for k in range(2)]
+        first_v = [(keep_v[k].astype(F32) + got_v[k].astype(F32)) for k in range(2)]
+        first_qk[1], first_v[1] = first_qk[1].astype(BF16), first_v[1].astype(BF16)
+        qk_1 = stage(lambda k: first_qk[k], BACK_QK[0])
+        v_1 = stage(lambda k: first_v[k], BACK_V[0])
+        dq_late = after(dq, first_qk[1], first_v[1])
+    else:
+        dq_late = dq
+
+    (grad_tokens,) = run(
+        functools.partial(input_grad_kernel, table_qk, table_v),
+        "input_grad",
+        [info, dq_late, dk, dv, resid_grad] + qk_parts + v_parts,
+        [SCALARS] + [FULL] * 4 + [ANY] * 8,
+        [shape((SEGL, D), F32)],
+        [FULL],
+        [VMEM(MATRIX, BF16)] * 3 + [DMA((2,))],
+        cost=5.0,
+        vmem=16,
+    )
+    if near:
+        down_3 = stage(combined(*down_2), BACK_DOWN[2])
+        up_3 = stage(combined(*up_2), BACK_UP[2])
+        hidden = after(hidden, grad_tokens, qk_1[1][0], v_1[1][0])
+    fed_own, fed_other = run(
+        functools.partial(output_kernel, table_down),
+        "output",
+        [info, hidden, residual] + down_parts,
+        [SCALARS] + [FULL] * 2 + [ANY] * 2,
+        [shape((SEGL, D), F32)] * 2,
+        [FULL] * 2,
+        [VMEM(WIDE, BF16), DMA((2,))],
+        cost=6.0,
+        vmem=18,
+    )
+    half = SEGL // 2
+    part = lambda value, at: lax.dynamic_slice_in_dim(value, at * half, half)
+    arrived = swap(jnp.stack([part(fed_own, 1 - core), part(fed_other, 1 - core)]))
+    own_rows, their_rows = part(fed_own, core) + arrived[1], part(fed_other, core) + arrived[0]
+    output = jnp.where(
+        core == 0, jnp.stack([own_rows, their_rows]), jnp.stack([their_rows, own_rows])
+    )
+
+    if near:
+        qk_2 = stage(combined(*qk_1), BACK_QK[1])
+        v_2 = stage(combined(*v_1), BACK_V[1])
+        to_qk, to_v = combined(*qk_2), combined(*v_2)
+        joined = final_sum(*stage(lambda k: jnp.concatenate([to_qk(k), to_v(k)]), "z"))
+        own_small = joined[192, :count]
+        narrow = joined[:192].reshape(4, 48, 384)
         mine = lax.dynamic_slice_in_dim(narrow, core * 192, 192, axis=2)
         partner = swap(lax.dynamic_slice_in_dim(narrow, (1 - core) * 192, 192, axis=2))
         narrow = jnp.where(
@@ -808,63 +913,40 @@
             jnp.concatenate([mine, partner], axis=1),
             jnp.concatenate([partner, mine], axis=1),
         )
+        own_up, own_down = final_sum(*up_3), final_sum(*down_3).T
     else:
         own_small = lax.psum_scatter(small_grads, AXES, scatter_dimension=0)
         pieces = [
-            whole_from(keep_qk, send_qk, BACK_QK).reshape(8, 2, 2, 2, 48, 384),
-            whole_from(keep_v, send_v, BACK_V)[:, :, :, None],
-            whole_from(keep_out, send_out, BACK_V)[:, :, :, None],
+            whole_from([keep_qk, send_qk], BACK_QK).reshape(8, 2, 2, 2, 48, 384),
+            whole_from([keep_v, send_v], BACK_V)[:, :, :, None],
+            whole_from([keep_out, send_out], BACK_V)[:, :, :, None],
         ]
         pieces = jnp.concatenate(pieces, axis=3).transpose(0, 2, 4, 3, 1, 5)
         pieces = pieces.reshape(dp_count, D // dp_count, 4, 4, 192).transpose(0, 3, 2, 1, 4)
-        narrow = lax.psum_scatter(
-            pieces.reshape((-1,) + pieces.shape[2:]).astype(F32), AXES, scatter_dimension=0
-        )
+        total = lambda value: lax.psum_scatter(value.astype(F32), AXES, scatter_dimension=0)
+        narrow = total(pieces.reshape((-1,) + pieces.shape[2:]))
+
+        def owned(keep, order):
+            mine = whole_from([keep], order)
+            both = jnp.concatenate(
+                [jnp.where(core == at, mine, jnp.zeros_like(mine)) for at in range(2)], axis=2
+            )
+            both = both.transpose(0, 3, 1, 2, 4).reshape(dp_count, D // dp_count, 4, D)
+            both = both.transpose(0, 2, 1, 3)
+            return total(both.reshape((-1,) + both.shape[2:]))
+
+        own_up, own_down = owned(keep_up, BACK_UP), owned(keep_down, BACK_DOWN).T
     own_qkv, own_out = narrow[:3], narrow[3].T
-    own_gauss = own_small[:gauss_size].reshape(w_gauss.shape)
-    own_gain = own_small[gauss_size : gauss_size + gain_size]
-    own_bias = own_small[gauss_size + gain_size :]
-
-    (grad_tokens,) = run(
-        functools.partial(input_grad_kernel, table_qk, table_v),
-        "input_grad",
-        [info, dq, dk, dv, resid_grad] + qk_parts + v_parts,
-        [SCALARS] + [FULL] * 4 + [ANY] * 8,
-        [shape((SEGL, D), F32)],
-        [FULL],
-        [VMEM(MATRIX, BF16)] * 3 + [DMA((2,))],
-        cost=5.0,
-    )
-    (output,) = run(
-        functools.partial(output_kernel, table_down),
-        "output",
-        [info, hidden, residual] + down_parts,
-        [SCALARS] + [FULL] * 2 + [ANY] * 4,
-        [shape((SEGL, D), F32)],
-        [FULL],
-        [VMEM(WIDE, BF16), DMA((4,))],
-        cost=6.0,
-    )
     return (
-        from_segment(output),
+        output,
         from_segment(grad_tokens),
         own_qkv,
-        own_gauss,
+        own_small[:gauss_size].reshape(w_gauss.shape),
         own_out,
-        own_gain,
-        own_bias,
+        own_small[gauss_size : gauss_size + gain_size],
+        own_small[gauss_size + gain_size :],
         own_up,
         own_down,
-    )
-
-
-def collect(keep, send, order, dp_count, columns):
-    if dp_count == 8:
-        return scatter(keep, send, order)
-    whole = whole_from(keep, send, order).transpose(0, 3, 1, 2, 4)
-    whole = whole.reshape(dp_count, D // dp_count, 4, columns).transpose(0, 2, 1, 3)
-    return lax.psum_scatter(
-        whole.reshape((-1,) + whole.shape[2:]).astype(F32), AXES, scatter_dimension=0
     )
 
 

time: 340 us -> 306 us (0.900)
  starting transfers between devices: 74.5 us -> 57.4 us
  waiting for transfers between devices: 72.1 us -> 56 us
  local copies, waits for them, and re-layouts: 42.7 us -> 28.8 us
  other arithmetic: 32 us -> 42.7 us
    ppermute x58 -> x48, waiting for transfers between devices: 69.4 us -> 50 us  [xor_permute(): return lax.ppermute(value, AXES, pairs)]
    ppermute x58 -> x48, starting transfers between devices: 69.4 us -> 52.6 us  [xor_permute(): return lax.ppermute(value, AXES, pairs)]
    unnamed x75 -> x64, local copies, waits for them, and re-layouts: 16.8 us -> 8.24 us
    another operation x9 -> x11, other arithmetic: 4.64 us -> 9.95 us  [the longest x2 4.24 us: local(): down_parts = spread(jnp.stack(down_parts), 'y')]
    convert_element_type x11 -> x7, other arithmetic: 14.1 us -> 11.8 us  [the longest x5 4.35 us: stage(): total(k).astype(BF16)]
  transfers between devices with their start and end apart: 60 -> 50, of which waited for: 20 -> 11; matrix products, arithmetic and copies ran while one was open for 17% -> 21% of each run, Pallas kernels for 34% -> 38%
where the time goes in v3:
time: 306 us; the launch traced here: 303 us
  Pallas kernels  116 us (38%)
  starting transfers between devices  57.4 us (19%)
  waiting for transfers between devices  56 us (18%)
  other arithmetic  42.7 us (14%)
  local copies, waits for them, and re-layouts  28.8 us (9%)
    pallas_call x10, Pallas kernels, run(): pl.pallas_call(body, name=name, out_shape=tuple((pltpu.HBM(out.shape, out...  116 us
    ppermute x48, starting transfers between devices, xor_permute(): return lax.ppermute(value, AXES, pairs)  52.6 us
    ppermute x48, waiting for transfers between devices, xor_permute(): return lax.ppermute(value, AXES, pairs)  50 us
    unnamed x64, local copies, waits for them, and re-layouts  8.24 us
  transfers between devices with their start and end apart: 50, of which 11 were waited for; matrix products, arithmetic and copies ran while one was open for 21% of the time, Pallas kernels for 38%

profile of v3, /device:TPU:0, one launch (start us, length us, event | category | flops | bytes accessed | tf_op | source)
XLA Modules:
  0.0 303.4 jit_solution(1014107589568358130)
XLA Ops:
  10.3 11.2 %collective-permute-done.4 = bf16[208,384]{1,0:T(8,128)(2,1)S(1)} collective-permute-done((bf16[208,384]{1,0:T(8,128)(2,1)S(1)}, bf16[208,384]{1,0:T(8,128)(2,1)S(1)}, u32[]{:S(2)}, u32[]{:S(2)}) %collective-permute-start.4) | collective-permute-done | bytes 159776 | tf_op jit(solution)/shard_map/ppermute | solution.py:45
  26.7 3.3 %collective-permute-start.16 = (bf16[96,768]{1,0:T(8,128)(2,1)S(1)}, bf16[96,768]{1,0:T(8,128)(2,1)S(1)}, u32[]{:S(2)}, u32[]{:S(2)}) collective-permute-start(bf16[96,768]{1,0:T(8,128)(2,1)S(1)} %copy-done.26), channel_id=1, source_target_pairs={{0,8},{1,9},{2,10},{3,11},{4,12},{5,13},{6,14},{7,15},{8,0},{9,1},... | collective-permute-start | bytes 442376 | tf_op jit(solution)/shard_map/ppermute | solution.py:45
  35.3 7.8 %collective-permute-done.17 = bf16[96,768]{1,0:T(8,128)(2,1)S(1)} collective-permute-done((bf16[96,768]{1,0:T(8,128)(2,1)S(1)}, bf16[96,768]{1,0:T(8,128)(2,1)S(1)}, u32[]{:S(2)}, u32[]{:S(2)}) %collective-permute-start.17) | collective-permute-done | bytes 147488 | tf_op jit(solution)/shard_map/ppermute | solution.py:45
  52.4 9.3 %collective-permute-done.19 = bf16[4,96,768]{2,1,0:T(8,128)(2,1)} collective-permute-done((bf16[4,96,768]{2,1,0:T(8,128)(2,1)}, bf16[4,96,768]{2,1,0:T(8,128)(2,1)}, u32[]{:S(2)}, u32[]{:S(2)}) %collective-permute-start.19) | collective-permute-done | bytes 589856 | tf_op jit(solution)/shard_map/ppermute | solution.py:45
  66.7 3.0 collective-permute-start.22
  73.2 8.2 %qkv.1 = (bf16[512,768]{1,0:T(8,128)(2,1)}, bf16[512,768]{1,0:T(8,128)(2,1)}, bf16[512,768]{1,0:T(8,128)(2,1)}, bf16[512,768]{1,0:T(8,128)(2,1)}, bf16[256,768]{1,0:T(8,128)(2,1)}) custom-call(s32[6]{0:T(128)S(1)} %stack.161.info, bf16[256,768]{1,0:T(8,128)(2,1)} %get-tuple-element.160.own, bf16[256,768]{1,0:T(8,128)(2,1)} %collective-permute-done.other, ...), custom_call_target="tpu_custom_call" | custom-call | flops 1200000000 | bytes 1000000 | tf_op jit(solution)/shard_map/qkv/pallas_call | solution.py:568
  82.3 3.4 %collective-permute-start.13 = (bf16[256,768]{1,0:T(8,128)(2,1)}, bf16[256,768]{1,0:T(8,128)(2,1)S(1)}, u32[]{:S(2)}, u32[]{:S(2)}) collective-permute-start(bf16[256,768]{1,0:T(8,128)(2,1)} %get-tuple-element.55), channel_id=1, source_target_pairs={{0,2},{1,3},{4,6},{5,7},{8,10},{9,11},{12,14},{13,15},{16,18},{17,... | collective-permute-start | bytes 1179656 | tf_op jit(solution)/shard_map/ppermute | solution.py:678
  89.1 6.0 %collective-permute-done.13.coef = bf16[256,768]{1,0:T(8,128)(2,1)S(1)} collective-permute-done((bf16[256,768]{1,0:T(8,128)(2,1)}, bf16[256,768]{1,0:T(8,128)(2,1)S(1)}, u32[]{:S(2)}, u32[]{:S(2)}) %collective-permute-start.13) | collective-permute-done | bytes 393248 | tf_op jit(solution)/shard_map/ppermute | solution.py:678
  97.5 13.1 %attend.1 = (bf16[12,512,512]{2,1,0:T(8,128)(2,1)}, f32[768,512]{1,0:T(8,128)}, bf16[12,256,512]{2,1,0:T(8,128)(2,1)}) custom-call(s32[6]{0:T(128)S(1)} %stack.161.info, bf16[512,768]{1,0:T(8,128)(2,1)} %get-tuple-element.51.q, bf16[512,768]{1,0:T(8,128)(2,1)} %get-tuple-element.52.k, bf16[512,768]{1,0:T(8,128)(2,1)} %get-tuple-element.53.v, ...), custom_call_target="tpu_custom_call" | custom-call | flops 2400000000 | bytes 1000000 | tf_op jit(solution)/shard_map/attend/pallas_call | solution.py:568
  110.6 8.9 %recall.1 = (bf16[512,768]{1,0:T(8,128)(2,1)}, f32[512,768]{1,0:T(8,128)}, bf16[512,768]{1,0:T(8,128)(2,1)}) custom-call(s32[6]{0:T(128)S(1)} %stack.161.info, bf16[12,256,512]{2,1,0:T(8,128)(2,1)} %get-tuple-element.54.dens_t, bf16[256,768]{1,0:T(8,128)(2,1)} %copy-done.12, f32[768,512]{1,0:T(8,128)} %get-tuple-element.56.local_t, ...), custom_call_target="tpu_custom_call" | custom-call | flops 1400000000 | bytes 1000000 | tf_op jit(solution)/shard_map/recall/pallas_call | solution.py:568
  126.3 16.6 %up.1 = (bf16[2,512,1536]{2,1,0:T(8,128)(2,1)}, bf16[2,512,1536]{2,1,0:T(8,128)(2,1)}, bf16[2,4,2,96,768]{4,3,2,1,0:T(8,128)(2,1)}) custom-call(s32[6]{0:T(128)S(1)} %stack.161.info, bf16[512,768]{1,0:T(8,128)(2,1)} %get-tuple-element.58.own, bf16[512,768]{1,0:T(8,128)(2,1)} %collective-permute-done.14.other, bf16[768,1024]{1,0:T(8,128)(2,1)} %bitcast.326, ...), custom_call_target="tpu_custom_call" | custom-call | flops 2400000000 | bytes 1000000 | tf_op jit(solution)/shard_map/up/pallas_call | solution.py:568
  142.9 3.8 %slice_convert_fusion = (f32[1,4,2,96,768]{4,3,2,1,0:T(8,128)}, bf16[4,2,96,768]{3,2,1,0:T(8,128)(2,1)}) fusion(bf16[2,4,2,96,768]{4,3,2,1,0:T(8,128)(2,1)} %get-tuple-element.70), kind=kLoop, calls=%fused_computation.19 | loop fusion | flops 589824 | bytes 5898240 | tf_op jit(solution)/shard_map/convert_element_type | solution.py:760
  147.2 4.0 %collective-permute-done.25.refs_1_ = bf16[4,2,96,768]{3,2,1,0:T(8,128)(2,1)} collective-permute-done((bf16[4,2,96,768]{3,2,1,0:T(8,128)(2,1)}, bf16[4,2,96,768]{3,2,1,0:T(8,128)(2,1)}, u32[]{:S(2)}, u32[]{:S(2)}) %collective-permute-start.25) | collective-permute-done | bytes 1179680 | tf_op jit(solution)/shard_map/ppermute | solution.py:45
  151.2 19.1 %down.1 = (bf16[2,2,4,96,768]{4,3,2,1,0:T(8,128)(2,1)}, f32[512,768]{1,0:T(8,128)}, bf16[512,768]{1,0:T(8,128)(2,1)}) custom-call(s32[6]{0:T(128)S(1)} %stack.161.info, bf16[2,512,768]{2,1,0:T(8,128)(2,1)} %copy-done.9, bf16[512,768]{1,0:T(8,128)(2,1)} %get-tuple-element.58.own, bf16[512,768]{1,0:T(8,128)(2,1)} %collective-permute-done.14.other, ...), custom_call_target="tpu_custom_call" | custom-call | flops 3000000000 | bytes 1000000 | tf_op jit(solution)/shard_map/down/pallas_call | solution.py:568
  171.1 3.7 %slice_convert_fusion.1 = (f32[1,2,4,96,768]{4,3,2,1,0:T(8,128)}, bf16[2,4,96,768]{3,2,1,0:T(8,128)(2,1)}) fusion(bf16[2,2,4,96,768]{4,3,2,1,0:T(8,128)(2,1)} %get-tuple-element.73), kind=kLoop, calls=%fused_computation.20 | loop fusion | flops 589824 | bytes 5898240 | tf_op jit(solution)/shard_map/convert_element_type | solution.py:775
  177.7 11.7 %mix_back.1 = (f32[512,768]{1,0:T(8,128)}, bf16[512,768]{1,0:T(8,128)(2,1)}, bf16[256,768]{1,0:T(8,128)(2,1)}, f32[1,768]{1,0:T(1,128)}, f32[1,768]{1,0:T(1,128)...) custom-call(s32[6]{0:T(128)S(1)} %stack.161.info, f32[512,768]{1,0:T(8,128)} %get-tuple-element.65.own, ...), custom_call_target="tpu_custom_call" | custom-call | flops 1200000000 | bytes 1000000 | tf_op jit(solution)/shard_map/mix_back/pallas_call | solution.py:568
  199.0 12.8 %attend_back.1 = (bf16[512,768]{1,0:T(8,128)(2,1)}, bf16[512,768]{1,0:T(8,128)(2,1)}, f32[512,768]{1,0:T(8,128)}, f32[6,16,128]{2,1,0:T(8,128)}) custom-call(bf16[12,512,512]{2,1,0:T(8,128)(2,1)} %get-tuple-element.62.attn_t, bf16[512,768]{1,0:T(8,128)(2,1)} %get-tuple-element.51.q, bf16[512,768]{1,0:T(8,128)(2,1)} %get-tuple-element.52.k, ...), custom_call_target="tpu_custom_call" | custom-call | flops 3200000000 | bytes 1000000 | tf_op jit(solution)/shard_map/attend_back/pallas_call | solution.py:568
  214.5 8.9 %qkv_grad.1 = (bf16[2,2,4,96,384]{4,3,2,1,0:T(8,128)(2,1)}, bf16[2,2,4,96,384]{4,3,2,1,0:T(8,128)(2,1)}, bf16[2,2,4,48,384]{4,3,2,1,0:T(8,128)(2,1)}, bf16[2,2,4...) custom-call(s32[6]{0:T(128)S(1)} %stack.161.info, bf16[512,768]{1,0:T(8,128)(2,1)} %get-tuple-element.57.x, ...), custom_call_target="tpu_custom_call" | custom-call | flops 1200000000 | bytes 1000000 | tf_op jit(solution)/shard_map/qkv_grad/pallas_call | solution.py:568
  242.9 5.4 %collective-permute-done.42 = bf16[4,96,768]{2,1,0:T(8,128)(2,1)S(1)} collective-permute-done((bf16[4,96,768]{2,1,0:T(8,128)(2,1)S(1)}, bf16[4,96,768]{2,1,0:T(8,128)(2,1)S(1)}, u32[]{:S(2)}, u32[]{:S(2)}) %collective-permute-start.42) | collective-permute-done | bytes 589856 | tf_op jit(solution)/shard_map/ppermute | solution.py:45
  248.4 2.8 collective-permute-start.44
  252.8 7.7 %input_grad.1 = f32[512,768]{1,0:T(8,128)} custom-call(s32[6]{0:T(128)S(1)} %stack.161.info, bf16[512,768]{1,0:T(8,128)(2,1)} %get-tuple-element.87.dq, bf16[512,768]{1,0:T(8,128)(2,1)} %get-tuple-element.75.dk, bf16[512,768]{1,0:T(8,128)(2,1)} %get-tuple-element.88.dv, f32[512,768]{1,0:T(8,128)} %get-tuple-element.89.resid_grad, ...), custom_call_target="tpu_custom_call" | custom-call | flops 1000000000 | bytes 1000000 | tf_op jit(solution)/shard_map/input_grad/pallas_call | solution.py:568
  264.0 8.8 %output.1 = (f32[512,768]{1,0:T(8,128)}, f32[512,768]{1,0:T(8,128)}) custom-call(s32[6]{0:T(128)S(1)} %stack.161.info, bf16[2,512,1536]{2,1,0:T(8,128)(2,1)} %get-tuple-element.90.hidden, f32[512,768]{1,0:T(8,128)} %get-tuple-element.67.residual, bf16[4,2,96,768]{3,2,1,0:T(8,128)(2,1)} %pad_maximum_fusion.5.refs_0_, ...), custom_call_target="tpu_custom_call" | custom-call | flops 1200000000 | bytes 1000000 | tf_op jit(solution)/shard_map/output/pallas_call | solution.py:568
  275.3 2.9 collective-permute-start.39
  284.1 6.1 %collective-permute-done.39 = bf16[208,384]{1,0:T(8,128)(2,1)S(1)} collective-permute-done((bf16[208,384]{1,0:T(8,128)(2,1)S(1)}, bf16[208,384]{1,0:T(8,128)(2,1)S(1)}, u32[]{:S(2)}, u32[]{:S(2)}) %collective-permute-start.39) | collective-permute-done | bytes 159776 | tf_op jit(solution)/shard_map/ppermute | solution.py:45
  (272 shorter events, 112.3 us)
Async XLA Ops:
  33.3 18.4 %collective-permute-start.10 = (bf16[2,4,112,384]{3,2,1,0:T(8,128)(2,1)S(1)}, bf16[2,4,112,384]{3,2,1,0:T(8,128)(2,1)S(1)}, u32[]{:S(2)}, u32[]{:S(2)}) collective-permute-start(bf16[2,4,112,384]{3,2,1,0:T(8,128)(2,1)S(1)} %pad_maximum_fusion.6.refs_4_.refs_0_), channel_id=1, source_target_pairs={{0,4},{1,5},{2,6},{3,7},{4,0},{5,1},{6,2},{7,3},{8,12},{9,13},{10,... | collective-permute-start | bytes 2064392 | tf_op jit(solution)/shard_map/ppermute | solution.py:45
  34.0 18.3 %collective-permute-start.6 = (bf16[2,4,96,384]{3,2,1,0:T(8,128)(2,1)S(1)}, bf16[2,4,96,384]{3,2,1,0:T(8,128)(2,1)}, u32[]{:S(2)}, u32[]{:S(2)}) collective-permute-start(bf16[2,4,96,384]{3,2,1,0:T(8,128)(2,1)S(1)} %pad_maximum_fusion.7.refs_0_), channel_id=1, source_target_pairs={{0,2},{1,3},{2,0},{3,1},{4,6},{5,7},{6,4},{7,5},{8,10},{9,11},{10,... | collective-permute-start | bytes 1769480 | tf_op jit(solution)/shard_map/ppermute | solution.py:45
  46.0 20.7 %collective-permute-start.11 = (bf16[2,4,112,384]{3,2,1,0:T(8,128)(2,1)S(1)}, bf16[2,4,112,384]{3,2,1,0:T(8,128)(2,1)S(1)}, u32[]{:S(2)}, u32[]{:S(2)}) collective-permute-start(bf16[2,4,112,384]{3,2,1,0:T(8,128)(2,1)S(1)} %pad_maximum_fusion.6.refs_4_.refs_0_), channel_id=1, source_target_pairs={{0,1},{1,0},{2,3},{3,2},{4,5},{5,4},{6,7},{7,6},{8,9},{9,8},{10,11... | collective-permute-start | bytes 2064392 | tf_op jit(solution)/shard_map/ppermute | solution.py:45
  51.7 20.7 %collective-permute-start.12 = (bf16[2,4,112,384]{3,2,1,0:T(8,128)(2,1)S(1)}, bf16[2,4,112,384]{3,2,1,0:T(8,128)(2,1)S(1)}, u32[]{:S(2)}, u32[]{:S(2)}) collective-permute-start(bf16[2,4,112,384]{3,2,1,0:T(8,128)(2,1)S(1)} %collective-permute-done.10.refs_5_.refs_1_), channel_id=1, source_target_pairs={{0,1},{1,0},{2,3},{3,2},{4,5},{5,4},{6,7},{7,6},{8,9},{9,8},{10,11... | collective-permute-start | bytes 2064392 | tf_op jit(solution)/shard_map/ppermute | solution.py:45
  51.7 19.1 %collective-permute-start.7 = (bf16[2,4,96,384]{3,2,1,0:T(8,128)(2,1)S(1)}, bf16[2,4,96,384]{3,2,1,0:T(8,128)(2,1)}, u32[]{:S(2)}, u32[]{:S(2)}) collective-permute-start(bf16[2,4,96,384]{3,2,1,0:T(8,128)(2,1)S(1)} %pad_maximum_fusion.7.refs_0_), channel_id=1, source_target_pairs={{0,1},{1,0},{2,3},{3,2},{4,5},{5,4},{6,7},{7,6},{8,9},{9,8},{10,11... | collective-permute-start | bytes 1769480 | tf_op jit(solution)/shard_map/ppermute | solution.py:45
  52.3 20.1 %collective-permute-start.8 = (bf16[2,4,96,384]{3,2,1,0:T(8,128)(2,1)}, bf16[2,4,96,384]{3,2,1,0:T(8,128)(2,1)}, u32[]{:S(2)}, u32[]{:S(2)}) collective-permute-start(bf16[2,4,96,384]{3,2,1,0:T(8,128)(2,1)} %collective-permute-done.6.refs_1_), channel_id=1, source_target_pairs={{0,1},{1,0},{2,3},{3,2},{4,5},{5,4},{6,7},{7,6},{8,9},{9,8},{10,11... | collective-permute-start | bytes 1769480 | tf_op jit(solution)/shard_map/ppermute | solution.py:45
  66.7 52.8 %collective-permute-start.22 = (bf16[2,96,768]{2,1,0:T(8,128)(2,1)}, bf16[2,96,768]{2,1,0:T(8,128)(2,1)}, u32[]{:S(2)}, u32[]{:S(2)}) collective-permute-start(bf16[2,96,768]{2,1,0:T(8,128)(2,1)} %get-tuple-element.170), channel_id=1, source_target_pairs={{0,8},{1,9},{2,10},{3,11},{4,12},{5,13},{6,14},{7,15},{8,0},{9,1},... | collective-permute-start | bytes 884744 | tf_op jit(solution)/shard_map/ppermute | solution.py:45
  69.8 49.8 %collective-permute-start.23 = (bf16[2,96,768]{2,1,0:T(8,128)(2,1)}, bf16[2,96,768]{2,1,0:T(8,128)(2,1)}, u32[]{:S(2)}, u32[]{:S(2)}) collective-permute-start(bf16[2,96,768]{2,1,0:T(8,128)(2,1)} %get-tuple-element.170), channel_id=1, source_target_pairs={{0,16},{1,17},{2,18},{3,19},{4,20},{5,21},{6,22},{7,23},{8,24},{9,... | collective-permute-start | bytes 884744 | tf_op jit(solution)/shard_map/ppermute | solution.py:45
  70.9 48.7 %collective-permute-start.24 = (bf16[2,96,768]{2,1,0:T(8,128)(2,1)}, bf16[2,96,768]{2,1,0:T(8,128)(2,1)}, u32[]{:S(2)}, u32[]{:S(2)}) collective-permute-start(bf16[2,96,768]{2,1,0:T(8,128)(2,1)} %get-tuple-element.170), channel_id=1, source_target_pairs={{0,24},{1,25},{2,26},{3,27},{4,28},{5,29},{6,30},{7,31},{8,16},{9,... | collective-permute-start | bytes 884744 | tf_op jit(solution)/shard_map/ppermute | solution.py:45
  81.5 42.1 %collective-permute-start.15 = (bf16[2,256,768]{2,1,0:T(8,128)(2,1)S(1)}, bf16[2,256,768]{2,1,0:T(8,128)(2,1)S(1)}, u32[]{:S(2)}, u32[]{:S(2)}) collective-permute-start(bf16[2,256,768]{2,1,0:T(8,128)(2,1)S(1)} %copy-done.20), channel_id=1, source_target_pairs={{0,1},{1,0},{2,3},{3,2},{4,5},{5,4},{6,7},{7,6},{8,9},{9,8},{10,11... | collective-permute-start | bytes 2359304 | tf_op jit(solution)/shard_map/ppermute | solution.py:45
  95.1 31.2 %collective-permute-start.20 = (bf16[2,4,96,768]{3,2,1,0:T(8,128)(2,1)}, bf16[2,4,96,768]{3,2,1,0:T(8,128)(2,1)}, u32[]{:S(2)}, u32[]{:S(2)}) collective-permute-start(bf16[2,4,96,768]{3,2,1,0:T(8,128)(2,1)} %pad_maximum_fusion.4.refs_0_.refs_2_), channel_id=1, source_target_pairs={{0,2},{1,3},{2,0},{3,1},{4,6},{5,7},{6,4},{7,5},{8,10},{9,11},{10,... | collective-permute-start | bytes 3538952 | tf_op jit(solution)/shard_map/ppermute | solution.py:45
  122.1 29.2 %collective-permute-start.25 = (bf16[4,2,96,768]{3,2,1,0:T(8,128)(2,1)}, bf16[4,2,96,768]{3,2,1,0:T(8,128)(2,1)}, u32[]{:S(2)}, u32[]{:S(2)}) collective-permute-start(bf16[4,2,96,768]{3,2,1,0:T(8,128)(2,1)} %pad_maximum_fusion.5.refs_0_), channel_id=1, source_target_pairs={{0,4},{1,5},{2,6},{3,7},{4,0},{5,1},{6,2},{7,3},{8,12},{9,13},{10,... | collective-permute-start | bytes 3538952 | tf_op jit(solution)/shard_map/ppermute | solution.py:45
  146.7 45.5 %collective-permute-start.27 = (bf16[4,2,96,768]{3,2,1,0:T(8,128)(2,1)}, bf16[4,2,96,768]{3,2,1,0:T(8,128)(2,1)}, u32[]{:S(2)}, u32[]{:S(2)}) collective-permute-start(bf16[4,2,96,768]{3,2,1,0:T(8,128)(2,1)} %get-tuple-element.133), channel_id=1, source_target_pairs={{0,4},{1,5},{2,6},{3,7},{4,0},{5,1},{6,2},{7,3},{8,12},{9,13},{10,... | collective-permute-start | bytes 3538952 | tf_op jit(solution)/shard_map/ppermute | solution.py:45
  174.8 37.9 %collective-permute-start.28 = (bf16[2,4,96,768]{3,2,1,0:T(8,128)(2,1)}, bf16[2,4,96,768]{3,2,1,0:T(8,128)(2,1)}, u32[]{:S(2)}, u32[]{:S(2)}) collective-permute-start(bf16[2,4,96,768]{3,2,1,0:T(8,128)(2,1)} %get-tuple-element.135), channel_id=1, source_target_pairs={{0,2},{1,3},{2,0},{3,1},{4,6},{5,7},{6,4},{7,5},{8,10},{9,11},{10,... | collective-permute-start | bytes 3538952 | tf_op jit(solution)/shard_map/ppermute | solution.py:45
  189.3 24.4 %collective-permute-start.29 = (bf16[256,768]{1,0:T(8,128)(2,1)}, bf16[256,768]{1,0:T(8,128)(2,1)S(1)}, u32[]{:S(2)}, u32[]{:S(2)}) collective-permute-start(bf16[256,768]{1,0:T(8,128)(2,1)} %get-tuple-element.77), channel_id=1, source_target_pairs={{2,0},{3,1},{6,4},{7,5},{10,8},{11,9},{14,12},{15,13},{18,16},{19,... | collective-permute-start | bytes 1179656 | tf_op jit(solution)/shard_map/ppermute | solution.py:796
  194.6 31.8 %collective-permute-start.46 = (bf16[2,96,768]{2,1,0:T(8,128)(2,1)}, bf16[2,96,768]{2,1,0:T(8,128)(2,1)}, u32[]{:S(2)}, u32[]{:S(2)}) collective-permute-start(bf16[2,96,768]{2,1,0:T(8,128)(2,1)} %get-tuple-element.124), channel_id=1, source_target_pairs={{0,8},{1,9},{2,10},{3,11},{4,12},{5,13},{6,14},{7,15},{8,0},{9,1},... | collective-permute-start | bytes 884744 | tf_op jit(solution)/shard_map/ppermute | solution.py:45
  195.5 30.9 %collective-permute-start.47 = (bf16[2,96,768]{2,1,0:T(8,128)(2,1)}, bf16[2,96,768]{2,1,0:T(8,128)(2,1)}, u32[]{:S(2)}, u32[]{:S(2)}) collective-permute-start(bf16[2,96,768]{2,1,0:T(8,128)(2,1)} %get-tuple-element.126), channel_id=1, source_target_pairs={{0,16},{1,17},{2,18},{3,19},{4,20},{5,21},{6,22},{7,23},{8,24},{9,... | collective-permute-start | bytes 884744 | tf_op jit(solution)/shard_map/ppermute | solution.py:45
  197.5 28.9 %collective-permute-start.48 = (bf16[2,96,768]{2,1,0:T(8,128)(2,1)}, bf16[2,96,768]{2,1,0:T(8,128)(2,1)}, u32[]{:S(2)}, u32[]{:S(2)}) collective-permute-start(bf16[2,96,768]{2,1,0:T(8,128)(2,1)} %get-tuple-element.125), channel_id=1, source_target_pairs={{0,24},{1,25},{2,26},{3,27},{4,28},{5,29},{6,30},{7,31},{8,16},{9,... | collective-permute-start | bytes 884744 | tf_op jit(solution)/shard_map/ppermute | solution.py:45
  237.8 24.1 %collective-permute-start.32 = (bf16[2,4,96,384]{3,2,1,0:T(8,128)(2,1)S(1)}, bf16[2,4,96,384]{3,2,1,0:T(8,128)(2,1)S(1)}, u32[]{:S(2)}, u32[]{:S(2)}) collective-permute-start(bf16[2,4,96,384]{3,2,1,0:T(8,128)(2,1)S(1)} %get-tuple-element.137), channel_id=1, source_target_pairs={{0,2},{1,3},{2,0},{3,1},{4,6},{5,7},{6,4},{7,5},{8,10},{9,11},{10,... | collective-permute-start | bytes 1769480 | tf_op jit(solution)/shard_map/ppermute | solution.py:45
  241.3 22.4 %collective-permute-start.33 = (bf16[2,4,112,384]{3,2,1,0:T(8,128)(2,1)S(1)}, bf16[2,4,112,384]{3,2,1,0:T(8,128)(2,1)S(1)}, u32[]{:S(2)}, u32[]{:S(2)}) collective-permute-start(bf16[2,4,112,384]{3,2,1,0:T(8,128)(2,1)S(1)} %get-tuple-element.131), channel_id=1, source_target_pairs={{0,4},{1,5},{2,6},{3,7},{4,0},{5,1},{6,2},{7,3},{8,12},{9,13},{10,... | collective-permute-start | bytes 2064392 | tf_op jit(solution)/shard_map/ppermute | solution.py:45
  248.3 26.9 %collective-permute-start.43 = (bf16[96,768]{1,0:T(8,128)(2,1)S(1)}, bf16[96,768]{1,0:T(8,128)(2,1)S(1)}, u32[]{:S(2)}, u32[]{:S(2)}) collective-permute-start(bf16[96,768]{1,0:T(8,128)(2,1)S(1)} %get-tuple-element.140), channel_id=1, source_target_pairs={{0,8},{1,9},{2,10},{3,11},{4,12},{5,13},{6,14},{7,15},{8,0},{9,1},... | collective-permute-start | bytes 442376 | tf_op jit(solution)/shard_map/ppermute | solution.py:45
  248.4 26.9 %collective-permute-start.44 = (bf16[96,768]{1,0:T(8,128)(2,1)S(1)}, bf16[96,768]{1,0:T(8,128)(2,1)S(1)}, u32[]{:S(2)}, u32[]{:S(2)}) collective-permute-start(bf16[96,768]{1,0:T(8,128)(2,1)S(1)} %get-tuple-element.142), channel_id=1, source_target_pairs={{0,16},{1,17},{2,18},{3,19},{4,20},{5,21},{6,22},{7,23},{8,24},{9,... | collective-permute-start | bytes 442376 | tf_op jit(solution)/shard_map/ppermute | solution.py:45
  251.2 26.9 %collective-permute-start.45 = (bf16[96,768]{1,0:T(8,128)(2,1)S(1)}, bf16[96,768]{1,0:T(8,128)(2,1)S(1)}, u32[]{:S(2)}, u32[]{:S(2)}) collective-permute-start(bf16[96,768]{1,0:T(8,128)(2,1)S(1)} %get-tuple-element.141), channel_id=1, source_target_pairs={{0,24},{1,25},{2,26},{3,27},{4,28},{5,29},{6,30},{7,31},{8,16},{9,... | collective-permute-start | bytes 442376 | tf_op jit(solution)/shard_map/ppermute | solution.py:45
  274.5 26.0 %collective-permute-start.34 = (f32[2,256,768]{2,1,0:T(8,128)S(1)}, f32[2,256,768]{2,1,0:T(8,128)S(1)}, u32[]{:S(2)}, u32[]{:S(2)}) collective-permute-start(f32[2,256,768]{2,1,0:T(8,128)S(1)} %pad_maximum_fusion.1), channel_id=1, source_target_pairs={{0,1},{1,0},{2,3},{3,2},{4,5},{5,4},{6,7},{7,6},{8,9},{9,8},{10,11... | collective-permute-start | bytes 4718600 | tf_op jit(solution)/shard_map/ppermute | solution.py:45
  (55 other events, 531.4 us)

commit v4 on v3

--- a/solution.py
+++ b/solution.py
@@ -84,7 +84,7 @@
 
 
 def combined(own, arrived):
-    return lambda k: sum((a[k].astype(F32) for a in arrived), own[k])
+    return lambda k: sum((a[k].astype(F32) for a in arrived), own[k].astype(F32))
 
 
 def final_sum(own, arrived):
@@ -104,14 +104,6 @@
     core = lax.axis_index("tensor") % 2
     own = lax.dynamic_index_in_dim(local, core, 0, keepdims=False)
     return own, swap(lax.dynamic_index_in_dim(local, 1 - core, 0, keepdims=False))
-
-
-def from_segment(segment):
-    core = lax.axis_index("tensor") % 2
-    half = segment.shape[0] // 2
-    own = lax.dynamic_slice_in_dim(segment, core * half, half)
-    other = swap(lax.dynamic_slice_in_dim(segment, (1 - core) * half, half))
-    return jnp.where(core == 0, jnp.stack([own, other]), jnp.stack([other, own]))
 
 
 def exact_triple(value):
@@ -187,12 +179,50 @@
     return (lax.broadcasted_iota(jnp.int32, (SEGL, 1), 0) < info[3]).astype(F32)
 
 
-def qkv_kernel(table_qk, table_v, info, own, other, ridge, *refs):
+def small_layout():
+    column = np.arange(D)
+    owner = [(column % DH // 8) * 4 + column // 192, column // 24]
+    place = [column // DH % 3 * 8 + column % 8, 48 + column % 24]
+    return np.stack(owner + place + [column] * 4).astype(np.int32)
+
+
+def small_places(layout, i, count):
+    row = lax.broadcasted_iota(jnp.int32, (count, D), 0)
+    place = layout[2 + i // 2][None] + 24 * (i % 2)
+    hit = row == place
+    if i > 1 and count > 128:
+        hit = hit | (row == place + 48) | (row == place + 96)
+    return hit.astype(F32).astype(BF16)
+
+
+def small_masks(info, table, owner):
+    row = lax.broadcasted_iota(jnp.int32, (512, D), 0)
+    device = row * 0 - 1
+    me = info[0] * 4 + info[1] * 2 + info[2]
+    for n, (_, _, r, kx, kc) in enumerate(table):
+        device = jnp.where(row == 16 * n, me ^ (r * 4 + kx * 2 + kc), device)
+    return device == owner[0:1], device == owner[1:2]
+
+
+def qkv_kernel(table_qk, table_v, near, info, own, other, ridge, *refs):
     qk, v_parts = refs[0:4], refs[4:8]
+    if near:
+        layout = refs[8][...]
+        refs = refs[:8] + refs[9:]
     x_out, q_out, k_out, v_out, coef_out = refs[8:13]
-    wq, wk, wv, sems = refs[13:]
+    if near:
+        gauss_out, gain_out, bias_out = refs[13:16]
+        refs = refs[:13] + refs[16:]
+    wq, wk, wv, small, sems = refs[13:]
     copies = list(narrow_copies(info, table_qk, qk, [(0, wq), (48, wk)], sems.at[0]))
     copies += list(narrow_copies(info, table_v, v_parts, [(0, wv)], sems.at[1]))
+    if near:
+        for n, (at, index, _, _, _) in enumerate(table_v):
+            copies.append(
+                pltpu.make_async_copy(
+                    v_parts[at].at[index + (pl.ds(96, 16),)], small.at[pl.ds(16 * n, 16)], sems.at[2]
+                )
+            )
     for copy in copies:
         copy.start()
     core = info[5]
@@ -220,6 +250,25 @@
         v_out[:, at] = values
         pooled = (values.astype(F32) * scale).astype(BF16)
         coef_out[:, at] = dot(ridge[...], pooled).astype(BF16)
+
+    if near:
+        wait_whole(small, sems.at[2])
+        gauss_mask, scale_mask = small_masks(info, table_v, layout)
+        rows = small[:, :256]
+
+        def collect(at, mask):
+            return jnp.sum(jnp.where(mask, dot(rows, small_places(layout, at, 256)), 0.0), axis=0, keepdims=True)
+
+        means, variances = collect(0, gauss_mask), collect(1, gauss_mask)
+        gain_out[...] = collect(2, scale_mask)
+        bias_out[...] = collect(3, scale_mask)
+        row = lax.broadcasted_iota(jnp.int32, (16, 128), 0)
+        for p in range(PAIRS):
+            at = slice(128 * p, 128 * (p + 1))
+            value = jnp.where(row < 2, means[:, at], variances[:, at])
+            for h in range(2):
+                value = jnp.where((row % 2 == h) & ~half_lanes(h), 0.0, value)
+            gauss_out[p] = jnp.where(row < 4, value, 0.0).astype(BF16)
 
 
 def density_rows(logits, h):
@@ -316,7 +365,7 @@
     for index, r, kx, _ in scatter_table(order, 1):
         rows = pl.ds(aligned(info[0] ^ r, 96), 96)
         yield kx, pltpu.make_async_copy(
-            source.at[rows, pl.ds(kx * D, D)], keep.at[index], sems.at[kx]
+            source.at[rows, pl.ds(kx * D, D)], keep[index[0]].at[index[1:]], sems.at[kx]
         )
 
 
@@ -327,8 +376,9 @@
 
 def up_kernel(table, order, info, own, other, seed_t, *refs):
     parts = refs[0:2]
-    hidden, slope, keep = refs[2:5]
-    w_up, grad, sems, out_sems = refs[5:]
+    hidden_out, slope_out = refs[2:4]
+    keep = refs[4:6]
+    w_up, grad, hidden, slope, sems, out_sems, side_sems = refs[6:]
     for copy in wide_copies(info, table, parts, w_up, sems):
         copy.start()
     outs = list(wide_out(info, order, keep, grad, out_sems))
@@ -346,21 +396,31 @@
                 slope[half, :, at] = derivative.astype(BF16)
                 sums.append(dot(seed_t[:, half * SEGL : (half + 1) * SEGL], value))
             grad[:, at] = (sums[0] + sums[1]).astype(BF16)
+            for i, (source, target) in enumerate(((hidden, hidden_out), (slope, slope_out))):
+                pltpu.make_async_copy(
+                    source.at[:, :, at], target.at[:, :, at], side_sems.at[i]
+                ).start()
 
         for owner, copy in outs:
             if owner == j:
                 copy.start()
     wait_out(grad, out_sems)
-
-
-def down_kernel(tables, order, info, seed, own, other, slope, *refs):
+    wait_whole(hidden, side_sems.at[0])
+    wait_whole(slope, side_sems.at[1])
+
+
+def down_kernel(tables, order, info, seed, own, other, slope_in, *refs):
     down_parts, up_parts = refs[0:2], refs[2:4]
-    keep, own_grad, other_grad = refs[4:7]
-    w_down, w_up, grad, total, normed_t, down_sems, up_sems, out_sems = refs[7:]
+    keep = refs[4:6]
+    own_grad, other_grad = refs[6:8]
+    w_down, w_up, grad, slope, total, normed_t, down_sems, up_sems, out_sems, side_sems = refs[8:]
     for copy in wide_copies(info, tables[0], down_parts, w_down, down_sems):
         copy.start()
     for copy in wide_copies(info, tables[1], up_parts, w_up, up_sems):
         copy.start()
+    for j in range(2):
+        at = pl.ds(j * D, D)
+        pltpu.make_async_copy(slope_in.at[:, :, at], slope.at[:, :, at], side_sems.at[j]).start()
     outs = list(wide_out(info, order, keep, grad, out_sems))
     total[...] = jnp.zeros_like(total)
     normed_t[:, :SEGL] = flip(own[...]).astype(BF16)
@@ -368,6 +428,7 @@
     for j in range(2):
         wait_wide(w_down, down_sems, j)
         wait_wide(w_up, up_sems, j)
+        wait_whole(slope.at[:, :, pl.ds(j * D, D)], side_sems.at[j])
 
         @pl.loop(0, 3)
         def _(chunk):
@@ -434,13 +495,14 @@
 
 
 def attend_back_kernel(
-    attn_t, q, k, v, grad, local_t, dens_t, coef, gauss, gauss_column, *refs
+    attn_t, q, k, v, grad, local_t, dens_t, coef, gauss, *refs
 ):
     dq_out, dk_out, dv_out, gauss_grad, dq_t, dk_sum, dv_sum, rows_of = refs
     keys_t = flip(k[...]).astype(BF16)
     grad_t = flip(grad[...])
     logits = dot(gauss[0], q[...], 1, 1)
     centres = centre_column()
+    gauss_columns = flip(gauss[0])
     dk_sum[...] = jnp.zeros_like(dk_sum)
     dv_sum[...] = jnp.zeros_like(dv_sum)
     rows_of[...] = jnp.zeros_like(rows_of)
@@ -471,17 +533,23 @@
         var_grad = spread_grad * 0.05 * jax.nn.sigmoid(var_logit)
         rows_of[h : h + 1] = mean_grad
         rows_of[2 + h : 3 + h] = var_grad
-        column = gauss_column[0, rows]
-        dq_t[rows] += column[:, 0:1] * mean_grad + column[:, 1:2] * var_grad
+        column = gauss_columns[rows]
+        dq_t[rows] += column[:, h : h + 1] * mean_grad + column[:, 2 + h : 3 + h] * var_grad
     dq_out[...] = jnp.transpose(dq_t[...]).astype(BF16)
     dk_out[...] = (dk_sum[...] * DH**-0.5).astype(BF16)
     dv_out[...] = dv_sum[...]
     high = rows_of[...].astype(BF16)
-    gauss_grad[0] = dot(high, q[...]) + dot((rows_of[...] - high.astype(F32)).astype(BF16), q[...])
-
-
-def qkv_grad_kernel(orders, info, x, dq, dk, dv, coef_grad, ridge_t, *refs):
-    keep_qk, send_qk, keep_v, send_v, dv_out, x_t, gq, gk, gv, sems = refs
+    both = dot(high, q[...]) + dot((rows_of[...] - high.astype(F32)).astype(BF16), q[...])
+    gauss_grad[0:1] = jnp.where(half_lanes(0), both[0:1], both[1:2])
+    gauss_grad[1:2] = jnp.where(half_lanes(0), both[2:3], both[3:4])
+
+
+def qkv_grad_kernel(orders, near, info, x, dq, dk, dv, coef_grad, ridge_t, *refs):
+    if near:
+        gauss_grad, gain_grad, bias_grad = refs[:3]
+        layout = refs[3][...]
+        refs = refs[4:]
+    keep_qk, send_qk, keep_v, send_v, dv_out, x_t, gq, gk, gv, small, sems = refs
     x_t[...] = flip(x[...]).astype(BF16)
     scale = column_validity(info) * info[4].astype(F32)
 
@@ -505,19 +573,49 @@
 
     for copy in out_narrow(info, orders[1], keep_v, send_v, [(0, gv)], sems.at[1]):
         copy.start()
+    if near:
+        table = scatter_table(orders[1])
+        gauss_mask, scale_mask = small_masks(info, [(0,) + row for row in table], layout)
+        rows = (
+            (gauss_mask, gauss_grad[0:1]),
+            (gauss_mask, gauss_grad[1:2]),
+            (scale_mask, gain_grad[...]),
+            (scale_mask, bias_grad[...]),
+        )
+        small[...] = jnp.zeros_like(small)
+        small[:, :128] = sum(
+            dot(jnp.where(mask, row, 0.0).astype(BF16), small_places(layout, i, 128), 1, 1)
+            for i, (mask, row) in enumerate(rows)
+        ).astype(BF16)
+        for n, (index, _, _, kc) in enumerate(table):
+            pltpu.make_async_copy(
+                small.at[pl.ds(16 * n, 16)],
+                (keep_v, send_v)[kc].at[index + (pl.ds(48, 16),)],
+                sems.at[2],
+            ).start()
+        wait_whole(small, sems.at[2])
     both = pltpu.make_async_copy(gq, gq, sems.at[0])
     both.wait()
     both.wait()
     wait_whole(gv, sems.at[1])
 
 
-def input_grad_kernel(table_qk, table_v, info, dq, dk, dv, resid_grad, *refs):
-    qk, v_parts = refs[0:4], refs[4:8]
-    out, wq, wk, wv, sems = refs[8:]
-    for copy in narrow_copies(info, table_qk, qk, [(0, wq), (48, wk)], sems.at[0]):
+def finish_kernel(tables, info, dq, dk, dv, resid_grad, hidden, residual, *refs):
+    qk, v_parts, down_parts = refs[0:4], refs[4:8], refs[8:10]
+    token_keep, token_send, fed_keep, fed_send = refs[10:14]
+    wq, wk, wv, w_down, sems, down_sems = refs[14:]
+    for copy in narrow_copies(info, tables[0], qk, [(0, wq), (48, wk)], sems.at[0]):
         copy.start()
-    for copy in narrow_copies(info, table_v, v_parts, [(0, wv)], sems.at[1]):
+    for copy in narrow_copies(info, tables[1], v_parts, [(0, wv)], sems.at[1]):
         copy.start()
+    for copy in wide_copies(info, tables[2], down_parts, w_down, down_sems):
+        copy.start()
+    first = info[5] == 0
+
+    def split(value):
+        top, bottom = value[:HALF_SEG], value[HALF_SEG:]
+        return jnp.where(first, top, bottom), jnp.where(first, bottom, top).astype(BF16)
+
     pair_wait = pltpu.make_async_copy(wq, wq, sems.at[0])
     pair_wait.wait()
     pair_wait.wait()
@@ -527,21 +625,18 @@
     def _(chunk):
         at = pl.ds(aligned(chunk, 256), 256)
         part = dot(dq[...], wq[at, :], 1, 1) + dot(dk[...], wk[at, :], 1, 1)
-        out[:, at] = resid_grad[:, at] + part + dot(dv[...], wv[at, :], 1, 1)
-
-
-def output_kernel(table, info, hidden, residual, *refs):
-    parts = refs[0:2]
-    out, other, w_down, sems = refs[2:]
-    for copy in wide_copies(info, table, parts, w_down, sems):
-        copy.start()
-    wait_out(w_down, sems)
+        value = resid_grad[:, at] + part + dot(dv[...], wv[at, :], 1, 1)
+        token_keep[:, at], token_send[:, at] = split(value)
+
+    wait_out(w_down, down_sems)
 
     @pl.loop(0, 3)
     def _(chunk):
         at = pl.ds(aligned(chunk, 256), 256)
-        out[:, at] = residual[:, at] + dot(hidden[0], w_down[at, :], 1, 1)
-        other[:, at] = dot(hidden[1], w_down[at, :], 1, 1)
+        value = residual[:, at] + dot(hidden[0], w_down[at, :], 1, 1)
+        fed_keep[0, :, at], fed_send[0, :, at] = split(value)
+        value = dot(hidden[1], w_down[at, :], 1, 1)
+        fed_keep[1, :, at], fed_send[1, :, at] = split(value)
 
 
 FULL = pl.BlockSpec()
@@ -549,6 +644,7 @@
 SCALARS = pl.BlockSpec(memory_space=SMEM)
 MATRIX = (D, D)
 HALF = FF // 2
+HALF_SEG = SEGL // 2
 WIDE = (D, HALF)
 DMA = pltpu.SemaphoreType.DMA
 
@@ -591,8 +687,8 @@
     return pl.BlockSpec((1,) + dims, lambda p: (p, 0, 0))
 
 
-ORDER_QK, ORDER_V, ORDER_UP, ORDER_DOWN = "zyx", "zxy", "zyx", "xzy"
-BACK_QK, BACK_V, BACK_UP, BACK_DOWN = "xyz", "yxz", "xyz", "yzx"
+ORDER_QK, ORDER_V, ORDER_UP, ORDER_DOWN = "zyx", "zxy", "zxy", "zxy"
+BACK_QK, BACK_V, BACK_UP, BACK_DOWN = "xyz", "yxz", "xyz", "yxz"
 
 
 def local(
@@ -612,6 +708,24 @@
     pair = lax.dynamic_index_in_dim(mem_mask, core, 0, False)[1, 0]
     where = (dp, segment, core) if near else (0, 0, 0)
     info = jnp.stack([jnp.asarray(value, jnp.int32) for value in where + (used[0], pair, core)])
+
+    own, other = to_segment_parts(tokens)
+    theirs = swap(cotangent)
+    everything = jnp.where(
+        core == 0,
+        jnp.concatenate([cotangent, theirs], axis=1),
+        jnp.concatenate([theirs, cotangent], axis=1),
+    )
+    seed = jnp.stack(
+        [lax.dynamic_index_in_dim(everything, at, 0, False) for at in (core, 1 - core)]
+    )
+    seed = jnp.stack(
+        [
+            jnp.where(jnp.arange(SEGL)[:, None] < count, part, 0.0).astype(BF16)
+            for count, part in zip(used, seed)
+        ]
+    )
+    seed_t = seed.reshape(2 * SEGL, D).T
 
     projections = jnp.concatenate([w_qkv, w_out.T[None]])
     if near:
@@ -626,19 +740,18 @@
             [w_gauss.reshape(-1)] + exact_triple(jnp.concatenate([ln_gain, ln_bias]))
         )
         small_rows = jnp.pad(small[None], ((0, 15), (0, 384 - small.size)))
-        along_z = spread(jnp.concatenate([projections.reshape(192, 384), small_rows]), "z")
-        qk_parts = spread(jnp.stack([part[:96] for part in along_z]), "y")
-        v_parts = spread(jnp.stack([part[96:] for part in along_z]), "x")
-        qk_parts = spread(jnp.stack(qk_parts), "x")
-        v_parts = spread(jnp.stack(v_parts), "y")
-        qk_parts = qk_parts + [swap(part) for part in qk_parts]
-        v_parts = v_parts + [swap(part) for part in v_parts]
-        up_parts = spread(after(w_up, *along_z[1:]), "z")
-        up_parts = spread(jnp.stack(up_parts), "y")
-        up_parts = spread(jnp.stack(up_parts), "x")
-        down_parts = spread(after(w_down.T, *along_z[1:]), "x")
-        down_parts = spread(jnp.stack(down_parts), "z")
-        down_parts = spread(jnp.stack(down_parts), "y")
+        packed = jnp.concatenate([projections.reshape(192, 384), small_rows])
+        along_z = spread(after(packed, other, theirs), "z")
+        along_z[1] = after(along_z[1], seed, seed_t)
+        qk_near = jnp.stack(spread(jnp.stack([part[:96] for part in along_z]), "y"))
+        v_near = jnp.stack(spread(jnp.stack([part[96:] for part in along_z]), "x"))
+        qk_far, v_far = xor_permute(qk_near, "x", 1), xor_permute(v_near, "y", 1)
+        qk_swap, v_swap = swap(qk_near), swap(v_near)
+        up_z = spread(after(w_up, qk_swap, v_swap), "z")
+        qk_parts = [qk_near, qk_far, qk_swap, swap(after(qk_far, *up_z[1:]))]
+        v_parts = [v_near, v_far, v_swap, swap(after(v_far, *up_z[1:]))]
+        up_x = spread(after(jnp.stack(up_z), qk_parts[3], v_parts[3]), "x")
+        down_z = spread(after(w_down.T, qk_parts[3], v_parts[3]), "z")
     else:
         every = lambda value: lax.all_gather(value, AXES, axis=0)
         cut = lambda value: value.reshape((8, dp_count // 8) + value.shape[1:])
@@ -662,65 +775,44 @@
     table_qk, table_v = piece_table(ORDER_QK), piece_table(ORDER_V)
     table_up, table_down = piece_table(ORDER_UP, 1), piece_table(ORDER_DOWN, 1)
 
-    own, other = to_segment_parts(tokens)
     tall = shape((SEGL, D))
-    x, q, k, v, coef = run(
-        functools.partial(qkv_kernel, table_qk, table_v),
+    row = shape((1, D), F32)
+    small_in, small_out = [], []
+    if near:
+        small_in = [jnp.asarray(small_layout())]
+        small_out = [shape((PAIRS, 16, 128)), row, row]
+    x, q, k, v, coef, *small_params = run(
+        functools.partial(qkv_kernel, table_qk, table_v, near),
         "qkv",
-        [info, own, other, jnp.asarray(ridge)] + qk_parts + v_parts,
-        [SCALARS, FULL, FULL, FULL] + [ANY] * 8,
-        [tall] * 4 + [shape((NB, D))],
-        [FULL] * 5,
-        [VMEM(MATRIX, BF16)] * 3 + [DMA((2,))],
+        [info, own, other, jnp.asarray(ridge)] + qk_parts + v_parts + small_in,
+        [SCALARS, FULL, FULL, FULL] + [ANY] * 8 + [FULL] * len(small_in),
+        [tall] * 4 + [shape((NB, D))] + small_out,
+        [FULL] * (5 + len(small_out)),
+        [VMEM(MATRIX, BF16)] * 3 + [VMEM((512, 384), BF16), DMA((3,))],
         cost=6.0,
-        vmem=14,
+        vmem=24,
     )
     coef = lax.ppermute(coef, "tensor", [(0, 2), (1, 3)])
 
-    if near:
-        rows = jnp.concatenate(
-            [part[:, :, 96, : small.size].reshape(-1, small.size) for part in v_parts]
-        )
-        flat = [r * 4 + kx * 2 + kc for _, _, r, kx, kc in table_v]
-        position = jnp.asarray(np.argsort(np.array(flat)))
-        rows = rows[position[jnp.arange(32) ^ (dp * 4 + rank)]]
-        triple = rows[:, gauss_size:].astype(F32).reshape(32, 3, 2, gain_size)
-        scales = triple[:, 0] + triple[:, 1] + triple[:, 2]
-        gauss_parts = rows[:, :gauss_size]
+    q_late = q
+    if near:
+        q_late = after(q, up_x[1])
+        up_parts = spread(after(jnp.stack(up_x), q), "y")
+        gauss_rows, norm_gain, norm_bias = small_params
     else:
         scales = every(jnp.stack([ln_gain, ln_bias]))
         gauss_parts = every(w_gauss.reshape(-1))
-    norm_gain, norm_bias = scales[:, 0].reshape(1, D), scales[:, 1].reshape(1, D)
-    gauss = gauss_parts.reshape(dp_count, 4, 2, 3, -1).transpose(2, 1, 3, 0, 4)
-    gauss = gauss.reshape(2, PAIRS, 2, DH)
-    spread_rows = jnp.eye(2, dtype=BF16)[None, None, :, :, None] * gauss[:, :, :, None, :]
-    gauss_rows = spread_rows.transpose(1, 0, 2, 3, 4).reshape(PAIRS, 4, 128)
-    gauss_rows = jnp.pad(gauss_rows, ((0, 0), (0, 12), (0, 0)))
-    gauss_column = gauss.astype(F32).reshape(2, PAIRS, 128).transpose(1, 2, 0)
-    gauss_column = jnp.pad(gauss_column, ((0, 0), (0, 0), (0, 126)))
-
-    cotangent = after(cotangent, q)
-    theirs = swap(cotangent)
-    everything = jnp.where(
-        core == 0,
-        jnp.concatenate([cotangent, theirs], axis=1),
-        jnp.concatenate([theirs, cotangent], axis=1),
-    )
-    seed = jnp.stack(
-        [lax.dynamic_index_in_dim(everything, at, 0, False) for at in (core, 1 - core)]
-    )
-    seed = jnp.stack(
-        [
-            jnp.where(jnp.arange(SEGL)[:, None] < count, part, 0.0).astype(BF16)
-            for count, part in zip(used, seed)
-        ]
-    )
-    seed_t = seed.reshape(2 * SEGL, D).T
+        norm_gain, norm_bias = scales[:, 0].reshape(1, D), scales[:, 1].reshape(1, D)
+        gauss = gauss_parts.reshape(dp_count, 4, 2, 3, -1).transpose(2, 1, 3, 0, 4)
+        gauss = gauss.reshape(2, PAIRS, 2, DH)
+        spread_rows = jnp.eye(2, dtype=BF16)[None, None, :, :, None] * gauss[:, :, :, None, :]
+        gauss_rows = spread_rows.transpose(1, 0, 2, 3, 4).reshape(PAIRS, 4, 128)
+        gauss_rows = jnp.pad(gauss_rows, ((0, 0), (0, 12), (0, 0)))
 
     attn_t, local_t, dens_t = run(
         attend_kernel,
         "attend",
-        [info, q, k, v, gauss_rows],
+        [info, q_late, k, v, gauss_rows],
         [SCALARS] + [PAIR_COLUMNS] * 3 + [pair_block(16, 128)],
         [shape((H, SEGL, SEGL)), shape((D, SEGL), F32), shape((H, NB, SEGL))],
         [PAIR_ATTN, PAIR_ROWS, PAIR_DENS],
@@ -729,6 +821,9 @@
         cost=12.0,
         vmem=14,
     )
+    if near:
+        down_z[1:] = lax.optimization_barrier((attn_t, coef, up_parts[1], *down_z[1:]))[3:]
+        down_x = spread(jnp.stack(down_z), "x")
     whole = lambda *dims: pl.BlockSpec(dims, lambda p: (0,) * len(dims))
     heads_out, residual, normed = run(
         functools.partial(recall_kernel, table_v),
@@ -743,39 +838,41 @@
         cost=7.0,
         vmem=18,
     )
+    if near:
+        down_parts = spread(after(jnp.stack(down_x), normed), "y")
     normed_other = swap(normed)
     piece_dims = lambda order: tuple(SIZES[letter] for letter in order)
-    hidden, slope, keep_down = run(
+    hidden, slope, *keep_down = run(
         functools.partial(up_kernel, table_up, BACK_DOWN),
         "up",
         [info, normed, normed_other, seed_t] + up_parts,
         [SCALARS, FULL, FULL, FULL] + [ANY] * 2,
-        [shape((2, SEGL, HALF))] * 2 + [shape(piece_dims(BACK_DOWN) + (96, D))],
-        [FULL] * 2 + [ANY],
-        [VMEM(WIDE, BF16)] * 2 + [DMA((2,))] * 2,
+        [shape((2, SEGL, HALF))] * 2 + [shape(piece_dims(BACK_DOWN)[1:] + (96, D))] * 2,
+        [ANY] * 4,
+        [VMEM(WIDE, BF16)] * 2 + [VMEM((2, SEGL, HALF), BF16)] * 2 + [DMA((2,))] * 3,
         cost=12.0,
         vmem=22,
     )
     if near:
-        down_1 = stage(lambda k: keep_down[k].astype(F32), BACK_DOWN[0])
-    keep_up, own_grad, other_grad = run(
+        down_1 = stage(lambda k: keep_down[k], BACK_DOWN[0])
+    *keep_up, own_grad, other_grad = run(
         functools.partial(down_kernel, (table_down, table_up), BACK_UP),
         "down",
         [info, seed, normed, normed_other, slope] + down_parts + up_parts,
-        [SCALARS] + [FULL] * 4 + [ANY] * 4,
-        [shape(piece_dims(BACK_UP) + (96, D)), shape((SEGL, D), F32), tall],
-        [ANY] + [FULL] * 2,
+        [SCALARS] + [FULL] * 3 + [ANY] * 5,
+        [shape(piece_dims(BACK_UP)[1:] + (96, D))] * 2 + [shape((SEGL, D), F32), tall],
+        [ANY] * 2 + [FULL] * 2,
         [VMEM(WIDE, BF16)] * 3
-        + [VMEM((2, SEGL, D), F32), VMEM((D, 2 * SEGL), BF16)]
-        + [DMA((2,))] * 3,
+        + [VMEM((2, SEGL, HALF), BF16), VMEM((2, SEGL, D), F32), VMEM((D, 2 * SEGL), BF16)]
+        + [DMA((2,))] * 4,
         cost=15.0,
         vmem=30,
     )
     if near:
-        up_1 = stage(lambda k: keep_up[k].astype(F32), BACK_UP[0])
+        up_1 = stage(lambda k: keep_up[k], BACK_UP[0])
+        own_grad = after(own_grad, *down_1[1])
     other_grad = swap(other_grad)
     narrow_grad = [shape(piece_dims(BACK_V) + (48, 384))] * 2
-    row = shape((1, D), F32)
     resid_grad, head_grad, coef_grad, gain_part, bias_part, keep_out, send_out = run(
         functools.partial(mix_back_kernel, table_v, BACK_V),
         "mix_back",
@@ -795,17 +892,16 @@
     )
     coef_grad = lax.ppermute(coef_grad, "tensor", [(2, 0), (3, 1)])
     if near:
-        head_grad = after(head_grad, *down_1[1])
-        down_2 = stage(combined(*down_1), BACK_DOWN[1])
+        got_out = swap(send_out)
     dq, dk, dv, gauss_grad = run(
         attend_back_kernel,
         "attend_back",
-        [attn_t, q, k, v, head_grad, local_t, dens_t, coef, gauss_rows, gauss_column],
+        [attn_t, q, k, v, head_grad, local_t, dens_t, coef, gauss_rows],
         [PAIR_ATTN]
         + [PAIR_COLUMNS] * 4
-        + [PAIR_ROWS, PAIR_DENS, PAIR_COEF, pair_block(16, 128), pair_block(128, 128)],
-        [tall, tall, shape((SEGL, D), F32), shape((PAIRS, 16, 128), F32)],
-        [PAIR_COLUMNS] * 3 + [pair_block(16, 128)],
+        + [PAIR_ROWS, PAIR_DENS, PAIR_COEF, pair_block(16, 128)],
+        [tall, tall, shape((SEGL, D), F32), shape((2, D), F32)],
+        [PAIR_COLUMNS] * 3 + [pl.BlockSpec((2, 128), lambda p: (0, p))],
         [
             VMEM((128, SEGL), F32),
             VMEM((SEGL, 128), F32),
@@ -817,94 +913,74 @@
         vmem=16,
     )
     if near:
+        up_1 = (up_1[0], [after(a, dk, coef_grad, got_out) for a in up_1[1]])
         dq = after(dq, *up_1[1])
+        down_1 = (down_1[0], [after(a, *up_1[1]) for a in down_1[1]])
+        down_2 = stage(combined(*down_1), BACK_DOWN[1])
         up_2 = stage(combined(*up_1), BACK_UP[1])
     keep_qk, send_qk, keep_v, send_v, dv = run(
-        functools.partial(qkv_grad_kernel, (BACK_QK, BACK_V)),
+        functools.partial(qkv_grad_kernel, (BACK_QK, BACK_V), near),
         "qkv_grad",
-        [info, x, dq, dk, dv, coef_grad, jnp.asarray(ridge.T)],
-        [SCALARS] + [FULL] * 6,
-        [shape(piece_dims(BACK_QK) + (96, 384))] * 2 + narrow_grad + [tall],
+        [info, x, dq, dk, dv, coef_grad, jnp.asarray(ridge.T)]
+        + ([gauss_grad, gain_part, bias_part] + small_in if near else []),
+        [SCALARS] + [FULL] * (10 if near else 6),
+        [shape(piece_dims(BACK_QK) + (96, 384))] * 2
+        + [shape(piece_dims(BACK_V) + (64, 384))] * 2
+        + [tall],
         [ANY] * 4 + [FULL],
-        [VMEM((D, SEGL), BF16)] + [VMEM(MATRIX, BF16)] * 3 + [DMA((2,))],
+        [VMEM((D, SEGL), BF16)] + [VMEM(MATRIX, BF16)] * 3 + [VMEM((512, 384), BF16), DMA((3,))],
         cost=6.0,
-        vmem=18,
-    )
-
-    gauss_grad = gauss_grad[:, :4].reshape(PAIRS, 2, 2, 2, DH)
-    gauss_grad = jnp.stack([gauss_grad[:, :, h, h] for h in range(2)], axis=2)
-    gauss_grad = gauss_grad.transpose(1, 0, 2, 3).reshape(2, 4, 3, dp_count, -1)
-    small_grads = jnp.concatenate(
-        [
-            gauss_grad.transpose(3, 1, 0, 2, 4).reshape(dp_count * 4, -1),
-            gain_part.reshape(dp_count * 4, -1),
-            bias_part.reshape(dp_count * 4, -1),
-        ],
-        axis=1,
-    )
-    count = small_grads.shape[1]
-    if near:
-        small_grads = small_grads[jnp.arange(32) ^ (dp * 4 + rank)]
-        at = {"z": 0, "y": 1, "x": 2, "c": 3}
-        small_grads = small_grads.reshape(4, 2, 2, 2, count).transpose(
-            [at["c"]] + [at[letter] for letter in BACK_V] + [4]
-        )
-        small_grads = jnp.pad(small_grads[..., None, :], ((0, 0),) * 4 + ((0, 15), (0, 384 - count)))
-        small_grads = small_grads.astype(BF16)
-        keep_v, send_v = (
-            jnp.concatenate(parts, axis=3)
-            for parts in ((keep_v, keep_out, small_grads[0]), (send_v, send_out, small_grads[1]))
-        )
+        vmem=26,
+    )
+
+    if near:
+        send_qk = after(send_qk, *down_2[1], *up_2[1])
+        send_v = after(send_v, *down_2[1], *up_2[1])
         got_qk, got_v = swap(send_qk), swap(send_v)
-        first_qk = [(keep_qk[k].astype(F32) + got_qk[k].astype(F32)) for k in range(2)]
-        first_v = [(keep_v[k].astype(F32) + got_v[k].astype(F32)) for k in range(2)]
+        first_qk = [keep_qk[k].astype(F32) + got_qk[k].astype(F32) for k in range(2)]
+        rest = ((keep_out, got_out), (keep_v, got_v))
+        first_v = [
+            jnp.concatenate([a[k].astype(F32) + b[k].astype(F32) for a, b in rest], axis=2)
+            for k in range(2)
+        ]
         first_qk[1], first_v[1] = first_qk[1].astype(BF16), first_v[1].astype(BF16)
         qk_1 = stage(lambda k: first_qk[k], BACK_QK[0])
         v_1 = stage(lambda k: first_v[k], BACK_V[0])
-        dq_late = after(dq, first_qk[1], first_v[1])
+        down_2 = (down_2[0], [after(a, first_qk[1], first_v[1]) for a in down_2[1]])
+        to_down, to_up = combined(*down_2), combined(*up_2)
+        wide = [jnp.concatenate([to_down(k), to_up(k)]) for k in range(4)]
+        wide[1:] = [value.astype(BF16) for value in wide[1:]]
+        wide_3 = stage(lambda k: wide[k], "z")
+        dq_late = after(dq, first_qk[1], first_v[1], *wide[1:])
     else:
         dq_late = dq
 
-    (grad_tokens,) = run(
-        functools.partial(input_grad_kernel, table_qk, table_v),
-        "input_grad",
-        [info, dq_late, dk, dv, resid_grad] + qk_parts + v_parts,
-        [SCALARS] + [FULL] * 4 + [ANY] * 8,
-        [shape((SEGL, D), F32)],
-        [FULL],
-        [VMEM(MATRIX, BF16)] * 3 + [DMA((2,))],
-        cost=5.0,
-        vmem=16,
-    )
-    if near:
-        down_3 = stage(combined(*down_2), BACK_DOWN[2])
-        up_3 = stage(combined(*up_2), BACK_UP[2])
-        hidden = after(hidden, grad_tokens, qk_1[1][0], v_1[1][0])
-    fed_own, fed_other = run(
-        functools.partial(output_kernel, table_down),
-        "output",
-        [info, hidden, residual] + down_parts,
-        [SCALARS] + [FULL] * 2 + [ANY] * 2,
-        [shape((SEGL, D), F32)] * 2,
-        [FULL] * 2,
-        [VMEM(WIDE, BF16), DMA((2,))],
-        cost=6.0,
-        vmem=18,
-    )
-    half = SEGL // 2
-    part = lambda value, at: lax.dynamic_slice_in_dim(value, at * half, half)
-    arrived = swap(jnp.stack([part(fed_own, 1 - core), part(fed_other, 1 - core)]))
-    own_rows, their_rows = part(fed_own, core) + arrived[1], part(fed_other, core) + arrived[0]
-    output = jnp.where(
-        core == 0, jnp.stack([own_rows, their_rows]), jnp.stack([their_rows, own_rows])
-    )
+    token_keep, token_send, fed_keep, fed_send = run(
+        functools.partial(finish_kernel, (table_qk, table_v, table_down)),
+        "finish",
+        [info, dq_late, dk, dv, resid_grad, hidden, residual] + qk_parts + v_parts + down_parts,
+        [SCALARS] + [FULL] * 6 + [ANY] * 10,
+        [shape((HALF_SEG, D), F32), shape((HALF_SEG, D))]
+        + [shape((2, HALF_SEG, D), F32), shape((2, HALF_SEG, D))],
+        [FULL] * 4,
+        [VMEM(MATRIX, BF16)] * 3 + [VMEM(WIDE, BF16)] + [DMA((2,))] * 2,
+        cost=14.0,
+        vmem=32,
+    )
+    token_got, fed_got = swap(token_send).astype(F32), swap(fed_send).astype(F32)
+    own_rows, their_rows = fed_keep[0] + fed_got[1], fed_keep[1] + fed_got[0]
+    by_sequence = lambda mine, theirs: jnp.where(
+        core == 0, jnp.stack([mine, theirs]), jnp.stack([theirs, mine])
+    )
+    output = by_sequence(own_rows, their_rows)
+    grad_tokens = by_sequence(token_keep, token_got)
 
     if near:
         qk_2 = stage(combined(*qk_1), BACK_QK[1])
         v_2 = stage(combined(*v_1), BACK_V[1])
         to_qk, to_v = combined(*qk_2), combined(*v_2)
         joined = final_sum(*stage(lambda k: jnp.concatenate([to_qk(k), to_v(k)]), "z"))
-        own_small = joined[192, :count]
+        own_small = joined[192]
         narrow = joined[:192].reshape(4, 48, 384)
         mine = lax.dynamic_slice_in_dim(narrow, core * 192, 192, axis=2)
         partner = swap(lax.dynamic_slice_in_dim(narrow, (1 - core) * 192, 192, axis=2))
@@ -913,13 +989,19 @@
             jnp.concatenate([mine, partner], axis=1),
             jnp.concatenate([partner, mine], axis=1),
         )
-        own_up, own_down = final_sum(*up_3), final_sum(*down_3).T
+        own_wide = final_sum(*wide_3)
+        own_up, own_down = own_wide[96:], own_wide[:96].T
     else:
+        gauss_grad = gauss_grad.reshape(2, 4, 3, dp_count, -1).transpose(3, 1, 0, 2, 4)
+        small_grads = jnp.concatenate(
+            [value.reshape(dp_count * 4, -1) for value in (gauss_grad, gain_part, bias_part)],
+            axis=1,
+        )
         own_small = lax.psum_scatter(small_grads, AXES, scatter_dimension=0)
         pieces = [
             whole_from([keep_qk, send_qk], BACK_QK).reshape(8, 2, 2, 2, 48, 384),
-            whole_from([keep_v, send_v], BACK_V)[:, :, :, None],
             whole_from([keep_out, send_out], BACK_V)[:, :, :, None],
+            whole_from([keep_v, send_v], BACK_V)[:, :, :, None, :48],
         ]
         pieces = jnp.concatenate(pieces, axis=3).transpose(0, 2, 4, 3, 1, 5)
         pieces = pieces.reshape(dp_count, D // dp_count, 4, 4, 192).transpose(0, 3, 2, 1, 4)
@@ -927,7 +1009,7 @@
         narrow = total(pieces.reshape((-1,) + pieces.shape[2:]))
 
         def owned(keep, order):
-            mine = whole_from([keep], order)
+            mine = whole_from([jnp.stack(keep)], order)
             both = jnp.concatenate(
                 [jnp.where(core == at, mine, jnp.zeros_like(mine)) for at in range(2)], axis=2
             )
@@ -936,15 +1018,15 @@
             return total(both.reshape((-1,) + both.shape[2:]))
 
         own_up, own_down = owned(keep_up, BACK_UP), owned(keep_down, BACK_DOWN).T
-    own_qkv, own_out = narrow[:3], narrow[3].T
+    own_qkv, own_out = jnp.concatenate([narrow[:2], narrow[3:]]), narrow[2].T
     return (
         output,
-        from_segment(grad_tokens),
+        grad_tokens,
         own_qkv,
         own_small[:gauss_size].reshape(w_gauss.shape),
         own_out,
         own_small[gauss_size : gauss_size + gain_size],
-        own_small[gauss_size + gain_size :],
+        own_small[gauss_size + gain_size : gauss_size + 2 * gain_size],
         own_up,
         own_down,
     )

time: 306 us -> 287 us (0.938)
  waiting for transfers between devices: 56 us -> 87.9 us
  other arithmetic: 42.7 us -> 15.6 us
  local copies, waits for them, and re-layouts: 28.8 us -> 16 us
  starting transfers between devices: 57.4 us -> 52.2 us
  Pallas kernels: 116 us -> 111 us
    ppermute x48 -> x46, waiting for transfers between devices: 50 us -> 80.6 us  [xor_permute(): return lax.ppermute(value, AXES, pairs)]
    convert_element_type x3 -> x1, other arithmetic: 7.45 us -> 0.11 us  [local(): swap(fed_send).astype(F32)]
    ppermute x1, waiting for transfers between devices: 0.01 us -> 7.34 us  [local(): coef_grad = lax.ppermute(coef_grad, 'tensor', [(2, 0), (3, 1)])]
    another operation x10 -> x9, other arithmetic: 9.8 us -> 2.79 us  [the longest x1 1.35 us: local(): up_parts = spread(after(jnp.stack(up_x), q), 'y')]
    ppermute x1, waiting for transfers between devices: 5.98 us -> 0.01 us  [local(): coef = lax.ppermute(coef, 'tensor', [(0, 2), (1, 3)])]
    ppermute x48 -> x46, starting transfers between devices: 52.6 us -> 47.5 us  [xor_permute(): return lax.ppermute(value, AXES, pairs)]
    another operation x15 -> x8, local copies, waits for them, and re-layouts: 4.44 us -> 0.08 us  [the longest x4 0.04 us: local(): v_near = jnp.stack(spread(jnp.stack([part[96:] for part in along_z]), 'x'))]
    pallas_call x10 -> x9, Pallas kernels: 116 us -> 111 us  [run(): pl.pallas_call(body, name=name, out_shape=tuple((pltpu.HBM(out.shape, out...]
  transfers between devices with their start and end apart: 50 -> 48, of which waited for: 11 -> 21; matrix products, arithmetic and copies ran while one was open for 21% -> 6% of each run, Pallas kernels for 38% -> 39%
where the time goes in v4:
time: 287 us; the launch traced here: 286 us
  Pallas kernels  111 us (39%)
  waiting for transfers between devices  87.9 us (31%)
  starting transfers between devices  52.2 us (18%)
  local copies, waits for them, and re-layouts  16 us (6%)
  other arithmetic  15.6 us (5%)
  between operations  2.89 us (1%)
    pallas_call x9, Pallas kernels, run(): pl.pallas_call(body, name=name, out_shape=tuple((pltpu.HBM(out.shape, out...  111 us
    ppermute x46, waiting for transfers between devices, xor_permute(): return lax.ppermute(value, AXES, pairs)  80.6 us
    ppermute x46, starting transfers between devices, xor_permute(): return lax.ppermute(value, AXES, pairs)  47.5 us
    ppermute x1, waiting for transfers between devices, local(): coef_grad = lax.ppermute(coef_grad, 'tensor', [(2, 0), (3, 1)])  7.34 us
    unnamed x81, local copies, waits for them, and re-layouts  7.02 us
  transfers between devices with their start and end apart: 48, of which 21 were waited for; matrix products, arithmetic and copies ran while one was open for 6% of the time, Pallas kernels for 39%

profile of v4, /device:TPU:0, one launch (start us, length us, event | category | flops | bytes accessed | tf_op | source)
XLA Modules:
  0.0 286.1 jit_solution(4540384806102976302)
XLA Ops:
  8.1 4.7 %collective-permute-start.5 = (bf16[208,384]{1,0:T(8,128)(2,1)S(1)}, bf16[208,384]{1,0:T(8,128)(2,1)S(1)}, u32[]{:S(2)}, u32[]{:S(2)}) collective-permute-start(bf16[208,384]{1,0:T(8,128)(2,1)S(1)} %fusion.43), channel_id=1, source_target_pairs={{0,24},{1,25},{2,26},{3,27},{4,28},{5,29},{6,30},{7,31},{8,16},{9,... | collective-permute-start | bytes 479240 | tf_op jit(solution)/shard_map/ppermute | solution.py:45
  17.1 6.6 %collective-permute-done.3 = bf16[208,384]{1,0:T(8,128)(2,1)S(1)} collective-permute-done((bf16[208,384]{1,0:T(8,128)(2,1)S(1)}, bf16[208,384]{1,0:T(8,128)(2,1)S(1)}, u32[]{:S(2)}, u32[]{:S(2)}) %collective-permute-start.3) | collective-permute-done | bytes 159776 | tf_op jit(solution)/shard_map/ppermute | solution.py:45
  30.3 6.4 %collective-permute-done.9 = bf16[4,112,384]{2,1,0:T(8,128)(2,1)S(1)} collective-permute-done((bf16[4,112,384]{2,1,0:T(8,128)(2,1)S(1)}, bf16[4,112,384]{2,1,0:T(8,128)(2,1)S(1)}, u32[]{:S(2)}, u32[]{:S(2)}) %collective-permute-start.9) | collective-permute-done | bytes 344096 | tf_op jit(solution)/shard_map/ppermute | solution.py:45
  45.0 10.0 %collective-permute-done.15.refs_5_.refs_1_ = bf16[2,4,112,384]{3,2,1,0:T(8,128)(2,1)S(1)} collective-permute-done((bf16[2,4,112,384]{3,2,1,0:T(8,128)(2,1)S(1)}, bf16[2,4,112,384]{3,2,1,0:T(8,128)(2,1)S(1)}, u32[]{:S(2)}, u32[]{:S(2)}) %collective-permute-start.15) | collective-permute-done | bytes 688160 | tf_op jit(solution)/shard_map/ppermute | solution.py:45
  61.6 9.0 %qkv.1 = (bf16[512,768]{1,0:T(8,128)(2,1)}, bf16[512,768]{1,0:T(8,128)(2,1)}, bf16[512,768]{1,0:T(8,128)(2,1)}, bf16[512,768]{1,0:T(8,128)(2,1)}, bf16[256,768]{...) custom-call(s32[6]{0:T(128)S(1)} %stack.148.info, ...), custom_call_target="tpu_custom_call" | custom-call | flops 1200000000 | bytes 1000000 | tf_op jit(solution)/shard_map/qkv/pallas_call | solution.py:664
  70.7 3.9 %collective-permute-done.17 = bf16[4,96,768]{2,1,0:T(8,128)(2,1)} collective-permute-done((bf16[4,96,768]{2,1,0:T(8,128)(2,1)}, bf16[4,96,768]{2,1,0:T(8,128)(2,1)}, u32[]{:S(2)}, u32[]{:S(2)}) %collective-permute-start.17) | collective-permute-done | bytes 589856 | tf_op jit(solution)/shard_map/ppermute | solution.py:45
  77.6 3.5 %collective-permute-start.18 = (bf16[256,768]{1,0:T(8,128)(2,1)S(1)}, bf16[256,768]{1,0:T(8,128)(2,1)S(1)}, u32[]{:S(2)}, u32[]{:S(2)}) collective-permute-start(bf16[256,768]{1,0:T(8,128)(2,1)S(1)} %copy-done.37), channel_id=1, source_target_pairs={{0,2},{1,3},{4,6},{5,7},{8,10},{9,11},{12,14},{13,15},{16,18},{17,... | collective-permute-start | bytes 1179656 | tf_op jit(solution)/shard_map/ppermute | solution.py:795
  85.6 13.1 %attend.1 = (bf16[12,512,512]{2,1,0:T(8,128)(2,1)}, f32[768,512]{1,0:T(8,128)}, bf16[12,256,512]{2,1,0:T(8,128)(2,1)}) custom-call(s32[6]{0:T(128)S(1)} %stack.148.info, bf16[512,768]{1,0:T(8,128)(2,1)} %get-tuple-element.79.q, bf16[512,768]{1,0:T(8,128)(2,1)} %get-tuple-element.80.k, bf16[512,768]{1,0:T(8,128)(2,1)} %get-tuple-element.81.v, ...), custom_call_target="tpu_custom_call" | custom-call | flops 2400000000 | bytes 1000000 | tf_op jit(solution)/shard_map/attend/pallas_call | solution.py:664
  98.7 4.5 %collective-permute-done.20.refs_1_.refs_3_ = bf16[2,4,96,768]{3,2,1,0:T(8,128)(2,1)S(1)} collective-permute-done((bf16[2,4,96,768]{3,2,1,0:T(8,128)(2,1)S(1)}, bf16[2,4,96,768]{3,2,1,0:T(8,128)(2,1)S(1)}, u32[]{:S(2)}, u32[]{:S(2)}) %collective-permute-start.20) | collective-permute-done | bytes 1179680 | tf_op jit(solution)/shard_map/ppermute | solution.py:45
  104.8 8.8 %recall.1 = (bf16[512,768]{1,0:T(8,128)(2,1)}, f32[512,768]{1,0:T(8,128)}, bf16[512,768]{1,0:T(8,128)(2,1)}) custom-call(s32[6]{0:T(128)S(1)} %stack.148.info, bf16[12,256,512]{2,1,0:T(8,128)(2,1)} %get-tuple-element.84.dens_t, bf16[256,768]{1,0:T(8,128)(2,1)} %copy-done.14, f32[768,512]{1,0:T(8,128)} %get-tuple-element.86.local_t, ...), custom_call_target="tpu_custom_call" | custom-call | flops 1400000000 | bytes 1000000 | tf_op jit(solution)/shard_map/recall/pallas_call | solution.py:664
  113.7 3.4 %collective-permute-done.24 = bf16[4,96,768]{2,1,0:T(8,128)(2,1)S(1)} collective-permute-done((bf16[4,96,768]{2,1,0:T(8,128)(2,1)S(1)}, bf16[4,96,768]{2,1,0:T(8,128)(2,1)S(1)}, u32[]{:S(2)}, u32[]{:S(2)}) %collective-permute-start.24) | collective-permute-done | bytes 589856 | tf_op jit(solution)/shard_map/ppermute | solution.py:45
  121.9 14.1 %up.1 = (bf16[2,512,1536]{2,1,0:T(8,128)(2,1)}, bf16[2,512,1536]{2,1,0:T(8,128)(2,1)}, bf16[2,4,96,768]{3,2,1,0:T(8,128)(2,1)}, bf16[2,4,96,768]{3,2,1,0:T(8,128)(2,1)}) custom-call(s32[6]{0:T(128)S(1)} %stack.148.info, bf16[512,768]{1,0:T(8,128)(2,1)} %get-tuple-element.90.own, bf16[512,768]{1,0:T(8,128)(2,1)} %copy-done.36, bf16[768,1024]{1,0:T(8,128)(2,1)} %bitcast.257, ...), custom_call_target="tpu_custom_call" | custom-call | flops 2400000000 | bytes 1000000 | tf_op jit(solution)/shard_map/up/pallas_call | solution.py:664
  136.6 9.5 %collective-permute-done.25.refs_1_.refs_9_ = bf16[2,4,96,768]{3,2,1,0:T(8,128)(2,1)S(1)} collective-permute-done((bf16[2,4,96,768]{3,2,1,0:T(8,128)(2,1)S(1)}, bf16[2,4,96,768]{3,2,1,0:T(8,128)(2,1)S(1)}, u32[]{:S(2)}, u32[]{:S(2)}) %collective-permute-start.25) | collective-permute-done | bytes 1179680 | tf_op jit(solution)/shard_map/ppermute | solution.py:45
  147.1 18.8 %down.1 = (bf16[2,4,96,768]{3,2,1,0:T(8,128)(2,1)}, bf16[2,4,96,768]{3,2,1,0:T(8,128)(2,1)}, f32[512,768]{1,0:T(8,128)}, bf16[512,768]{1,0:T(8,128)(2,1)}) custom-call(s32[6]{0:T(128)S(1)} %stack.148.info, bf16[2,512,768]{2,1,0:T(8,128)(2,1)} %copy-done.8, bf16[512,768]{1,0:T(8,128)(2,1)} %get-tuple-element.90.own, bf16[512,768]{1,0:T(8,128)(2,1)} %copy-done.36, ...), custom_call_target="tpu_custom_call" | custom-call | flops 3000000000 | bytes 1000000 | tf_op jit(solution)/shard_map/down/pallas_call | solution.py:664
  169.4 11.3 %mix_back.1 = (f32[512,768]{1,0:T(8,128)}, bf16[512,768]{1,0:T(8,128)(2,1)}, bf16[256,768]{1,0:T(8,128)(2,1)}, f32[1,768]{1,0:T(1,128)}, f32[1,768]{1,0:T(1,128)...) custom-call(s32[6]{0:T(128)S(1)} %stack.148.info, f32[512,768]{1,0:T(8,128)} %get-tuple-element.100.own, ...), custom_call_target="tpu_custom_call" | custom-call | flops 1200000000 | bytes 1000000 | tf_op jit(solution)/shard_map/mix_back/pallas_call | solution.py:664
  182.2 13.4 %attend_back.1 = (bf16[512,768]{1,0:T(8,128)(2,1)}, bf16[512,768]{1,0:T(8,128)(2,1)}, f32[512,768]{1,0:T(8,128)}, f32[2,768]{1,0:T(2,128)}) custom-call(bf16[12,512,512]{2,1,0:T(8,128)(2,1)} %get-tuple-element.83.attn_t, bf16[512,768]{1,0:T(8,128)(2,1)} %get-tuple-element.79.q, bf16[512,768]{1,0:T(8,128)(2,1)} %get-tuple-element.80.k, ...), custom_call_target="tpu_custom_call" | custom-call | flops 3200000000 | bytes 1000000 | tf_op jit(solution)/shard_map/attend_back/pallas_call | solution.py:664
  195.7 7.3 %collective-permute-done.29.coef_grad = bf16[256,768]{1,0:T(8,128)(2,1)S(1)} collective-permute-done((bf16[256,768]{1,0:T(8,128)(2,1)}, bf16[256,768]{1,0:T(8,128)(2,1)S(1)}, u32[]{:S(2)}, u32[]{:S(2)}) %collective-permute-start.29) | collective-permute-done | bytes 393248 | tf_op jit(solution)/shard_map/ppermute | solution.py:893
  205.6 9.6 %qkv_grad.1 = (bf16[2,2,4,96,384]{4,3,2,1,0:T(8,128)(2,1)}, bf16[2,2,4,96,384]{4,3,2,1,0:T(8,128)(2,1)}, bf16[2,2,4,64,384]{4,3,2,1,0:T(8,128)(2,1)}, bf16[2,2,4...) custom-call(s32[6]{0:T(128)S(1)} %stack.148.info, bf16[512,768]{1,0:T(8,128)(2,1)} %get-tuple-element.87.x, ...), custom_call_target="tpu_custom_call" | custom-call | flops 1200000000 | bytes 1000000 | tf_op jit(solution)/shard_map/qkv_grad/pallas_call | solution.py:664
  215.3 3.3 %collective-permute-done.32 = bf16[4,96,768]{2,1,0:T(8,128)(2,1)S(1)} collective-permute-done((bf16[4,96,768]{2,1,0:T(8,128)(2,1)S(1)}, bf16[4,96,768]{2,1,0:T(8,128)(2,1)S(1)}, u32[]{:S(2)}, u32[]{:S(2)}) %collective-permute-start.32) | collective-permute-done | bytes 589856 | tf_op jit(solution)/shard_map/ppermute | solution.py:45
  232.9 13.1 %finish.1 = (f32[256,768]{1,0:T(8,128)}, bf16[256,768]{1,0:T(8,128)(2,1)}, f32[2,256,768]{2,1,0:T(8,128)}, bf16[2,256,768]{2,1,0:T(8,128)(2,1)}) custom-call(s32[6]{0:T(128)S(1)} %stack.148.info, bf16[512,768]{1,0:T(8,128)(2,1)} %get-tuple-element.127.dq, bf16[512,768]{1,0:T(8,128)(2,1)} %get-tuple-element.107.dk, bf16[512,768]{1,0:T(8,128)(2,1)} %get-tuple-element.128.dv, ...), custom_call_target="tpu_custom_call" | custom-call | flops 2800000000 | bytes 1000000 | tf_op jit(solution)/shard_map/finish/pallas_call | solution.py:664
  246.1 5.0 %collective-permute-done.46 = bf16[192,768]{1,0:T(8,128)(2,1)} collective-permute-done((bf16[192,768]{1,0:T(8,128)(2,1)}, bf16[192,768]{1,0:T(8,128)(2,1)}, u32[]{:S(2)}, u32[]{:S(2)}) %collective-permute-start.46) | collective-permute-done | bytes 294944 | tf_op jit(solution)/shard_map/ppermute | solution.py:45
  256.2 7.7 %collective-permute-done.40 = bf16[4,112,384]{2,1,0:T(8,128)(2,1)S(1)} collective-permute-done((bf16[4,112,384]{2,1,0:T(8,128)(2,1)S(1)}, bf16[4,112,384]{2,1,0:T(8,128)(2,1)S(1)}, u32[]{:S(2)}, u32[]{:S(2)}) %collective-permute-start.40) | collective-permute-done | bytes 344096 | tf_op jit(solution)/shard_map/ppermute | solution.py:45
  264.2 5.8 %collective-permute-start.42 = (bf16[208,384]{1,0:T(8,128)(2,1)S(1)}, bf16[208,384]{1,0:T(8,128)(2,1)S(1)}, u32[]{:S(2)}, u32[]{:S(2)}) collective-permute-start(bf16[208,384]{1,0:T(8,128)(2,1)S(1)} %pad_maximum_fusion.16), channel_id=1, source_target_pairs={{0,16},{1,17},{2,18},{3,19},{4,20},{5,21},{6,22},{7,23},{8,24},{9,... | collective-permute-start | bytes 479240 | tf_op jit(solution)/shard_map/ppermute | solution.py:45
  273.1 7.7 %collective-permute-done.42 = bf16[208,384]{1,0:T(8,128)(2,1)S(1)} collective-permute-done((bf16[208,384]{1,0:T(8,128)(2,1)S(1)}, bf16[208,384]{1,0:T(8,128)(2,1)S(1)}, u32[]{:S(2)}, u32[]{:S(2)}) %collective-permute-start.42) | collective-permute-done | bytes 159776 | tf_op jit(solution)/shard_map/ppermute | solution.py:45
  (233 shorter events, 82.5 us)
Async XLA Ops:
  8.1 15.6 %collective-permute-start.5 = (bf16[208,384]{1,0:T(8,128)(2,1)S(1)}, bf16[208,384]{1,0:T(8,128)(2,1)S(1)}, u32[]{:S(2)}, u32[]{:S(2)}) collective-permute-start(bf16[208,384]{1,0:T(8,128)(2,1)S(1)} %fusion.43), channel_id=1, source_target_pairs={{0,24},{1,25},{2,26},{3,27},{4,28},{5,29},{6,30},{7,31},{8,16},{9,... | collective-permute-start | bytes 479240 | tf_op jit(solution)/shard_map/ppermute | solution.py:45
  12.8 14.2 %collective-permute-start.4 = (bf16[208,384]{1,0:T(8,128)(2,1)S(1)}, bf16[208,384]{1,0:T(8,128)(2,1)S(1)}, u32[]{:S(2)}, u32[]{:S(2)}) collective-permute-start(bf16[208,384]{1,0:T(8,128)(2,1)S(1)} %fusion.43), channel_id=1, source_target_pairs={{0,16},{1,17},{2,18},{3,19},{4,20},{5,21},{6,22},{7,23},{8,24},{9,... | collective-permute-start | bytes 479240 | tf_op jit(solution)/shard_map/ppermute | solution.py:45
  37.5 17.5 %collective-permute-start.15 = (bf16[2,4,112,384]{3,2,1,0:T(8,128)(2,1)S(1)}, bf16[2,4,112,384]{3,2,1,0:T(8,128)(2,1)S(1)}, u32[]{:S(2)}, u32[]{:S(2)}) collective-permute-start(bf16[2,4,112,384]{3,2,1,0:T(8,128)(2,1)S(1)} %pad_maximum_fusion.4.refs_4_.refs_0_), channel_id=1, source_target_pairs={{0,4},{1,5},{2,6},{3,7},{4,0},{5,1},{6,2},{7,3},{8,12},{9,13},{10,... | collective-permute-start | bytes 2064392 | tf_op jit(solution)/shard_map/ppermute | solution.py:45
  39.0 16.1 %collective-permute-start.7 = (bf16[2,4,96,384]{3,2,1,0:T(8,128)(2,1)S(1)}, bf16[2,4,96,384]{3,2,1,0:T(8,128)(2,1)S(1)}, u32[]{:S(2)}, u32[]{:S(2)}) collective-permute-start(bf16[2,4,96,384]{3,2,1,0:T(8,128)(2,1)S(1)} %pad_maximum_fusion.6.refs_0_), channel_id=1, source_target_pairs={{0,2},{1,3},{2,0},{3,1},{4,6},{5,7},{6,4},{7,5},{8,10},{9,11},{10,... | collective-permute-start | bytes 1769480 | tf_op jit(solution)/shard_map/ppermute | solution.py:45
  40.5 14.5 %collective-permute-start.13 = (bf16[96,768]{1,0:T(8,128)(2,1)S(1)}, bf16[96,768]{1,0:T(8,128)(2,1)S(1)}, u32[]{:S(2)}, u32[]{:S(2)}) collective-permute-start(bf16[96,768]{1,0:T(8,128)(2,1)S(1)} %copy-done.28), channel_id=1, source_target_pairs={{0,24},{1,25},{2,26},{3,27},{4,28},{5,29},{6,30},{7,31},{8,16},{9,... | collective-permute-start | bytes 442376 | tf_op jit(solution)/shard_map/ppermute | solution.py:45
  59.0 15.7 %collective-permute-start.17 = (bf16[4,96,768]{2,1,0:T(8,128)(2,1)}, bf16[4,96,768]{2,1,0:T(8,128)(2,1)}, u32[]{:S(2)}, u32[]{:S(2)}) collective-permute-start(bf16[4,96,768]{2,1,0:T(8,128)(2,1)} %pad_maximum_fusion.7), channel_id=1, source_target_pairs={{0,2},{1,3},{2,0},{3,1},{4,6},{5,7},{6,4},{7,5},{8,10},{9,11},{10,... | collective-permute-start | bytes 1769480 | tf_op jit(solution)/shard_map/ppermute | solution.py:45
  76.0 27.2 %collective-permute-start.20 = (bf16[2,4,96,768]{3,2,1,0:T(8,128)(2,1)S(1)}, bf16[2,4,96,768]{3,2,1,0:T(8,128)(2,1)S(1)}, u32[]{:S(2)}, u32[]{:S(2)}) collective-permute-start(bf16[2,4,96,768]{3,2,1,0:T(8,128)(2,1)S(1)} %pad_maximum_fusion.1.refs_0_.refs_2_), channel_id=1, source_target_pairs={{0,4},{1,5},{2,6},{3,7},{4,0},{5,1},{6,2},{7,3},{8,12},{9,13},{10,... | collective-permute-start | bytes 3538952 | tf_op jit(solution)/shard_map/ppermute | solution.py:45
  77.6 21.1 %collective-permute-start.18 = (bf16[256,768]{1,0:T(8,128)(2,1)S(1)}, bf16[256,768]{1,0:T(8,128)(2,1)S(1)}, u32[]{:S(2)}, u32[]{:S(2)}) collective-permute-start(bf16[256,768]{1,0:T(8,128)(2,1)S(1)} %copy-done.37), channel_id=1, source_target_pairs={{0,2},{1,3},{4,6},{5,7},{8,10},{9,11},{12,14},{13,15},{16,18},{17,... | collective-permute-start | bytes 1179656 | tf_op jit(solution)/shard_map/ppermute | solution.py:795
  81.1 17.6 %collective-permute-start.23 = (bf16[96,768]{1,0:T(8,128)(2,1)S(1)}, bf16[96,768]{1,0:T(8,128)(2,1)S(1)}, u32[]{:S(2)}, u32[]{:S(2)}) collective-permute-start(bf16[96,768]{1,0:T(8,128)(2,1)S(1)} %bitcast.264), channel_id=1, source_target_pairs={{0,24},{1,25},{2,26},{3,27},{4,28},{5,29},{6,30},{7,31},{8,16},{9,... | collective-permute-start | bytes 442376 | tf_op jit(solution)/shard_map/ppermute | solution.py:45
  83.6 15.1 %collective-permute-start.22 = (bf16[96,768]{1,0:T(8,128)(2,1)S(1)}, bf16[96,768]{1,0:T(8,128)(2,1)S(1)}, u32[]{:S(2)}, u32[]{:S(2)}) collective-permute-start(bf16[96,768]{1,0:T(8,128)(2,1)S(1)} %bitcast.265), channel_id=1, source_target_pairs={{0,16},{1,17},{2,18},{3,19},{4,20},{5,21},{6,22},{7,23},{8,24},{9,... | collective-permute-start | bytes 442376 | tf_op jit(solution)/shard_map/ppermute | solution.py:45
  83.6 15.1 %collective-permute-start.21 = (bf16[96,768]{1,0:T(8,128)(2,1)S(1)}, bf16[96,768]{1,0:T(8,128)(2,1)S(1)}, u32[]{:S(2)}, u32[]{:S(2)}) collective-permute-start(bf16[96,768]{1,0:T(8,128)(2,1)S(1)} %bitcast.266), channel_id=1, source_target_pairs={{0,8},{1,9},{2,10},{3,11},{4,12},{5,13},{6,14},{7,15},{8,0},{9,1},... | collective-permute-start | bytes 442376 | tf_op jit(solution)/shard_map/ppermute | solution.py:45
  117.2 28.9 %collective-permute-start.25 = (bf16[2,4,96,768]{3,2,1,0:T(8,128)(2,1)S(1)}, bf16[2,4,96,768]{3,2,1,0:T(8,128)(2,1)S(1)}, u32[]{:S(2)}, u32[]{:S(2)}) collective-permute-start(bf16[2,4,96,768]{3,2,1,0:T(8,128)(2,1)S(1)} %pad_maximum_fusion.2.refs_0_.refs_8_), channel_id=1, source_target_pairs={{0,4},{1,5},{2,6},{3,7},{4,0},{5,1},{6,2},{7,3},{8,12},{9,13},{10,... | collective-permute-start | bytes 3538952 | tf_op jit(solution)/shard_map/ppermute | solution.py:45
  136.0 32.4 %collective-permute-start.26 = (bf16[2,4,96,768]{3,2,1,0:T(8,128)(2,1)}, bf16[2,4,96,768]{3,2,1,0:T(8,128)(2,1)S(1)}, u32[]{:S(2)}, u32[]{:S(2)}) collective-permute-start(bf16[2,4,96,768]{3,2,1,0:T(8,128)(2,1)} %get-tuple-element.99), channel_id=1, source_target_pairs={{0,4},{1,5},{2,6},{3,7},{4,0},{5,1},{6,2},{7,3},{8,12},{9,13},{10,... | collective-permute-start | bytes 3538952 | tf_op jit(solution)/shard_map/ppermute | solution.py:45
  166.0 29.7 %collective-permute-start.28 = (bf16[2,4,96,768]{3,2,1,0:T(8,128)(2,1)}, bf16[2,4,96,768]{3,2,1,0:T(8,128)(2,1)S(1)}, u32[]{:S(2)}, u32[]{:S(2)}) collective-permute-start(bf16[2,4,96,768]{3,2,1,0:T(8,128)(2,1)} %get-tuple-element.106), channel_id=1, source_target_pairs={{0,2},{1,3},{2,0},{3,1},{4,6},{5,7},{6,4},{7,5},{8,10},{9,11},{10,... | collective-permute-start | bytes 3538952 | tf_op jit(solution)/shard_map/ppermute | solution.py:45
  180.7 22.3 %collective-permute-start.30 = (bf16[2,2,4,48,384]{4,3,2,1,0:T(8,128)(2,1)}, bf16[2,2,4,48,384]{4,3,2,1,0:T(8,128)(2,1)S(1)}, u32[]{:S(2)}, u32[]{:S(2)}) collective-permute-start(bf16[2,2,4,48,384]{4,3,2,1,0:T(8,128)(2,1)} %get-tuple-element.109), channel_id=1, source_target_pairs={{0,1},{1,0},{2,3},{3,2},{4,5},{5,4},{6,7},{7,6},{8,9},{9,8},{10,11... | collective-permute-start | bytes 1769480 | tf_op jit(solution)/shard_map/ppermute | solution.py:45
  180.9 22.1 %collective-permute-start.29 = (bf16[256,768]{1,0:T(8,128)(2,1)}, bf16[256,768]{1,0:T(8,128)(2,1)S(1)}, u32[]{:S(2)}, u32[]{:S(2)}) collective-permute-start(bf16[256,768]{1,0:T(8,128)(2,1)} %get-tuple-element.108), channel_id=1, source_target_pairs={{2,0},{3,1},{6,4},{7,5},{10,8},{11,9},{14,12},{15,13},{18,16},{19,... | collective-permute-start | bytes 1179656 | tf_op jit(solution)/shard_map/ppermute | solution.py:893
  203.8 14.8 %collective-permute-start.32 = (bf16[4,96,768]{2,1,0:T(8,128)(2,1)S(1)}, bf16[4,96,768]{2,1,0:T(8,128)(2,1)S(1)}, u32[]{:S(2)}, u32[]{:S(2)}) collective-permute-start(bf16[4,96,768]{2,1,0:T(8,128)(2,1)S(1)} %get-tuple-element.162), channel_id=1, source_target_pairs={{0,4},{1,5},{2,6},{3,7},{4,0},{5,1},{6,2},{7,3},{8,12},{9,13},{10,... | collective-permute-start | bytes 1769480 | tf_op jit(solution)/shard_map/ppermute | solution.py:45
  205.6 14.6 %collective-permute-start.31 = (bf16[4,96,768]{2,1,0:T(8,128)(2,1)S(1)}, bf16[4,96,768]{2,1,0:T(8,128)(2,1)S(1)}, u32[]{:S(2)}, u32[]{:S(2)}) collective-permute-start(bf16[4,96,768]{2,1,0:T(8,128)(2,1)S(1)} %get-tuple-element.160), channel_id=1, source_target_pairs={{0,2},{1,3},{2,0},{3,1},{4,6},{5,7},{6,4},{7,5},{8,10},{9,11},{10,... | collective-permute-start | bytes 1769480 | tf_op jit(solution)/shard_map/ppermute | solution.py:45
  226.5 19.6 %collective-permute-start.45 = (bf16[192,768]{1,0:T(8,128)(2,1)}, bf16[192,768]{1,0:T(8,128)(2,1)}, u32[]{:S(2)}, u32[]{:S(2)}) collective-permute-start(bf16[192,768]{1,0:T(8,128)(2,1)} %pad_maximum_fusion.11), channel_id=1, source_target_pairs={{0,8},{1,9},{2,10},{3,11},{4,12},{5,13},{6,14},{7,15},{8,0},{9,1},... | collective-permute-start | bytes 884744 | tf_op jit(solution)/shard_map/ppermute | solution.py:45
  227.2 23.9 %collective-permute-start.46 = (bf16[192,768]{1,0:T(8,128)(2,1)}, bf16[192,768]{1,0:T(8,128)(2,1)}, u32[]{:S(2)}, u32[]{:S(2)}) collective-permute-start(bf16[192,768]{1,0:T(8,128)(2,1)} %pad_maximum_fusion.12), channel_id=1, source_target_pairs={{0,16},{1,17},{2,18},{3,19},{4,20},{5,21},{6,22},{7,23},{8,24},{9,... | collective-permute-start | bytes 884744 | tf_op jit(solution)/shard_map/ppermute | solution.py:45
  230.3 20.8 %collective-permute-start.47 = (bf16[192,768]{1,0:T(8,128)(2,1)S(1)}, bf16[192,768]{1,0:T(8,128)(2,1)}, u32[]{:S(2)}, u32[]{:S(2)}) collective-permute-start(bf16[192,768]{1,0:T(8,128)(2,1)S(1)} %pad_maximum_fusion.13), channel_id=1, source_target_pairs={{0,24},{1,25},{2,26},{3,27},{4,28},{5,29},{6,30},{7,31},{8,16},{9,... | collective-permute-start | bytes 884744 | tf_op jit(solution)/shard_map/ppermute | solution.py:45
  231.7 21.6 %collective-permute-start.39 = (bf16[2,4,112,384]{3,2,1,0:T(8,128)(2,1)}, bf16[2,4,112,384]{3,2,1,0:T(8,128)(2,1)S(1)}, u32[]{:S(2)}, u32[]{:S(2)}) collective-permute-start(bf16[2,4,112,384]{3,2,1,0:T(8,128)(2,1)} %pad_maximum_fusion.5), channel_id=1, source_target_pairs={{0,4},{1,5},{2,6},{3,7},{4,0},{5,1},{6,2},{7,3},{8,12},{9,13},{10,... | collective-permute-start | bytes 2064392 | tf_op jit(solution)/shard_map/ppermute | solution.py:45
  232.6 21.2 %collective-permute-start.37 = (bf16[2,4,96,384]{3,2,1,0:T(8,128)(2,1)}, bf16[2,4,96,384]{3,2,1,0:T(8,128)(2,1)S(1)}, u32[]{:S(2)}, u32[]{:S(2)}) collective-permute-start(bf16[2,4,96,384]{3,2,1,0:T(8,128)(2,1)} %get-tuple-element.158), channel_id=1, source_target_pairs={{0,2},{1,3},{2,0},{3,1},{4,6},{5,7},{6,4},{7,5},{8,10},{9,11},{10,... | collective-permute-start | bytes 1769480 | tf_op jit(solution)/shard_map/ppermute | solution.py:45
  264.2 16.6 %collective-permute-start.42 = (bf16[208,384]{1,0:T(8,128)(2,1)S(1)}, bf16[208,384]{1,0:T(8,128)(2,1)S(1)}, u32[]{:S(2)}, u32[]{:S(2)}) collective-permute-start(bf16[208,384]{1,0:T(8,128)(2,1)S(1)} %pad_maximum_fusion.16), channel_id=1, source_target_pairs={{0,16},{1,17},{2,18},{3,19},{4,20},{5,21},{6,22},{7,23},{8,24},{9,... | collective-permute-start | bytes 479240 | tf_op jit(solution)/shard_map/ppermute | solution.py:45
  (62 other events, 535.9 us)

commit v5 on v4

--- a/solution.py
+++ b/solution.py
@@ -62,6 +62,15 @@
                 k = {first: i1, second: i2, third: k3}
                 table.append((at, (i2, i1), k["z"] * 2 + k["y"], k["x"], kc))
     return table
+
+
+def wide_table():
+    return [
+        (2 * ky + kx, (kz,), 2 * kz + ky, kx, 0)
+        for ky in range(2)
+        for kx in range(2)
+        for kz in range(4)
+    ]
 
 
 def spread(piece, letter):
@@ -375,10 +384,10 @@
 
 
 def up_kernel(table, order, info, own, other, seed_t, *refs):
-    parts = refs[0:2]
-    hidden_out, slope_out = refs[2:4]
-    keep = refs[4:6]
-    w_up, grad, hidden, slope, sems, out_sems, side_sems = refs[6:]
+    parts = refs[0:4]
+    hidden_out, slope_out = refs[4:6]
+    keep = refs[6:8]
+    w_up, grad, hidden, slope, sems, out_sems, side_sems = refs[8:]
     for copy in wide_copies(info, table, parts, w_up, sems):
         copy.start()
     outs = list(wide_out(info, order, keep, grad, out_sems))
@@ -410,10 +419,10 @@
 
 
 def down_kernel(tables, order, info, seed, own, other, slope_in, *refs):
-    down_parts, up_parts = refs[0:2], refs[2:4]
-    keep = refs[4:6]
-    own_grad, other_grad = refs[6:8]
-    w_down, w_up, grad, slope, total, normed_t, down_sems, up_sems, out_sems, side_sems = refs[8:]
+    down_parts, up_parts = refs[0:4], refs[4:8]
+    keep = refs[8:10]
+    own_grad, other_grad = refs[10:12]
+    w_down, w_up, grad, slope, total, normed_t, down_sems, up_sems, out_sems, side_sems = refs[12:]
     for copy in wide_copies(info, tables[0], down_parts, w_down, down_sems):
         copy.start()
     for copy in wide_copies(info, tables[1], up_parts, w_up, up_sems):
@@ -601,9 +610,9 @@
 
 
 def finish_kernel(tables, info, dq, dk, dv, resid_grad, hidden, residual, *refs):
-    qk, v_parts, down_parts = refs[0:4], refs[4:8], refs[8:10]
-    token_keep, token_send, fed_keep, fed_send = refs[10:14]
-    wq, wk, wv, w_down, sems, down_sems = refs[14:]
+    qk, v_parts, down_parts = refs[0:4], refs[4:8], refs[8:12]
+    token_keep, token_send, fed_keep, fed_send = refs[12:16]
+    wq, wk, wv, w_down, sems, down_sems = refs[16:]
     for copy in narrow_copies(info, tables[0], qk, [(0, wq), (48, wk)], sems.at[0]):
         copy.start()
     for copy in narrow_copies(info, tables[1], v_parts, [(0, wv)], sems.at[1]):
@@ -687,8 +696,8 @@
     return pl.BlockSpec((1,) + dims, lambda p: (p, 0, 0))
 
 
-ORDER_QK, ORDER_V, ORDER_UP, ORDER_DOWN = "zyx", "zxy", "zxy", "zxy"
-BACK_QK, BACK_V, BACK_UP, BACK_DOWN = "xyz", "yxz", "xyz", "yxz"
+ORDER_QK, ORDER_V = "zyx", "zxy"
+BACK_QK, BACK_V, BACK_UP, BACK_DOWN = "xyz", "yxz", "yxz", "xyz"
 
 
 def local(
@@ -741,8 +750,8 @@
         )
         small_rows = jnp.pad(small[None], ((0, 15), (0, 384 - small.size)))
         packed = jnp.concatenate([projections.reshape(192, 384), small_rows])
-        along_z = spread(after(packed, other, theirs), "z")
-        along_z[1] = after(along_z[1], seed, seed_t)
+        along_z = spread(packed, "z")
+        along_z[1] = after(along_z[1], seed, seed_t, other)
         qk_near = jnp.stack(spread(jnp.stack([part[:96] for part in along_z]), "y"))
         v_near = jnp.stack(spread(jnp.stack([part[96:] for part in along_z]), "x"))
         qk_far, v_far = xor_permute(qk_near, "x", 1), xor_permute(v_near, "y", 1)
@@ -750,7 +759,8 @@
         up_z = spread(after(w_up, qk_swap, v_swap), "z")
         qk_parts = [qk_near, qk_far, qk_swap, swap(after(qk_far, *up_z[1:]))]
         v_parts = [v_near, v_far, v_swap, swap(after(v_far, *up_z[1:]))]
-        up_x = spread(after(jnp.stack(up_z), qk_parts[3], v_parts[3]), "x")
+        up_z = after(jnp.stack(up_z), qk_parts[3], v_parts[3])
+        up_x, up_y = xor_permute(up_z, "x", 1), xor_permute(up_z, "y", 1)
         down_z = spread(after(w_down.T, qk_parts[3], v_parts[3]), "z")
     else:
         every = lambda value: lax.all_gather(value, AXES, axis=0)
@@ -769,11 +779,13 @@
             value = value.reshape(8, 2, 2, 96, D)
             return lax.dynamic_slice_in_dim(value, core, 1, axis=2)
 
-        double = lambda value: jnp.concatenate([value, value], axis=2)
-        up_parts = as_gathered(double(wide(w_up)), ORDER_UP)[:2]
-        down_parts = as_gathered(double(wide(w_down.T)), ORDER_DOWN)[:2]
+        def in_parts(whole):
+            whole = whole.reshape((4, 2, 2) + whole.shape[3:])
+            return [whole[:, ky, kx] for ky in range(2) for kx in range(2)]
+
+        up_parts, down_parts = in_parts(wide(w_up)), in_parts(wide(w_down.T))
     table_qk, table_v = piece_table(ORDER_QK), piece_table(ORDER_V)
-    table_up, table_down = piece_table(ORDER_UP, 1), piece_table(ORDER_DOWN, 1)
+    table_wide = wide_table()
 
     tall = shape((SEGL, D))
     row = shape((1, D), F32)
@@ -796,8 +808,8 @@
 
     q_late = q
     if near:
-        q_late = after(q, up_x[1])
-        up_parts = spread(after(jnp.stack(up_x), q), "y")
+        q_late = after(q, up_x, up_y)
+        up_parts = [up_z, up_x, up_y, xor_permute(after(up_x, q), "y", 1)]
         gauss_rows, norm_gain, norm_bias = small_params
     else:
         scales = every(jnp.stack([ln_gain, ln_bias]))
@@ -822,8 +834,9 @@
         vmem=14,
     )
     if near:
-        down_z[1:] = lax.optimization_barrier((attn_t, coef, up_parts[1], *down_z[1:]))[3:]
-        down_x = spread(jnp.stack(down_z), "x")
+        down_z[1:] = lax.optimization_barrier((attn_t, coef, up_parts[3], *down_z[1:]))[3:]
+        down_z = jnp.stack(down_z)
+        down_x, down_y = xor_permute(down_z, "x", 1), xor_permute(down_z, "y", 1)
     whole = lambda *dims: pl.BlockSpec(dims, lambda p: (0,) * len(dims))
     heads_out, residual, normed = run(
         functools.partial(recall_kernel, table_v),
@@ -839,14 +852,14 @@
         vmem=18,
     )
     if near:
-        down_parts = spread(after(jnp.stack(down_x), normed), "y")
+        down_parts = [down_z, down_x, down_y, xor_permute(after(down_x, down_y, normed), "y", 1)]
     normed_other = swap(normed)
     piece_dims = lambda order: tuple(SIZES[letter] for letter in order)
     hidden, slope, *keep_down = run(
-        functools.partial(up_kernel, table_up, BACK_DOWN),
+        functools.partial(up_kernel, table_wide, BACK_DOWN),
         "up",
         [info, normed, normed_other, seed_t] + up_parts,
-        [SCALARS, FULL, FULL, FULL] + [ANY] * 2,
+        [SCALARS, FULL, FULL, FULL] + [ANY] * 4,
         [shape((2, SEGL, HALF))] * 2 + [shape(piece_dims(BACK_DOWN)[1:] + (96, D))] * 2,
         [ANY] * 4,
         [VMEM(WIDE, BF16)] * 2 + [VMEM((2, SEGL, HALF), BF16)] * 2 + [DMA((2,))] * 3,
@@ -856,10 +869,10 @@
     if near:
         down_1 = stage(lambda k: keep_down[k], BACK_DOWN[0])
     *keep_up, own_grad, other_grad = run(
-        functools.partial(down_kernel, (table_down, table_up), BACK_UP),
+        functools.partial(down_kernel, (table_wide, table_wide), BACK_UP),
         "down",
         [info, seed, normed, normed_other, slope] + down_parts + up_parts,
-        [SCALARS] + [FULL] * 3 + [ANY] * 5,
+        [SCALARS] + [FULL] * 3 + [ANY] * 9,
         [shape(piece_dims(BACK_UP)[1:] + (96, D))] * 2 + [shape((SEGL, D), F32), tall],
         [ANY] * 2 + [FULL] * 2,
         [VMEM(WIDE, BF16)] * 3
@@ -956,10 +969,10 @@
         dq_late = dq
 
     token_keep, token_send, fed_keep, fed_send = run(
-        functools.partial(finish_kernel, (table_qk, table_v, table_down)),
+        functools.partial(finish_kernel, (table_qk, table_v, table_wide)),
         "finish",
         [info, dq_late, dk, dv, resid_grad, hidden, residual] + qk_parts + v_parts + down_parts,
-        [SCALARS] + [FULL] * 6 + [ANY] * 10,
+        [SCALARS] + [FULL] * 6 + [ANY] * 12,
         [shape((HALF_SEG, D), F32), shape((HALF_SEG, D))]
         + [shape((2, HALF_SEG, D), F32), shape((2, HALF_SEG, D))],
         [FULL] * 4,
@@ -979,7 +992,9 @@
         qk_2 = stage(combined(*qk_1), BACK_QK[1])
         v_2 = stage(combined(*v_1), BACK_V[1])
         to_qk, to_v = combined(*qk_2), combined(*v_2)
-        joined = final_sum(*stage(lambda k: jnp.concatenate([to_qk(k), to_v(k)]), "z"))
+        last = [jnp.concatenate([to_qk(k), to_v(k)]) for k in range(4)]
+        last[1:] = [value.astype(BF16) for value in last[1:]]
+        joined = final_sum(*stage(lambda k: last[k], "z"))
         own_small = joined[192]
         narrow = joined[:192].reshape(4, 48, 384)
         mine = lax.dynamic_slice_in_dim(narrow, core * 192, 192, axis=2)

time: 287 us -> 269 us (0.937)
  waiting for transfers between devices: 87.9 us -> 67.4 us
  starting transfers between devices: 52.2 us -> 56.8 us
    ppermute x46 -> x48, waiting for transfers between devices: 80.6 us -> 67.4 us  [xor_permute(): return lax.ppermute(value, AXES, pairs)]
    ppermute x1, waiting for transfers between devices: 7.34 us -> 0.01 us  [local(): coef_grad = lax.ppermute(coef_grad, 'tensor', [(2, 0), (3, 1)])]
    ppermute x46 -> x48, starting transfers between devices: 47.5 us -> 52 us  [xor_permute(): return lax.ppermute(value, AXES, pairs)]
    unnamed x81 -> x79, local copies, waits for them, and re-layouts: 7.02 us -> 6.07 us
  transfers between devices with their start and end apart: 48 -> 50, of which waited for: 21 -> 18; matrix products, arithmetic and copies ran while one was open for 6% -> 6% of each run, Pallas kernels for 39% -> 42%
where the time goes in v5:
time: 269 us; the launch traced here: 268 us
  Pallas kernels  112 us (42%)
  waiting for transfers between devices  67.4 us (25%)
  starting transfers between devices  56.8 us (21%)
  local copies, waits for them, and re-layouts  15 us (6%)
  other arithmetic  14.2 us (5%)
  between operations  2.91 us (1%)
    pallas_call x9, Pallas kernels, run(): pl.pallas_call(body, name=name, out_shape=tuple((pltpu.HBM(out.shape, out...  112 us
    ppermute x48, waiting for transfers between devices, xor_permute(): return lax.ppermute(value, AXES, pairs)  67.4 us
    ppermute x48, starting transfers between devices, xor_permute(): return lax.ppermute(value, AXES, pairs)  52 us
    unnamed x79, local copies, waits for them, and re-layouts  6.07 us
  transfers between devices with their start and end apart: 50, of which 18 were waited for; matrix products, arithmetic and copies ran while one was open for 6% of the time, Pallas kernels for 42%

profile of v5, /device:TPU:0, one launch (start us, length us, event | category | flops | bytes accessed | tf_op | source)
XLA Modules:
  0.0 267.9 jit_solution(15806586780042109089)
XLA Ops:
  8.0 4.7 %collective-permute-start.5 = (bf16[208,384]{1,0:T(8,128)(2,1)S(1)}, bf16[208,384]{1,0:T(8,128)(2,1)S(1)}, u32[]{:S(2)}, u32[]{:S(2)}) collective-permute-start(bf16[208,384]{1,0:T(8,128)(2,1)S(1)} %fusion.43), channel_id=1, source_target_pairs={{0,24},{1,25},{2,26},{3,27},{4,28},{5,29},{6,30},{7,31},{8,16},{9,... | collective-permute-start | bytes 479240 | tf_op jit(solution)/shard_map/ppermute | solution.py:45
  13.5 4.3 %collective-permute-done.5 = bf16[208,384]{1,0:T(8,128)(2,1)S(1)} collective-permute-done((bf16[208,384]{1,0:T(8,128)(2,1)S(1)}, bf16[208,384]{1,0:T(8,128)(2,1)S(1)}, u32[]{:S(2)}, u32[]{:S(2)}) %collective-permute-start.5) | collective-permute-done | bytes 159776 | tf_op jit(solution)/shard_map/ppermute | solution.py:45
  17.8 9.1 %collective-permute-done.4 = bf16[208,384]{1,0:T(8,128)(2,1)S(1)} collective-permute-done((bf16[208,384]{1,0:T(8,128)(2,1)S(1)}, bf16[208,384]{1,0:T(8,128)(2,1)S(1)}, u32[]{:S(2)}, u32[]{:S(2)}) %collective-permute-start.4) | collective-permute-done | bytes 159776 | tf_op jit(solution)/shard_map/ppermute | solution.py:45
  34.0 6.4 %collective-permute-done.9 = bf16[4,112,384]{2,1,0:T(8,128)(2,1)S(1)} collective-permute-done((bf16[4,112,384]{2,1,0:T(8,128)(2,1)S(1)}, bf16[4,112,384]{2,1,0:T(8,128)(2,1)S(1)}, u32[]{:S(2)}, u32[]{:S(2)}) %collective-permute-start.9) | collective-permute-done | bytes 344096 | tf_op jit(solution)/shard_map/ppermute | solution.py:45
  44.2 2.5 collective-permute-start.13
  48.7 10.0 %collective-permute-done.15.refs_5_.refs_1_ = bf16[2,4,112,384]{3,2,1,0:T(8,128)(2,1)S(1)} collective-permute-done((bf16[2,4,112,384]{3,2,1,0:T(8,128)(2,1)S(1)}, bf16[2,4,112,384]{3,2,1,0:T(8,128)(2,1)S(1)}, u32[]{:S(2)}, u32[]{:S(2)}) %collective-permute-start.15) | collective-permute-done | bytes 688160 | tf_op jit(solution)/shard_map/ppermute | solution.py:45
  66.1 9.1 %qkv.1 = (bf16[512,768]{1,0:T(8,128)(2,1)}, bf16[512,768]{1,0:T(8,128)(2,1)}, bf16[512,768]{1,0:T(8,128)(2,1)}, bf16[512,768]{1,0:T(8,128)(2,1)}, bf16[256,768]{...) custom-call(s32[6]{0:T(128)S(1)} %stack.130.info, ...), custom_call_target="tpu_custom_call" | custom-call | flops 1200000000 | bytes 1000000 | tf_op jit(solution)/shard_map/qkv/pallas_call | solution.py:673
  79.1 3.5 %collective-permute-start.19 = (bf16[256,768]{1,0:T(8,128)(2,1)}, bf16[256,768]{1,0:T(8,128)(2,1)S(1)}, u32[]{:S(2)}, u32[]{:S(2)}) collective-permute-start(bf16[256,768]{1,0:T(8,128)(2,1)} %get-tuple-element.83), channel_id=1, source_target_pairs={{0,2},{1,3},{4,6},{5,7},{8,10},{9,11},{12,14},{13,15},{16,18},{17,... | collective-permute-start | bytes 1179656 | tf_op jit(solution)/shard_map/ppermute | solution.py:807
  87.1 13.1 %attend.1 = (bf16[12,512,512]{2,1,0:T(8,128)(2,1)}, f32[768,512]{1,0:T(8,128)}, bf16[12,256,512]{2,1,0:T(8,128)(2,1)}) custom-call(s32[6]{0:T(128)S(1)} %stack.130.info, bf16[512,768]{1,0:T(8,128)(2,1)} %get-tuple-element.77.q, bf16[512,768]{1,0:T(8,128)(2,1)} %get-tuple-element.78.k, bf16[512,768]{1,0:T(8,128)(2,1)} %get-tuple-element.79.v, ...), custom_call_target="tpu_custom_call" | custom-call | flops 2400000000 | bytes 1000000 | tf_op jit(solution)/shard_map/attend/pallas_call | solution.py:673
  101.0 8.9 %recall.1 = (bf16[512,768]{1,0:T(8,128)(2,1)}, f32[512,768]{1,0:T(8,128)}, bf16[512,768]{1,0:T(8,128)(2,1)}) custom-call(s32[6]{0:T(128)S(1)} %stack.130.info, bf16[12,256,512]{2,1,0:T(8,128)(2,1)} %get-tuple-element.82.dens_t, bf16[256,768]{1,0:T(8,128)(2,1)} %copy-done.14, f32[768,512]{1,0:T(8,128)} %get-tuple-element.84.local_t, ...), custom_call_target="tpu_custom_call" | custom-call | flops 1400000000 | bytes 1000000 | tf_op jit(solution)/shard_map/recall/pallas_call | solution.py:673
  110.0 3.9 %collective-permute-done.26.refs_2_.refs_10_ = bf16[4,96,768]{2,1,0:T(8,128)(2,1)S(1)} collective-permute-done((bf16[4,96,768]{2,1,0:T(8,128)(2,1)S(1)}, bf16[4,96,768]{2,1,0:T(8,128)(2,1)S(1)}, u32[]{:S(2)}, u32[]{:S(2)}) %collective-permute-start.26) | collective-permute-done | bytes 589856 | tf_op jit(solution)/shard_map/ppermute | solution.py:45
  116.2 14.1 %up.1 = (bf16[2,512,1536]{2,1,0:T(8,128)(2,1)}, bf16[2,512,1536]{2,1,0:T(8,128)(2,1)}, bf16[2,4,96,768]{3,2,1,0:T(8,128)(2,1)}, bf16[2,4,96,768]{3,2,1,0:T(8,128)(2,1)}) custom-call(s32[6]{0:T(128)S(1)} %stack.130.info, bf16[512,768]{1,0:T(8,128)(2,1)} %get-tuple-element.88.own, bf16[512,768]{1,0:T(8,128)(2,1)} %copy-done.35, bf16[768,1024]{1,0:T(8,128)(2,1)} %bitcast.251, ...), custom_call_target="tpu_custom_call" | custom-call | flops 2400000000 | bytes 1000000 | tf_op jit(solution)/shard_map/up/pallas_call | solution.py:673
  131.5 18.8 %down.1 = (bf16[2,4,96,768]{3,2,1,0:T(8,128)(2,1)}, bf16[2,4,96,768]{3,2,1,0:T(8,128)(2,1)}, f32[512,768]{1,0:T(8,128)}, bf16[512,768]{1,0:T(8,128)(2,1)}) custom-call(s32[6]{0:T(128)S(1)} %stack.130.info, bf16[2,512,768]{2,1,0:T(8,128)(2,1)} %copy-done.8, bf16[512,768]{1,0:T(8,128)(2,1)} %get-tuple-element.88.own, bf16[512,768]{1,0:T(8,128)(2,1)} %copy-done.35, ...), custom_call_target="tpu_custom_call" | custom-call | flops 3000000000 | bytes 1000000 | tf_op jit(solution)/shard_map/down/pallas_call | solution.py:673
  152.0 4.0 %collective-permute-done.28 = bf16[2,4,96,768]{3,2,1,0:T(8,128)(2,1)S(1)} collective-permute-done((bf16[2,4,96,768]{3,2,1,0:T(8,128)(2,1)}, bf16[2,4,96,768]{3,2,1,0:T(8,128)(2,1)S(1)}, u32[]{:S(2)}, u32[]{:S(2)}) %collective-permute-start.28) | collective-permute-done | bytes 1179680 | tf_op jit(solution)/shard_map/ppermute | solution.py:45
  156.9 11.3 %mix_back.1 = (f32[512,768]{1,0:T(8,128)}, bf16[512,768]{1,0:T(8,128)(2,1)}, bf16[256,768]{1,0:T(8,128)(2,1)}, f32[1,768]{1,0:T(1,128)}, f32[1,768]{1,0:T(1,128)...) custom-call(s32[6]{0:T(128)S(1)} %stack.130.info, f32[512,768]{1,0:T(8,128)} %get-tuple-element.98.own, ...), custom_call_target="tpu_custom_call" | custom-call | flops 1200000000 | bytes 1000000 | tf_op jit(solution)/shard_map/mix_back/pallas_call | solution.py:673
  169.6 13.4 %attend_back.1 = (bf16[512,768]{1,0:T(8,128)(2,1)}, bf16[512,768]{1,0:T(8,128)(2,1)}, f32[512,768]{1,0:T(8,128)}, f32[2,768]{1,0:T(2,128)}) custom-call(bf16[12,512,512]{2,1,0:T(8,128)(2,1)} %get-tuple-element.81.attn_t, bf16[512,768]{1,0:T(8,128)(2,1)} %get-tuple-element.77.q, bf16[512,768]{1,0:T(8,128)(2,1)} %get-tuple-element.78.k, ...), custom_call_target="tpu_custom_call" | custom-call | flops 3200000000 | bytes 1000000 | tf_op jit(solution)/shard_map/attend_back/pallas_call | solution.py:673
  183.8 2.7 collective-permute-start.34
  188.3 9.6 %qkv_grad.1 = (bf16[2,2,4,96,384]{4,3,2,1,0:T(8,128)(2,1)}, bf16[2,2,4,96,384]{4,3,2,1,0:T(8,128)(2,1)}, bf16[2,2,4,64,384]{4,3,2,1,0:T(8,128)(2,1)}, bf16[2,2,4...) custom-call(s32[6]{0:T(128)S(1)} %stack.130.info, bf16[512,768]{1,0:T(8,128)(2,1)} %get-tuple-element.85.x, ...), custom_call_target="tpu_custom_call" | custom-call | flops 1200000000 | bytes 1000000 | tf_op jit(solution)/shard_map/qkv_grad/pallas_call | solution.py:673
  209.1 2.9 %collective-permute-start.48 = (bf16[192,768]{1,0:T(8,128)(2,1)}, bf16[192,768]{1,0:T(8,128)(2,1)}, u32[]{:S(2)}, u32[]{:S(2)}) collective-permute-start(bf16[192,768]{1,0:T(8,128)(2,1)} %pad_maximum_fusion.10), channel_id=1, source_target_pairs={{0,16},{1,17},{2,18},{3,19},{4,20},{5,21},{6,22},{7,23},{8,24},{9,... | collective-permute-start | bytes 884744 | tf_op jit(solution)/shard_map/ppermute | solution.py:45
  216.0 13.1 %finish.1 = (f32[256,768]{1,0:T(8,128)}, bf16[256,768]{1,0:T(8,128)(2,1)}, f32[2,256,768]{2,1,0:T(8,128)}, bf16[2,256,768]{2,1,0:T(8,128)(2,1)}) custom-call(s32[6]{0:T(128)S(1)} %stack.130.info, bf16[512,768]{1,0:T(8,128)(2,1)} %get-tuple-element.125.dq, bf16[512,768]{1,0:T(8,128)(2,1)} %get-tuple-element.105.dk, bf16[512,768]{1,0:T(8,128)(2,1)} %get-tuple-element.126.dv, ...), custom_call_target="tpu_custom_call" | custom-call | flops 2800000000 | bytes 1000000 | tf_op jit(solution)/shard_map/finish/pallas_call | solution.py:673
  229.2 3.8 %collective-permute-done.48 = bf16[192,768]{1,0:T(8,128)(2,1)} collective-permute-done((bf16[192,768]{1,0:T(8,128)(2,1)}, bf16[192,768]{1,0:T(8,128)(2,1)}, u32[]{:S(2)}, u32[]{:S(2)}) %collective-permute-start.48) | collective-permute-done | bytes 294944 | tf_op jit(solution)/shard_map/ppermute | solution.py:45
  239.2 6.5 %collective-permute-done.42 = bf16[4,112,384]{2,1,0:T(8,128)(2,1)S(1)} collective-permute-done((bf16[4,112,384]{2,1,0:T(8,128)(2,1)S(1)}, bf16[4,112,384]{2,1,0:T(8,128)(2,1)S(1)}, u32[]{:S(2)}, u32[]{:S(2)}) %collective-permute-start.42) | collective-permute-done | bytes 344096 | tf_op jit(solution)/shard_map/ppermute | solution.py:45
  246.0 5.8 %collective-permute-start.44 = (bf16[208,384]{1,0:T(8,128)(2,1)S(1)}, bf16[208,384]{1,0:T(8,128)(2,1)S(1)}, u32[]{:S(2)}, u32[]{:S(2)}) collective-permute-start(bf16[208,384]{1,0:T(8,128)(2,1)S(1)} %pad_maximum_fusion.14), channel_id=1, source_target_pairs={{0,16},{1,17},{2,18},{3,19},{4,20},{5,21},{6,22},{7,23},{8,24},{9,... | collective-permute-start | bytes 479240 | tf_op jit(solution)/shard_map/ppermute | solution.py:45
  254.9 7.7 %collective-permute-done.44 = bf16[208,384]{1,0:T(8,128)(2,1)S(1)} collective-permute-done((bf16[208,384]{1,0:T(8,128)(2,1)S(1)}, bf16[208,384]{1,0:T(8,128)(2,1)S(1)}, u32[]{:S(2)}, u32[]{:S(2)}) %collective-permute-start.44) | collective-permute-done | bytes 159776 | tf_op jit(solution)/shard_map/ppermute | solution.py:45
  (233 shorter events, 75.8 us)
Async XLA Ops:
  5.1 25.5 %collective-permute-start = (bf16[256,768]{1,0:T(8,128)(2,1)S(1)}, bf16[256,768]{1,0:T(8,128)(2,1)S(1)}, u32[]{:S(2)}, u32[]{:S(2)}) collective-permute-start(bf16[256,768]{1,0:T(8,128)(2,1)S(1)} %get-tuple-element.187), channel_id=1, source_target_pairs={{0,1},{1,0},{2,3},{3,2},{4,5},{5,4},{6,7},{7,6},{8,9},{9,8},{10,11... | collective-permute-start | bytes 1179656 | tf_op jit(solution)/shard_map/ppermute | solution.py:45
  5.2 21.8 %collective-permute-start.3 = (bf16[2,256,768]{2,1,0:T(8,128)(2,1)S(1)}, bf16[2,256,768]{2,1,0:T(8,128)(2,1)S(1)}, u32[]{:S(2)}, u32[]{:S(2)}) collective-permute-start(bf16[2,256,768]{2,1,0:T(8,128)(2,1)S(1)} %copy-done.21), channel_id=1, source_target_pairs={{0,1},{1,0},{2,3},{3,2},{4,5},{5,4},{6,7},{7,6},{8,9},{9,8},{10,11... | collective-permute-start | bytes 2359304 | tf_op jit(solution)/shard_map/ppermute | solution.py:45
  12.8 17.8 %collective-permute-start.2 = (bf16[208,384]{1,0:T(8,128)(2,1)S(1)}, bf16[208,384]{1,0:T(8,128)(2,1)S(1)}, u32[]{:S(2)}, u32[]{:S(2)}) collective-permute-start(bf16[208,384]{1,0:T(8,128)(2,1)S(1)} %fusion.43), channel_id=1, source_target_pairs={{0,8},{1,9},{2,10},{3,11},{4,12},{5,13},{6,14},{7,15},{8,0},{9,1},... | collective-permute-start | bytes 479240 | tf_op jit(solution)/shard_map/ppermute | solution.py:45
  41.2 17.5 %collective-permute-start.15 = (bf16[2,4,112,384]{3,2,1,0:T(8,128)(2,1)S(1)}, bf16[2,4,112,384]{3,2,1,0:T(8,128)(2,1)S(1)}, u32[]{:S(2)}, u32[]{:S(2)}) collective-permute-start(bf16[2,4,112,384]{3,2,1,0:T(8,128)(2,1)S(1)} %pad_maximum_fusion.2.refs_4_.refs_0_), channel_id=1, source_target_pairs={{0,4},{1,5},{2,6},{3,7},{4,0},{5,1},{6,2},{7,3},{8,12},{9,13},{10,... | collective-permute-start | bytes 2064392 | tf_op jit(solution)/shard_map/ppermute | solution.py:45
  42.7 16.1 %collective-permute-start.7 = (bf16[2,4,96,384]{3,2,1,0:T(8,128)(2,1)S(1)}, bf16[2,4,96,384]{3,2,1,0:T(8,128)(2,1)S(1)}, u32[]{:S(2)}, u32[]{:S(2)}) collective-permute-start(bf16[2,4,96,384]{3,2,1,0:T(8,128)(2,1)S(1)} %pad_maximum_fusion.4.refs_0_), channel_id=1, source_target_pairs={{0,2},{1,3},{2,0},{3,1},{4,6},{5,7},{6,4},{7,5},{8,10},{9,11},{10,... | collective-permute-start | bytes 1769480 | tf_op jit(solution)/shard_map/ppermute | solution.py:45
  61.8 15.7 %collective-permute-start.17 = (bf16[4,96,768]{2,1,0:T(8,128)(2,1)}, bf16[4,96,768]{2,1,0:T(8,128)(2,1)}, u32[]{:S(2)}, u32[]{:S(2)}) collective-permute-start(bf16[4,96,768]{2,1,0:T(8,128)(2,1)} %pad_maximum_fusion.5.refs_0_.refs_4_), channel_id=1, source_target_pairs={{0,2},{1,3},{2,0},{3,1},{4,6},{5,7},{6,4},{7,5},{8,10},{9,11},{10,... | collective-permute-start | bytes 1769480 | tf_op jit(solution)/shard_map/ppermute | solution.py:45
  63.3 21.9 %collective-permute-start.18 = (bf16[4,96,768]{2,1,0:T(8,128)(2,1)}, bf16[4,96,768]{2,1,0:T(8,128)(2,1)}, u32[]{:S(2)}, u32[]{:S(2)}) collective-permute-start(bf16[4,96,768]{2,1,0:T(8,128)(2,1)} %pad_maximum_fusion.5.refs_0_.refs_4_), channel_id=1, source_target_pairs={{0,4},{1,5},{2,6},{3,7},{4,0},{5,1},{6,2},{7,3},{8,12},{9,13},{10,... | collective-permute-start | bytes 1769480 | tf_op jit(solution)/shard_map/ppermute | solution.py:45
  77.5 22.7 %collective-permute-start.21 = (bf16[4,96,768]{2,1,0:T(8,128)(2,1)}, bf16[4,96,768]{2,1,0:T(8,128)(2,1)S(1)}, u32[]{:S(2)}, u32[]{:S(2)}) collective-permute-start(bf16[4,96,768]{2,1,0:T(8,128)(2,1)} %collective-permute-done.17.refs_1_.refs_5_), channel_id=1, source_target_pairs={{0,4},{1,5},{2,6},{3,7},{4,0},{5,1},{6,2},{7,3},{8,12},{9,13},{10,... | collective-permute-start | bytes 1769480 | tf_op jit(solution)/shard_map/ppermute | solution.py:45
  79.1 21.2 %collective-permute-start.19 = (bf16[256,768]{1,0:T(8,128)(2,1)}, bf16[256,768]{1,0:T(8,128)(2,1)S(1)}, u32[]{:S(2)}, u32[]{:S(2)}) collective-permute-start(bf16[256,768]{1,0:T(8,128)(2,1)} %get-tuple-element.83), channel_id=1, source_target_pairs={{0,2},{1,3},{4,6},{5,7},{8,10},{9,11},{12,14},{13,15},{16,18},{17,... | collective-permute-start | bytes 1179656 | tf_op jit(solution)/shard_map/ppermute | solution.py:807
  82.6 17.6 %collective-permute-start.24 = (bf16[96,768]{1,0:T(8,128)(2,1)S(1)}, bf16[96,768]{1,0:T(8,128)(2,1)S(1)}, u32[]{:S(2)}, u32[]{:S(2)}) collective-permute-start(bf16[96,768]{1,0:T(8,128)(2,1)S(1)} %bitcast.259), channel_id=1, source_target_pairs={{0,24},{1,25},{2,26},{3,27},{4,28},{5,29},{6,30},{7,31},{8,16},{9,... | collective-permute-start | bytes 442376 | tf_op jit(solution)/shard_map/ppermute | solution.py:45
  85.1 15.1 %collective-permute-start.23 = (bf16[96,768]{1,0:T(8,128)(2,1)S(1)}, bf16[96,768]{1,0:T(8,128)(2,1)S(1)}, u32[]{:S(2)}, u32[]{:S(2)}) collective-permute-start(bf16[96,768]{1,0:T(8,128)(2,1)S(1)} %bitcast.260), channel_id=1, source_target_pairs={{0,16},{1,17},{2,18},{3,19},{4,20},{5,21},{6,22},{7,23},{8,24},{9,... | collective-permute-start | bytes 442376 | tf_op jit(solution)/shard_map/ppermute | solution.py:45
  85.1 15.1 %collective-permute-start.22 = (bf16[96,768]{1,0:T(8,128)(2,1)S(1)}, bf16[96,768]{1,0:T(8,128)(2,1)S(1)}, u32[]{:S(2)}, u32[]{:S(2)}) collective-permute-start(bf16[96,768]{1,0:T(8,128)(2,1)S(1)} %bitcast.261), channel_id=1, source_target_pairs={{0,8},{1,9},{2,10},{3,11},{4,12},{5,13},{6,14},{7,15},{8,0},{9,1},... | collective-permute-start | bytes 442376 | tf_op jit(solution)/shard_map/ppermute | solution.py:45
  113.8 16.8 %collective-permute-start.27 = (bf16[4,96,768]{2,1,0:T(8,128)(2,1)S(1)}, bf16[4,96,768]{2,1,0:T(8,128)(2,1)S(1)}, u32[]{:S(2)}, u32[]{:S(2)}) collective-permute-start(bf16[4,96,768]{2,1,0:T(8,128)(2,1)S(1)} %collective-permute-done.25.refs_1_.refs_9_), channel_id=1, source_target_pairs={{0,4},{1,5},{2,6},{3,7},{4,0},{5,1},{6,2},{7,3},{8,12},{9,13},{10,... | collective-permute-start | bytes 1769480 | tf_op jit(solution)/shard_map/ppermute | solution.py:45
  130.3 25.7 %collective-permute-start.28 = (bf16[2,4,96,768]{3,2,1,0:T(8,128)(2,1)}, bf16[2,4,96,768]{3,2,1,0:T(8,128)(2,1)S(1)}, u32[]{:S(2)}, u32[]{:S(2)}) collective-permute-start(bf16[2,4,96,768]{3,2,1,0:T(8,128)(2,1)} %get-tuple-element.97), channel_id=1, source_target_pairs={{0,2},{1,3},{2,0},{3,1},{4,6},{5,7},{6,4},{7,5},{8,10},{9,11},{10,... | collective-permute-start | bytes 3538952 | tf_op jit(solution)/shard_map/ppermute | solution.py:45
  150.4 32.6 %collective-permute-start.30 = (bf16[2,4,96,768]{3,2,1,0:T(8,128)(2,1)}, bf16[2,4,96,768]{3,2,1,0:T(8,128)(2,1)S(1)}, u32[]{:S(2)}, u32[]{:S(2)}) collective-permute-start(bf16[2,4,96,768]{3,2,1,0:T(8,128)(2,1)} %get-tuple-element.104), channel_id=1, source_target_pairs={{0,4},{1,5},{2,6},{3,7},{4,0},{5,1},{6,2},{7,3},{8,12},{9,13},{10,... | collective-permute-start | bytes 3538952 | tf_op jit(solution)/shard_map/ppermute | solution.py:45
  168.2 14.9 %collective-permute-start.32 = (bf16[2,2,4,48,384]{4,3,2,1,0:T(8,128)(2,1)}, bf16[2,2,4,48,384]{4,3,2,1,0:T(8,128)(2,1)S(1)}, u32[]{:S(2)}, u32[]{:S(2)}) collective-permute-start(bf16[2,2,4,48,384]{4,3,2,1,0:T(8,128)(2,1)} %get-tuple-element.107), channel_id=1, source_target_pairs={{0,1},{1,0},{2,3},{3,2},{4,5},{5,4},{6,7},{7,6},{8,9},{9,8},{10,11... | collective-permute-start | bytes 1769480 | tf_op jit(solution)/shard_map/ppermute | solution.py:45
  183.8 16.4 %collective-permute-start.34 = (bf16[4,96,768]{2,1,0:T(8,128)(2,1)S(1)}, bf16[4,96,768]{2,1,0:T(8,128)(2,1)S(1)}, u32[]{:S(2)}, u32[]{:S(2)}) collective-permute-start(bf16[4,96,768]{2,1,0:T(8,128)(2,1)S(1)} %get-tuple-element.160), channel_id=1, source_target_pairs={{0,2},{1,3},{2,0},{3,1},{4,6},{5,7},{6,4},{7,5},{8,10},{9,11},{10,... | collective-permute-start | bytes 1769480 | tf_op jit(solution)/shard_map/ppermute | solution.py:45
  186.8 15.2 %collective-permute-start.33 = (bf16[4,96,768]{2,1,0:T(8,128)(2,1)S(1)}, bf16[4,96,768]{2,1,0:T(8,128)(2,1)S(1)}, u32[]{:S(2)}, u32[]{:S(2)}) collective-permute-start(bf16[4,96,768]{2,1,0:T(8,128)(2,1)S(1)} %get-tuple-element.158), channel_id=1, source_target_pairs={{0,4},{1,5},{2,6},{3,7},{4,0},{5,1},{6,2},{7,3},{8,12},{9,13},{10,... | collective-permute-start | bytes 1769480 | tf_op jit(solution)/shard_map/ppermute | solution.py:45
  208.3 20.8 %collective-permute-start.47 = (bf16[192,768]{1,0:T(8,128)(2,1)}, bf16[192,768]{1,0:T(8,128)(2,1)}, u32[]{:S(2)}, u32[]{:S(2)}) collective-permute-start(bf16[192,768]{1,0:T(8,128)(2,1)} %pad_maximum_fusion.9), channel_id=1, source_target_pairs={{0,8},{1,9},{2,10},{3,11},{4,12},{5,13},{6,14},{7,15},{8,0},{9,1},... | collective-permute-start | bytes 884744 | tf_op jit(solution)/shard_map/ppermute | solution.py:45
  209.1 23.8 %collective-permute-start.48 = (bf16[192,768]{1,0:T(8,128)(2,1)}, bf16[192,768]{1,0:T(8,128)(2,1)}, u32[]{:S(2)}, u32[]{:S(2)}) collective-permute-start(bf16[192,768]{1,0:T(8,128)(2,1)} %pad_maximum_fusion.10), channel_id=1, source_target_pairs={{0,16},{1,17},{2,18},{3,19},{4,20},{5,21},{6,22},{7,23},{8,24},{9,... | collective-permute-start | bytes 884744 | tf_op jit(solution)/shard_map/ppermute | solution.py:45
  212.1 20.8 %collective-permute-start.49 = (bf16[192,768]{1,0:T(8,128)(2,1)S(1)}, bf16[192,768]{1,0:T(8,128)(2,1)}, u32[]{:S(2)}, u32[]{:S(2)}) collective-permute-start(bf16[192,768]{1,0:T(8,128)(2,1)S(1)} %pad_maximum_fusion.11), channel_id=1, source_target_pairs={{0,24},{1,25},{2,26},{3,27},{4,28},{5,29},{6,30},{7,31},{8,16},{9,... | collective-permute-start | bytes 884744 | tf_op jit(solution)/shard_map/ppermute | solution.py:45
  213.5 21.6 %collective-permute-start.41 = (bf16[2,4,112,384]{3,2,1,0:T(8,128)(2,1)}, bf16[2,4,112,384]{3,2,1,0:T(8,128)(2,1)S(1)}, u32[]{:S(2)}, u32[]{:S(2)}) collective-permute-start(bf16[2,4,112,384]{3,2,1,0:T(8,128)(2,1)} %pad_maximum_fusion.3), channel_id=1, source_target_pairs={{0,4},{1,5},{2,6},{3,7},{4,0},{5,1},{6,2},{7,3},{8,12},{9,13},{10,... | collective-permute-start | bytes 2064392 | tf_op jit(solution)/shard_map/ppermute | solution.py:45
  215.0 21.3 %collective-permute-start.39 = (bf16[2,4,96,384]{3,2,1,0:T(8,128)(2,1)}, bf16[2,4,96,384]{3,2,1,0:T(8,128)(2,1)S(1)}, u32[]{:S(2)}, u32[]{:S(2)}) collective-permute-start(bf16[2,4,96,384]{3,2,1,0:T(8,128)(2,1)} %get-tuple-element.156), channel_id=1, source_target_pairs={{0,2},{1,3},{2,0},{3,1},{4,6},{5,7},{6,4},{7,5},{8,10},{9,11},{10,... | collective-permute-start | bytes 1769480 | tf_op jit(solution)/shard_map/ppermute | solution.py:45
  246.0 16.6 %collective-permute-start.44 = (bf16[208,384]{1,0:T(8,128)(2,1)S(1)}, bf16[208,384]{1,0:T(8,128)(2,1)S(1)}, u32[]{:S(2)}, u32[]{:S(2)}) collective-permute-start(bf16[208,384]{1,0:T(8,128)(2,1)S(1)} %pad_maximum_fusion.14), channel_id=1, source_target_pairs={{0,16},{1,17},{2,18},{3,19},{4,20},{5,21},{6,22},{7,23},{8,24},{9,... | collective-permute-start | bytes 479240 | tf_op jit(solution)/shard_map/ppermute | solution.py:45
  (63 other events, 586.2 us)

commit v6 on v5

--- a/solution.py
+++ b/solution.py
@@ -422,7 +422,8 @@
     down_parts, up_parts = refs[0:4], refs[4:8]
     keep = refs[8:10]
     own_grad, other_grad = refs[10:12]
-    w_down, w_up, grad, slope, total, normed_t, down_sems, up_sems, out_sems, side_sems = refs[12:]
+    w_down, w_up, grad, slope, hidden_grad, normed_t = refs[12:18]
+    down_sems, up_sems, out_sems, side_sems = refs[18:]
     for copy in wide_copies(info, tables[0], down_parts, w_down, down_sems):
         copy.start()
     for copy in wide_copies(info, tables[1], up_parts, w_up, up_sems):
@@ -431,7 +432,6 @@
         at = pl.ds(j * D, D)
         pltpu.make_async_copy(slope_in.at[:, :, at], slope.at[:, :, at], side_sems.at[j]).start()
     outs = list(wide_out(info, order, keep, grad, out_sems))
-    total[...] = jnp.zeros_like(total)
     normed_t[:, :SEGL] = flip(own[...]).astype(BF16)
     normed_t[:, SEGL:] = flip(other[...]).astype(BF16)
     for j in range(2):
@@ -447,14 +447,19 @@
                 back = dot(seed[half], w_down[:, at]).astype(BF16).astype(F32)
                 back = (back * slope[half, :, at].astype(F32)).astype(BF16)
                 sums.append(dot(normed_t[:, half * SEGL : (half + 1) * SEGL], back))
-                total[half] += dot(back, w_up[:, at], 1, 1)
+                hidden_grad[half, :, at] = back
             grad[:, at] = (sums[0] + sums[1]).astype(BF16)
 
         for owner, copy in outs:
             if owner == j:
                 copy.start()
-    own_grad[...] = total[0]
-    other_grad[...] = total[1].astype(BF16)
+
+    @pl.loop(0, 3)
+    def _(chunk):
+        at = pl.ds(aligned(chunk, 256), 256)
+        own_grad[:, at] = dot(hidden_grad[0], w_up[at, :], 1, 1)
+        other_grad[:, at] = dot(hidden_grad[1], w_up[at, :], 1, 1).astype(BF16)
+
     wait_out(grad, out_sems)
 
 
@@ -477,7 +482,7 @@
         back = back - jnp.mean(back, axis=-1, keepdims=True) - unit * jnp.mean(
             back * unit, axis=-1, keepdims=True
         )
-        back = seed[...].astype(F32) + scale * back
+        back = seed[0].astype(F32) + scale * back
         resid_grad[...] = back
         mix[...] = back.astype(BF16)
         mix_t[...] = flip(mix[...]).astype(BF16)
@@ -650,6 +655,8 @@
 
 FULL = pl.BlockSpec()
 ANY = pl.BlockSpec(memory_space=pl.ANY)
+FREE = pl.BlockSpec((SEGL, D), lambda: (0, 0))
+FREE_ROWS = pl.BlockSpec((SEGL, D), lambda p: (0, 0))
 SCALARS = pl.BlockSpec(memory_space=SMEM)
 MATRIX = (D, D)
 HALF = FF // 2
@@ -666,7 +673,7 @@
     kwargs = {} if grid is None else {"grid": grid}
     args = [
         value
-        if spec is SCALARS
+        if any(spec is free for free in (SCALARS, FREE, FREE_ROWS))
         else pltpu.with_memory_space_constraint(value, pltpu.HBM)
         for value, spec in zip(args, in_specs)
     ]
@@ -750,8 +757,8 @@
         )
         small_rows = jnp.pad(small[None], ((0, 15), (0, 384 - small.size)))
         packed = jnp.concatenate([projections.reshape(192, 384), small_rows])
-        along_z = spread(packed, "z")
-        along_z[1] = after(along_z[1], seed, seed_t, other)
+        along_z = spread(after(packed, other, theirs), "z")
+        along_z[1] = after(along_z[1], seed, seed_t, info)
         qk_near = jnp.stack(spread(jnp.stack([part[:96] for part in along_z]), "y"))
         v_near = jnp.stack(spread(jnp.stack([part[96:] for part in along_z]), "x"))
         qk_far, v_far = xor_permute(qk_near, "x", 1), xor_permute(v_near, "y", 1)
@@ -859,7 +866,7 @@
         functools.partial(up_kernel, table_wide, BACK_DOWN),
         "up",
         [info, normed, normed_other, seed_t] + up_parts,
-        [SCALARS, FULL, FULL, FULL] + [ANY] * 4,
+        [SCALARS, FULL, FREE, FULL] + [ANY] * 4,
         [shape((2, SEGL, HALF))] * 2 + [shape(piece_dims(BACK_DOWN)[1:] + (96, D))] * 2,
         [ANY] * 4,
         [VMEM(WIDE, BF16)] * 2 + [VMEM((2, SEGL, HALF), BF16)] * 2 + [DMA((2,))] * 3,
@@ -872,27 +879,27 @@
         functools.partial(down_kernel, (table_wide, table_wide), BACK_UP),
         "down",
         [info, seed, normed, normed_other, slope] + down_parts + up_parts,
-        [SCALARS] + [FULL] * 3 + [ANY] * 9,
+        [SCALARS] + [FULL] * 2 + [FREE] + [ANY] * 9,
         [shape(piece_dims(BACK_UP)[1:] + (96, D))] * 2 + [shape((SEGL, D), F32), tall],
         [ANY] * 2 + [FULL] * 2,
         [VMEM(WIDE, BF16)] * 3
-        + [VMEM((2, SEGL, HALF), BF16), VMEM((2, SEGL, D), F32), VMEM((D, 2 * SEGL), BF16)]
+        + [VMEM((2, SEGL, HALF), BF16)] * 2
+        + [VMEM((D, 2 * SEGL), BF16)]
         + [DMA((2,))] * 4,
         cost=15.0,
         vmem=30,
     )
     if near:
         up_1 = stage(lambda k: keep_up[k], BACK_UP[0])
-        own_grad = after(own_grad, *down_1[1])
     other_grad = swap(other_grad)
     narrow_grad = [shape(piece_dims(BACK_V) + (48, 384))] * 2
     resid_grad, head_grad, coef_grad, gain_part, bias_part, keep_out, send_out = run(
         functools.partial(mix_back_kernel, table_v, BACK_V),
         "mix_back",
-        [info, own_grad, other_grad, seed[0], residual, norm_gain, heads_out, dens_t] + v_parts,
+        [info, own_grad, other_grad, seed, residual, norm_gain, heads_out, dens_t] + v_parts,
         [SCALARS]
-        + [whole(SEGL, D)] * 4
-        + [whole(1, D), whole(SEGL, D), PAIR_DENS]
+        + [whole(SEGL, D), FREE_ROWS, pl.BlockSpec((1, SEGL, D), lambda p: (0, 0, 0))]
+        + [whole(SEGL, D), whole(1, D), whole(SEGL, D), PAIR_DENS]
         + [ANY] * 4,
         [shape((SEGL, D), F32), tall, shape((NB, D)), row, row] + narrow_grad,
         [whole(SEGL, D), whole(SEGL, D), PAIR_COEF, whole(1, D), whole(1, D)] + [ANY] * 2,
@@ -903,7 +910,7 @@
         cost=6.0,
         vmem=26,
     )
-    coef_grad = lax.ppermute(coef_grad, "tensor", [(2, 0), (3, 1)])
+    coef_grad = lax.ppermute(coef_grad if not near else after(coef_grad, *down_1[1]), "tensor", [(2, 0), (3, 1)])
     if near:
         got_out = swap(send_out)
     dq, dk, dv, gauss_grad = run(

time: 269 us -> 257 us (0.955)
  Pallas kernels: 112 us -> 108 us
  starting transfers between devices: 56.8 us -> 53.5 us
    pallas_call x9, Pallas kernels: 112 us -> 108 us  [run(): pl.pallas_call(body, name=name, out_shape=tuple((pltpu.HBM(out.shape, out...]
    ppermute x48, starting transfers between devices: 52 us -> 48.5 us  [xor_permute(): return lax.ppermute(value, AXES, pairs)]
    unnamed x79 -> x77, local copies, waits for them, and re-layouts: 6.07 us -> 3.75 us
where the time goes in v6:
time: 257 us; the launch traced here: 256 us
  Pallas kernels  108 us (42%)
  waiting for transfers between devices  66.9 us (26%)
  starting transfers between devices  53.5 us (21%)
  local copies, waits for them, and re-layouts  12.8 us (5%)
  other arithmetic  12.3 us (5%)
  between operations  2.91 us (1%)
    pallas_call x9, Pallas kernels, run(): pl.pallas_call(body, name=name, out_shape=tuple((pltpu.HBM(out.shape, out...  108 us
    ppermute x48, waiting for transfers between devices, xor_permute(): return lax.ppermute(value, AXES, pairs)  66.9 us
    ppermute x48, starting transfers between devices, xor_permute(): return lax.ppermute(value, AXES, pairs)  48.5 us
  transfers between devices with their start and end apart: 50, of which 18 were waited for; matrix products, arithmetic and copies ran while one was open for 6% of the time, Pallas kernels for 42%

profile of v6, /device:TPU:0, one launch (start us, length us, event | category | flops | bytes accessed | tf_op | source)
XLA Modules:
  0.0 256.3 jit_solution(13261744626825188012)
XLA Ops:
  9.3 4.7 %collective-permute-start.5 = (bf16[208,384]{1,0:T(8,128)(2,1)S(1)}, bf16[208,384]{1,0:T(8,128)(2,1)S(1)}, u32[]{:S(2)}, u32[]{:S(2)}) collective-permute-start(bf16[208,384]{1,0:T(8,128)(2,1)S(1)} %fusion.43), channel_id=1, source_target_pairs={{0,24},{1,25},{2,26},{3,27},{4,28},{5,29},{6,30},{7,31},{8,16},{9,... | collective-permute-start | bytes 479240 | tf_op jit(solution)/shard_map/ppermute | solution.py:45
  17.4 7.5 %collective-permute-done.3 = bf16[208,384]{1,0:T(8,128)(2,1)S(1)} collective-permute-done((bf16[208,384]{1,0:T(8,128)(2,1)S(1)}, bf16[208,384]{1,0:T(8,128)(2,1)S(1)}, u32[]{:S(2)}, u32[]{:S(2)}) %collective-permute-start.3) | collective-permute-done | bytes 159776 | tf_op jit(solution)/shard_map/ppermute | solution.py:45
  25.0 3.2 %collective-permute-done.4 = bf16[208,384]{1,0:T(8,128)(2,1)S(1)} collective-permute-done((bf16[208,384]{1,0:T(8,128)(2,1)S(1)}, bf16[208,384]{1,0:T(8,128)(2,1)S(1)}, u32[]{:S(2)}, u32[]{:S(2)}) %collective-permute-start.4) | collective-permute-done | bytes 159776 | tf_op jit(solution)/shard_map/ppermute | solution.py:45
  31.5 6.4 %collective-permute-done.9 = bf16[4,112,384]{2,1,0:T(8,128)(2,1)S(1)} collective-permute-done((bf16[4,112,384]{2,1,0:T(8,128)(2,1)S(1)}, bf16[4,112,384]{2,1,0:T(8,128)(2,1)S(1)}, u32[]{:S(2)}, u32[]{:S(2)}) %collective-permute-start.9) | collective-permute-done | bytes 344096 | tf_op jit(solution)/shard_map/ppermute | solution.py:45
  46.2 10.0 %collective-permute-done.15.refs_5_.refs_1_ = bf16[2,4,112,384]{3,2,1,0:T(8,128)(2,1)S(1)} collective-permute-done((bf16[2,4,112,384]{3,2,1,0:T(8,128)(2,1)S(1)}, bf16[2,4,112,384]{3,2,1,0:T(8,128)(2,1)S(1)}, u32[]{:S(2)}, u32[]{:S(2)}) %collective-permute-start.15) | collective-permute-done | bytes 688160 | tf_op jit(solution)/shard_map/ppermute | solution.py:45
  62.4 9.1 %qkv.1 = (bf16[512,768]{1,0:T(8,128)(2,1)}, bf16[512,768]{1,0:T(8,128)(2,1)}, bf16[512,768]{1,0:T(8,128)(2,1)}, bf16[512,768]{1,0:T(8,128)(2,1)}, bf16[256,768]{...) custom-call(s32[6]{0:T(128)S(1)} %stack.130.info, ...), custom_call_target="tpu_custom_call" | custom-call | flops 1200000000 | bytes 1000000 | tf_op jit(solution)/shard_map/qkv/pallas_call | solution.py:680
  71.5 3.2 %collective-permute-done.17.refs_1_.refs_5_ = bf16[4,96,768]{2,1,0:T(8,128)(2,1)S(1)} collective-permute-done((bf16[4,96,768]{2,1,0:T(8,128)(2,1)S(1)}, bf16[4,96,768]{2,1,0:T(8,128)(2,1)S(1)}, u32[]{:S(2)}, u32[]{:S(2)}) %collective-permute-start.17) | collective-permute-done | bytes 589856 | tf_op jit(solution)/shard_map/ppermute | solution.py:45
  76.2 3.5 %collective-permute-start.19 = (bf16[256,768]{1,0:T(8,128)(2,1)}, bf16[256,768]{1,0:T(8,128)(2,1)S(1)}, u32[]{:S(2)}, u32[]{:S(2)}) collective-permute-start(bf16[256,768]{1,0:T(8,128)(2,1)} %get-tuple-element.85), channel_id=1, source_target_pairs={{0,2},{1,3},{4,6},{5,7},{8,10},{9,11},{12,14},{13,15},{16,18},{17,... | collective-permute-start | bytes 1179656 | tf_op jit(solution)/shard_map/ppermute | solution.py:814
  84.2 13.1 %attend.1 = (bf16[12,512,512]{2,1,0:T(8,128)(2,1)}, f32[768,512]{1,0:T(8,128)}, bf16[12,256,512]{2,1,0:T(8,128)(2,1)}) custom-call(s32[6]{0:T(128)S(1)} %stack.130.info, bf16[512,768]{1,0:T(8,128)(2,1)} %get-tuple-element.79.q, bf16[512,768]{1,0:T(8,128)(2,1)} %get-tuple-element.80.k, bf16[512,768]{1,0:T(8,128)(2,1)} %get-tuple-element.81.v, ...), custom_call_target="tpu_custom_call" | custom-call | flops 2400000000 | bytes 1000000 | tf_op jit(solution)/shard_map/attend/pallas_call | solution.py:680
  98.1 9.0 %recall.1 = (bf16[512,768]{1,0:T(8,128)(2,1)}, f32[512,768]{1,0:T(8,128)}, bf16[512,768]{1,0:T(8,128)(2,1)}) custom-call(s32[6]{0:T(128)S(1)} %stack.130.info, bf16[12,256,512]{2,1,0:T(8,128)(2,1)} %get-tuple-element.84.dens_t, bf16[256,768]{1,0:T(8,128)(2,1)} %copy-done.12, f32[768,512]{1,0:T(8,128)} %get-tuple-element.86.local_t, ...), custom_call_target="tpu_custom_call" | custom-call | flops 1400000000 | bytes 1000000 | tf_op jit(solution)/shard_map/recall/pallas_call | solution.py:680
  107.2 3.7 %collective-permute-done.26.refs_2_.refs_10_ = bf16[4,96,768]{2,1,0:T(8,128)(2,1)S(1)} collective-permute-done((bf16[4,96,768]{2,1,0:T(8,128)(2,1)S(1)}, bf16[4,96,768]{2,1,0:T(8,128)(2,1)S(1)}, u32[]{:S(2)}, u32[]{:S(2)}) %collective-permute-start.26) | collective-permute-done | bytes 589856 | tf_op jit(solution)/shard_map/ppermute | solution.py:45
  112.4 13.9 %up.1 = (bf16[2,512,1536]{2,1,0:T(8,128)(2,1)}, bf16[2,512,1536]{2,1,0:T(8,128)(2,1)}, bf16[2,4,96,768]{3,2,1,0:T(8,128)(2,1)}, bf16[2,4,96,768]{3,2,1,0:T(8,128)(2,1)}) custom-call(s32[6]{0:T(128)S(1)} %stack.130.info, bf16[512,768]{1,0:T(8,128)(2,1)} %get-tuple-element.90.own, bf16[512,768]{1,0:T(8,128)(2,1)S(1)} %collective-permute-done.20.other, ...), custom_call_target="tpu_custom_call" | custom-call | flops 2400000000 | bytes 1000000 | tf_op jit(solution)/shard_map/up/pallas_call | solution.py:680
  127.5 15.5 %down.1 = (bf16[2,4,96,768]{3,2,1,0:T(8,128)(2,1)}, bf16[2,4,96,768]{3,2,1,0:T(8,128)(2,1)}, f32[512,768]{1,0:T(8,128)}, bf16[512,768]{1,0:T(8,128)(2,1)}) custom-call(s32[6]{0:T(128)S(1)} %stack.130.info, bf16[2,512,768]{2,1,0:T(8,128)(2,1)} %copy-done.3, bf16[512,768]{1,0:T(8,128)(2,1)} %get-tuple-element.90.own, ...), custom_call_target="tpu_custom_call" | custom-call | flops 3000000000 | bytes 1000000 | tf_op jit(solution)/shard_map/down/pallas_call | solution.py:680
  145.6 11.5 %mix_back.1 = (f32[512,768]{1,0:T(8,128)}, bf16[512,768]{1,0:T(8,128)(2,1)}, bf16[256,768]{1,0:T(8,128)(2,1)}, f32[1,768]{1,0:T(1,128)}, f32[1,768]{1,0:T(1,128)...) custom-call(s32[6]{0:T(128)S(1)} %stack.130.info, f32[512,768]{1,0:T(8,128)} %get-tuple-element.98.own, ...), custom_call_target="tpu_custom_call" | custom-call | flops 1200000000 | bytes 1000000 | tf_op jit(solution)/shard_map/mix_back/pallas_call | solution.py:680
  158.8 13.2 %attend_back.1 = (bf16[512,768]{1,0:T(8,128)(2,1)}, bf16[512,768]{1,0:T(8,128)(2,1)}, f32[512,768]{1,0:T(8,128)}, f32[2,768]{1,0:T(2,128)}) custom-call(bf16[12,512,512]{2,1,0:T(8,128)(2,1)} %get-tuple-element.83.attn_t, bf16[512,768]{1,0:T(8,128)(2,1)} %get-tuple-element.79.q, bf16[512,768]{1,0:T(8,128)(2,1)} %get-tuple-element.80.k, ...), custom_call_target="tpu_custom_call" | custom-call | flops 3200000000 | bytes 1000000 | tf_op jit(solution)/shard_map/attend_back/pallas_call | solution.py:680
  172.8 2.6 %collective-permute-start.34 = (bf16[4,96,768]{2,1,0:T(8,128)(2,1)S(1)}, bf16[4,96,768]{2,1,0:T(8,128)(2,1)S(1)}, u32[]{:S(2)}, u32[]{:S(2)}) collective-permute-start(bf16[4,96,768]{2,1,0:T(8,128)(2,1)S(1)} %get-tuple-element.162), channel_id=1, source_target_pairs={{0,2},{1,3},{2,0},{3,1},{4,6},{5,7},{6,4},{7,5},{8,10},{9,11},{10,... | collective-permute-start | bytes 1769480 | tf_op jit(solution)/shard_map/ppermute | solution.py:45
  176.3 9.6 %qkv_grad.1 = (bf16[2,2,4,96,384]{4,3,2,1,0:T(8,128)(2,1)}, bf16[2,2,4,96,384]{4,3,2,1,0:T(8,128)(2,1)}, bf16[2,2,4,64,384]{4,3,2,1,0:T(8,128)(2,1)}, bf16[2,2,4...) custom-call(s32[6]{0:T(128)S(1)} %stack.130.info, bf16[512,768]{1,0:T(8,128)(2,1)} %get-tuple-element.87.x, ...), custom_call_target="tpu_custom_call" | custom-call | flops 1200000000 | bytes 1000000 | tf_op jit(solution)/shard_map/qkv_grad/pallas_call | solution.py:680
  185.9 3.1 %collective-permute-done.34 = bf16[4,96,768]{2,1,0:T(8,128)(2,1)S(1)} collective-permute-done((bf16[4,96,768]{2,1,0:T(8,128)(2,1)S(1)}, bf16[4,96,768]{2,1,0:T(8,128)(2,1)S(1)}, u32[]{:S(2)}, u32[]{:S(2)}) %collective-permute-start.34) | collective-permute-done | bytes 589856 | tf_op jit(solution)/shard_map/ppermute | solution.py:45
  198.2 2.5 collective-permute-start.48
  203.6 13.1 %finish.1 = (f32[256,768]{1,0:T(8,128)}, bf16[256,768]{1,0:T(8,128)(2,1)}, f32[2,256,768]{2,1,0:T(8,128)}, bf16[2,256,768]{2,1,0:T(8,128)(2,1)}) custom-call(s32[6]{0:T(128)S(1)} %stack.130.info, bf16[512,768]{1,0:T(8,128)(2,1)} %get-tuple-element.127.dq, bf16[512,768]{1,0:T(8,128)(2,1)} %get-tuple-element.105.dk, bf16[512,768]{1,0:T(8,128)(2,1)} %get-tuple-element.128.dv, ...), custom_call_target="tpu_custom_call" | custom-call | flops 2800000000 | bytes 1000000 | tf_op jit(solution)/shard_map/finish/pallas_call | solution.py:680
  216.8 5.1 %collective-permute-done.48 = bf16[192,768]{1,0:T(8,128)(2,1)} collective-permute-done((bf16[192,768]{1,0:T(8,128)(2,1)}, bf16[192,768]{1,0:T(8,128)(2,1)}, u32[]{:S(2)}, u32[]{:S(2)}) %collective-permute-start.48) | collective-permute-done | bytes 294944 | tf_op jit(solution)/shard_map/ppermute | solution.py:45
  227.6 7.1 %collective-permute-done.42 = bf16[4,112,384]{2,1,0:T(8,128)(2,1)S(1)} collective-permute-done((bf16[4,112,384]{2,1,0:T(8,128)(2,1)S(1)}, bf16[4,112,384]{2,1,0:T(8,128)(2,1)S(1)}, u32[]{:S(2)}, u32[]{:S(2)}) %collective-permute-start.42) | collective-permute-done | bytes 344096 | tf_op jit(solution)/shard_map/ppermute | solution.py:45
  235.0 5.4 %collective-permute-start.44 = (bf16[208,384]{1,0:T(8,128)(2,1)S(1)}, bf16[208,384]{1,0:T(8,128)(2,1)S(1)}, u32[]{:S(2)}, u32[]{:S(2)}) collective-permute-start(bf16[208,384]{1,0:T(8,128)(2,1)S(1)} %pad_maximum_fusion.14), channel_id=1, source_target_pairs={{0,16},{1,17},{2,18},{3,19},{4,20},{5,21},{6,22},{7,23},{8,24},{9,... | collective-permute-start | bytes 479240 | tf_op jit(solution)/shard_map/ppermute | solution.py:45
  243.5 7.5 %collective-permute-done.44 = bf16[208,384]{1,0:T(8,128)(2,1)S(1)} collective-permute-done((bf16[208,384]{1,0:T(8,128)(2,1)S(1)}, bf16[208,384]{1,0:T(8,128)(2,1)S(1)}, u32[]{:S(2)}, u32[]{:S(2)}) %collective-permute-start.44) | collective-permute-done | bytes 159776 | tf_op jit(solution)/shard_map/ppermute | solution.py:45
  (230 shorter events, 69.8 us)
Async XLA Ops:
  9.3 15.6 %collective-permute-start.5 = (bf16[208,384]{1,0:T(8,128)(2,1)S(1)}, bf16[208,384]{1,0:T(8,128)(2,1)S(1)}, u32[]{:S(2)}, u32[]{:S(2)}) collective-permute-start(bf16[208,384]{1,0:T(8,128)(2,1)S(1)} %fusion.43), channel_id=1, source_target_pairs={{0,24},{1,25},{2,26},{3,27},{4,28},{5,29},{6,30},{7,31},{8,16},{9,... | collective-permute-start | bytes 479240 | tf_op jit(solution)/shard_map/ppermute | solution.py:45
  38.7 17.5 %collective-permute-start.15 = (bf16[2,4,112,384]{3,2,1,0:T(8,128)(2,1)S(1)}, bf16[2,4,112,384]{3,2,1,0:T(8,128)(2,1)S(1)}, u32[]{:S(2)}, u32[]{:S(2)}) collective-permute-start(bf16[2,4,112,384]{3,2,1,0:T(8,128)(2,1)S(1)} %pad_maximum_fusion.2.refs_4_.refs_0_), channel_id=1, source_target_pairs={{0,4},{1,5},{2,6},{3,7},{4,0},{5,1},{6,2},{7,3},{8,12},{9,13},{10,... | collective-permute-start | bytes 2064392 | tf_op jit(solution)/shard_map/ppermute | solution.py:45
  40.3 16.1 %collective-permute-start.7 = (bf16[2,4,96,384]{3,2,1,0:T(8,128)(2,1)S(1)}, bf16[2,4,96,384]{3,2,1,0:T(8,128)(2,1)S(1)}, u32[]{:S(2)}, u32[]{:S(2)}) collective-permute-start(bf16[2,4,96,384]{3,2,1,0:T(8,128)(2,1)S(1)} %pad_maximum_fusion.4.refs_0_), channel_id=1, source_target_pairs={{0,2},{1,3},{2,0},{3,1},{4,6},{5,7},{6,4},{7,5},{8,10},{9,11},{10,... | collective-permute-start | bytes 1769480 | tf_op jit(solution)/shard_map/ppermute | solution.py:45
  41.8 14.5 %collective-permute-start.13 = (bf16[96,768]{1,0:T(8,128)(2,1)S(1)}, bf16[96,768]{1,0:T(8,128)(2,1)S(1)}, u32[]{:S(2)}, u32[]{:S(2)}) collective-permute-start(bf16[96,768]{1,0:T(8,128)(2,1)S(1)} %copy-done.27), channel_id=1, source_target_pairs={{0,24},{1,25},{2,26},{3,27},{4,28},{5,29},{6,30},{7,31},{8,16},{9,... | collective-permute-start | bytes 442376 | tf_op jit(solution)/shard_map/ppermute | solution.py:45
  59.3 15.4 %collective-permute-start.17 = (bf16[4,96,768]{2,1,0:T(8,128)(2,1)S(1)}, bf16[4,96,768]{2,1,0:T(8,128)(2,1)S(1)}, u32[]{:S(2)}, u32[]{:S(2)}) collective-permute-start(bf16[4,96,768]{2,1,0:T(8,128)(2,1)S(1)} %pad_maximum_fusion.5.refs_0_.refs_4_), channel_id=1, source_target_pairs={{0,2},{1,3},{2,0},{3,1},{4,6},{5,7},{6,4},{7,5},{8,10},{9,11},{10,... | collective-permute-start | bytes 1769480 | tf_op jit(solution)/shard_map/ppermute | solution.py:45
  60.8 21.5 %collective-permute-start.18 = (bf16[4,96,768]{2,1,0:T(8,128)(2,1)S(1)}, bf16[4,96,768]{2,1,0:T(8,128)(2,1)S(1)}, u32[]{:S(2)}, u32[]{:S(2)}) collective-permute-start(bf16[4,96,768]{2,1,0:T(8,128)(2,1)S(1)} %pad_maximum_fusion.5.refs_0_.refs_4_), channel_id=1, source_target_pairs={{0,4},{1,5},{2,6},{3,7},{4,0},{5,1},{6,2},{7,3},{8,12},{9,13},{10,... | collective-permute-start | bytes 1769480 | tf_op jit(solution)/shard_map/ppermute | solution.py:45
  74.7 22.7 %collective-permute-start.21 = (bf16[4,96,768]{2,1,0:T(8,128)(2,1)S(1)}, bf16[4,96,768]{2,1,0:T(8,128)(2,1)S(1)}, u32[]{:S(2)}, u32[]{:S(2)}) collective-permute-start(bf16[4,96,768]{2,1,0:T(8,128)(2,1)S(1)} %collective-permute-done.17.refs_1_.refs_5_), channel_id=1, source_target_pairs={{0,4},{1,5},{2,6},{3,7},{4,0},{5,1},{6,2},{7,3},{8,12},{9,13},{10,... | collective-permute-start | bytes 1769480 | tf_op jit(solution)/shard_map/ppermute | solution.py:45
  76.2 21.1 %collective-permute-start.19 = (bf16[256,768]{1,0:T(8,128)(2,1)}, bf16[256,768]{1,0:T(8,128)(2,1)S(1)}, u32[]{:S(2)}, u32[]{:S(2)}) collective-permute-start(bf16[256,768]{1,0:T(8,128)(2,1)} %get-tuple-element.85), channel_id=1, source_target_pairs={{0,2},{1,3},{4,6},{5,7},{8,10},{9,11},{12,14},{13,15},{16,18},{17,... | collective-permute-start | bytes 1179656 | tf_op jit(solution)/shard_map/ppermute | solution.py:814
  79.7 17.6 %collective-permute-start.24 = (bf16[96,768]{1,0:T(8,128)(2,1)S(1)}, bf16[96,768]{1,0:T(8,128)(2,1)S(1)}, u32[]{:S(2)}, u32[]{:S(2)}) collective-permute-start(bf16[96,768]{1,0:T(8,128)(2,1)S(1)} %bitcast.256), channel_id=1, source_target_pairs={{0,24},{1,25},{2,26},{3,27},{4,28},{5,29},{6,30},{7,31},{8,16},{9,... | collective-permute-start | bytes 442376 | tf_op jit(solution)/shard_map/ppermute | solution.py:45
  82.3 15.1 %collective-permute-start.23 = (bf16[96,768]{1,0:T(8,128)(2,1)S(1)}, bf16[96,768]{1,0:T(8,128)(2,1)S(1)}, u32[]{:S(2)}, u32[]{:S(2)}) collective-permute-start(bf16[96,768]{1,0:T(8,128)(2,1)S(1)} %bitcast.257), channel_id=1, source_target_pairs={{0,16},{1,17},{2,18},{3,19},{4,20},{5,21},{6,22},{7,23},{8,24},{9,... | collective-permute-start | bytes 442376 | tf_op jit(solution)/shard_map/ppermute | solution.py:45
  82.3 15.1 %collective-permute-start.22 = (bf16[96,768]{1,0:T(8,128)(2,1)S(1)}, bf16[96,768]{1,0:T(8,128)(2,1)S(1)}, u32[]{:S(2)}, u32[]{:S(2)}) collective-permute-start(bf16[96,768]{1,0:T(8,128)(2,1)S(1)} %bitcast.258), channel_id=1, source_target_pairs={{0,8},{1,9},{2,10},{3,11},{4,12},{5,13},{6,14},{7,15},{8,0},{9,1},... | collective-permute-start | bytes 442376 | tf_op jit(solution)/shard_map/ppermute | solution.py:45
  110.9 15.8 %collective-permute-start.27 = (bf16[4,96,768]{2,1,0:T(8,128)(2,1)S(1)}, bf16[4,96,768]{2,1,0:T(8,128)(2,1)S(1)}, u32[]{:S(2)}, u32[]{:S(2)}) collective-permute-start(bf16[4,96,768]{2,1,0:T(8,128)(2,1)S(1)} %collective-permute-done.25.refs_1_.refs_9_), channel_id=1, source_target_pairs={{0,4},{1,5},{2,6},{3,7},{4,0},{5,1},{6,2},{7,3},{8,12},{9,13},{10,... | collective-permute-start | bytes 1769480 | tf_op jit(solution)/shard_map/ppermute | solution.py:45
  126.3 31.0 %collective-permute-start.30 = (bf16[2,4,96,768]{3,2,1,0:T(8,128)(2,1)}, bf16[2,4,96,768]{3,2,1,0:T(8,128)(2,1)S(1)}, u32[]{:S(2)}, u32[]{:S(2)}) collective-permute-start(bf16[2,4,96,768]{3,2,1,0:T(8,128)(2,1)} %get-tuple-element.107), channel_id=1, source_target_pairs={{0,2},{1,3},{2,0},{3,1},{4,6},{5,7},{6,4},{7,5},{8,10},{9,11},{10,... | collective-permute-start | bytes 3538952 | tf_op jit(solution)/shard_map/ppermute | solution.py:45
  143.1 28.8 %collective-permute-start.29 = (bf16[2,4,96,768]{3,2,1,0:T(8,128)(2,1)}, bf16[2,4,96,768]{3,2,1,0:T(8,128)(2,1)S(1)}, u32[]{:S(2)}, u32[]{:S(2)}) collective-permute-start(bf16[2,4,96,768]{3,2,1,0:T(8,128)(2,1)} %get-tuple-element.104), channel_id=1, source_target_pairs={{0,4},{1,5},{2,6},{3,7},{4,0},{5,1},{6,2},{7,3},{8,12},{9,13},{10,... | collective-permute-start | bytes 3538952 | tf_op jit(solution)/shard_map/ppermute | solution.py:45
  157.1 14.9 %collective-permute-start.32 = (bf16[2,2,4,48,384]{4,3,2,1,0:T(8,128)(2,1)}, bf16[2,2,4,48,384]{4,3,2,1,0:T(8,128)(2,1)S(1)}, u32[]{:S(2)}, u32[]{:S(2)}) collective-permute-start(bf16[2,2,4,48,384]{4,3,2,1,0:T(8,128)(2,1)} %get-tuple-element.109), channel_id=1, source_target_pairs={{0,1},{1,0},{2,3},{3,2},{4,5},{5,4},{6,7},{7,6},{8,9},{9,8},{10,11... | collective-permute-start | bytes 1769480 | tf_op jit(solution)/shard_map/ppermute | solution.py:45
  157.3 14.7 %collective-permute-start.31 = (bf16[256,768]{1,0:T(8,128)(2,1)}, bf16[256,768]{1,0:T(8,128)(2,1)S(1)}, u32[]{:S(2)}, u32[]{:S(2)}) collective-permute-start(bf16[256,768]{1,0:T(8,128)(2,1)} %get-tuple-element.108), channel_id=1, source_target_pairs={{2,0},{3,1},{6,4},{7,5},{10,8},{11,9},{14,12},{15,13},{18,16},{19,... | collective-permute-start | bytes 1179656 | tf_op jit(solution)/shard_map/ppermute | solution.py:913
  172.8 16.2 %collective-permute-start.34 = (bf16[4,96,768]{2,1,0:T(8,128)(2,1)S(1)}, bf16[4,96,768]{2,1,0:T(8,128)(2,1)S(1)}, u32[]{:S(2)}, u32[]{:S(2)}) collective-permute-start(bf16[4,96,768]{2,1,0:T(8,128)(2,1)S(1)} %get-tuple-element.162), channel_id=1, source_target_pairs={{0,2},{1,3},{2,0},{3,1},{4,6},{5,7},{6,4},{7,5},{8,10},{9,11},{10,... | collective-permute-start | bytes 1769480 | tf_op jit(solution)/shard_map/ppermute | solution.py:45
  175.7 15.1 %collective-permute-start.33 = (bf16[4,96,768]{2,1,0:T(8,128)(2,1)S(1)}, bf16[4,96,768]{2,1,0:T(8,128)(2,1)S(1)}, u32[]{:S(2)}, u32[]{:S(2)}) collective-permute-start(bf16[4,96,768]{2,1,0:T(8,128)(2,1)S(1)} %get-tuple-element.160), channel_id=1, source_target_pairs={{0,4},{1,5},{2,6},{3,7},{4,0},{5,1},{6,2},{7,3},{8,12},{9,13},{10,... | collective-permute-start | bytes 1769480 | tf_op jit(solution)/shard_map/ppermute | solution.py:45
  197.0 19.8 %collective-permute-start.47 = (bf16[192,768]{1,0:T(8,128)(2,1)}, bf16[192,768]{1,0:T(8,128)(2,1)}, u32[]{:S(2)}, u32[]{:S(2)}) collective-permute-start(bf16[192,768]{1,0:T(8,128)(2,1)} %pad_maximum_fusion.9), channel_id=1, source_target_pairs={{0,8},{1,9},{2,10},{3,11},{4,12},{5,13},{6,14},{7,15},{8,0},{9,1},... | collective-permute-start | bytes 884744 | tf_op jit(solution)/shard_map/ppermute | solution.py:45
  198.2 23.7 %collective-permute-start.48 = (bf16[192,768]{1,0:T(8,128)(2,1)}, bf16[192,768]{1,0:T(8,128)(2,1)}, u32[]{:S(2)}, u32[]{:S(2)}) collective-permute-start(bf16[192,768]{1,0:T(8,128)(2,1)} %pad_maximum_fusion.10), channel_id=1, source_target_pairs={{0,16},{1,17},{2,18},{3,19},{4,20},{5,21},{6,22},{7,23},{8,24},{9,... | collective-permute-start | bytes 884744 | tf_op jit(solution)/shard_map/ppermute | solution.py:45
  200.8 21.2 %collective-permute-start.49 = (bf16[192,768]{1,0:T(8,128)(2,1)S(1)}, bf16[192,768]{1,0:T(8,128)(2,1)}, u32[]{:S(2)}, u32[]{:S(2)}) collective-permute-start(bf16[192,768]{1,0:T(8,128)(2,1)S(1)} %pad_maximum_fusion.11), channel_id=1, source_target_pairs={{0,24},{1,25},{2,26},{3,27},{4,28},{5,29},{6,30},{7,31},{8,16},{9,... | collective-permute-start | bytes 884744 | tf_op jit(solution)/shard_map/ppermute | solution.py:45
  202.2 21.9 %collective-permute-start.41 = (bf16[2,4,112,384]{3,2,1,0:T(8,128)(2,1)}, bf16[2,4,112,384]{3,2,1,0:T(8,128)(2,1)S(1)}, u32[]{:S(2)}, u32[]{:S(2)}) collective-permute-start(bf16[2,4,112,384]{3,2,1,0:T(8,128)(2,1)} %pad_maximum_fusion.3), channel_id=1, source_target_pairs={{0,4},{1,5},{2,6},{3,7},{4,0},{5,1},{6,2},{7,3},{8,12},{9,13},{10,... | collective-permute-start | bytes 2064392 | tf_op jit(solution)/shard_map/ppermute | solution.py:45
  202.7 22.6 %collective-permute-start.39 = (bf16[2,4,96,384]{3,2,1,0:T(8,128)(2,1)}, bf16[2,4,96,384]{3,2,1,0:T(8,128)(2,1)S(1)}, u32[]{:S(2)}, u32[]{:S(2)}) collective-permute-start(bf16[2,4,96,384]{3,2,1,0:T(8,128)(2,1)} %get-tuple-element.158), channel_id=1, source_target_pairs={{0,2},{1,3},{2,0},{3,1},{4,6},{5,7},{6,4},{7,5},{8,10},{9,11},{10,... | collective-permute-start | bytes 1769480 | tf_op jit(solution)/shard_map/ppermute | solution.py:45
  235.0 15.9 %collective-permute-start.44 = (bf16[208,384]{1,0:T(8,128)(2,1)S(1)}, bf16[208,384]{1,0:T(8,128)(2,1)S(1)}, u32[]{:S(2)}, u32[]{:S(2)}) collective-permute-start(bf16[208,384]{1,0:T(8,128)(2,1)S(1)} %pad_maximum_fusion.14), channel_id=1, source_target_pairs={{0,16},{1,17},{2,18},{3,19},{4,20},{5,21},{6,22},{7,23},{8,24},{9,... | collective-permute-start | bytes 479240 | tf_op jit(solution)/shard_map/ppermute | solution.py:45
  (62 other events, 551.1 us)

commit v7 on v6

--- a/solution.py
+++ b/solution.py
@@ -109,12 +109,6 @@
     return whole.reshape((8,) + whole.shape[2:])
 
 
-def to_segment_parts(local):
-    core = lax.axis_index("tensor") % 2
-    own = lax.dynamic_index_in_dim(local, core, 0, keepdims=False)
-    return own, swap(lax.dynamic_index_in_dim(local, 1 - core, 0, keepdims=False))
-
-
 def exact_triple(value):
     high = lax.reduce_precision(value, 8, 7)
     middle = lax.reduce_precision(value - high, 8, 7)
@@ -235,8 +229,8 @@
     for copy in copies:
         copy.start()
     core = info[5]
-    x_out[pl.ds(aligned(core, 256), 256), :] = own[...]
-    x_out[pl.ds(aligned(1 - core, 256), 256), :] = other[...]
+    x_out[pl.ds(aligned(core, 256), 256), :] = own[core]
+    x_out[pl.ds(aligned(1 - core, 256), 256), :] = other[core]
     scale = column_validity(info) * info[4].astype(F32)
     pair_wait = pltpu.make_async_copy(wq, wq, sems.at[0])
     pair_wait.wait()
@@ -725,7 +719,7 @@
     where = (dp, segment, core) if near else (0, 0, 0)
     info = jnp.stack([jnp.asarray(value, jnp.int32) for value in where + (used[0], pair, core)])
 
-    own, other = to_segment_parts(tokens)
+    their_tokens = swap(tokens)
     theirs = swap(cotangent)
     everything = jnp.where(
         core == 0,
@@ -757,7 +751,7 @@
         )
         small_rows = jnp.pad(small[None], ((0, 15), (0, 384 - small.size)))
         packed = jnp.concatenate([projections.reshape(192, 384), small_rows])
-        along_z = spread(after(packed, other, theirs), "z")
+        along_z = spread(after(packed, their_tokens, theirs), "z")
         along_z[1] = after(along_z[1], seed, seed_t, info)
         qk_near = jnp.stack(spread(jnp.stack([part[:96] for part in along_z]), "y"))
         v_near = jnp.stack(spread(jnp.stack([part[96:] for part in along_z]), "x"))
@@ -803,7 +797,7 @@
     x, q, k, v, coef, *small_params = run(
         functools.partial(qkv_kernel, table_qk, table_v, near),
         "qkv",
-        [info, own, other, jnp.asarray(ridge)] + qk_parts + v_parts + small_in,
+        [info, tokens, their_tokens, jnp.asarray(ridge)] + qk_parts + v_parts + small_in,
         [SCALARS, FULL, FULL, FULL] + [ANY] * 8 + [FULL] * len(small_in),
         [tall] * 4 + [shape((NB, D))] + small_out,
         [FULL] * (5 + len(small_out)),
@@ -987,6 +981,13 @@
         cost=14.0,
         vmem=32,
     )
+    if near:
+        qk_1 = (qk_1[0], [after(value, token_send) for value in qk_1[1]])
+        v_1 = (v_1[0], [after(value, token_send) for value in v_1[1]])
+        qk_2 = stage(combined(*qk_1), BACK_QK[1])
+        v_2 = stage(combined(*v_1), BACK_V[1])
+        token_send = after(token_send, v_1[1][0], qk_1[1][0])
+        fed_send = after(fed_send, v_1[1][0], qk_1[1][0])
     token_got, fed_got = swap(token_send).astype(F32), swap(fed_send).astype(F32)
     own_rows, their_rows = fed_keep[0] + fed_got[1], fed_keep[1] + fed_got[0]
     by_sequence = lambda mine, theirs: jnp.where(
@@ -996,12 +997,13 @@
     grad_tokens = by_sequence(token_keep, token_got)
 
     if near:
-        qk_2 = stage(combined(*qk_1), BACK_QK[1])
-        v_2 = stage(combined(*v_1), BACK_V[1])
+        wide_3 = (wide_3[0], [after(a, *qk_1[1], *v_1[1]) for a in wide_3[1]])
         to_qk, to_v = combined(*qk_2), combined(*v_2)
         last = [jnp.concatenate([to_qk(k), to_v(k)]) for k in range(4)]
         last[1:] = [value.astype(BF16) for value in last[1:]]
-        joined = final_sum(*stage(lambda k: last[k], "z"))
+        joined, arrived = stage(lambda k: last[k], "z")
+        arrived[0] = after(arrived[0], output, grad_tokens)
+        joined = final_sum(joined, arrived)
         own_small = joined[192]
         narrow = joined[:192].reshape(4, 48, 384)
         mine = lax.dynamic_slice_in_dim(narrow, core * 192, 192, axis=2)

time: 257 us -> 254 us (0.988)
  waiting for transfers between devices: 66.9 us -> 58.4 us
  starting transfers between devices: 53.5 us -> 56.7 us
  local copies, waits for them, and re-layouts: 12.8 us -> 15.6 us
    ppermute x48, waiting for transfers between devices: 66.9 us -> 58.4 us  [xor_permute(): return lax.ppermute(value, AXES, pairs)]
    unnamed x77 -> x81, local copies, waits for them, and re-layouts: 3.75 us -> 7.81 us
    ppermute x48, starting transfers between devices: 48.5 us -> 51.7 us  [xor_permute(): return lax.ppermute(value, AXES, pairs)]
  transfers between devices with their start and end apart: 50 -> 50, of which waited for: 18 -> 16; matrix products, arithmetic and copies ran while one was open for 6% -> 6% of each run, Pallas kernels for 42% -> 43%
where the time goes in v7:
time: 254 us; the launch traced here: 253 us
  Pallas kernels  108 us (43%)
  waiting for transfers between devices  58.4 us (23%)
  starting transfers between devices  56.7 us (22%)
  local copies, waits for them, and re-layouts  15.6 us (6%)
  other arithmetic  11.3 us (4%)
  between operations  2.85 us (1%)
    pallas_call x9, Pallas kernels, run(): pl.pallas_call(body, name=name, out_shape=tuple((pltpu.HBM(out.shape, out...  108 us
    ppermute x48, waiting for transfers between devices, xor_permute(): return lax.ppermute(value, AXES, pairs)  58.4 us
    ppermute x48, starting transfers between devices, xor_permute(): return lax.ppermute(value, AXES, pairs)  51.7 us
    unnamed x81, local copies, waits for them, and re-layouts  7.81 us
  transfers between devices with their start and end apart: 50, of which 16 were waited for; matrix products, arithmetic and copies ran while one was open for 6% of the time, Pallas kernels for 43%

profile of v7, /device:TPU:0, one launch (start us, length us, event | category | flops | bytes accessed | tf_op | source)
XLA Modules:
  0.0 253.0 jit_solution(13118401124987328000)
XLA Ops:
  9.4 4.7 %collective-permute-start.5 = (bf16[208,384]{1,0:T(8,128)(2,1)S(1)}, bf16[208,384]{1,0:T(8,128)(2,1)S(1)}, u32[]{:S(2)}, u32[]{:S(2)}) collective-permute-start(bf16[208,384]{1,0:T(8,128)(2,1)S(1)} %fusion.43), channel_id=1, source_target_pairs={{0,24},{1,25},{2,26},{3,27},{4,28},{5,29},{6,30},{7,31},{8,16},{9,... | collective-permute-start | bytes 479240 | tf_op jit(solution)/shard_map/ppermute | solution.py:45
  17.6 7.5 %collective-permute-done.3 = bf16[208,384]{1,0:T(8,128)(2,1)S(1)} collective-permute-done((bf16[208,384]{1,0:T(8,128)(2,1)S(1)}, bf16[208,384]{1,0:T(8,128)(2,1)S(1)}, u32[]{:S(2)}, u32[]{:S(2)}) %collective-permute-start.3) | collective-permute-done | bytes 159776 | tf_op jit(solution)/shard_map/ppermute | solution.py:45
  25.1 3.2 %collective-permute-done.4 = bf16[208,384]{1,0:T(8,128)(2,1)S(1)} collective-permute-done((bf16[208,384]{1,0:T(8,128)(2,1)S(1)}, bf16[208,384]{1,0:T(8,128)(2,1)S(1)}, u32[]{:S(2)}, u32[]{:S(2)}) %collective-permute-start.4) | collective-permute-done | bytes 159776 | tf_op jit(solution)/shard_map/ppermute | solution.py:45
  31.6 6.3 %collective-permute-done.9 = bf16[4,112,384]{2,1,0:T(8,128)(2,1)S(1)} collective-permute-done((bf16[4,112,384]{2,1,0:T(8,128)(2,1)S(1)}, bf16[4,112,384]{2,1,0:T(8,128)(2,1)S(1)}, u32[]{:S(2)}, u32[]{:S(2)}) %collective-permute-start.9) | collective-permute-done | bytes 344096 | tf_op jit(solution)/shard_map/ppermute | solution.py:45
  46.3 10.0 %collective-permute-done.15.refs_5_.refs_1_ = bf16[2,4,112,384]{3,2,1,0:T(8,128)(2,1)S(1)} collective-permute-done((bf16[2,4,112,384]{3,2,1,0:T(8,128)(2,1)S(1)}, bf16[2,4,112,384]{3,2,1,0:T(8,128)(2,1)S(1)}, u32[]{:S(2)}, u32[]{:S(2)}) %collective-permute-start.15) | collective-permute-done | bytes 688160 | tf_op jit(solution)/shard_map/ppermute | solution.py:45
  62.4 9.3 %qkv.1 = (bf16[512,768]{1,0:T(8,128)(2,1)}, bf16[512,768]{1,0:T(8,128)(2,1)}, bf16[512,768]{1,0:T(8,128)(2,1)}, bf16[512,768]{1,0:T(8,128)(2,1)}, bf16[256,768]{...) custom-call(s32[6]{0:T(128)S(1)} %stack.130.info, bf16[2,256,768]{2,1,0:T(8,128)(2,1)} %own.1, ...), custom_call_target="tpu_custom_call" | custom-call | flops 1200000000 | bytes 1000000 | tf_op jit(solution)/shard_map/qkv/pallas_call | solution.py:674
  71.7 3.1 %collective-permute-done.17.refs_1_.refs_5_ = bf16[4,96,768]{2,1,0:T(8,128)(2,1)S(1)} collective-permute-done((bf16[4,96,768]{2,1,0:T(8,128)(2,1)S(1)}, bf16[4,96,768]{2,1,0:T(8,128)(2,1)S(1)}, u32[]{:S(2)}, u32[]{:S(2)}) %collective-permute-start.17) | collective-permute-done | bytes 589856 | tf_op jit(solution)/shard_map/ppermute | solution.py:45
  76.3 3.5 %collective-permute-start.19 = (bf16[256,768]{1,0:T(8,128)(2,1)}, bf16[256,768]{1,0:T(8,128)(2,1)S(1)}, u32[]{:S(2)}, u32[]{:S(2)}) collective-permute-start(bf16[256,768]{1,0:T(8,128)(2,1)} %get-tuple-element.93), channel_id=1, source_target_pairs={{0,2},{1,3},{4,6},{5,7},{8,10},{9,11},{12,14},{13,15},{16,18},{17,... | collective-permute-start | bytes 1179656 | tf_op jit(solution)/shard_map/ppermute | solution.py:808
  84.3 13.1 %attend.1 = (bf16[12,512,512]{2,1,0:T(8,128)(2,1)}, f32[768,512]{1,0:T(8,128)}, bf16[12,256,512]{2,1,0:T(8,128)(2,1)}) custom-call(s32[6]{0:T(128)S(1)} %stack.130.info, bf16[512,768]{1,0:T(8,128)(2,1)} %get-tuple-element.87.q, bf16[512,768]{1,0:T(8,128)(2,1)} %get-tuple-element.88.k, bf16[512,768]{1,0:T(8,128)(2,1)} %get-tuple-element.89.v, ...), custom_call_target="tpu_custom_call" | custom-call | flops 2400000000 | bytes 1000000 | tf_op jit(solution)/shard_map/attend/pallas_call | solution.py:674
  98.2 8.9 %recall.1 = (bf16[512,768]{1,0:T(8,128)(2,1)}, f32[512,768]{1,0:T(8,128)}, bf16[512,768]{1,0:T(8,128)(2,1)}) custom-call(s32[6]{0:T(128)S(1)} %stack.130.info, bf16[12,256,512]{2,1,0:T(8,128)(2,1)} %get-tuple-element.92.dens_t, bf16[256,768]{1,0:T(8,128)(2,1)} %copy-done.12, f32[768,512]{1,0:T(8,128)} %get-tuple-element.94.local_t, ...), custom_call_target="tpu_custom_call" | custom-call | flops 1400000000 | bytes 1000000 | tf_op jit(solution)/shard_map/recall/pallas_call | solution.py:674
  107.3 3.7 %collective-permute-done.26.refs_2_.refs_10_ = bf16[4,96,768]{2,1,0:T(8,128)(2,1)S(1)} collective-permute-done((bf16[4,96,768]{2,1,0:T(8,128)(2,1)S(1)}, bf16[4,96,768]{2,1,0:T(8,128)(2,1)S(1)}, u32[]{:S(2)}, u32[]{:S(2)}) %collective-permute-start.26) | collective-permute-done | bytes 589856 | tf_op jit(solution)/shard_map/ppermute | solution.py:45
  112.5 13.9 %up.1 = (bf16[2,512,1536]{2,1,0:T(8,128)(2,1)}, bf16[2,512,1536]{2,1,0:T(8,128)(2,1)}, bf16[2,4,96,768]{3,2,1,0:T(8,128)(2,1)}, bf16[2,4,96,768]{3,2,1,0:T(8,128)(2,1)}) custom-call(s32[6]{0:T(128)S(1)} %stack.130.info, bf16[512,768]{1,0:T(8,128)(2,1)} %get-tuple-element.98.own, bf16[512,768]{1,0:T(8,128)(2,1)S(1)} %collective-permute-done.20.other, ...), custom_call_target="tpu_custom_call" | custom-call | flops 2400000000 | bytes 1000000 | tf_op jit(solution)/shard_map/up/pallas_call | solution.py:674
  127.6 15.6 %down.1 = (bf16[2,4,96,768]{3,2,1,0:T(8,128)(2,1)}, bf16[2,4,96,768]{3,2,1,0:T(8,128)(2,1)}, f32[512,768]{1,0:T(8,128)}, bf16[512,768]{1,0:T(8,128)(2,1)}) custom-call(s32[6]{0:T(128)S(1)} %stack.130.info, bf16[2,512,768]{2,1,0:T(8,128)(2,1)} %copy-done.3, bf16[512,768]{1,0:T(8,128)(2,1)} %get-tuple-element.98.own, ...), custom_call_target="tpu_custom_call" | custom-call | flops 3000000000 | bytes 1000000 | tf_op jit(solution)/shard_map/down/pallas_call | solution.py:674
  145.7 11.4 %mix_back.1 = (f32[512,768]{1,0:T(8,128)}, bf16[512,768]{1,0:T(8,128)(2,1)}, bf16[256,768]{1,0:T(8,128)(2,1)}, f32[1,768]{1,0:T(1,128)}, f32[1,768]{1,0:T(1,128)...) custom-call(s32[6]{0:T(128)S(1)} %stack.130.info, f32[512,768]{1,0:T(8,128)} %get-tuple-element.106.own, ...), custom_call_target="tpu_custom_call" | custom-call | flops 1200000000 | bytes 1000000 | tf_op jit(solution)/shard_map/mix_back/pallas_call | solution.py:674
  158.9 13.2 %attend_back.1 = (bf16[512,768]{1,0:T(8,128)(2,1)}, bf16[512,768]{1,0:T(8,128)(2,1)}, f32[512,768]{1,0:T(8,128)}, f32[2,768]{1,0:T(2,128)}) custom-call(bf16[12,512,512]{2,1,0:T(8,128)(2,1)} %get-tuple-element.91.attn_t, bf16[512,768]{1,0:T(8,128)(2,1)} %get-tuple-element.87.q, bf16[512,768]{1,0:T(8,128)(2,1)} %get-tuple-element.88.k, ...), custom_call_target="tpu_custom_call" | custom-call | flops 3200000000 | bytes 1000000 | tf_op jit(solution)/shard_map/attend_back/pallas_call | solution.py:674
  173.2 2.7 %collective-permute-start.34 = (bf16[4,96,768]{2,1,0:T(8,128)(2,1)S(1)}, bf16[4,96,768]{2,1,0:T(8,128)(2,1)S(1)}, u32[]{:S(2)}, u32[]{:S(2)}) collective-permute-start(bf16[4,96,768]{2,1,0:T(8,128)(2,1)S(1)} %get-tuple-element.178), channel_id=1, source_target_pairs={{0,2},{1,3},{2,0},{3,1},{4,6},{5,7},{6,4},{7,5},{8,10},{9,11},{10,... | collective-permute-start | bytes 1769480 | tf_op jit(solution)/shard_map/ppermute | solution.py:45
  176.8 9.6 %qkv_grad.1 = (bf16[2,2,4,96,384]{4,3,2,1,0:T(8,128)(2,1)}, bf16[2,2,4,96,384]{4,3,2,1,0:T(8,128)(2,1)}, bf16[2,2,4,64,384]{4,3,2,1,0:T(8,128)(2,1)}, bf16[2,2,4...) custom-call(s32[6]{0:T(128)S(1)} %stack.130.info, bf16[512,768]{1,0:T(8,128)(2,1)} %get-tuple-element.95.x, ...), custom_call_target="tpu_custom_call" | custom-call | flops 1200000000 | bytes 1000000 | tf_op jit(solution)/shard_map/qkv_grad/pallas_call | solution.py:674
  186.4 3.2 %collective-permute-done.34 = bf16[4,96,768]{2,1,0:T(8,128)(2,1)S(1)} collective-permute-done((bf16[4,96,768]{2,1,0:T(8,128)(2,1)S(1)}, bf16[4,96,768]{2,1,0:T(8,128)(2,1)S(1)}, u32[]{:S(2)}, u32[]{:S(2)}) %collective-permute-start.34) | collective-permute-done | bytes 589856 | tf_op jit(solution)/shard_map/ppermute | solution.py:45
  199.2 2.6 %collective-permute-start.48 = (bf16[192,768]{1,0:T(8,128)(2,1)S(1)}, bf16[192,768]{1,0:T(8,128)(2,1)S(1)}, u32[]{:S(2)}, u32[]{:S(2)}) collective-permute-start(bf16[192,768]{1,0:T(8,128)(2,1)S(1)} %pad_maximum_fusion.10), channel_id=1, source_target_pairs={{0,16},{1,17},{2,18},{3,19},{4,20},{5,21},{6,22},{7,23},{8,24},{9,... | collective-permute-start | bytes 884744 | tf_op jit(solution)/shard_map/ppermute | solution.py:45
  203.3 13.1 %finish.1 = (f32[256,768]{1,0:T(8,128)}, bf16[256,768]{1,0:T(8,128)(2,1)}, f32[2,256,768]{2,1,0:T(8,128)}, bf16[2,256,768]{2,1,0:T(8,128)(2,1)}) custom-call(s32[6]{0:T(128)S(1)} %stack.130.info, bf16[512,768]{1,0:T(8,128)(2,1)} %get-tuple-element.135.dq, bf16[512,768]{1,0:T(8,128)(2,1)} %get-tuple-element.113.dk, bf16[512,768]{1,0:T(8,128)(2,1)} %get-tuple-element.136.dv, ...), custom_call_target="tpu_custom_call" | custom-call | flops 2800000000 | bytes 1000000 | tf_op jit(solution)/shard_map/finish/pallas_call | solution.py:674
  217.4 5.3 %collective-permute-done.48 = bf16[192,768]{1,0:T(8,128)(2,1)S(1)} collective-permute-done((bf16[192,768]{1,0:T(8,128)(2,1)S(1)}, bf16[192,768]{1,0:T(8,128)(2,1)S(1)}, u32[]{:S(2)}, u32[]{:S(2)}) %collective-permute-start.48) | collective-permute-done | bytes 294944 | tf_op jit(solution)/shard_map/ppermute | solution.py:45
  226.0 3.6 %collective-permute-done.41 = bf16[4,96,384]{2,1,0:T(8,128)(2,1)S(1)} collective-permute-done((bf16[4,96,384]{2,1,0:T(8,128)(2,1)S(1)}, bf16[4,96,384]{2,1,0:T(8,128)(2,1)S(1)}, u32[]{:S(2)}, u32[]{:S(2)}) %collective-permute-start.41) | collective-permute-done | bytes 294944 | tf_op jit(solution)/shard_map/ppermute | solution.py:45
  229.7 7.6 %collective-permute-start.44 = (bf16[208,384]{1,0:T(8,128)(2,1)S(1)}, bf16[208,384]{1,0:T(8,128)(2,1)S(1)}, u32[]{:S(2)}, u32[]{:S(2)}) collective-permute-start(bf16[208,384]{1,0:T(8,128)(2,1)S(1)} %pad_maximum_fusion.14), channel_id=1, source_target_pairs={{0,16},{1,17},{2,18},{3,19},{4,20},{5,21},{6,22},{7,23},{8,24},{9,... | collective-permute-start | bytes 479240 | tf_op jit(solution)/shard_map/ppermute | solution.py:45
  243.0 5.0 %collective-permute-done.43 = bf16[208,384]{1,0:T(8,128)(2,1)S(1)} collective-permute-done((bf16[208,384]{1,0:T(8,128)(2,1)S(1)}, bf16[208,384]{1,0:T(8,128)(2,1)S(1)}, u32[]{:S(2)}, u32[]{:S(2)}) %collective-permute-start.43) | collective-permute-done | bytes 159776 | tf_op jit(solution)/shard_map/ppermute | solution.py:45
  (233 shorter events, 70.1 us)
Async XLA Ops:
  9.4 15.6 %collective-permute-start.5 = (bf16[208,384]{1,0:T(8,128)(2,1)S(1)}, bf16[208,384]{1,0:T(8,128)(2,1)S(1)}, u32[]{:S(2)}, u32[]{:S(2)}) collective-permute-start(bf16[208,384]{1,0:T(8,128)(2,1)S(1)} %fusion.43), channel_id=1, source_target_pairs={{0,24},{1,25},{2,26},{3,27},{4,28},{5,29},{6,30},{7,31},{8,16},{9,... | collective-permute-start | bytes 479240 | tf_op jit(solution)/shard_map/ppermute | solution.py:45
  38.8 17.5 %collective-permute-start.15 = (bf16[2,4,112,384]{3,2,1,0:T(8,128)(2,1)S(1)}, bf16[2,4,112,384]{3,2,1,0:T(8,128)(2,1)S(1)}, u32[]{:S(2)}, u32[]{:S(2)}) collective-permute-start(bf16[2,4,112,384]{3,2,1,0:T(8,128)(2,1)S(1)} %pad_maximum_fusion.2.refs_4_.refs_0_), channel_id=1, source_target_pairs={{0,4},{1,5},{2,6},{3,7},{4,0},{5,1},{6,2},{7,3},{8,12},{9,13},{10,... | collective-permute-start | bytes 2064392 | tf_op jit(solution)/shard_map/ppermute | solution.py:45
  40.3 16.1 %collective-permute-start.7 = (bf16[2,4,96,384]{3,2,1,0:T(8,128)(2,1)S(1)}, bf16[2,4,96,384]{3,2,1,0:T(8,128)(2,1)S(1)}, u32[]{:S(2)}, u32[]{:S(2)}) collective-permute-start(bf16[2,4,96,384]{3,2,1,0:T(8,128)(2,1)S(1)} %pad_maximum_fusion.4.refs_0_), channel_id=1, source_target_pairs={{0,2},{1,3},{2,0},{3,1},{4,6},{5,7},{6,4},{7,5},{8,10},{9,11},{10,... | collective-permute-start | bytes 1769480 | tf_op jit(solution)/shard_map/ppermute | solution.py:45
  41.9 14.5 %collective-permute-start.13 = (bf16[96,768]{1,0:T(8,128)(2,1)S(1)}, bf16[96,768]{1,0:T(8,128)(2,1)S(1)}, u32[]{:S(2)}, u32[]{:S(2)}) collective-permute-start(bf16[96,768]{1,0:T(8,128)(2,1)S(1)} %copy-done.31), channel_id=1, source_target_pairs={{0,24},{1,25},{2,26},{3,27},{4,28},{5,29},{6,30},{7,31},{8,16},{9,... | collective-permute-start | bytes 442376 | tf_op jit(solution)/shard_map/ppermute | solution.py:45
  59.4 15.4 %collective-permute-start.17 = (bf16[4,96,768]{2,1,0:T(8,128)(2,1)S(1)}, bf16[4,96,768]{2,1,0:T(8,128)(2,1)S(1)}, u32[]{:S(2)}, u32[]{:S(2)}) collective-permute-start(bf16[4,96,768]{2,1,0:T(8,128)(2,1)S(1)} %pad_maximum_fusion.5.refs_0_.refs_4_), channel_id=1, source_target_pairs={{0,2},{1,3},{2,0},{3,1},{4,6},{5,7},{6,4},{7,5},{8,10},{9,11},{10,... | collective-permute-start | bytes 1769480 | tf_op jit(solution)/shard_map/ppermute | solution.py:45
  60.9 21.5 %collective-permute-start.18 = (bf16[4,96,768]{2,1,0:T(8,128)(2,1)S(1)}, bf16[4,96,768]{2,1,0:T(8,128)(2,1)S(1)}, u32[]{:S(2)}, u32[]{:S(2)}) collective-permute-start(bf16[4,96,768]{2,1,0:T(8,128)(2,1)S(1)} %pad_maximum_fusion.5.refs_0_.refs_4_), channel_id=1, source_target_pairs={{0,4},{1,5},{2,6},{3,7},{4,0},{5,1},{6,2},{7,3},{8,12},{9,13},{10,... | collective-permute-start | bytes 1769480 | tf_op jit(solution)/shard_map/ppermute | solution.py:45
  74.8 22.7 %collective-permute-start.21 = (bf16[4,96,768]{2,1,0:T(8,128)(2,1)S(1)}, bf16[4,96,768]{2,1,0:T(8,128)(2,1)S(1)}, u32[]{:S(2)}, u32[]{:S(2)}) collective-permute-start(bf16[4,96,768]{2,1,0:T(8,128)(2,1)S(1)} %collective-permute-done.17.refs_1_.refs_5_), channel_id=1, source_target_pairs={{0,4},{1,5},{2,6},{3,7},{4,0},{5,1},{6,2},{7,3},{8,12},{9,13},{10,... | collective-permute-start | bytes 1769480 | tf_op jit(solution)/shard_map/ppermute | solution.py:45
  76.3 21.1 %collective-permute-start.19 = (bf16[256,768]{1,0:T(8,128)(2,1)}, bf16[256,768]{1,0:T(8,128)(2,1)S(1)}, u32[]{:S(2)}, u32[]{:S(2)}) collective-permute-start(bf16[256,768]{1,0:T(8,128)(2,1)} %get-tuple-element.93), channel_id=1, source_target_pairs={{0,2},{1,3},{4,6},{5,7},{8,10},{9,11},{12,14},{13,15},{16,18},{17,... | collective-permute-start | bytes 1179656 | tf_op jit(solution)/shard_map/ppermute | solution.py:808
  79.8 17.6 %collective-permute-start.24 = (bf16[96,768]{1,0:T(8,128)(2,1)S(1)}, bf16[96,768]{1,0:T(8,128)(2,1)S(1)}, u32[]{:S(2)}, u32[]{:S(2)}) collective-permute-start(bf16[96,768]{1,0:T(8,128)(2,1)S(1)} %bitcast.252), channel_id=1, source_target_pairs={{0,24},{1,25},{2,26},{3,27},{4,28},{5,29},{6,30},{7,31},{8,16},{9,... | collective-permute-start | bytes 442376 | tf_op jit(solution)/shard_map/ppermute | solution.py:45
  82.4 15.1 %collective-permute-start.23 = (bf16[96,768]{1,0:T(8,128)(2,1)S(1)}, bf16[96,768]{1,0:T(8,128)(2,1)S(1)}, u32[]{:S(2)}, u32[]{:S(2)}) collective-permute-start(bf16[96,768]{1,0:T(8,128)(2,1)S(1)} %bitcast.253), channel_id=1, source_target_pairs={{0,16},{1,17},{2,18},{3,19},{4,20},{5,21},{6,22},{7,23},{8,24},{9,... | collective-permute-start | bytes 442376 | tf_op jit(solution)/shard_map/ppermute | solution.py:45
  82.4 15.1 %collective-permute-start.22 = (bf16[96,768]{1,0:T(8,128)(2,1)S(1)}, bf16[96,768]{1,0:T(8,128)(2,1)S(1)}, u32[]{:S(2)}, u32[]{:S(2)}) collective-permute-start(bf16[96,768]{1,0:T(8,128)(2,1)S(1)} %bitcast.254), channel_id=1, source_target_pairs={{0,8},{1,9},{2,10},{3,11},{4,12},{5,13},{6,14},{7,15},{8,0},{9,1},... | collective-permute-start | bytes 442376 | tf_op jit(solution)/shard_map/ppermute | solution.py:45
  111.0 15.8 %collective-permute-start.27 = (bf16[4,96,768]{2,1,0:T(8,128)(2,1)S(1)}, bf16[4,96,768]{2,1,0:T(8,128)(2,1)S(1)}, u32[]{:S(2)}, u32[]{:S(2)}) collective-permute-start(bf16[4,96,768]{2,1,0:T(8,128)(2,1)S(1)} %collective-permute-done.25.refs_1_.refs_9_), channel_id=1, source_target_pairs={{0,4},{1,5},{2,6},{3,7},{4,0},{5,1},{6,2},{7,3},{8,12},{9,13},{10,... | collective-permute-start | bytes 1769480 | tf_op jit(solution)/shard_map/ppermute | solution.py:45
  126.4 31.0 %collective-permute-start.30 = (bf16[2,4,96,768]{3,2,1,0:T(8,128)(2,1)}, bf16[2,4,96,768]{3,2,1,0:T(8,128)(2,1)S(1)}, u32[]{:S(2)}, u32[]{:S(2)}) collective-permute-start(bf16[2,4,96,768]{3,2,1,0:T(8,128)(2,1)} %get-tuple-element.115), channel_id=1, source_target_pairs={{0,2},{1,3},{2,0},{3,1},{4,6},{5,7},{6,4},{7,5},{8,10},{9,11},{10,... | collective-permute-start | bytes 3538952 | tf_op jit(solution)/shard_map/ppermute | solution.py:45
  143.2 28.8 %collective-permute-start.29 = (bf16[2,4,96,768]{3,2,1,0:T(8,128)(2,1)}, bf16[2,4,96,768]{3,2,1,0:T(8,128)(2,1)S(1)}, u32[]{:S(2)}, u32[]{:S(2)}) collective-permute-start(bf16[2,4,96,768]{3,2,1,0:T(8,128)(2,1)} %get-tuple-element.112), channel_id=1, source_target_pairs={{0,4},{1,5},{2,6},{3,7},{4,0},{5,1},{6,2},{7,3},{8,12},{9,13},{10,... | collective-permute-start | bytes 3538952 | tf_op jit(solution)/shard_map/ppermute | solution.py:45
  157.2 14.9 %collective-permute-start.32 = (bf16[2,2,4,48,384]{4,3,2,1,0:T(8,128)(2,1)}, bf16[2,2,4,48,384]{4,3,2,1,0:T(8,128)(2,1)S(1)}, u32[]{:S(2)}, u32[]{:S(2)}) collective-permute-start(bf16[2,2,4,48,384]{4,3,2,1,0:T(8,128)(2,1)} %get-tuple-element.117), channel_id=1, source_target_pairs={{0,1},{1,0},{2,3},{3,2},{4,5},{5,4},{6,7},{7,6},{8,9},{9,8},{10,11... | collective-permute-start | bytes 1769480 | tf_op jit(solution)/shard_map/ppermute | solution.py:45
  157.4 14.7 %collective-permute-start.31 = (bf16[256,768]{1,0:T(8,128)(2,1)}, bf16[256,768]{1,0:T(8,128)(2,1)S(1)}, u32[]{:S(2)}, u32[]{:S(2)}) collective-permute-start(bf16[256,768]{1,0:T(8,128)(2,1)} %get-tuple-element.116), channel_id=1, source_target_pairs={{2,0},{3,1},{6,4},{7,5},{10,8},{11,9},{14,12},{15,13},{18,16},{19,... | collective-permute-start | bytes 1179656 | tf_op jit(solution)/shard_map/ppermute | solution.py:907
  173.2 16.3 %collective-permute-start.34 = (bf16[4,96,768]{2,1,0:T(8,128)(2,1)S(1)}, bf16[4,96,768]{2,1,0:T(8,128)(2,1)S(1)}, u32[]{:S(2)}, u32[]{:S(2)}) collective-permute-start(bf16[4,96,768]{2,1,0:T(8,128)(2,1)S(1)} %get-tuple-element.178), channel_id=1, source_target_pairs={{0,2},{1,3},{2,0},{3,1},{4,6},{5,7},{6,4},{7,5},{8,10},{9,11},{10,... | collective-permute-start | bytes 1769480 | tf_op jit(solution)/shard_map/ppermute | solution.py:45
  176.2 15.1 %collective-permute-start.33 = (bf16[4,96,768]{2,1,0:T(8,128)(2,1)S(1)}, bf16[4,96,768]{2,1,0:T(8,128)(2,1)S(1)}, u32[]{:S(2)}, u32[]{:S(2)}) collective-permute-start(bf16[4,96,768]{2,1,0:T(8,128)(2,1)S(1)} %get-tuple-element.176), channel_id=1, source_target_pairs={{0,4},{1,5},{2,6},{3,7},{4,0},{5,1},{6,2},{7,3},{8,12},{9,13},{10,... | collective-permute-start | bytes 1769480 | tf_op jit(solution)/shard_map/ppermute | solution.py:45
  196.3 20.1 %collective-permute-start.37 = (bf16[2,4,112,384]{3,2,1,0:T(8,128)(2,1)S(1)}, bf16[2,4,112,384]{3,2,1,0:T(8,128)(2,1)S(1)}, u32[]{:S(2)}, u32[]{:S(2)}) collective-permute-start(bf16[2,4,112,384]{3,2,1,0:T(8,128)(2,1)S(1)} %pad_maximum_fusion.3), channel_id=1, source_target_pairs={{0,4},{1,5},{2,6},{3,7},{4,0},{5,1},{6,2},{7,3},{8,12},{9,13},{10,... | collective-permute-start | bytes 2064392 | tf_op jit(solution)/shard_map/ppermute | solution.py:45
  197.2 20.2 %collective-permute-start.38 = (bf16[2,4,96,384]{3,2,1,0:T(8,128)(2,1)S(1)}, bf16[2,4,96,384]{3,2,1,0:T(8,128)(2,1)S(1)}, u32[]{:S(2)}, u32[]{:S(2)}) collective-permute-start(bf16[2,4,96,384]{3,2,1,0:T(8,128)(2,1)S(1)} %get-tuple-element.174), channel_id=1, source_target_pairs={{0,2},{1,3},{2,0},{3,1},{4,6},{5,7},{6,4},{7,5},{8,10},{9,11},{10,... | collective-permute-start | bytes 1769480 | tf_op jit(solution)/shard_map/ppermute | solution.py:45
  198.6 24.1 %collective-permute-start.47 = (bf16[192,768]{1,0:T(8,128)(2,1)S(1)}, bf16[192,768]{1,0:T(8,128)(2,1)S(1)}, u32[]{:S(2)}, u32[]{:S(2)}) collective-permute-start(bf16[192,768]{1,0:T(8,128)(2,1)S(1)} %pad_maximum_fusion.9), channel_id=1, source_target_pairs={{0,8},{1,9},{2,10},{3,11},{4,12},{5,13},{6,14},{7,15},{8,0},{9,1},... | collective-permute-start | bytes 884744 | tf_op jit(solution)/shard_map/ppermute | solution.py:45
  199.2 23.5 %collective-permute-start.48 = (bf16[192,768]{1,0:T(8,128)(2,1)S(1)}, bf16[192,768]{1,0:T(8,128)(2,1)S(1)}, u32[]{:S(2)}, u32[]{:S(2)}) collective-permute-start(bf16[192,768]{1,0:T(8,128)(2,1)S(1)} %pad_maximum_fusion.10), channel_id=1, source_target_pairs={{0,16},{1,17},{2,18},{3,19},{4,20},{5,21},{6,22},{7,23},{8,24},{9,... | collective-permute-start | bytes 884744 | tf_op jit(solution)/shard_map/ppermute | solution.py:45
  201.9 21.0 %collective-permute-start.49 = (bf16[192,768]{1,0:T(8,128)(2,1)S(1)}, bf16[192,768]{1,0:T(8,128)(2,1)S(1)}, u32[]{:S(2)}, u32[]{:S(2)}) collective-permute-start(bf16[192,768]{1,0:T(8,128)(2,1)S(1)} %pad_maximum_fusion.11), channel_id=1, source_target_pairs={{0,24},{1,25},{2,26},{3,27},{4,28},{5,29},{6,30},{7,31},{8,16},{9,... | collective-permute-start | bytes 884744 | tf_op jit(solution)/shard_map/ppermute | solution.py:45
  229.7 18.2 %collective-permute-start.44 = (bf16[208,384]{1,0:T(8,128)(2,1)S(1)}, bf16[208,384]{1,0:T(8,128)(2,1)S(1)}, u32[]{:S(2)}, u32[]{:S(2)}) collective-permute-start(bf16[208,384]{1,0:T(8,128)(2,1)S(1)} %pad_maximum_fusion.14), channel_id=1, source_target_pairs={{0,16},{1,17},{2,18},{3,19},{4,20},{5,21},{6,22},{7,23},{8,24},{9,... | collective-permute-start | bytes 479240 | tf_op jit(solution)/shard_map/ppermute | solution.py:45
  (64 other events, 551.9 us)

commit v8 on v7

--- a/solution.py
+++ b/solution.py
@@ -377,14 +377,17 @@
         wait_wide(source, sems, j)
 
 
-def up_kernel(table, order, info, own, other, seed_t, *refs):
+def up_kernel(table, order, info, own, other, seed_in, *refs):
     parts = refs[0:4]
     hidden_out, slope_out = refs[4:6]
     keep = refs[6:8]
-    w_up, grad, hidden, slope, sems, out_sems, side_sems = refs[8:]
+    w_up, grad, hidden, slope, seed_t, sems, out_sems, side_sems = refs[8:]
+    seed_copy = pltpu.make_async_copy(seed_in, seed_t, side_sems.at[2])
+    seed_copy.start()
     for copy in wide_copies(info, table, parts, w_up, sems):
         copy.start()
     outs = list(wide_out(info, order, keep, grad, out_sems))
+    seed_copy.wait()
     for j in range(2):
         wait_wide(w_up, sems, j)
 
@@ -860,10 +863,14 @@
         functools.partial(up_kernel, table_wide, BACK_DOWN),
         "up",
         [info, normed, normed_other, seed_t] + up_parts,
-        [SCALARS, FULL, FREE, FULL] + [ANY] * 4,
+        [SCALARS, FULL, FREE, ANY] + [ANY] * 4,
         [shape((2, SEGL, HALF))] * 2 + [shape(piece_dims(BACK_DOWN)[1:] + (96, D))] * 2,
         [ANY] * 4,
-        [VMEM(WIDE, BF16)] * 2 + [VMEM((2, SEGL, HALF), BF16)] * 2 + [DMA((2,))] * 3,
+        [VMEM(WIDE, BF16)] * 2
+        + [VMEM((2, SEGL, HALF), BF16)] * 2
+        + [VMEM((D, 2 * SEGL), BF16)]
+        + [DMA((2,))] * 2
+        + [DMA((3,))],
         cost=12.0,
         vmem=22,
     )

time: 254 us -> 254 us (level)
  no operation moved by 1% of the time
where the time goes in v8:
time: 254 us; the launch traced here: 253 us
  Pallas kernels  108 us (43%)
  waiting for transfers between devices  58.4 us (23%)
  starting transfers between devices  56.7 us (22%)
  local copies, waits for them, and re-layouts  15.6 us (6%)
  other arithmetic  11.3 us (4%)
  between operations  2.85 us (1%)
    pallas_call x9, Pallas kernels, run(): pl.pallas_call(body, name=name, out_shape=tuple((pltpu.HBM(out.shape, out...  108 us
    ppermute x48, waiting for transfers between devices, xor_permute(): return lax.ppermute(value, AXES, pairs)  58.4 us
    ppermute x48, starting transfers between devices, xor_permute(): return lax.ppermute(value, AXES, pairs)  51.7 us
    unnamed x81, local copies, waits for them, and re-layouts  7.81 us
  transfers between devices with their start and end apart: 50, of which 16 were waited for; matrix products, arithmetic and copies ran while one was open for 6% of the time, Pallas kernels for 43%

profile of v8, /device:TPU:0, one launch (start us, length us, event | category | flops | bytes accessed | tf_op | source)
XLA Modules:
  0.0 253.1 jit_solution(11374683744818057638)
XLA Ops:
  9.4 4.7 %collective-permute-start.5 = (bf16[208,384]{1,0:T(8,128)(2,1)S(1)}, bf16[208,384]{1,0:T(8,128)(2,1)S(1)}, u32[]{:S(2)}, u32[]{:S(2)}) collective-permute-start(bf16[208,384]{1,0:T(8,128)(2,1)S(1)} %fusion.43), channel_id=1, source_target_pairs={{0,24},{1,25},{2,26},{3,27},{4,28},{5,29},{6,30},{7,31},{8,16},{9,... | collective-permute-start | bytes 479240 | tf_op jit(solution)/shard_map/ppermute | solution.py:45
  17.6 7.5 %collective-permute-done.3 = bf16[208,384]{1,0:T(8,128)(2,1)S(1)} collective-permute-done((bf16[208,384]{1,0:T(8,128)(2,1)S(1)}, bf16[208,384]{1,0:T(8,128)(2,1)S(1)}, u32[]{:S(2)}, u32[]{:S(2)}) %collective-permute-start.3) | collective-permute-done | bytes 159776 | tf_op jit(solution)/shard_map/ppermute | solution.py:45
  25.1 3.2 %collective-permute-done.4 = bf16[208,384]{1,0:T(8,128)(2,1)S(1)} collective-permute-done((bf16[208,384]{1,0:T(8,128)(2,1)S(1)}, bf16[208,384]{1,0:T(8,128)(2,1)S(1)}, u32[]{:S(2)}, u32[]{:S(2)}) %collective-permute-start.4) | collective-permute-done | bytes 159776 | tf_op jit(solution)/shard_map/ppermute | solution.py:45
  31.6 6.3 %collective-permute-done.9 = bf16[4,112,384]{2,1,0:T(8,128)(2,1)S(1)} collective-permute-done((bf16[4,112,384]{2,1,0:T(8,128)(2,1)S(1)}, bf16[4,112,384]{2,1,0:T(8,128)(2,1)S(1)}, u32[]{:S(2)}, u32[]{:S(2)}) %collective-permute-start.9) | collective-permute-done | bytes 344096 | tf_op jit(solution)/shard_map/ppermute | solution.py:45
  46.3 10.0 %collective-permute-done.15.refs_5_.refs_1_ = bf16[2,4,112,384]{3,2,1,0:T(8,128)(2,1)S(1)} collective-permute-done((bf16[2,4,112,384]{3,2,1,0:T(8,128)(2,1)S(1)}, bf16[2,4,112,384]{3,2,1,0:T(8,128)(2,1)S(1)}, u32[]{:S(2)}, u32[]{:S(2)}) %collective-permute-start.15) | collective-permute-done | bytes 688160 | tf_op jit(solution)/shard_map/ppermute | solution.py:45
  62.4 9.3 %qkv.1 = (bf16[512,768]{1,0:T(8,128)(2,1)}, bf16[512,768]{1,0:T(8,128)(2,1)}, bf16[512,768]{1,0:T(8,128)(2,1)}, bf16[512,768]{1,0:T(8,128)(2,1)}, bf16[256,768]{...) custom-call(s32[6]{0:T(128)S(1)} %stack.130.info, bf16[2,256,768]{2,1,0:T(8,128)(2,1)} %own.1, ...), custom_call_target="tpu_custom_call" | custom-call | flops 1200000000 | bytes 1000000 | tf_op jit(solution)/shard_map/qkv/pallas_call | solution.py:677
  71.7 3.1 %collective-permute-done.17.refs_1_.refs_5_ = bf16[4,96,768]{2,1,0:T(8,128)(2,1)S(1)} collective-permute-done((bf16[4,96,768]{2,1,0:T(8,128)(2,1)S(1)}, bf16[4,96,768]{2,1,0:T(8,128)(2,1)S(1)}, u32[]{:S(2)}, u32[]{:S(2)}) %collective-permute-start.17) | collective-permute-done | bytes 589856 | tf_op jit(solution)/shard_map/ppermute | solution.py:45
  76.3 3.5 %collective-permute-start.19 = (bf16[256,768]{1,0:T(8,128)(2,1)}, bf16[256,768]{1,0:T(8,128)(2,1)S(1)}, u32[]{:S(2)}, u32[]{:S(2)}) collective-permute-start(bf16[256,768]{1,0:T(8,128)(2,1)} %get-tuple-element.93), channel_id=1, source_target_pairs={{0,2},{1,3},{4,6},{5,7},{8,10},{9,11},{12,14},{13,15},{16,18},{17,... | collective-permute-start | bytes 1179656 | tf_op jit(solution)/shard_map/ppermute | solution.py:811
  84.3 13.1 %attend.1 = (bf16[12,512,512]{2,1,0:T(8,128)(2,1)}, f32[768,512]{1,0:T(8,128)}, bf16[12,256,512]{2,1,0:T(8,128)(2,1)}) custom-call(s32[6]{0:T(128)S(1)} %stack.130.info, bf16[512,768]{1,0:T(8,128)(2,1)} %get-tuple-element.87.q, bf16[512,768]{1,0:T(8,128)(2,1)} %get-tuple-element.88.k, bf16[512,768]{1,0:T(8,128)(2,1)} %get-tuple-element.89.v, ...), custom_call_target="tpu_custom_call" | custom-call | flops 2400000000 | bytes 1000000 | tf_op jit(solution)/shard_map/attend/pallas_call | solution.py:677
  98.2 8.9 %recall.1 = (bf16[512,768]{1,0:T(8,128)(2,1)}, f32[512,768]{1,0:T(8,128)}, bf16[512,768]{1,0:T(8,128)(2,1)}) custom-call(s32[6]{0:T(128)S(1)} %stack.130.info, bf16[12,256,512]{2,1,0:T(8,128)(2,1)} %get-tuple-element.92.dens_t, bf16[256,768]{1,0:T(8,128)(2,1)} %copy-done.12, f32[768,512]{1,0:T(8,128)} %get-tuple-element.94.local_t, ...), custom_call_target="tpu_custom_call" | custom-call | flops 1400000000 | bytes 1000000 | tf_op jit(solution)/shard_map/recall/pallas_call | solution.py:677
  107.3 3.7 %collective-permute-done.26.refs_2_.refs_10_ = bf16[4,96,768]{2,1,0:T(8,128)(2,1)S(1)} collective-permute-done((bf16[4,96,768]{2,1,0:T(8,128)(2,1)S(1)}, bf16[4,96,768]{2,1,0:T(8,128)(2,1)S(1)}, u32[]{:S(2)}, u32[]{:S(2)}) %collective-permute-start.26) | collective-permute-done | bytes 589856 | tf_op jit(solution)/shard_map/ppermute | solution.py:45
  112.5 14.1 %up.1 = (bf16[2,512,1536]{2,1,0:T(8,128)(2,1)}, bf16[2,512,1536]{2,1,0:T(8,128)(2,1)}, bf16[2,4,96,768]{3,2,1,0:T(8,128)(2,1)}, bf16[2,4,96,768]{3,2,1,0:T(8,128)(2,1)}) custom-call(s32[6]{0:T(128)S(1)} %stack.130.info, bf16[512,768]{1,0:T(8,128)(2,1)} %get-tuple-element.98.own, bf16[512,768]{1,0:T(8,128)(2,1)S(1)} %collective-permute-done.20.other, ...), custom_call_target="tpu_custom_call" | custom-call | flops 2400000000 | bytes 1000000 | tf_op jit(solution)/shard_map/up/pallas_call | solution.py:677
  127.8 15.6 %down.1 = (bf16[2,4,96,768]{3,2,1,0:T(8,128)(2,1)}, bf16[2,4,96,768]{3,2,1,0:T(8,128)(2,1)}, f32[512,768]{1,0:T(8,128)}, bf16[512,768]{1,0:T(8,128)(2,1)}) custom-call(s32[6]{0:T(128)S(1)} %stack.130.info, bf16[2,512,768]{2,1,0:T(8,128)(2,1)} %copy-done.3, bf16[512,768]{1,0:T(8,128)(2,1)} %get-tuple-element.98.own, ...), custom_call_target="tpu_custom_call" | custom-call | flops 3000000000 | bytes 1000000 | tf_op jit(solution)/shard_map/down/pallas_call | solution.py:677
  145.9 11.4 %mix_back.1 = (f32[512,768]{1,0:T(8,128)}, bf16[512,768]{1,0:T(8,128)(2,1)}, bf16[256,768]{1,0:T(8,128)(2,1)}, f32[1,768]{1,0:T(1,128)}, f32[1,768]{1,0:T(1,128)...) custom-call(s32[6]{0:T(128)S(1)} %stack.130.info, f32[512,768]{1,0:T(8,128)} %get-tuple-element.106.own, ...), custom_call_target="tpu_custom_call" | custom-call | flops 1200000000 | bytes 1000000 | tf_op jit(solution)/shard_map/mix_back/pallas_call | solution.py:677
  159.1 13.2 %attend_back.1 = (bf16[512,768]{1,0:T(8,128)(2,1)}, bf16[512,768]{1,0:T(8,128)(2,1)}, f32[512,768]{1,0:T(8,128)}, f32[2,768]{1,0:T(2,128)}) custom-call(bf16[12,512,512]{2,1,0:T(8,128)(2,1)} %get-tuple-element.91.attn_t, bf16[512,768]{1,0:T(8,128)(2,1)} %get-tuple-element.87.q, bf16[512,768]{1,0:T(8,128)(2,1)} %get-tuple-element.88.k, ...), custom_call_target="tpu_custom_call" | custom-call | flops 3200000000 | bytes 1000000 | tf_op jit(solution)/shard_map/attend_back/pallas_call | solution.py:677
  173.4 2.7 %collective-permute-start.34 = (bf16[4,96,768]{2,1,0:T(8,128)(2,1)S(1)}, bf16[4,96,768]{2,1,0:T(8,128)(2,1)S(1)}, u32[]{:S(2)}, u32[]{:S(2)}) collective-permute-start(bf16[4,96,768]{2,1,0:T(8,128)(2,1)S(1)} %get-tuple-element.178), channel_id=1, source_target_pairs={{0,2},{1,3},{2,0},{3,1},{4,6},{5,7},{6,4},{7,5},{8,10},{9,11},{10,... | collective-permute-start | bytes 1769480 | tf_op jit(solution)/shard_map/ppermute | solution.py:45
  177.0 9.6 %qkv_grad.1 = (bf16[2,2,4,96,384]{4,3,2,1,0:T(8,128)(2,1)}, bf16[2,2,4,96,384]{4,3,2,1,0:T(8,128)(2,1)}, bf16[2,2,4,64,384]{4,3,2,1,0:T(8,128)(2,1)}, bf16[2,2,4...) custom-call(s32[6]{0:T(128)S(1)} %stack.130.info, bf16[512,768]{1,0:T(8,128)(2,1)} %get-tuple-element.95.x, ...), custom_call_target="tpu_custom_call" | custom-call | flops 1200000000 | bytes 1000000 | tf_op jit(solution)/shard_map/qkv_grad/pallas_call | solution.py:677
  186.5 3.2 %collective-permute-done.34 = bf16[4,96,768]{2,1,0:T(8,128)(2,1)S(1)} collective-permute-done((bf16[4,96,768]{2,1,0:T(8,128)(2,1)S(1)}, bf16[4,96,768]{2,1,0:T(8,128)(2,1)S(1)}, u32[]{:S(2)}, u32[]{:S(2)}) %collective-permute-start.34) | collective-permute-done | bytes 589856 | tf_op jit(solution)/shard_map/ppermute | solution.py:45
  199.4 2.6 %collective-permute-start.48 = (bf16[192,768]{1,0:T(8,128)(2,1)S(1)}, bf16[192,768]{1,0:T(8,128)(2,1)S(1)}, u32[]{:S(2)}, u32[]{:S(2)}) collective-permute-start(bf16[192,768]{1,0:T(8,128)(2,1)S(1)} %pad_maximum_fusion.10), channel_id=1, source_target_pairs={{0,16},{1,17},{2,18},{3,19},{4,20},{5,21},{6,22},{7,23},{8,24},{9,... | collective-permute-start | bytes 884744 | tf_op jit(solution)/shard_map/ppermute | solution.py:45
  203.4 13.1 %finish.1 = (f32[256,768]{1,0:T(8,128)}, bf16[256,768]{1,0:T(8,128)(2,1)}, f32[2,256,768]{2,1,0:T(8,128)}, bf16[2,256,768]{2,1,0:T(8,128)(2,1)}) custom-call(s32[6]{0:T(128)S(1)} %stack.130.info, bf16[512,768]{1,0:T(8,128)(2,1)} %get-tuple-element.135.dq, bf16[512,768]{1,0:T(8,128)(2,1)} %get-tuple-element.113.dk, bf16[512,768]{1,0:T(8,128)(2,1)} %get-tuple-element.136.dv, ...), custom_call_target="tpu_custom_call" | custom-call | flops 2800000000 | bytes 1000000 | tf_op jit(solution)/shard_map/finish/pallas_call | solution.py:677
  217.6 5.3 %collective-permute-done.48 = bf16[192,768]{1,0:T(8,128)(2,1)S(1)} collective-permute-done((bf16[192,768]{1,0:T(8,128)(2,1)S(1)}, bf16[192,768]{1,0:T(8,128)(2,1)S(1)}, u32[]{:S(2)}, u32[]{:S(2)}) %collective-permute-start.48) | collective-permute-done | bytes 294944 | tf_op jit(solution)/shard_map/ppermute | solution.py:45
  226.2 3.6 %collective-permute-done.41 = bf16[4,96,384]{2,1,0:T(8,128)(2,1)S(1)} collective-permute-done((bf16[4,96,384]{2,1,0:T(8,128)(2,1)S(1)}, bf16[4,96,384]{2,1,0:T(8,128)(2,1)S(1)}, u32[]{:S(2)}, u32[]{:S(2)}) %collective-permute-start.41) | collective-permute-done | bytes 294944 | tf_op jit(solution)/shard_map/ppermute | solution.py:45
  229.9 7.6 %collective-permute-start.44 = (bf16[208,384]{1,0:T(8,128)(2,1)S(1)}, bf16[208,384]{1,0:T(8,128)(2,1)S(1)}, u32[]{:S(2)}, u32[]{:S(2)}) collective-permute-start(bf16[208,384]{1,0:T(8,128)(2,1)S(1)} %pad_maximum_fusion.14), channel_id=1, source_target_pairs={{0,16},{1,17},{2,18},{3,19},{4,20},{5,21},{6,22},{7,23},{8,24},{9,... | collective-permute-start | bytes 479240 | tf_op jit(solution)/shard_map/ppermute | solution.py:45
  243.2 4.9 %collective-permute-done.43 = bf16[208,384]{1,0:T(8,128)(2,1)S(1)} collective-permute-done((bf16[208,384]{1,0:T(8,128)(2,1)S(1)}, bf16[208,384]{1,0:T(8,128)(2,1)S(1)}, u32[]{:S(2)}, u32[]{:S(2)}) %collective-permute-start.43) | collective-permute-done | bytes 159776 | tf_op jit(solution)/shard_map/ppermute | solution.py:45
  (233 shorter events, 70.1 us)
Async XLA Ops:
  9.4 15.6 %collective-permute-start.5 = (bf16[208,384]{1,0:T(8,128)(2,1)S(1)}, bf16[208,384]{1,0:T(8,128)(2,1)S(1)}, u32[]{:S(2)}, u32[]{:S(2)}) collective-permute-start(bf16[208,384]{1,0:T(8,128)(2,1)S(1)} %fusion.43), channel_id=1, source_target_pairs={{0,24},{1,25},{2,26},{3,27},{4,28},{5,29},{6,30},{7,31},{8,16},{9,... | collective-permute-start | bytes 479240 | tf_op jit(solution)/shard_map/ppermute | solution.py:45
  38.8 17.5 %collective-permute-start.15 = (bf16[2,4,112,384]{3,2,1,0:T(8,128)(2,1)S(1)}, bf16[2,4,112,384]{3,2,1,0:T(8,128)(2,1)S(1)}, u32[]{:S(2)}, u32[]{:S(2)}) collective-permute-start(bf16[2,4,112,384]{3,2,1,0:T(8,128)(2,1)S(1)} %pad_maximum_fusion.2.refs_4_.refs_0_), channel_id=1, source_target_pairs={{0,4},{1,5},{2,6},{3,7},{4,0},{5,1},{6,2},{7,3},{8,12},{9,13},{10,... | collective-permute-start | bytes 2064392 | tf_op jit(solution)/shard_map/ppermute | solution.py:45
  40.3 16.1 %collective-permute-start.7 = (bf16[2,4,96,384]{3,2,1,0:T(8,128)(2,1)S(1)}, bf16[2,4,96,384]{3,2,1,0:T(8,128)(2,1)S(1)}, u32[]{:S(2)}, u32[]{:S(2)}) collective-permute-start(bf16[2,4,96,384]{3,2,1,0:T(8,128)(2,1)S(1)} %pad_maximum_fusion.4.refs_0_), channel_id=1, source_target_pairs={{0,2},{1,3},{2,0},{3,1},{4,6},{5,7},{6,4},{7,5},{8,10},{9,11},{10,... | collective-permute-start | bytes 1769480 | tf_op jit(solution)/shard_map/ppermute | solution.py:45
  41.9 14.5 %collective-permute-start.13 = (bf16[96,768]{1,0:T(8,128)(2,1)S(1)}, bf16[96,768]{1,0:T(8,128)(2,1)S(1)}, u32[]{:S(2)}, u32[]{:S(2)}) collective-permute-start(bf16[96,768]{1,0:T(8,128)(2,1)S(1)} %copy-done.31), channel_id=1, source_target_pairs={{0,24},{1,25},{2,26},{3,27},{4,28},{5,29},{6,30},{7,31},{8,16},{9,... | collective-permute-start | bytes 442376 | tf_op jit(solution)/shard_map/ppermute | solution.py:45
  59.4 15.4 %collective-permute-start.17 = (bf16[4,96,768]{2,1,0:T(8,128)(2,1)S(1)}, bf16[4,96,768]{2,1,0:T(8,128)(2,1)S(1)}, u32[]{:S(2)}, u32[]{:S(2)}) collective-permute-start(bf16[4,96,768]{2,1,0:T(8,128)(2,1)S(1)} %pad_maximum_fusion.5.refs_0_.refs_4_), channel_id=1, source_target_pairs={{0,2},{1,3},{2,0},{3,1},{4,6},{5,7},{6,4},{7,5},{8,10},{9,11},{10,... | collective-permute-start | bytes 1769480 | tf_op jit(solution)/shard_map/ppermute | solution.py:45
  60.9 21.5 %collective-permute-start.18 = (bf16[4,96,768]{2,1,0:T(8,128)(2,1)S(1)}, bf16[4,96,768]{2,1,0:T(8,128)(2,1)S(1)}, u32[]{:S(2)}, u32[]{:S(2)}) collective-permute-start(bf16[4,96,768]{2,1,0:T(8,128)(2,1)S(1)} %pad_maximum_fusion.5.refs_0_.refs_4_), channel_id=1, source_target_pairs={{0,4},{1,5},{2,6},{3,7},{4,0},{5,1},{6,2},{7,3},{8,12},{9,13},{10,... | collective-permute-start | bytes 1769480 | tf_op jit(solution)/shard_map/ppermute | solution.py:45
  74.8 22.7 %collective-permute-start.21 = (bf16[4,96,768]{2,1,0:T(8,128)(2,1)S(1)}, bf16[4,96,768]{2,1,0:T(8,128)(2,1)S(1)}, u32[]{:S(2)}, u32[]{:S(2)}) collective-permute-start(bf16[4,96,768]{2,1,0:T(8,128)(2,1)S(1)} %collective-permute-done.17.refs_1_.refs_5_), channel_id=1, source_target_pairs={{0,4},{1,5},{2,6},{3,7},{4,0},{5,1},{6,2},{7,3},{8,12},{9,13},{10,... | collective-permute-start | bytes 1769480 | tf_op jit(solution)/shard_map/ppermute | solution.py:45
  76.3 21.1 %collective-permute-start.19 = (bf16[256,768]{1,0:T(8,128)(2,1)}, bf16[256,768]{1,0:T(8,128)(2,1)S(1)}, u32[]{:S(2)}, u32[]{:S(2)}) collective-permute-start(bf16[256,768]{1,0:T(8,128)(2,1)} %get-tuple-element.93), channel_id=1, source_target_pairs={{0,2},{1,3},{4,6},{5,7},{8,10},{9,11},{12,14},{13,15},{16,18},{17,... | collective-permute-start | bytes 1179656 | tf_op jit(solution)/shard_map/ppermute | solution.py:811
  79.8 17.6 %collective-permute-start.24 = (bf16[96,768]{1,0:T(8,128)(2,1)S(1)}, bf16[96,768]{1,0:T(8,128)(2,1)S(1)}, u32[]{:S(2)}, u32[]{:S(2)}) collective-permute-start(bf16[96,768]{1,0:T(8,128)(2,1)S(1)} %bitcast.252), channel_id=1, source_target_pairs={{0,24},{1,25},{2,26},{3,27},{4,28},{5,29},{6,30},{7,31},{8,16},{9,... | collective-permute-start | bytes 442376 | tf_op jit(solution)/shard_map/ppermute | solution.py:45
  82.4 15.1 %collective-permute-start.23 = (bf16[96,768]{1,0:T(8,128)(2,1)S(1)}, bf16[96,768]{1,0:T(8,128)(2,1)S(1)}, u32[]{:S(2)}, u32[]{:S(2)}) collective-permute-start(bf16[96,768]{1,0:T(8,128)(2,1)S(1)} %bitcast.253), channel_id=1, source_target_pairs={{0,16},{1,17},{2,18},{3,19},{4,20},{5,21},{6,22},{7,23},{8,24},{9,... | collective-permute-start | bytes 442376 | tf_op jit(solution)/shard_map/ppermute | solution.py:45
  82.4 15.1 %collective-permute-start.22 = (bf16[96,768]{1,0:T(8,128)(2,1)S(1)}, bf16[96,768]{1,0:T(8,128)(2,1)S(1)}, u32[]{:S(2)}, u32[]{:S(2)}) collective-permute-start(bf16[96,768]{1,0:T(8,128)(2,1)S(1)} %bitcast.254), channel_id=1, source_target_pairs={{0,8},{1,9},{2,10},{3,11},{4,12},{5,13},{6,14},{7,15},{8,0},{9,1},... | collective-permute-start | bytes 442376 | tf_op jit(solution)/shard_map/ppermute | solution.py:45
  111.0 16.0 %collective-permute-start.27 = (bf16[4,96,768]{2,1,0:T(8,128)(2,1)S(1)}, bf16[4,96,768]{2,1,0:T(8,128)(2,1)S(1)}, u32[]{:S(2)}, u32[]{:S(2)}) collective-permute-start(bf16[4,96,768]{2,1,0:T(8,128)(2,1)S(1)} %collective-permute-done.25.refs_1_.refs_9_), channel_id=1, source_target_pairs={{0,4},{1,5},{2,6},{3,7},{4,0},{5,1},{6,2},{7,3},{8,12},{9,13},{10,... | collective-permute-start | bytes 1769480 | tf_op jit(solution)/shard_map/ppermute | solution.py:45
  126.6 31.0 %collective-permute-start.30 = (bf16[2,4,96,768]{3,2,1,0:T(8,128)(2,1)}, bf16[2,4,96,768]{3,2,1,0:T(8,128)(2,1)S(1)}, u32[]{:S(2)}, u32[]{:S(2)}) collective-permute-start(bf16[2,4,96,768]{3,2,1,0:T(8,128)(2,1)} %get-tuple-element.115), channel_id=1, source_target_pairs={{0,2},{1,3},{2,0},{3,1},{4,6},{5,7},{6,4},{7,5},{8,10},{9,11},{10,... | collective-permute-start | bytes 3538952 | tf_op jit(solution)/shard_map/ppermute | solution.py:45
  143.4 28.8 %collective-permute-start.29 = (bf16[2,4,96,768]{3,2,1,0:T(8,128)(2,1)}, bf16[2,4,96,768]{3,2,1,0:T(8,128)(2,1)S(1)}, u32[]{:S(2)}, u32[]{:S(2)}) collective-permute-start(bf16[2,4,96,768]{3,2,1,0:T(8,128)(2,1)} %get-tuple-element.112), channel_id=1, source_target_pairs={{0,4},{1,5},{2,6},{3,7},{4,0},{5,1},{6,2},{7,3},{8,12},{9,13},{10,... | collective-permute-start | bytes 3538952 | tf_op jit(solution)/shard_map/ppermute | solution.py:45
  157.3 14.9 %collective-permute-start.32 = (bf16[2,2,4,48,384]{4,3,2,1,0:T(8,128)(2,1)}, bf16[2,2,4,48,384]{4,3,2,1,0:T(8,128)(2,1)S(1)}, u32[]{:S(2)}, u32[]{:S(2)}) collective-permute-start(bf16[2,2,4,48,384]{4,3,2,1,0:T(8,128)(2,1)} %get-tuple-element.117), channel_id=1, source_target_pairs={{0,1},{1,0},{2,3},{3,2},{4,5},{5,4},{6,7},{7,6},{8,9},{9,8},{10,11... | collective-permute-start | bytes 1769480 | tf_op jit(solution)/shard_map/ppermute | solution.py:45
  157.5 14.7 %collective-permute-start.31 = (bf16[256,768]{1,0:T(8,128)(2,1)}, bf16[256,768]{1,0:T(8,128)(2,1)S(1)}, u32[]{:S(2)}, u32[]{:S(2)}) collective-permute-start(bf16[256,768]{1,0:T(8,128)(2,1)} %get-tuple-element.116), channel_id=1, source_target_pairs={{2,0},{3,1},{6,4},{7,5},{10,8},{11,9},{14,12},{15,13},{18,16},{19,... | collective-permute-start | bytes 1179656 | tf_op jit(solution)/shard_map/ppermute | solution.py:914
  173.4 16.3 %collective-permute-start.34 = (bf16[4,96,768]{2,1,0:T(8,128)(2,1)S(1)}, bf16[4,96,768]{2,1,0:T(8,128)(2,1)S(1)}, u32[]{:S(2)}, u32[]{:S(2)}) collective-permute-start(bf16[4,96,768]{2,1,0:T(8,128)(2,1)S(1)} %get-tuple-element.178), channel_id=1, source_target_pairs={{0,2},{1,3},{2,0},{3,1},{4,6},{5,7},{6,4},{7,5},{8,10},{9,11},{10,... | collective-permute-start | bytes 1769480 | tf_op jit(solution)/shard_map/ppermute | solution.py:45
  176.4 15.1 %collective-permute-start.33 = (bf16[4,96,768]{2,1,0:T(8,128)(2,1)S(1)}, bf16[4,96,768]{2,1,0:T(8,128)(2,1)S(1)}, u32[]{:S(2)}, u32[]{:S(2)}) collective-permute-start(bf16[4,96,768]{2,1,0:T(8,128)(2,1)S(1)} %get-tuple-element.176), channel_id=1, source_target_pairs={{0,4},{1,5},{2,6},{3,7},{4,0},{5,1},{6,2},{7,3},{8,12},{9,13},{10,... | collective-permute-start | bytes 1769480 | tf_op jit(solution)/shard_map/ppermute | solution.py:45
  196.5 20.1 %collective-permute-start.37 = (bf16[2,4,112,384]{3,2,1,0:T(8,128)(2,1)S(1)}, bf16[2,4,112,384]{3,2,1,0:T(8,128)(2,1)S(1)}, u32[]{:S(2)}, u32[]{:S(2)}) collective-permute-start(bf16[2,4,112,384]{3,2,1,0:T(8,128)(2,1)S(1)} %pad_maximum_fusion.3), channel_id=1, source_target_pairs={{0,4},{1,5},{2,6},{3,7},{4,0},{5,1},{6,2},{7,3},{8,12},{9,13},{10,... | collective-permute-start | bytes 2064392 | tf_op jit(solution)/shard_map/ppermute | solution.py:45
  197.3 20.2 %collective-permute-start.38 = (bf16[2,4,96,384]{3,2,1,0:T(8,128)(2,1)S(1)}, bf16[2,4,96,384]{3,2,1,0:T(8,128)(2,1)S(1)}, u32[]{:S(2)}, u32[]{:S(2)}) collective-permute-start(bf16[2,4,96,384]{3,2,1,0:T(8,128)(2,1)S(1)} %get-tuple-element.174), channel_id=1, source_target_pairs={{0,2},{1,3},{2,0},{3,1},{4,6},{5,7},{6,4},{7,5},{8,10},{9,11},{10,... | collective-permute-start | bytes 1769480 | tf_op jit(solution)/shard_map/ppermute | solution.py:45
  198.8 24.1 %collective-permute-start.47 = (bf16[192,768]{1,0:T(8,128)(2,1)S(1)}, bf16[192,768]{1,0:T(8,128)(2,1)S(1)}, u32[]{:S(2)}, u32[]{:S(2)}) collective-permute-start(bf16[192,768]{1,0:T(8,128)(2,1)S(1)} %pad_maximum_fusion.9), channel_id=1, source_target_pairs={{0,8},{1,9},{2,10},{3,11},{4,12},{5,13},{6,14},{7,15},{8,0},{9,1},... | collective-permute-start | bytes 884744 | tf_op jit(solution)/shard_map/ppermute | solution.py:45
  199.4 23.5 %collective-permute-start.48 = (bf16[192,768]{1,0:T(8,128)(2,1)S(1)}, bf16[192,768]{1,0:T(8,128)(2,1)S(1)}, u32[]{:S(2)}, u32[]{:S(2)}) collective-permute-start(bf16[192,768]{1,0:T(8,128)(2,1)S(1)} %pad_maximum_fusion.10), channel_id=1, source_target_pairs={{0,16},{1,17},{2,18},{3,19},{4,20},{5,21},{6,22},{7,23},{8,24},{9,... | collective-permute-start | bytes 884744 | tf_op jit(solution)/shard_map/ppermute | solution.py:45
  202.0 21.0 %collective-permute-start.49 = (bf16[192,768]{1,0:T(8,128)(2,1)S(1)}, bf16[192,768]{1,0:T(8,128)(2,1)S(1)}, u32[]{:S(2)}, u32[]{:S(2)}) collective-permute-start(bf16[192,768]{1,0:T(8,128)(2,1)S(1)} %pad_maximum_fusion.11), channel_id=1, source_target_pairs={{0,24},{1,25},{2,26},{3,27},{4,28},{5,29},{6,30},{7,31},{8,16},{9,... | collective-permute-start | bytes 884744 | tf_op jit(solution)/shard_map/ppermute | solution.py:45
  229.9 18.2 %collective-permute-start.44 = (bf16[208,384]{1,0:T(8,128)(2,1)S(1)}, bf16[208,384]{1,0:T(8,128)(2,1)S(1)}, u32[]{:S(2)}, u32[]{:S(2)}) collective-permute-start(bf16[208,384]{1,0:T(8,128)(2,1)S(1)} %pad_maximum_fusion.14), channel_id=1, source_target_pairs={{0,16},{1,17},{2,18},{3,19},{4,20},{5,21},{6,22},{7,23},{8,24},{9,... | collective-permute-start | bytes 479240 | tf_op jit(solution)/shard_map/ppermute | solution.py:45
  (64 other events, 552.2 us)
